TPU v7x, 32 devices: a whole 2x2x4 slice. The times are simulated.
32 devices in a mesh: slab: 8 (over y, x, core), comp: 4 (over z).
Axes of the slice: x: 2, y: 2, z: 4, core: 2. Of those that a mesh axis runs over, the one named last changes fastest.
Arguments:
- current_field: float32 [3, 64, 64, 256], P(None, 'slab', 'comp'), may hold values from -6 to 6
- earlier_field: float32 [3, 64, 64, 256], P(None, 'slab', 'comp'), may hold values from -6 to 6
- wave_coef: float32 [64, 64, 256], P('slab', 'comp'), may hold values from 0.05 to 0.24
- layer_mask: int32 [64, 64, 256], P('slab', 'comp'), may hold values from 0 to 2
- point_xyz: float32 [3, 32768], P(None, ('slab', 'comp')), may hold values from 0 to 4
- point_owner: int32 [32768, 1], P(('slab', 'comp')), may hold values from 0 to 31; in each aligned block of 1024 rows (0 to 1023, 1024 to 2047, ...) at most 64 rows name the same one
- cell_offset: int32 [32768], P(('slab', 'comp')), may hold values from 0 to 32767
- wave_vector: float32 [3, 4096], P(None, 'comp'), may hold values from -8 to 8
- frequency: float32 [4096], P('comp'), may hold values from 0.5 to 8
- amplitude: float32 [3, 4096], P(None, 'comp'), may hold values from -0.09375 to 0.09375
- phase_index: int32 [4096], P('comp'), may hold values from 0 to 255
- phase_table: float32 [256], replicated, may hold values from -3.140625 to 3.140625
Outputs:
- final_field: float32 [3, 64, 64, 256], P(None, 'slab', 'comp')
- prior_field: float32 [3, 64, 64, 256], P(None, 'slab', 'comp')
Inputs may be any that keep to these rules, and one draw needn't show every extreme that they name: `point_owner`: the device at position s of slab and c of comp is numbered s times the size of comp plus c. Among the rows of one device at most 64 points name one owner.
All inputs are finite; a program needn't handle non-finite values.
Results may differ from a plain program's by a relative error of at most 0.0003.
Values sent between devices are 32-bit elements; how exact they have to be, the bound alone decides.
No kernel may reach another device: no remote copies, remote signals or barrier semaphores. Data moves between devices by JAX's collectives and lax.ppermute only.
A program may use at most 192 MiB of HBM per device.

v0:
```python
import jax
import jax.numpy as jnp
from jax import lax
from jax.sharding import PartitionSpec as P

STEPS = 3


step_size = 0.05
near_weight = 4.0 / 3.0
far_weight = -1.0 / 12.0
centre_weight = -7.5


def with_halo(block, sides, width):
    for axis, dim in sides:
        count = lax.axis_size(axis)
        forward = [(i, i + 1) for i in range(count - 1)]
        backward = [(target, source) for source, target in forward]
        low = lax.ppermute(
            lax.slice_in_dim(block, block.shape[dim] - width, None, axis=dim), axis, forward
        )
        high = lax.ppermute(lax.slice_in_dim(block, 0, width, axis=dim), axis, backward)
        block = jnp.concatenate([low, block, high], axis=dim)
    return block


def shifted(padded, axis_pos, offset):
    result = padded
    for dim_pos in (1, 2, 3):
        first_cell = 2 + offset if dim_pos == axis_pos else 2
        result = lax.slice_in_dim(
            result, first_cell, first_cell + padded.shape[dim_pos] - 4, axis=dim_pos
        )
    return result


def laplace_four(padded):
    summed = centre_weight * shifted(padded, 0, 0)
    for axis_pos in (1, 2, 3):
        summed = summed + near_weight * (
            shifted(padded, axis_pos, 1) + shifted(padded, axis_pos, -1)
        )
        summed = summed + far_weight * (
            shifted(padded, axis_pos, 2) + shifted(padded, axis_pos, -2)
        )
    return summed


def incident_terms(comp_block, coords):
    angles = (
        comp_block[0][:, None] * coords[0][None, :]
        + comp_block[1][:, None] * coords[1][None, :]
        + comp_block[2][:, None] * coords[2][None, :]
    )
    cosine = jnp.cos(angles)
    sine_part = jnp.sin(angles)
    moments = step_size * (jnp.arange(STEPS) + 1).astype(jnp.float32)
    delays = moments[:, None] * comp_block[3][None, :] - comp_block[7][None, :]
    block_width = comp_block.shape[1]
    left_cos = (jnp.cos(delays)[:, None, :] * comp_block[4:7][None, :, :]).reshape(
        STEPS * 3, block_width
    )
    left_sin = (jnp.sin(delays)[:, None, :] * comp_block[4:7][None, :, :]).reshape(
        STEPS * 3, block_width
    )
    first_part = jnp.dot(
        left_cos, cosine, precision=lax.Precision.HIGHEST, preferred_element_type=jnp.float32
    )
    second_part = jnp.dot(
        left_sin, sine_part, precision=lax.Precision.HIGHEST, preferred_element_type=jnp.float32
    )
    return first_part + second_part


def local(
    current_field,
    earlier_field,
    wave_coef,
    layer_mask,
    point_xyz,
    point_owner,
    cell_offset,
    wave_vector,
    frequency,
    amplitude,
    phase_index,
    phase_table,
):
    table_size = phase_table.shape[0]
    matches = (phase_index[None, :] == jnp.arange(table_size)[:, None]).astype(jnp.float32)
    phases = jnp.dot(
        phase_table[None, :],
        matches,
        precision=lax.Precision.HIGHEST,
        preferred_element_type=jnp.float32,
    )[0]
    own_block = jnp.concatenate(
        [wave_vector, frequency[None, :], amplitude, phases[None, :]], axis=0
    )
    point_count = point_xyz.shape[1]
    slab_count = lax.axis_size("slab")
    comp_count = lax.axis_size("comp")
    device_count = slab_count * comp_count
    slot_count = max(2, 2 * point_count // device_count)
    rows_out = STEPS * 3
    incident = incident_terms(lax.all_gather(own_block, "comp", axis=1, tiled=True), point_xyz)
    owners = point_owner[:, 0]
    matched = (owners[:, None] == jnp.arange(device_count)[None, :]).astype(jnp.int32)
    ranking = jnp.sum((jnp.cumsum(matched, axis=0) - 1) * matched, axis=1)
    value_index = (
        owners[None, :] * (rows_out * slot_count)
        + jnp.arange(rows_out)[:, None] * slot_count
        + ranking[None, :]
    )
    value_buffer = (
        jnp.zeros((device_count * rows_out * slot_count,), jnp.float32)
        .at[value_index.reshape(-1)]
        .set(incident.reshape(-1))
    )
    offset_buffer = (
        jnp.zeros((device_count * slot_count,), jnp.int32)
        .at[owners * slot_count + ranking]
        .set(cell_offset)
    )
    got_values, got_offsets = (
        lax.all_to_all(
            value_buffer.reshape(device_count, rows_out * slot_count),
            ("slab", "comp"),
            split_axis=0,
            concat_axis=0,
            tiled=True,
        ),
        lax.all_to_all(
            offset_buffer.reshape(device_count, slot_count),
            ("slab", "comp"),
            split_axis=0,
            concat_axis=0,
            tiled=True,
        ),
    )
    arrived = jnp.transpose(
        got_values.reshape(device_count, rows_out, slot_count), (1, 0, 2)
    ).reshape(rows_out, device_count * slot_count)
    cell_count = current_field.shape[1] * current_field.shape[2] * current_field.shape[3]
    forcing = (
        jnp.zeros((rows_out, cell_count), jnp.float32).at[:, got_offsets.reshape(-1)].add(arrived)
    )
    sign_field = ((layer_mask == 1).astype(jnp.float32) - (layer_mask == 2).astype(jnp.float32))[
        None
    ]
    current = current_field
    earlier = earlier_field
    for step_index in range(STEPS):
        widened = with_halo(current, (("slab", 1), ("comp", 2)), 2)
        padded = jnp.pad(widened, ((0, 0), (0, 0), (0, 0), (2, 2)))
        source = forcing[3 * step_index : 3 * step_index + 3].reshape(current.shape)
        following = (
            2.0 * current - earlier + wave_coef[None] * laplace_four(padded) + sign_field * source
        )
        earlier = current
        current = following
    return (current, earlier)


def solution(mesh):
    in_specs = (
        P(None, "slab", "comp", None),
        P(None, "slab", "comp", None),
        P("slab", "comp", None),
        P("slab", "comp", None),
        P(None, ("slab", "comp")),
        P(("slab", "comp"), None),
        P(("slab", "comp")),
        P(None, "comp"),
        P("comp"),
        P(None, "comp"),
        P("comp"),
        P(),
    )
    out_specs = (P(None, "slab", "comp", None), P(None, "slab", "comp", None))
    return jax.shard_map(local, mesh=mesh, in_specs=in_specs, out_specs=out_specs, check_vma=False)
```

profile of v0, /device:TPU:4, one launch (start us, length us, event | category | flops | bytes accessed | tf_op | source)
XLA Modules:
  0.0 345.5 jit_solution(13951917813462576049)
XLA Ops:
  0.6 0.0 copy-start
  0.7 0.7 fusion.82
  1.5 9.0 %reduce-window.6 = s32[32,8,128]{2,1,0:T(8,128)S(1)} reduce-window(s32[32,8,128]{2,1,0:T(8,128)S(1)} %fusion.82, s32[]{:T(128)} %constant.5.clone.1), window={size=1x1x128 pad=0_0x0_0x127_0}, to_apply=%region_0.0 | reduce-window | flops 4161536 | bytes 262148 | tf_op jit(solution)/shard_map/reduce-window
  10.5 0.1 slice.472
  10.6 0.1 copy.29
  10.7 0.1 copy.30
  10.8 0.1 add_add_fusion
  10.9 0.7 fusion.81
  11.7 0.7 compare_select_fusion.2
  12.4 4.5 %scatter_custom_fusion = s32[2048]{0:T(1024)S(1)} fusion(s32[1024]{0:T(1024)S(1)} %bitcast.70, s32[1024]{0:T(1024)} %param.18, s32[]{:T(128)} %constant.5.clone.1), kind=kCustom, calls=%fused_computation.165 | custom fusion | bytes 8704 | tf_op jit(solution)/shard_map/scatter | solution.py:124
  16.9 0.7 all_to_all.12
  17.5 6.1 %all-to-all-start = ((s32[32,1,64]{2,1,0:T(1,128)}), s32[32,1,64]{2,1,0:T(1,128)S(1)}, u32[]{:S(2)}, u32[]{:S(2)}) async-start(s32[32,1,64]{2,1,0:T(1,128)} %all_to_all.12), calls=%async_computation | async-start | bytes 32768 | tf_op jit(solution)/shard_map/all_to_all | solution.py:134
  23.7 2.0 collective-permute-start.1
  25.7 4.4 %collective-permute-start = (f32[3,2,16,256]{3,2,1,0:T(8,128)S(1)}, f32[3,2,16,256]{3,2,1,0:T(8,128)S(1)}, u32[]{:S(2)}, u32[]{:S(2)}) collective-permute-start(f32[3,2,16,256]{3,2,1,0:T(8,128)S(1)} %get-tuple-element.18), channel_id=1, source_target_pairs={{4,0},{8,4},{12,8},{16,12},{20,16},{24,20},{28,24},{5,1},{9,5},{13... | collective-permute-start | bytes 294920 | tf_op jit(solution)/shard_map/ppermute | solution.py:23
  30.2 0.4 fusion.22
  30.7 13.5 %all_gather.3 = f32[8,4096]{1,0:T(8,128)S(1)} all-gather(f32[8,1024]{1,0:T(8,128)S(1)} %pad_maximum_fusion.24), channel_id=1, replica_groups=mesh['slab'=8,'comp'=4] {'comp'}, dimensions={1}, use_global_device_ids=true | all-gather | bytes 163840 | tf_op jit(solution)/shard_map/all_gather | solution.py:107
  44.1 0.1 fusion.94
  44.3 0.5 fusion.84
  44.8 0.1 broadcast_multiply_fusion.1
  44.9 0.1 mul.296
  45.0 0.1 mul.278
  45.1 0.1 add_bitcast_fusion
  45.2 66.0 %fusion = f32[9,1024]{1,0:T(8,128)S(1)} fusion(f32[9,4096]{1,0:T(8,128)S(1)} %mul.296, f32[1024]{0:T(1024)S(1)} %bitcast.73, f32[4096]{0:T(1024)S(1)} %bitcast.63, f32[1024]{0:T(1024)S(1)} %bitcast.75, f32[4096]{0:T(1024)S(1)} %bitcast.65, f32[1024]{0:T(1024)S(1)} %bitcast.71, f32[4096]{0:T(1024)S(1)} %bitcast.61), kind=kOutput, calls=%fused_computation.3 | convolution fusion | flops 473956352 | bytes 245760 | tf_op jit(solution)/shard_map/dot_general | solution.py:70
  111.2 65.0 %fusion.19 = f32[9,1024]{1,0:T(8,128)S(1)} fusion(f32[9,1024]{1,0:T(8,128)S(1)} %fusion, f32[9,4096]{1,0:T(8,128)S(1)} %mul.278, f32[1024]{0:T(1024)S(1)} %bitcast.74, f32[4096]{0:T(1024)S(1)} %bitcast.64, f32[1024]{0:T(1024)S(1)} %bitcast.76, f32[4096]{0:T(1024)S(1)} %bitcast.66, f32[1024]{0:T(1024)S(1)} %bitcast.72, f32[4096]{0:T(1024)S(1)} %bitcast.62), kind=kOutput, calls=%fused_computation.35 | convolution fusion | flops 473965568 | bytes 282624 | tf_op jit(solution)/shard_map/dot_general | solution.py:67
  176.3 34.2 %scatter_custom_fusion.1 = f32[18432]{0:T(1024)S(1)} fusion(s32[9216]{0:T(1024)S(1)} %bitcast.60, f32[9216]{0:T(1024)S(1)} %reshape.255, f32[]{:T(128)} %constant.19.clone.1), kind=kCustom, calls=%fused_computation.154 | custom fusion | bytes 73732 | tf_op jit(solution)/shard_map/scatter | solution.py:119
  210.5 0.8 all_to_all.14
  211.2 4.9 %all-to-all-start.1 = ((f32[32,1,576]{2,1,0:T(1,128)}), f32[32,1,576]{2,1,0:T(1,128)S(1)}, u32[]{:S(2)}, u32[]{:S(2)}) async-start(f32[32,1,576]{2,1,0:T(1,128)} %all_to_all.14), calls=%async_computation.1 | async-start | bytes 163840 | tf_op jit(solution)/shard_map/all_to_all | solution.py:127
  216.1 0.5 broadcast.240
  216.6 0.7 reduce.4
  217.3 0.1 reshape.236
  217.5 0.1 constant_dynamic-update-slice_fusion.1
  217.6 0.1 fusion.90
  217.7 1.3 collective-permute-start.2
  219.0 4.5 %collective-permute-start.3 = (f32[3,12,2,256]{3,2,1,0:T(2,128)S(1)}, f32[3,12,2,256]{3,2,1,0:T(2,128)S(1)}, u32[]{:S(2)}, u32[]{:S(2)}) collective-permute-start(f32[3,12,2,256]{3,2,1,0:T(2,128)S(1)} %get-tuple-element.9), channel_id=1, source_target_pairs={{0,1},{1,2},{2,3},{4,5},{5,6},{6,7},{8,9},{9,10},{10,11},{12,13},{... | collective-permute-start | bytes 221192 | tf_op jit(solution)/shard_map/ppermute | solution.py:20
  223.6 0.2 reduce.1
  223.8 0.1 reshape.238
  223.9 0.1 copy.31
  223.9 0.1 reshape.260
  224.0 1.4 copy.32
  225.4 20.2 %scatter_custom_fusion.2 = f32[9,32768]{0,1:T(8,128)} fusion(s32[2048]{0:T(1024)S(1)} %bitcast.68, f32[2048,9]{1,0:T(8,128)} %copy.32, f32[]{:T(128)} %constant.19.clone.1), kind=kCustom, calls=%fused_computation.20 | custom fusion | flops 18432 | bytes 1180160 | tf_op jit(solution)/shard_map/scatter-add | solution.py:147
  245.5 34.8 %fusion.89 = (f32[3,32768]{0,1:T(8,128)}, f32[3,32768]{0,1:T(8,128)}, f32[3,32768]{0,1:T(8,128)}) fusion(f32[9,32768]{0,1:T(8,128)} %scatter_custom_fusion.2), kind=kLoop, calls=%fused_computation.170 | loop fusion | bytes 2359296 | tf_op jit(solution)/shard_map/slice | solution.py:157
  280.3 10.0 %copy.33 = f32[3,8,16,256]{3,2,1,0:T(8,128)S(1)} copy(f32[3,8,16,256]{0,3,2,1:T(8,128)} %bitcast.49) | data formatting | bytes 786432 | tf_op jit(solution)/shard_map/reshape | solution.py:157
  290.3 0.7 select_maximum_fusion.8
  291.0 0.2 copy-done.4
  291.2 0.2 copy-done.5
  291.4 0.6 fusion.68
  292.0 1.9 collective-permute-start.4
  293.9 2.4 collective-permute-start.5
  296.4 4.4 %collective-permute-done.5 = f32[3,2,16,256]{3,2,1,0:T(8,128)S(1)} collective-permute-done((f32[3,2,16,256]{3,2,1,0:T(8,128)S(1)}, f32[3,2,16,256]{3,2,1,0:T(8,128)S(1)}, u32[]{:S(2)}, u32[]{:S(2)}) %collective-permute-start.5) | collective-permute-done | bytes 98336 | tf_op jit(solution)/shard_map/ppermute | solution.py:20
  300.8 0.1 pad_maximum_fusion.21
  300.8 1.3 collective-permute-start.6
  302.1 4.6 %collective-permute-start.7 = (f32[3,12,2,256]{3,2,1,0:T(2,128)S(1)}, f32[3,12,2,256]{3,2,1,0:T(2,128)S(1)}, u32[]{:S(2)}, u32[]{:S(2)}) collective-permute-start(f32[3,12,2,256]{3,2,1,0:T(2,128)S(1)} %get-tuple-element.7), channel_id=1, source_target_pairs={{0,1},{1,2},{2,3},{4,5},{5,6},{6,7},{8,9},{9,10},{10,11},{12,13},{... | collective-permute-start | bytes 221192 | tf_op jit(solution)/shard_map/ppermute | solution.py:20
  306.7 10.2 %copy.34 = f32[3,8,16,256]{3,2,1,0:T(8,128)S(1)} copy(f32[3,8,16,256]{0,3,2,1:T(8,128)} %bitcast.48) | data formatting | bytes 786432 | tf_op jit(solution)/shard_map/reshape | solution.py:157
  317.0 0.7 select_maximum_fusion.4
  317.7 0.7 fusion.48
  318.4 1.9 collective-permute-start.8
  320.3 2.4 collective-permute-start.9
  322.7 4.4 %collective-permute-done.9 = f32[3,2,16,256]{3,2,1,0:T(8,128)S(1)} collective-permute-done((f32[3,2,16,256]{3,2,1,0:T(8,128)S(1)}, f32[3,2,16,256]{3,2,1,0:T(8,128)S(1)}, u32[]{:S(2)}, u32[]{:S(2)}) %collective-permute-start.9) | collective-permute-done | bytes 98336 | tf_op jit(solution)/shard_map/ppermute | solution.py:20
  327.1 0.1 pad_maximum_fusion.18
  327.2 1.3 collective-permute-start.10
  328.5 4.6 %collective-permute-start.11 = (f32[3,12,2,256]{3,2,1,0:T(2,128)S(1)}, f32[3,12,2,256]{3,2,1,0:T(2,128)S(1)}, u32[]{:S(2)}, u32[]{:S(2)}) collective-permute-start(f32[3,12,2,256]{3,2,1,0:T(2,128)S(1)} %get-tuple-element.5), channel_id=1, source_target_pairs={{0,1},{1,2},{2,3},{4,5},{5,6},{6,7},{8,9},{9,10},{10,11},{12,13},{... | collective-permute-start | bytes 221192 | tf_op jit(solution)/shard_map/ppermute | solution.py:20
  333.1 10.0 %copy.35 = f32[3,8,16,256]{3,2,1,0:T(8,128)S(1)} copy(f32[3,8,16,256]{0,3,2,1:T(8,128)} %bitcast.47) | data formatting | bytes 786432 | tf_op jit(solution)/shard_map/reshape | solution.py:157
  343.1 0.7 select_maximum_fusion
  343.8 1.4 fusion.35
  (53 shorter events, 0.4 us)
Async XLA Ops:
  0.6 29.5 %copy-start = (f32[256]{0:T(256)S(1)}, f32[256]{0:T(256)}, u32[]{:S(2)}) copy-start(f32[256]{0:T(256)} %param.23) | copy-start | bytes 3076
  0.6 43.6 %copy-start.7 = (s32[1024,1]{0,1:T(1,128)S(1)}, s32[1024,1]{0,1:T(1,128)}, u32[]{:S(2)}) copy-start(s32[1024,1]{0,1:T(1,128)} %param.17) | copy-start | bytes 12292
  0.7 23.0 %copy-start.3 = (f32[3,8,16,256]{3,2,1,0:T(8,128)S(1)}, f32[3,8,16,256]{3,2,1,0:T(8,128)}, u32[]{:S(2)}) copy-start(f32[3,8,16,256]{3,2,1,0:T(8,128)} %param.12) | copy-start | bytes 1179652
  0.7 29.5 %copy-start.12 = (s32[1024]{0:T(1024)S(1)}, s32[1024]{0:T(1024)}, u32[]{:S(2)}) copy-start(s32[1024]{0:T(1024)} %param.22) | copy-start | bytes 12292
  0.7 29.9 %copy-start.11 = (f32[1024]{0:T(1024)S(1)}, f32[1024]{0:T(1024)}, u32[]{:S(2)}) copy-start(f32[1024]{0:T(1024)} %param.20) | copy-start | bytes 12292
  0.7 29.9 %copy-start.9 = (f32[3,1024]{1,0:T(4,128)S(1)}, f32[3,1024]{1,0:T(4,128)}, u32[]{:S(2)}) copy-start(f32[3,1024]{1,0:T(4,128)} %param.19) | copy-start | bytes 36868
  0.7 29.9 %copy-start.8 = (f32[3,1024]{1,0:T(4,128)S(1)}, f32[3,1024]{1,0:T(4,128)}, u32[]{:S(2)}) copy-start(f32[3,1024]{1,0:T(4,128)} %param.21) | copy-start | bytes 36868
  10.9 34.0 %copy-start.10 = (f32[3,1024]{1,0:T(4,128)S(1)}, f32[3,1024]{1,0:T(4,128)}, u32[]{:S(2)}) copy-start(f32[3,1024]{1,0:T(4,128)} %param.16) | copy-start | bytes 36868
  17.5 193.7 %all-to-all-start = ((s32[32,1,64]{2,1,0:T(1,128)}), s32[32,1,64]{2,1,0:T(1,128)S(1)}, u32[]{:S(2)}, u32[]{:S(2)}) async-start(s32[32,1,64]{2,1,0:T(1,128)} %all_to_all.12), calls=%async_computation | async-start | bytes 32768 | tf_op jit(solution)/shard_map/all_to_all | solution.py:134
  23.7 193.7 %collective-permute-start.1 = (f32[3,2,16,256]{3,2,1,0:T(8,128)S(1)}, f32[3,2,16,256]{3,2,1,0:T(8,128)S(1)}, u32[]{:S(2)}, u32[]{:S(2)}) collective-permute-start(f32[3,2,16,256]{3,2,1,0:T(8,128)S(1)} %get-tuple-element.19), channel_id=1, source_target_pairs={{0,4},{4,8},{8,12},{12,16},{16,20},{20,24},{24,28},{1,5},{5,9},{9,... | collective-permute-start | bytes 294920 | tf_op jit(solution)/shard_map/ppermute | solution.py:20
  25.7 191.9 %collective-permute-start = (f32[3,2,16,256]{3,2,1,0:T(8,128)S(1)}, f32[3,2,16,256]{3,2,1,0:T(8,128)S(1)}, u32[]{:S(2)}, u32[]{:S(2)}) collective-permute-start(f32[3,2,16,256]{3,2,1,0:T(8,128)S(1)} %get-tuple-element.18), channel_id=1, source_target_pairs={{4,0},{8,4},{12,8},{16,12},{20,16},{24,20},{28,24},{5,1},{9,5},{13... | collective-permute-start | bytes 294920 | tf_op jit(solution)/shard_map/ppermute | solution.py:23
  111.2 65.0 %copy-start.6 = (s32[8,16,256]{2,1,0:T(8,128)S(1)}, s32[8,16,256]{2,1,0:T(8,128)}, u32[]{:S(2)}) copy-start(s32[8,16,256]{2,1,0:T(8,128)} %param.15) | copy-start | bytes 393220
  211.2 12.3 %all-to-all-start.1 = ((f32[32,1,576]{2,1,0:T(1,128)}), f32[32,1,576]{2,1,0:T(1,128)S(1)}, u32[]{:S(2)}, u32[]{:S(2)}) async-start(f32[32,1,576]{2,1,0:T(1,128)} %all_to_all.14), calls=%async_computation.1 | async-start | bytes 163840 | tf_op jit(solution)/shard_map/all_to_all | solution.py:127
  217.7 72.6 %collective-permute-start.2 = (f32[3,12,2,256]{3,2,1,0:T(2,128)S(1)}, f32[3,12,2,256]{3,2,1,0:T(2,128)S(1)}, u32[]{:S(2)}, u32[]{:S(2)}) collective-permute-start(f32[3,12,2,256]{3,2,1,0:T(2,128)S(1)} %get-tuple-element.10), channel_id=1, source_target_pairs={{1,0},{2,1},{3,2},{5,4},{6,5},{7,6},{9,8},{10,9},{11,10},{13,12},{... | collective-permute-start | bytes 221192 | tf_op jit(solution)/shard_map/ppermute | solution.py:23
  219.0 71.3 %collective-permute-start.3 = (f32[3,12,2,256]{3,2,1,0:T(2,128)S(1)}, f32[3,12,2,256]{3,2,1,0:T(2,128)S(1)}, u32[]{:S(2)}, u32[]{:S(2)}) collective-permute-start(f32[3,12,2,256]{3,2,1,0:T(2,128)S(1)} %get-tuple-element.9), channel_id=1, source_target_pairs={{0,1},{1,2},{2,3},{4,5},{5,6},{6,7},{8,9},{9,10},{10,11},{12,13},{... | collective-permute-start | bytes 221192 | tf_op jit(solution)/shard_map/ppermute | solution.py:20
  290.3 0.9 copy-start.4
  290.3 1.1 copy-start.5
  292.0 4.3 %collective-permute-start.4 = (f32[3,2,16,256]{3,2,1,0:T(8,128)S(1)}, f32[3,2,16,256]{3,2,1,0:T(8,128)S(1)}, u32[]{:S(2)}, u32[]{:S(2)}) collective-permute-start(f32[3,2,16,256]{3,2,1,0:T(8,128)S(1)} %get-tuple-element.13), channel_id=1, source_target_pairs={{4,0},{8,4},{12,8},{16,12},{20,16},{24,20},{28,24},{5,1},{9,5},{13... | collective-permute-start | bytes 294920 | tf_op jit(solution)/shard_map/ppermute | solution.py:23
  293.9 6.8 %collective-permute-start.5 = (f32[3,2,16,256]{3,2,1,0:T(8,128)S(1)}, f32[3,2,16,256]{3,2,1,0:T(8,128)S(1)}, u32[]{:S(2)}, u32[]{:S(2)}) collective-permute-start(f32[3,2,16,256]{3,2,1,0:T(8,128)S(1)} %get-tuple-element.14), channel_id=1, source_target_pairs={{0,4},{4,8},{8,12},{12,16},{16,20},{20,24},{24,28},{1,5},{5,9},{9,... | collective-permute-start | bytes 294920 | tf_op jit(solution)/shard_map/ppermute | solution.py:20
  300.8 16.1 %collective-permute-start.6 = (f32[3,12,2,256]{3,2,1,0:T(2,128)S(1)}, f32[3,12,2,256]{3,2,1,0:T(2,128)S(1)}, u32[]{:S(2)}, u32[]{:S(2)}) collective-permute-start(f32[3,12,2,256]{3,2,1,0:T(2,128)S(1)} %get-tuple-element.8), channel_id=1, source_target_pairs={{1,0},{2,1},{3,2},{5,4},{6,5},{7,6},{9,8},{10,9},{11,10},{13,12},{... | collective-permute-start | bytes 221192 | tf_op jit(solution)/shard_map/ppermute | solution.py:23
  302.1 14.8 %collective-permute-start.7 = (f32[3,12,2,256]{3,2,1,0:T(2,128)S(1)}, f32[3,12,2,256]{3,2,1,0:T(2,128)S(1)}, u32[]{:S(2)}, u32[]{:S(2)}) collective-permute-start(f32[3,12,2,256]{3,2,1,0:T(2,128)S(1)} %get-tuple-element.7), channel_id=1, source_target_pairs={{0,1},{1,2},{2,3},{4,5},{5,6},{6,7},{8,9},{9,10},{10,11},{12,13},{... | collective-permute-start | bytes 221192 | tf_op jit(solution)/shard_map/ppermute | solution.py:20
  318.3 25.5 %copy-start.2 = (f32[3,8,16,256]{3,2,1,0:T(8,128)}, f32[3,8,16,256]{3,2,1,0:T(8,128)S(1)}, u32[]{:S(2)}) copy-start(f32[3,8,16,256]{3,2,1,0:T(8,128)S(1)} %fusion.48) | copy-start | bytes 1179652
  318.4 4.3 %collective-permute-start.8 = (f32[3,2,16,256]{3,2,1,0:T(8,128)S(1)}, f32[3,2,16,256]{3,2,1,0:T(8,128)S(1)}, u32[]{:S(2)}, u32[]{:S(2)}) collective-permute-start(f32[3,2,16,256]{3,2,1,0:T(8,128)S(1)} %get-tuple-element.11), channel_id=1, source_target_pairs={{4,0},{8,4},{12,8},{16,12},{20,16},{24,20},{28,24},{5,1},{9,5},{13... | collective-permute-start | bytes 294920 | tf_op jit(solution)/shard_map/ppermute | solution.py:23
  320.3 6.8 %collective-permute-start.9 = (f32[3,2,16,256]{3,2,1,0:T(8,128)S(1)}, f32[3,2,16,256]{3,2,1,0:T(8,128)S(1)}, u32[]{:S(2)}, u32[]{:S(2)}) collective-permute-start(f32[3,2,16,256]{3,2,1,0:T(8,128)S(1)} %get-tuple-element.12), channel_id=1, source_target_pairs={{0,4},{4,8},{8,12},{12,16},{16,20},{20,24},{24,28},{1,5},{5,9},{9,... | collective-permute-start | bytes 294920 | tf_op jit(solution)/shard_map/ppermute | solution.py:20
  327.2 15.8 %collective-permute-start.10 = (f32[3,12,2,256]{3,2,1,0:T(2,128)S(1)}, f32[3,12,2,256]{3,2,1,0:T(2,128)S(1)}, u32[]{:S(2)}, u32[]{:S(2)}) collective-permute-start(f32[3,12,2,256]{3,2,1,0:T(2,128)S(1)} %get-tuple-element.6), channel_id=1, source_target_pairs={{1,0},{2,1},{3,2},{5,4},{6,5},{7,6},{9,8},{10,9},{11,10},{13,12},{... | collective-permute-start | bytes 221192 | tf_op jit(solution)/shard_map/ppermute | solution.py:23
  328.5 14.6 %collective-permute-start.11 = (f32[3,12,2,256]{3,2,1,0:T(2,128)S(1)}, f32[3,12,2,256]{3,2,1,0:T(2,128)S(1)}, u32[]{:S(2)}, u32[]{:S(2)}) collective-permute-start(f32[3,12,2,256]{3,2,1,0:T(2,128)S(1)} %get-tuple-element.5), channel_id=1, source_target_pairs={{0,1},{1,2},{2,3},{4,5},{5,6},{6,7},{8,9},{9,10},{10,11},{12,13},{... | collective-permute-start | bytes 221192 | tf_op jit(solution)/shard_map/ppermute | solution.py:20
  343.1 2.2 copy-start.1
where the time goes:
time: 350 us; the launch traced here: 345 us
  matrix products  131 us (37%)
  local copies, waits for them, and re-layouts  109 us (31%)
  starting transfers between devices  43.6 us (12%)
  other arithmetic  38.1 us (11%)
  blocking collectives  13.5 us (4%)
  waiting for transfers between devices  8.85 us (3%)
    dot_general x1, matrix products, incident_terms(): jnp.dot(left_sin, sine_part, precision=lax.Precision.HIGHEST, preferred_e...  66 us
    dot_general x1, matrix products, incident_terms(): jnp.dot(left_cos, cosine, precision=lax.Precision.HIGHEST, preferred_elem...  65 us
    slice x1, local copies, waits for them, and re-layouts, local(): source = forcing[3 * step_index:3 * step_index + 3].reshape(current.shape)  34.8 us
    scatter x1, local copies, waits for them, and re-layouts, local(): value_buffer = jnp.zeros((device_count * rows_out * slot_count,), jnp.flo...  34.2 us
    reshape x3, local copies, waits for them, and re-layouts, local(): source = forcing[3 * step_index:3 * step_index + 3].reshape(current.shape)  30.2 us
    ppermute x6, starting transfers between devices, with_halo(): lax.ppermute(lax.slice_in_dim(block, block.shape[dim] - width, None, axis...  20.5 us
    scatter-add x1, other arithmetic, local(): jnp.zeros((rows_out, cell_count), jnp.float32)  20.2 us
    all_gather x1, blocking collectives, local(): lax.all_gather(own_block, 'comp', axis=1, tiled=True)  13.5 us
  transfers between devices with their start and end apart: 14, of which 2 were waited for; matrix products, arithmetic and copies ran while one was open for 74% of the time, Pallas kernels for 0%

commit v1 on v0

v1 whole, which is shorter than its diff:
```python
import jax
import jax.numpy as jnp
from jax import lax
from jax.experimental import pallas as pl
from jax.experimental.pallas import tpu as pltpu
from jax.sharding import PartitionSpec as P

STEPS = 3
step_size = 0.05
near_weight = 4.0 / 3.0
far_weight = -1.0 / 12.0
centre_weight = -7.5
inv_two_pi = 0.15915494309189535
round_magic = 12582912.0

SIN_C = (4.4428679, -7.30744342, 3.59478806, -0.78437398)
COS_C = (1.4142135, -6.97885099, 5.73946117, -1.88356299, 0.31069819)

F32 = jnp.float32
BF16 = jnp.bfloat16


def horner(coefs, z):
    out = coefs[-1] * z + coefs[-2]
    for c in coefs[-3::-1]:
        out = out * z + c
    return out


def sincos_turns(u):
    r = u - ((u + round_magic) - round_magic)
    z = r * r
    s = r * horner(SIN_C, z)
    c = horner(COS_C, z)
    return s * c, 1.0 - s * s


def split_three(x):
    hi = x.astype(BF16).astype(F32)
    rest = x - hi
    mid = rest.astype(BF16).astype(F32)
    return hi, mid, rest - mid


def row_ids(shape):
    return lax.broadcasted_iota(jnp.int32, shape, 0)


def incident_kernel(slot_count, owner_count, par_ref, xyz_ref, own_ref, off_ref, out_ref, x8_ref, acc_ref):
    comps = par_ref.shape[1]
    points = xyz_ref.shape[1]
    kc = 256
    tile = 256
    x8_ref[...] = jnp.zeros(x8_ref.shape, F32)
    x8_ref[0:3, :] = xyz_ref[...]
    xhi, xmid, xlo = split_three(x8_ref[...])
    right = jnp.concatenate([xhi, xmid, xlo, xhi, xmid, xhi], axis=0).astype(BF16)
    acc_ref[...] = jnp.zeros(acc_ref.shape, F32)
    rows8 = row_ids((8, kc))
    times = step_size * (rows8 + 1).astype(F32)
    rows16 = row_ids((16, kc))
    comp_row = rows16 % 3

    def body(step, carry):
        blk = par_ref[:, pl.ds(pl.multiple_of(step * kc, kc), kc)]
        kv = jnp.where(rows8 < 3, blk * inv_two_pi, 0.0)
        khi, kmid, klo = split_three(kv)
        left = jnp.concatenate([khi, khi, khi, kmid, kmid, klo], axis=0).astype(BF16)
        delays = times * blk[3:4, :] - blk[7:8, :]
        sd, cd = sincos_turns(delays * inv_two_pi)
        amp = jnp.where(comp_row == 0, blk[4:5, :], jnp.where(comp_row == 1, blk[5:6, :], blk[6:7, :]))
        amp = jnp.where(rows16 < 9, amp, 0.0)

        def rows_of(t):
            w = amp * jnp.where(rows16 < 3, t[0:1, :], jnp.where(rows16 < 6, t[1:2, :], t[2:3, :]))
            hi = w.astype(BF16)
            lo = (w - hi.astype(F32)).astype(BF16)
            return jnp.concatenate([hi, lo], axis=0)

        lc = rows_of(cd)
        ls = rows_of(sd)
        for t in range(points // tile):
            cols = slice(t * tile, (t + 1) * tile)
            u = lax.dot_general(left, right[:, cols], (((0,), (0,)), ((), ())), preferred_element_type=F32)
            highs, lows = [], []
            for j in range(kc // 32):
                for value in sincos_turns(u[32 * j : 32 * j + 32]):
                    high = value.astype(BF16)
                    highs.append(high)
                    lows.append((value - high.astype(F32)).astype(BF16))
            part = jnp.dot(ls, jnp.concatenate(highs[0::2], axis=0), preferred_element_type=F32)
            part += jnp.dot(lc, jnp.concatenate(highs[1::2], axis=0), preferred_element_type=F32)
            part += jnp.dot(ls, jnp.concatenate(lows[0::2], axis=0), preferred_element_type=F32)
            part += jnp.dot(lc, jnp.concatenate(lows[1::2], axis=0), preferred_element_type=F32)
            acc_ref[:, cols] += part
        return carry

    lax.fori_loop(0, comps // kc, body, 0)
    vals = acc_ref[0:16, :] + acc_ref[16:32, :]
    prow = row_ids((16, points))
    vals = jnp.where(prow == 9, off_ref[...].astype(F32), vals)
    v1, v2, v3 = split_three(vals)
    vals3 = jnp.concatenate([v1, v2, v3], axis=0).astype(BF16)
    lanes = -(-owner_count // 128) * 128
    lane = lax.broadcasted_iota(jnp.int32, (points, lanes), 1)
    named = own_ref[...] == lane
    lower = lax.broadcasted_iota(jnp.int32, (points, points), 1) < row_ids((points, points))
    before = jnp.dot(lower.astype(F32).astype(BF16), named.astype(F32).astype(BF16), preferred_element_type=F32)
    slot = jnp.sum(jnp.where(named, before + (lane * slot_count).astype(F32), 0.0), axis=1, keepdims=True)
    slot = slot.astype(jnp.int32)
    width = 512
    slots = out_ref.shape[1]
    for t in range(slots // width):
        spot = lax.broadcasted_iota(jnp.int32, (points, width), 1) + t * width
        one_hot = (slot == spot).astype(F32).astype(BF16)
        got = jnp.dot(vals3, one_hot, preferred_element_type=F32)
        out_ref[:, t * width : (t + 1) * width] = got[0:16] + got[16:32] + got[32:48]


def scatter_kernel(nz, val_ref, out_ref):
    count = val_ref.shape[1]
    rows = out_ref.shape[1]
    chunk = 256
    out_ref[...] = jnp.zeros(out_ref.shape, F32)

    def body(step, carry):
        blk = val_ref[:, pl.ds(pl.multiple_of(step * chunk, chunk), chunk)]
        off = blk[9:10, :].astype(jnp.int32)
        row = off // nz
        lz = off - row * nz
        zt = (row_ids((nz, chunk)) == lz).astype(F32).astype(BF16)
        mask = (row_ids((rows, chunk)) == row).astype(F32).astype(BF16)
        hi = blk.astype(BF16)
        lo = (blk - hi.astype(F32)).astype(BF16)
        for i in range(9):
            left = jnp.concatenate([mask * hi[i : i + 1, :], mask * lo[i : i + 1, :]], axis=0)
            got = lax.dot_general(left, zt, (((1,), (1,)), ((), ())), preferred_element_type=F32)
            out_ref[i] += got[0:rows] + got[rows:]
        return carry

    lax.fori_loop(0, count // chunk, body, 0)


def with_halo(block, sides, width):
    for axis, dim in sides:
        count = lax.axis_size(axis)
        forward = [(i, i + 1) for i in range(count - 1)]
        backward = [(target, source) for source, target in forward]
        low = lax.ppermute(
            lax.slice_in_dim(block, block.shape[dim] - width, None, axis=dim), axis, forward
        )
        high = lax.ppermute(lax.slice_in_dim(block, 0, width, axis=dim), axis, backward)
        block = jnp.concatenate([low, block, high], axis=dim)
    return block


def shifted(padded, axis_pos, offset):
    result = padded
    for dim_pos in (1, 2, 3):
        first_cell = 2 + offset if dim_pos == axis_pos else 2
        result = lax.slice_in_dim(
            result, first_cell, first_cell + padded.shape[dim_pos] - 4, axis=dim_pos
        )
    return result


def laplace_four(padded):
    summed = centre_weight * shifted(padded, 0, 0)
    for axis_pos in (1, 2, 3):
        summed = summed + near_weight * (
            shifted(padded, axis_pos, 1) + shifted(padded, axis_pos, -1)
        )
        summed = summed + far_weight * (
            shifted(padded, axis_pos, 2) + shifted(padded, axis_pos, -2)
        )
    return summed


def local(
    current_field,
    earlier_field,
    wave_coef,
    layer_mask,
    point_xyz,
    point_owner,
    cell_offset,
    wave_vector,
    frequency,
    amplitude,
    phase_index,
    phase_table,
):
    table_size = phase_table.shape[0]
    matches = (phase_index[None, :] == jnp.arange(table_size)[:, None]).astype(F32)
    phases = jnp.dot(
        phase_table[None, :], matches, precision=lax.Precision.HIGHEST, preferred_element_type=F32
    )[0]
    own_block = jnp.concatenate(
        [wave_vector, frequency[None, :], amplitude, phases[None, :]], axis=0
    )
    point_count = point_xyz.shape[1]
    slab_count = lax.axis_size("slab")
    comp_count = lax.axis_size("comp")
    device_count = slab_count * comp_count
    slot_count = max(2, 2 * point_count // device_count)
    rows_out = STEPS * 3
    blocks = [own_block]
    for shift in range(1, comp_count):
        ring = [(i, (i + shift) % comp_count) for i in range(comp_count)]
        blocks.append(lax.ppermute(own_block, "comp", ring))
    params = jnp.concatenate(blocks, axis=1)
    slots = device_count * slot_count
    packed = pl.pallas_call(
        lambda *refs: incident_kernel(slot_count, device_count, *refs),
        out_shape=jax.ShapeDtypeStruct((16, slots), F32),
        scratch_shapes=[pltpu.VMEM((8, point_count), F32), pltpu.VMEM((32, point_count), F32)],
        name="incident",
    )(params, point_xyz, point_owner, cell_offset[None, :])
    rows_sent = rows_out + 1
    sent = jnp.transpose(
        packed[:rows_sent].reshape(rows_sent, device_count, slot_count), (1, 0, 2)
    ).reshape(device_count, rows_sent * slot_count)
    got = lax.all_to_all(sent, ("slab", "comp"), split_axis=0, concat_axis=0, tiled=True)
    arrived = jnp.transpose(
        got.reshape(device_count, rows_sent, slot_count), (1, 0, 2)
    ).reshape(rows_sent, slots)
    cx, cy, nz = current_field.shape[1:]
    forcing = pl.pallas_call(
        lambda *refs: scatter_kernel(nz, *refs),
        out_shape=jax.ShapeDtypeStruct((rows_out, cx * cy, nz), F32),
        name="scatter",
    )(arrived)
    forcing = forcing.reshape(rows_out, cx, cy, nz)
    sign_field = ((layer_mask == 1).astype(F32) - (layer_mask == 2).astype(F32))[None]
    current = current_field
    earlier = earlier_field
    for step_index in range(STEPS):
        widened = with_halo(current, (("slab", 1), ("comp", 2)), 2)
        padded = jnp.pad(widened, ((0, 0), (0, 0), (0, 0), (2, 2)))
        source = forcing[3 * step_index : 3 * step_index + 3]
        following = (
            2.0 * current - earlier + wave_coef[None] * laplace_four(padded) + sign_field * source
        )
        earlier = current
        current = following
    return (current, earlier)


def solution(mesh):
    in_specs = (
        P(None, "slab", "comp", None),
        P(None, "slab", "comp", None),
        P("slab", "comp", None),
        P("slab", "comp", None),
        P(None, ("slab", "comp")),
        P(("slab", "comp"), None),
        P(("slab", "comp")),
        P(None, "comp"),
        P("comp"),
        P(None, "comp"),
        P("comp"),
        P(),
    )
    out_specs = (P(None, "slab", "comp", None), P(None, "slab", "comp", None))
    return jax.shard_map(local, mesh=mesh, in_specs=in_specs, out_specs=out_specs, check_vma=False)
```

time: 350 us -> 119 us (0.34); the launches traced: 345 us -> 118 us
  matrix products: 131 us -> 1.12 us
  local copies, waits for them, and re-layouts: 109 us -> 12.6 us
  Pallas kernels: 0 us -> 34.9 us
  other arithmetic: 38.1 us -> 7.94 us
  waiting for transfers between devices: 8.85 us -> 23.6 us
  blocking collectives: 13.5 us -> 0 us
  starting transfers between devices: 43.6 us -> 37.1 us
    dot_general x2 -> x0, matrix products: 131 us -> none  [the longest x1 66 us: incident_terms(): jnp.dot(left_sin, sine_part, precision=lax.Precision.HIGHEST, preferred_e...]
    scatter x2 -> x0, local copies, waits for them, and re-layouts: 38.7 us -> none  [the longest x1 34.2 us: local(): value_buffer = jnp.zeros((device_count * rows_out * slot_count,), jnp.flo...]
    pallas_call x0 -> x2, Pallas kernels: none -> 34.9 us  [the longest x1 28.7 us: local(): pl.pallas_call(lambda *refs: incident_kernel(slot_count, device_count, *r...]
    slice x6 -> x1, local copies, waits for them, and re-layouts: 35.1 us -> 1.38 us  [local(): source = forcing[3 * step_index:3 * step_index + 3]]
    reshape x8 -> x4, local copies, waits for them, and re-layouts: 31.8 us -> 4.45 us  [the longest x1 1.68 us: local(): got.reshape(device_count, rows_sent, slot_count)]
    scatter-add x1 -> x0, other arithmetic: 20.2 us -> none  [local(): jnp.zeros((rows_out, cell_count), jnp.float32)]
    all_gather x1 -> x0, blocking collectives: 13.5 us -> none  [local(): lax.all_gather(own_block, 'comp', axis=1, tiled=True)]
    ppermute x6, waiting for transfers between devices: 0.02 us -> 12.9 us  [with_halo(): lax.ppermute(lax.slice_in_dim(block, 0, width, axis=dim), axis, backward)]
  transfers between devices with their start and end apart: 14 -> 16, of which waited for: 2 -> 8; matrix products, arithmetic and copies ran while one was open for 74% -> 5% of each run, Pallas kernels for 0% -> 24%
where the time goes in v1:
time: 119 us; the launch traced here: 118 us
  starting transfers between devices  37.1 us (31%)
  Pallas kernels  34.9 us (29%)
  waiting for transfers between devices  23.6 us (20%)
  local copies, waits for them, and re-layouts  12.6 us (11%)
  other arithmetic  7.94 us (7%)
    pallas_call x1, Pallas kernels, local(): pl.pallas_call(lambda *refs: incident_kernel(slot_count, device_count, *r...  28.7 us
    ppermute x6, starting transfers between devices, with_halo(): lax.ppermute(lax.slice_in_dim(block, block.shape[dim] - width, None, axis...  17.4 us
    ppermute x6, waiting for transfers between devices, with_halo(): lax.ppermute(lax.slice_in_dim(block, 0, width, axis=dim), axis, backward)  12.9 us
    ppermute x6, waiting for transfers between devices, with_halo(): lax.ppermute(lax.slice_in_dim(block, block.shape[dim] - width, None, axis...  10.8 us
    ppermute x6, starting transfers between devices, with_halo(): lax.ppermute(lax.slice_in_dim(block, 0, width, axis=dim), axis, backward)  9.66 us
    pallas_call x1, Pallas kernels, local(): pl.pallas_call(lambda *refs: scatter_kernel(nz, *refs), out_shape=jax.Sha...  6.24 us
    all_to_all x1, starting transfers between devices, local(): lax.all_to_all(sent, ('slab', 'comp'), split_axis=0, concat_axis=0, tiled...  5.37 us
    ppermute x3, starting transfers between devices, local(): blocks.append(lax.ppermute(own_block, 'comp', ring))  4.67 us
  transfers between devices with their start and end apart: 16, of which 8 were waited for; matrix products, arithmetic and copies ran while one was open for 5% of the time, Pallas kernels for 24%

profile of v1, /device:TPU:4, one launch (start us, length us, event | category | flops | bytes accessed | tf_op | source)
XLA Modules:
  0.0 118.2 jit_solution(17943332872911808004)
XLA Ops:
  0.6 0.0 copy-start
  0.6 0.7 copy-done
  1.3 1.1 fusion.1
  2.4 0.8 pad_maximum_fusion.25
  3.2 3.7 %collective-permute-start.6 = (f32[8,1024]{1,0:T(8,128)S(1)}, f32[8,1024]{1,0:T(8,128)S(1)}, u32[]{:S(2)}, u32[]{:S(2)}) collective-permute-start(f32[8,1024]{1,0:T(8,128)S(1)} %pad_maximum_fusion.25), channel_id=1, source_target_pairs={{0,3},{1,0},{2,1},{3,2},{4,7},{5,4},{6,5},{7,6},{8,11},{9,8},{10,9... | collective-permute-start | bytes 98312 | tf_op jit(solution)/shard_map/ppermute | solution.py:210
  6.9 0.0 collective-permute-start.5
  6.9 1.0 collective-permute-start.4
  7.9 1.0 fusion.63
  8.8 1.9 %collective-permute-start = (f32[3,2,16,256]{3,2,1,0:T(8,128)S(1)}, f32[3,2,16,256]{3,2,1,0:T(8,128)S(1)}, u32[]{:S(2)}, u32[]{:S(2)}) collective-permute-start(f32[3,2,16,256]{3,2,1,0:T(8,128)S(1)} %get-tuple-element.18), channel_id=1, source_target_pairs={{4,0},{8,4},{12,8},{16,12},{20,16},{24,20},{28,24},{5,1},{9,5},{13... | collective-permute-start | bytes 294920 | tf_op jit(solution)/shard_map/ppermute | solution.py:152
  10.8 2.4 %collective-permute-start.1 = (f32[3,2,16,256]{3,2,1,0:T(8,128)S(1)}, f32[3,2,16,256]{3,2,1,0:T(8,128)S(1)}, u32[]{:S(2)}, u32[]{:S(2)}) collective-permute-start(f32[3,2,16,256]{3,2,1,0:T(8,128)S(1)} %get-tuple-element.19), channel_id=1, source_target_pairs={{0,4},{4,8},{8,12},{12,16},{16,20},{20,24},{24,28},{1,5},{5,9},{9,... | collective-permute-start | bytes 294920 | tf_op jit(solution)/shard_map/ppermute | solution.py:149
  13.2 1.7 %copy.18.refs_2_ = s32[1024,1]{1,0:T(8,128)} copy(s32[1024,1]{0,1:T(1,128)} %param.17) | data formatting | bytes 8192 | tf_op args[5]
  14.9 0.0 collective-permute-done.6
  14.9 0.0 collective-permute-done.5
  14.9 0.0 collective-permute-done.4
  14.9 1.5 %pad_maximum_fusion.18.refs_0_ = f32[8,4096]{1,0:T(8,128)} fusion(f32[8,1024]{1,0:T(8,128)S(1)} %collective-permute-done.6, f32[8,1024]{1,0:T(8,128)S(1)} %collective-permute-done.5, f32[8,1024]{1,0:T(8,128)S(1)} %collective-permute-done.4, f32[1,1024]{1,0:T(1,128)S(1)} %fusion.1, f32[3,1024]{1,0:T(4,128)} %param.21, f32[1,1024]{1,0:T(1,128)} %bitcast.21, ...), kind=kLoop, calls=%fused_computation.110 | loop fusion | flops 196608 | bytes 262144 | tf_op jit(solution)/shard_map/concatenate | solution.py:211
  16.4 28.7 %incident.1 = f32[16,2048]{1,0:T(8,128)} custom-call(f32[8,4096]{1,0:T(8,128)} %pad_maximum_fusion.18.refs_0_, f32[3,1024]{1,0:T(4,128)} %refs_1_.1, s32[1024,1]{1,0:T(8,128)} %copy.18.refs_2_, s32[1,1024]{1,0:T(1,128)} %bitcast.22), custom_call_target="tpu_custom_call" | custom-call | tf_op jit(solution)/shard_map/incident/pallas_call | solution.py:213
  45.1 1.0 reshape.28
  46.1 0.1 copy.23
  46.2 0.8 all_to_all.8
  47.0 5.4 %all-to-all-start = ((f32[32,1,640]{2,1,0:T(1,128)}), f32[32,1,640]{2,1,0:T(1,128)S(1)}, u32[]{:S(2)}, u32[]{:S(2)}) async-start(f32[32,1,640]{2,1,0:T(1,128)} %all_to_all.8), calls=%async_computation | async-start | bytes 163840 | tf_op jit(solution)/shard_map/all_to_all | solution.py:223
  52.4 0.0 collective-permute-done.1
  52.4 0.1 constant_dynamic-update-slice_fusion.1
  52.5 0.0 collective-permute-done
  52.6 0.1 fusion.60
  52.6 3.4 %collective-permute-start.3 = (f32[3,12,2,256]{3,2,1,0:T(2,128)S(1)}, f32[3,12,2,256]{3,2,1,0:T(2,128)S(1)}, u32[]{:S(2)}, u32[]{:S(2)}) collective-permute-start(f32[3,12,2,256]{3,2,1,0:T(2,128)S(1)} %get-tuple-element.9), channel_id=1, source_target_pairs={{0,1},{1,2},{2,3},{4,5},{5,6},{6,7},{8,9},{9,10},{10,11},{12,13},{... | collective-permute-start | bytes 221192 | tf_op jit(solution)/shard_map/ppermute | solution.py:149
  56.0 1.3 %collective-permute-start.2 = (f32[3,12,2,256]{3,2,1,0:T(2,128)S(1)}, f32[3,12,2,256]{3,2,1,0:T(2,128)S(1)}, u32[]{:S(2)}, u32[]{:S(2)}) collective-permute-start(f32[3,12,2,256]{3,2,1,0:T(2,128)S(1)} %get-tuple-element.10), channel_id=1, source_target_pairs={{1,0},{2,1},{3,2},{5,4},{6,5},{7,6},{9,8},{10,9},{11,10},{13,12},{... | collective-permute-start | bytes 221192 | tf_op jit(solution)/shard_map/ppermute | solution.py:152
  57.4 0.6 collective-permute-done.3
  58.0 4.3 %collective-permute-done.2 = f32[3,12,2,256]{3,2,1,0:T(2,128)S(1)} collective-permute-done((f32[3,12,2,256]{3,2,1,0:T(2,128)S(1)}, f32[3,12,2,256]{3,2,1,0:T(2,128)S(1)}, u32[]{:S(2)}, u32[]{:S(2)}) %collective-permute-start.2) | collective-permute-done | bytes 73760 | tf_op jit(solution)/shard_map/ppermute | solution.py:152
  62.3 0.6 copy-done.7
  62.9 0.7 select_maximum_fusion.8
  63.6 0.0 all-to-all-done
  63.6 0.8 reduce
  64.4 1.7 %reshape.29 = f32[32,10,64]{2,1,0:T(8,128)} reshape(f32[32,640]{1,0:T(8,128)} %reduce) | data formatting | bytes 163840 | tf_op jit(solution)/shard_map/reshape | solution.py:225
  66.1 1.7 %copy.21 = f32[10,32,64]{2,1,0:T(8,128)} copy(f32[10,32,64]{2,0,1:T(8,128)} %bitcast.18) | data formatting | bytes 163840 | tf_op jit(solution)/shard_map/transpose | solution.py:224
  67.8 1.7 %reshape.30.refs_0_ = f32[10,2048]{1,0:T(8,128)} reshape(f32[10,32,64]{2,1,0:T(8,128)} %copy.21) | data formatting | bytes 163840 | tf_op jit(solution)/shard_map/reshape | solution.py:226
  69.5 6.2 %scatter.1 = f32[9,128,256]{2,1,0:T(8,128)} custom-call(f32[10,2048]{1,0:T(8,128)} %reshape.30.refs_0_), custom_call_target="tpu_custom_call" | custom-call | tf_op jit(solution)/shard_map/scatter/pallas_call | solution.py:228
  75.7 1.4 %fusion.59 = (f32[3,128,256]{2,1,0:T(8,128)S(1)}, f32[3,128,256]{2,1,0:T(8,128)S(1)}, f32[3,128,256]{2,1,0:T(8,128)S(1)}) fusion(f32[9,128,256]{2,1,0:T(8,128)} %scatter.1), kind=kLoop, calls=%fused_computation.126 | loop fusion | bytes 2359296 | tf_op jit(solution)/shard_map/slice | solution.py:240
  77.1 0.0 copy-done.4
  77.1 0.0 copy-done.8
  77.1 0.6 fusion.47
  77.8 1.9 %collective-permute-start.7 = (f32[3,2,16,256]{3,2,1,0:T(8,128)S(1)}, f32[3,2,16,256]{3,2,1,0:T(8,128)S(1)}, u32[]{:S(2)}, u32[]{:S(2)}) collective-permute-start(f32[3,2,16,256]{3,2,1,0:T(8,128)S(1)} %get-tuple-element.13), channel_id=1, source_target_pairs={{4,0},{8,4},{12,8},{16,12},{20,16},{24,20},{28,24},{5,1},{9,5},{13... | collective-permute-start | bytes 294920 | tf_op jit(solution)/shard_map/ppermute | solution.py:152
  79.7 2.4 %collective-permute-start.8 = (f32[3,2,16,256]{3,2,1,0:T(8,128)S(1)}, f32[3,2,16,256]{3,2,1,0:T(8,128)S(1)}, u32[]{:S(2)}, u32[]{:S(2)}) collective-permute-start(f32[3,2,16,256]{3,2,1,0:T(8,128)S(1)} %get-tuple-element.14), channel_id=1, source_target_pairs={{0,4},{4,8},{8,12},{12,16},{16,20},{20,24},{24,28},{1,5},{5,9},{9,... | collective-permute-start | bytes 294920 | tf_op jit(solution)/shard_map/ppermute | solution.py:149
  82.1 0.0 collective-permute-done.7
  82.1 4.4 %collective-permute-done.8 = f32[3,2,16,256]{3,2,1,0:T(8,128)S(1)} collective-permute-done((f32[3,2,16,256]{3,2,1,0:T(8,128)S(1)}, f32[3,2,16,256]{3,2,1,0:T(8,128)S(1)}, u32[]{:S(2)}, u32[]{:S(2)}) %collective-permute-start.8) | collective-permute-done | bytes 98336 | tf_op jit(solution)/shard_map/ppermute | solution.py:149
  86.6 0.1 pad_maximum_fusion.22
  86.6 3.4 %collective-permute-start.10 = (f32[3,12,2,256]{3,2,1,0:T(2,128)S(1)}, f32[3,12,2,256]{3,2,1,0:T(2,128)S(1)}, u32[]{:S(2)}, u32[]{:S(2)}) collective-permute-start(f32[3,12,2,256]{3,2,1,0:T(2,128)S(1)} %get-tuple-element.7), channel_id=1, source_target_pairs={{0,1},{1,2},{2,3},{4,5},{5,6},{6,7},{8,9},{9,10},{10,11},{12,13},{... | collective-permute-start | bytes 221192 | tf_op jit(solution)/shard_map/ppermute | solution.py:149
  90.0 1.3 %collective-permute-start.9 = (f32[3,12,2,256]{3,2,1,0:T(2,128)S(1)}, f32[3,12,2,256]{3,2,1,0:T(2,128)S(1)}, u32[]{:S(2)}, u32[]{:S(2)}) collective-permute-start(f32[3,12,2,256]{3,2,1,0:T(2,128)S(1)} %get-tuple-element.8), channel_id=1, source_target_pairs={{1,0},{2,1},{3,2},{5,4},{6,5},{7,6},{9,8},{10,9},{11,10},{13,12},{... | collective-permute-start | bytes 221192 | tf_op jit(solution)/shard_map/ppermute | solution.py:152
  91.3 0.7 collective-permute-done.10
  92.0 4.3 %collective-permute-done.9 = f32[3,12,2,256]{3,2,1,0:T(2,128)S(1)} collective-permute-done((f32[3,12,2,256]{3,2,1,0:T(2,128)S(1)}, f32[3,12,2,256]{3,2,1,0:T(2,128)S(1)}, u32[]{:S(2)}, u32[]{:S(2)}) %collective-permute-start.9) | collective-permute-done | bytes 73760 | tf_op jit(solution)/shard_map/ppermute | solution.py:152
  96.2 0.7 select_maximum_fusion.4
  96.9 0.6 fusion.27
  97.6 0.0 copy-start.1
  97.6 1.9 %collective-permute-start.11 = (f32[3,2,16,256]{3,2,1,0:T(8,128)S(1)}, f32[3,2,16,256]{3,2,1,0:T(8,128)S(1)}, u32[]{:S(2)}, u32[]{:S(2)}) collective-permute-start(f32[3,2,16,256]{3,2,1,0:T(8,128)S(1)} %get-tuple-element.11), channel_id=1, source_target_pairs={{4,0},{8,4},{12,8},{16,12},{20,16},{24,20},{28,24},{5,1},{9,5},{13... | collective-permute-start | bytes 294920 | tf_op jit(solution)/shard_map/ppermute | solution.py:152
  99.5 2.4 %collective-permute-start.12 = (f32[3,2,16,256]{3,2,1,0:T(8,128)S(1)}, f32[3,2,16,256]{3,2,1,0:T(8,128)S(1)}, u32[]{:S(2)}, u32[]{:S(2)}) collective-permute-start(f32[3,2,16,256]{3,2,1,0:T(8,128)S(1)} %get-tuple-element.12), channel_id=1, source_target_pairs={{0,4},{4,8},{8,12},{12,16},{16,20},{20,24},{24,28},{1,5},{5,9},{9,... | collective-permute-start | bytes 294920 | tf_op jit(solution)/shard_map/ppermute | solution.py:149
  102.0 0.0 collective-permute-done.11
  102.0 4.4 %collective-permute-done.12 = f32[3,2,16,256]{3,2,1,0:T(8,128)S(1)} collective-permute-done((f32[3,2,16,256]{3,2,1,0:T(8,128)S(1)}, f32[3,2,16,256]{3,2,1,0:T(8,128)S(1)}, u32[]{:S(2)}, u32[]{:S(2)}) %collective-permute-start.12) | collective-permute-done | bytes 98336 | tf_op jit(solution)/shard_map/ppermute | solution.py:149
  106.4 0.1 pad_maximum_fusion.19
  106.4 3.4 %collective-permute-start.14 = (f32[3,12,2,256]{3,2,1,0:T(2,128)S(1)}, f32[3,12,2,256]{3,2,1,0:T(2,128)S(1)}, u32[]{:S(2)}, u32[]{:S(2)}) collective-permute-start(f32[3,12,2,256]{3,2,1,0:T(2,128)S(1)} %get-tuple-element.5), channel_id=1, source_target_pairs={{0,1},{1,2},{2,3},{4,5},{5,6},{6,7},{8,9},{9,10},{10,11},{12,13},{... | collective-permute-start | bytes 221192 | tf_op jit(solution)/shard_map/ppermute | solution.py:149
  109.9 1.3 %collective-permute-start.13 = (f32[3,12,2,256]{3,2,1,0:T(2,128)S(1)}, f32[3,12,2,256]{3,2,1,0:T(2,128)S(1)}, u32[]{:S(2)}, u32[]{:S(2)}) collective-permute-start(f32[3,12,2,256]{3,2,1,0:T(2,128)S(1)} %get-tuple-element.6), channel_id=1, source_target_pairs={{1,0},{2,1},{3,2},{5,4},{6,5},{7,6},{9,8},{10,9},{11,10},{13,12},{... | collective-permute-start | bytes 221192 | tf_op jit(solution)/shard_map/ppermute | solution.py:152
  111.2 0.7 collective-permute-done.14
  111.8 4.3 %collective-permute-done.13 = f32[3,12,2,256]{3,2,1,0:T(2,128)S(1)} collective-permute-done((f32[3,12,2,256]{3,2,1,0:T(2,128)S(1)}, f32[3,12,2,256]{3,2,1,0:T(2,128)S(1)}, u32[]{:S(2)}, u32[]{:S(2)}) %collective-permute-start.13) | collective-permute-done | bytes 73760 | tf_op jit(solution)/shard_map/ppermute | solution.py:152
  116.1 0.7 select_maximum_fusion
  116.8 0.0 copy-done.1
  116.8 1.4 %fusion.14 = f32[3,8,16,256]{3,2,1,0:T(8,128)} fusion(f32[3,2,16,256]{3,2,1,0:T(8,128)S(1)} %collective-permute-done.12, f32[3,8,16,256]{3,2,1,0:T(8,128)S(1)} %fusion.27, f32[3,2,16,256]{3,2,1,0:T(8,128)S(1)} %collective-permute-done.11, f32[3,12,20,260]{3,2,1,0:T(8,128)S(1)} %select_maximum_fusion, f32[3,12,2,256]{3,2,1,0:T(2,128)S(1)} %collective-permute-done.14, ...), kind=kLoop, calls=%fused_computation.35 | loop fusion | flops 4030464 | bytes 3751936 | tf_op jit(solution)/shard_map/add | solution.py:242
  (18 shorter events, 0.1 us)
Async XLA Ops:
  0.6 0.7 copy-start
  3.2 11.7 %collective-permute-start.6 = (f32[8,1024]{1,0:T(8,128)S(1)}, f32[8,1024]{1,0:T(8,128)S(1)}, u32[]{:S(2)}, u32[]{:S(2)}) collective-permute-start(f32[8,1024]{1,0:T(8,128)S(1)} %pad_maximum_fusion.25), channel_id=1, source_target_pairs={{0,3},{1,0},{2,1},{3,2},{4,7},{5,4},{6,5},{7,6},{8,11},{9,8},{10,9... | collective-permute-start | bytes 98312 | tf_op jit(solution)/shard_map/ppermute | solution.py:210
  6.9 8.0 %collective-permute-start.5 = (f32[8,1024]{1,0:T(8,128)S(1)}, f32[8,1024]{1,0:T(8,128)S(1)}, u32[]{:S(2)}, u32[]{:S(2)}) collective-permute-start(f32[8,1024]{1,0:T(8,128)S(1)} %pad_maximum_fusion.25), channel_id=1, source_target_pairs={{0,2},{1,3},{2,0},{3,1},{4,6},{5,7},{6,4},{7,5},{8,10},{9,11},{10,... | collective-permute-start | bytes 98312 | tf_op jit(solution)/shard_map/ppermute | solution.py:210
  6.9 8.0 %collective-permute-start.4 = (f32[8,1024]{1,0:T(8,128)S(1)}, f32[8,1024]{1,0:T(8,128)S(1)}, u32[]{:S(2)}, u32[]{:S(2)}) collective-permute-start(f32[8,1024]{1,0:T(8,128)S(1)} %pad_maximum_fusion.25), channel_id=1, source_target_pairs={{0,1},{1,2},{2,3},{3,0},{4,5},{5,6},{6,7},{7,4},{8,9},{9,10},{10,1... | collective-permute-start | bytes 98312 | tf_op jit(solution)/shard_map/ppermute | solution.py:210
  8.8 43.7 %collective-permute-start = (f32[3,2,16,256]{3,2,1,0:T(8,128)S(1)}, f32[3,2,16,256]{3,2,1,0:T(8,128)S(1)}, u32[]{:S(2)}, u32[]{:S(2)}) collective-permute-start(f32[3,2,16,256]{3,2,1,0:T(8,128)S(1)} %get-tuple-element.18), channel_id=1, source_target_pairs={{4,0},{8,4},{12,8},{16,12},{20,16},{24,20},{28,24},{5,1},{9,5},{13... | collective-permute-start | bytes 294920 | tf_op jit(solution)/shard_map/ppermute | solution.py:152
  10.8 41.6 %collective-permute-start.1 = (f32[3,2,16,256]{3,2,1,0:T(8,128)S(1)}, f32[3,2,16,256]{3,2,1,0:T(8,128)S(1)}, u32[]{:S(2)}, u32[]{:S(2)}) collective-permute-start(f32[3,2,16,256]{3,2,1,0:T(8,128)S(1)} %get-tuple-element.19), channel_id=1, source_target_pairs={{0,4},{4,8},{8,12},{12,16},{16,20},{20,24},{24,28},{1,5},{5,9},{9,... | collective-permute-start | bytes 294920 | tf_op jit(solution)/shard_map/ppermute | solution.py:149
  14.9 37.5 %copy-start.2 = (f32[3,8,16,256]{3,2,1,0:T(8,128)S(1)}, f32[3,8,16,256]{3,2,1,0:T(8,128)}, u32[]{:S(2)}) copy-start(f32[3,8,16,256]{3,2,1,0:T(8,128)} %param.12) | copy-start | bytes 1179652
  47.0 10.3 %copy-start.9 = (s32[8,16,256]{2,1,0:T(8,128)S(1)}, s32[8,16,256]{2,1,0:T(8,128)}, u32[]{:S(2)}) copy-start(s32[8,16,256]{2,1,0:T(8,128)} %param.15) | copy-start | bytes 393220
  47.0 16.6 %all-to-all-start = ((f32[32,1,640]{2,1,0:T(1,128)}), f32[32,1,640]{2,1,0:T(1,128)S(1)}, u32[]{:S(2)}, u32[]{:S(2)}) async-start(f32[32,1,640]{2,1,0:T(1,128)} %all_to_all.8), calls=%async_computation | async-start | bytes 163840 | tf_op jit(solution)/shard_map/all_to_all | solution.py:223
  52.6 5.3 %collective-permute-start.3 = (f32[3,12,2,256]{3,2,1,0:T(2,128)S(1)}, f32[3,12,2,256]{3,2,1,0:T(2,128)S(1)}, u32[]{:S(2)}, u32[]{:S(2)}) collective-permute-start(f32[3,12,2,256]{3,2,1,0:T(2,128)S(1)} %get-tuple-element.9), channel_id=1, source_target_pairs={{0,1},{1,2},{2,3},{4,5},{5,6},{6,7},{8,9},{9,10},{10,11},{12,13},{... | collective-permute-start | bytes 221192 | tf_op jit(solution)/shard_map/ppermute | solution.py:149
  56.0 6.2 %collective-permute-start.2 = (f32[3,12,2,256]{3,2,1,0:T(2,128)S(1)}, f32[3,12,2,256]{3,2,1,0:T(2,128)S(1)}, u32[]{:S(2)}, u32[]{:S(2)}) collective-permute-start(f32[3,12,2,256]{3,2,1,0:T(2,128)S(1)} %get-tuple-element.10), channel_id=1, source_target_pairs={{1,0},{2,1},{3,2},{5,4},{6,5},{7,6},{9,8},{10,9},{11,10},{13,12},{... | collective-permute-start | bytes 221192 | tf_op jit(solution)/shard_map/ppermute | solution.py:152
  58.0 4.3 %copy-start.5 = (f32[3,12,2,256]{3,2,1,0:T(2,128)}, f32[3,12,2,256]{3,2,1,0:T(2,128)S(1)}, u32[]{:S(2)}) copy-start(f32[3,12,2,256]{3,2,1,0:T(2,128)S(1)} %collective-permute-done.3) | copy-start | bytes 221188
  62.3 0.6 copy-start.7
  75.7 1.4 %copy-start.3 = (f32[8,16,256]{2,1,0:T(8,128)S(1)}, f32[8,16,256]{2,1,0:T(8,128)}, u32[]{:S(2)}) copy-start(f32[8,16,256]{2,1,0:T(8,128)} %param.14) | copy-start | bytes 393220
  75.7 1.4 %copy-start.4 = (f32[3,8,16,256]{3,2,1,0:T(8,128)S(1)}, f32[3,8,16,256]{3,2,1,0:T(8,128)}, u32[]{:S(2)}) copy-start(f32[3,8,16,256]{3,2,1,0:T(8,128)} %param.13) | copy-start | bytes 1179652
  75.7 1.4 %copy-start.6 = (f32[3,12,2,256]{3,2,1,0:T(2,128)S(1)}, f32[3,12,2,256]{3,2,1,0:T(2,128)}, u32[]{:S(2)}) copy-start(f32[3,12,2,256]{3,2,1,0:T(2,128)} %copy-done.5) | copy-start | bytes 221188
  75.7 1.4 %copy-start.8 = (f32[3,12,2,256]{3,2,1,0:T(2,128)S(1)}, f32[3,12,2,256]{3,2,1,0:T(2,128)}, u32[]{:S(2)}) copy-start(f32[3,12,2,256]{3,2,1,0:T(2,128)} %copy-done.7) | copy-start | bytes 221188
  77.8 4.3 %collective-permute-start.7 = (f32[3,2,16,256]{3,2,1,0:T(8,128)S(1)}, f32[3,2,16,256]{3,2,1,0:T(8,128)S(1)}, u32[]{:S(2)}, u32[]{:S(2)}) collective-permute-start(f32[3,2,16,256]{3,2,1,0:T(8,128)S(1)} %get-tuple-element.13), channel_id=1, source_target_pairs={{4,0},{8,4},{12,8},{16,12},{20,16},{24,20},{28,24},{5,1},{9,5},{13... | collective-permute-start | bytes 294920 | tf_op jit(solution)/shard_map/ppermute | solution.py:152
  79.7 6.8 %collective-permute-start.8 = (f32[3,2,16,256]{3,2,1,0:T(8,128)S(1)}, f32[3,2,16,256]{3,2,1,0:T(8,128)S(1)}, u32[]{:S(2)}, u32[]{:S(2)}) collective-permute-start(f32[3,2,16,256]{3,2,1,0:T(8,128)S(1)} %get-tuple-element.14), channel_id=1, source_target_pairs={{0,4},{4,8},{8,12},{12,16},{16,20},{20,24},{24,28},{1,5},{5,9},{9,... | collective-permute-start | bytes 294920 | tf_op jit(solution)/shard_map/ppermute | solution.py:149
  86.6 5.3 %collective-permute-start.10 = (f32[3,12,2,256]{3,2,1,0:T(2,128)S(1)}, f32[3,12,2,256]{3,2,1,0:T(2,128)S(1)}, u32[]{:S(2)}, u32[]{:S(2)}) collective-permute-start(f32[3,12,2,256]{3,2,1,0:T(2,128)S(1)} %get-tuple-element.7), channel_id=1, source_target_pairs={{0,1},{1,2},{2,3},{4,5},{5,6},{6,7},{8,9},{9,10},{10,11},{12,13},{... | collective-permute-start | bytes 221192 | tf_op jit(solution)/shard_map/ppermute | solution.py:149
  90.0 6.2 %collective-permute-start.9 = (f32[3,12,2,256]{3,2,1,0:T(2,128)S(1)}, f32[3,12,2,256]{3,2,1,0:T(2,128)S(1)}, u32[]{:S(2)}, u32[]{:S(2)}) collective-permute-start(f32[3,12,2,256]{3,2,1,0:T(2,128)S(1)} %get-tuple-element.8), channel_id=1, source_target_pairs={{1,0},{2,1},{3,2},{5,4},{6,5},{7,6},{9,8},{10,9},{11,10},{13,12},{... | collective-permute-start | bytes 221192 | tf_op jit(solution)/shard_map/ppermute | solution.py:152
  97.6 19.3 %copy-start.1 = (f32[3,8,16,256]{3,2,1,0:T(8,128)}, f32[3,8,16,256]{3,2,1,0:T(8,128)S(1)}, u32[]{:S(2)}) copy-start(f32[3,8,16,256]{3,2,1,0:T(8,128)S(1)} %fusion.27) | copy-start | bytes 1179652
  97.6 4.3 %collective-permute-start.11 = (f32[3,2,16,256]{3,2,1,0:T(8,128)S(1)}, f32[3,2,16,256]{3,2,1,0:T(8,128)S(1)}, u32[]{:S(2)}, u32[]{:S(2)}) collective-permute-start(f32[3,2,16,256]{3,2,1,0:T(8,128)S(1)} %get-tuple-element.11), channel_id=1, source_target_pairs={{4,0},{8,4},{12,8},{16,12},{20,16},{24,20},{28,24},{5,1},{9,5},{13... | collective-permute-start | bytes 294920 | tf_op jit(solution)/shard_map/ppermute | solution.py:152
  99.5 6.8 %collective-permute-start.12 = (f32[3,2,16,256]{3,2,1,0:T(8,128)S(1)}, f32[3,2,16,256]{3,2,1,0:T(8,128)S(1)}, u32[]{:S(2)}, u32[]{:S(2)}) collective-permute-start(f32[3,2,16,256]{3,2,1,0:T(8,128)S(1)} %get-tuple-element.12), channel_id=1, source_target_pairs={{0,4},{4,8},{8,12},{12,16},{16,20},{20,24},{24,28},{1,5},{5,9},{9,... | collective-permute-start | bytes 294920 | tf_op jit(solution)/shard_map/ppermute | solution.py:149
  106.4 5.4 %collective-permute-start.14 = (f32[3,12,2,256]{3,2,1,0:T(2,128)S(1)}, f32[3,12,2,256]{3,2,1,0:T(2,128)S(1)}, u32[]{:S(2)}, u32[]{:S(2)}) collective-permute-start(f32[3,12,2,256]{3,2,1,0:T(2,128)S(1)} %get-tuple-element.5), channel_id=1, source_target_pairs={{0,1},{1,2},{2,3},{4,5},{5,6},{6,7},{8,9},{9,10},{10,11},{12,13},{... | collective-permute-start | bytes 221192 | tf_op jit(solution)/shard_map/ppermute | solution.py:149
  109.9 6.2 %collective-permute-start.13 = (f32[3,12,2,256]{3,2,1,0:T(2,128)S(1)}, f32[3,12,2,256]{3,2,1,0:T(2,128)S(1)}, u32[]{:S(2)}, u32[]{:S(2)}) collective-permute-start(f32[3,12,2,256]{3,2,1,0:T(2,128)S(1)} %get-tuple-element.6), channel_id=1, source_target_pairs={{1,0},{2,1},{3,2},{5,4},{6,5},{7,6},{9,8},{10,9},{11,10},{13,12},{... | collective-permute-start | bytes 221192 | tf_op jit(solution)/shard_map/ppermute | solution.py:152

commit v2 on v1

--- a/solution.py
+++ b/solution.py
@@ -13,8 +13,8 @@
 inv_two_pi = 0.15915494309189535
 round_magic = 12582912.0
 
-SIN_C = (4.4428679, -7.30744342, 3.59478806, -0.78437398)
-COS_C = (1.4142135, -6.97885099, 5.73946117, -1.88356299, 0.31069819)
+SIN_C = (4.442834854125977, -7.306587219238281, 3.588636875152588, -0.7713118195533752)
+HALF = 64
 
 F32 = jnp.float32
 BF16 = jnp.bfloat16
@@ -27,12 +27,12 @@
     return out
 
 
-def sincos_turns(u):
-    r = u - ((u + round_magic) - round_magic)
-    z = r * r
-    s = r * horner(SIN_C, z)
-    c = horner(COS_C, z)
-    return s * c, 1.0 - s * s
+def sin_versine(u):
+    r = u - jnp.round(u)
+    s = r * horner(SIN_C, r * r)
+    q = s * s
+    w = 2.0 - q
+    return s * (w * lax.rsqrt(w)), q
 
 
 def split_three(x):
@@ -46,9 +46,10 @@
     return lax.broadcasted_iota(jnp.int32, shape, 0)
 
 
-def incident_kernel(slot_count, owner_count, par_ref, xyz_ref, own_ref, off_ref, out_ref, x8_ref, acc_ref):
+def incident_kernel(slot_stride, par_ref, xyz_ref, own_ref, off_ref, out_ref, x8_ref, acc_ref):
     comps = par_ref.shape[1]
     points = xyz_ref.shape[1]
+    owners = out_ref.shape[0]
     kc = 256
     tile = 256
     x8_ref[...] = jnp.zeros(x8_ref.shape, F32)
@@ -59,32 +60,33 @@
     rows8 = row_ids((8, kc))
     times = step_size * (rows8 + 1).astype(F32)
     rows16 = row_ids((16, kc))
-    comp_row = rows16 % 3
-
-    def body(step, carry):
+    comp_row = jnp.where(rows16 < 6, rows16 % 3, (rows16 + 2) % 3)
+    valued = (rows16 < 10) & (rows16 != 6)
+
+    def body(step, total):
         blk = par_ref[:, pl.ds(pl.multiple_of(step * kc, kc), kc)]
         kv = jnp.where(rows8 < 3, blk * inv_two_pi, 0.0)
         khi, kmid, klo = split_three(kv)
         left = jnp.concatenate([khi, khi, khi, kmid, kmid, klo], axis=0).astype(BF16)
         delays = times * blk[3:4, :] - blk[7:8, :]
-        sd, cd = sincos_turns(delays * inv_two_pi)
+        sd, qd = sin_versine(delays * inv_two_pi)
         amp = jnp.where(comp_row == 0, blk[4:5, :], jnp.where(comp_row == 1, blk[5:6, :], blk[6:7, :]))
-        amp = jnp.where(rows16 < 9, amp, 0.0)
+        amp = jnp.where(valued, amp, 0.0)
 
         def rows_of(t):
             w = amp * jnp.where(rows16 < 3, t[0:1, :], jnp.where(rows16 < 6, t[1:2, :], t[2:3, :]))
             hi = w.astype(BF16)
             lo = (w - hi.astype(F32)).astype(BF16)
-            return jnp.concatenate([hi, lo], axis=0)
-
-        lc = rows_of(cd)
-        ls = rows_of(sd)
+            return w, jnp.concatenate([hi, lo], axis=0)
+
+        wc, lc = rows_of(qd - 1.0)
+        ls = rows_of(sd)[1]
         for t in range(points // tile):
             cols = slice(t * tile, (t + 1) * tile)
             u = lax.dot_general(left, right[:, cols], (((0,), (0,)), ((), ())), preferred_element_type=F32)
             highs, lows = [], []
             for j in range(kc // 32):
-                for value in sincos_turns(u[32 * j : 32 * j + 32]):
+                for value in sin_versine(u[32 * j : 32 * j + 32]):
                     high = value.astype(BF16)
                     highs.append(high)
                     lows.append((value - high.astype(F32)).astype(BF16))
@@ -93,39 +95,50 @@
             part += jnp.dot(ls, jnp.concatenate(lows[0::2], axis=0), preferred_element_type=F32)
             part += jnp.dot(lc, jnp.concatenate(lows[1::2], axis=0), preferred_element_type=F32)
             acc_ref[:, cols] += part
-        return carry
-
-    lax.fori_loop(0, comps // kc, body, 0)
-    vals = acc_ref[0:16, :] + acc_ref[16:32, :]
-    prow = row_ids((16, points))
-    vals = jnp.where(prow == 9, off_ref[...].astype(F32), vals)
+        return total - wc
+
+    total = lax.fori_loop(0, comps // kc, body, jnp.zeros((16, kc), F32))
+    vals = acc_ref[0:16, :] + acc_ref[16:32, :] + jnp.sum(total, axis=1, keepdims=True)
+    vals = jnp.where(row_ids((16, points)) == 6, off_ref[...].astype(F32), vals)
     v1, v2, v3 = split_three(vals)
     vals3 = jnp.concatenate([v1, v2, v3], axis=0).astype(BF16)
-    lanes = -(-owner_count // 128) * 128
-    lane = lax.broadcasted_iota(jnp.int32, (points, lanes), 1)
-    named = own_ref[...] == lane
-    lower = lax.broadcasted_iota(jnp.int32, (points, points), 1) < row_ids((points, points))
-    before = jnp.dot(lower.astype(F32).astype(BF16), named.astype(F32).astype(BF16), preferred_element_type=F32)
-    slot = jnp.sum(jnp.where(named, before + (lane * slot_count).astype(F32), 0.0), axis=1, keepdims=True)
+    owner_id = row_ids((owners, points))
+    named = own_ref[...] == owner_id
+    earlier = row_ids((points, points)) < lax.broadcasted_iota(jnp.int32, (points, points), 1)
+    before = jnp.dot(named.astype(F32).astype(BF16), earlier.astype(F32).astype(BF16), preferred_element_type=F32)
+    slot = jnp.sum(jnp.where(named, before + (owner_id * slot_stride).astype(F32), 0.0), axis=0, keepdims=True)
     slot = slot.astype(jnp.int32)
-    width = 512
-    slots = out_ref.shape[1]
-    for t in range(slots // width):
-        spot = lax.broadcasted_iota(jnp.int32, (points, width), 1) + t * width
+    width = 8 * slot_stride
+    left_half = lax.broadcasted_iota(jnp.int32, (8, 2 * slot_stride), 1) < slot_stride
+    for t in range(owners // 8):
+        spot = row_ids((width, points)) + t * width
         one_hot = (slot == spot).astype(F32).astype(BF16)
-        got = jnp.dot(vals3, one_hot, preferred_element_type=F32)
-        out_ref[:, t * width : (t + 1) * width] = got[0:16] + got[16:32] + got[32:48]
+        got = lax.dot_general(vals3, one_hot, (((1,), (1,)), ((), ())), preferred_element_type=F32)
+        got = got[0:16] + got[16:32] + got[32:48]
+        for pair in range(4):
+            cols = slice(pair * 2 * slot_stride, (pair + 1) * 2 * slot_stride)
+            low, high = got[0:8, cols], got[8:16, cols]
+            out_ref[8 * t + 2 * pair] = jnp.where(left_half, low, pltpu.roll(high, slot_stride, 1))
+            out_ref[8 * t + 2 * pair + 1] = jnp.where(left_half, pltpu.roll(low, slot_stride, 1), high)
 
 
 def scatter_kernel(nz, val_ref, out_ref):
-    count = val_ref.shape[1]
+    sources = val_ref.shape[0]
     rows = out_ref.shape[1]
     chunk = 256
+    lanes = val_ref.shape[2]
+    left_half = lax.broadcasted_iota(jnp.int32, (8, lanes), 1) < lanes // 2
     out_ref[...] = jnp.zeros(out_ref.shape, F32)
 
     def body(step, carry):
-        blk = val_ref[:, pl.ds(pl.multiple_of(step * chunk, chunk), chunk)]
-        off = blk[9:10, :].astype(jnp.int32)
+        lows, highs = [], []
+        for pair in range(2):
+            even, odd = val_ref[4 * step + 2 * pair], val_ref[4 * step + 2 * pair + 1]
+            lows.append(jnp.where(left_half, even, pltpu.roll(odd, lanes // 2, 1)))
+            highs.append(jnp.where(left_half, pltpu.roll(even, lanes // 2, 1), odd))
+        low = jnp.concatenate(lows, axis=1)
+        blk = jnp.concatenate([low, jnp.concatenate(highs, axis=1)], axis=0)
+        off = blk[6:7, :].astype(jnp.int32)
         row = off // nz
         lz = off - row * nz
         zt = (row_ids((nz, chunk)) == lz).astype(F32).astype(BF16)
@@ -133,12 +146,13 @@
         hi = blk.astype(BF16)
         lo = (blk - hi.astype(F32)).astype(BF16)
         for i in range(9):
-            left = jnp.concatenate([mask * hi[i : i + 1, :], mask * lo[i : i + 1, :]], axis=0)
+            r = i if i < 6 else i + 1
+            left = jnp.concatenate([mask * hi[r : r + 1, :], mask * lo[r : r + 1, :]], axis=0)
             got = lax.dot_general(left, zt, (((1,), (1,)), ((), ())), preferred_element_type=F32)
             out_ref[i] += got[0:rows] + got[rows:]
         return carry
 
-    lax.fori_loop(0, count // chunk, body, 0)
+    lax.fori_loop(0, sources // 4, body, 0)
 
 
 def with_halo(block, sides, width):
@@ -209,21 +223,14 @@
         ring = [(i, (i + shift) % comp_count) for i in range(comp_count)]
         blocks.append(lax.ppermute(own_block, "comp", ring))
     params = jnp.concatenate(blocks, axis=1)
-    slots = device_count * slot_count
+    assert slot_count <= HALF and device_count % 8 == 0
     packed = pl.pallas_call(
-        lambda *refs: incident_kernel(slot_count, device_count, *refs),
-        out_shape=jax.ShapeDtypeStruct((16, slots), F32),
+        lambda *refs: incident_kernel(HALF, *refs),
+        out_shape=jax.ShapeDtypeStruct((device_count, 8, 2 * HALF), F32),
         scratch_shapes=[pltpu.VMEM((8, point_count), F32), pltpu.VMEM((32, point_count), F32)],
         name="incident",
-    )(params, point_xyz, point_owner, cell_offset[None, :])
-    rows_sent = rows_out + 1
-    sent = jnp.transpose(
-        packed[:rows_sent].reshape(rows_sent, device_count, slot_count), (1, 0, 2)
-    ).reshape(device_count, rows_sent * slot_count)
-    got = lax.all_to_all(sent, ("slab", "comp"), split_axis=0, concat_axis=0, tiled=True)
-    arrived = jnp.transpose(
-        got.reshape(device_count, rows_sent, slot_count), (1, 0, 2)
-    ).reshape(rows_sent, slots)
+    )(params, point_xyz, point_owner.reshape(1, point_count), cell_offset.reshape(1, point_count))
+    arrived = lax.all_to_all(packed, ("slab", "comp"), split_axis=0, concat_axis=0, tiled=True)
     cx, cy, nz = current_field.shape[1:]
     forcing = pl.pallas_call(
         lambda *refs: scatter_kernel(nz, *refs),

time: 119 us -> 105 us (0.88)
  local copies, waits for them, and re-layouts: 12.6 us -> 3.93 us
  Pallas kernels: 34.9 us -> 29.9 us
    pallas_call x1, Pallas kernels: 28.7 us -> 23.2 us  [local(): pl.pallas_call(lambda *refs: incident_kernel(HALF, *refs), out_shape=jax....]
    reshape x4 -> x0, local copies, waits for them, and re-layouts: 4.45 us -> none  [the longest x1 1.68 us: local(): got.reshape(device_count, rows_sent, slot_count)]
    unnamed x23 -> x18, local copies, waits for them, and re-layouts: 3.23 us -> 1.51 us
    transpose x1 -> x0, local copies, waits for them, and re-layouts: 1.67 us -> none  [local(): jnp.transpose(got.reshape(device_count, rows_sent, slot_count), (1, 0, 2))]
  transfers between devices with their start and end apart: 16 -> 16, of which waited for: 8 -> 8; matrix products, arithmetic and copies ran while one was open for 5% -> 3% of each run, Pallas kernels for 24% -> 22%
where the time goes in v2:
time: 105 us; the launch traced here: 104 us
  starting transfers between devices  37.1 us (35%)
  Pallas kernels  29.9 us (28%)
  waiting for transfers between devices  23.6 us (22%)
  other arithmetic  7.07 us (7%)
  local copies, waits for them, and re-layouts  3.93 us (4%)
  matrix products  1.12 us (1%)
    pallas_call x1, Pallas kernels, local(): pl.pallas_call(lambda *refs: incident_kernel(HALF, *refs), out_shape=jax....  23.2 us
    ppermute x6, starting transfers between devices, with_halo(): lax.ppermute(lax.slice_in_dim(block, block.shape[dim] - width, None, axis...  17.4 us
    ppermute x6, waiting for transfers between devices, with_halo(): lax.ppermute(lax.slice_in_dim(block, 0, width, axis=dim), axis, backward)  12.9 us
    ppermute x6, waiting for transfers between devices, with_halo(): lax.ppermute(lax.slice_in_dim(block, block.shape[dim] - width, None, axis...  10.8 us
    ppermute x6, starting transfers between devices, with_halo(): lax.ppermute(lax.slice_in_dim(block, 0, width, axis=dim), axis, backward)  9.66 us
    pallas_call x1, Pallas kernels, local(): pl.pallas_call(lambda *refs: scatter_kernel(nz, *refs), out_shape=jax.Sha...  6.74 us
    all_to_all x1, starting transfers between devices, local(): lax.all_to_all(packed, ('slab', 'comp'), split_axis=0, concat_axis=0, til...  5.42 us
    ppermute x3, starting transfers between devices, local(): blocks.append(lax.ppermute(own_block, 'comp', ring))  4.67 us
  transfers between devices with their start and end apart: 16, of which 8 were waited for; matrix products, arithmetic and copies ran while one was open for 3% of the time, Pallas kernels for 22%

profile of v2, /device:TPU:4, one launch (start us, length us, event | category | flops | bytes accessed | tf_op | source)
XLA Modules:
  0.0 103.8 jit_solution(2753677747319292149)
XLA Ops:
  0.6 0.0 copy-start
  0.6 0.0 copy-start.2
  0.7 0.7 copy-done
  1.3 1.1 %fusion.1 = f32[1,1024]{1,0:T(1,128)S(1)} fusion(f32[256,1]{0,1:T(1,128)S(1)} %bitcast.9, s32[1024]{0:T(1024)} %param.22), kind=kOutput, calls=%fused_computation.14 | convolution fusion | flops 3407872 | bytes 9216 | tf_op jit(solution)/shard_map/dot_general | solution.py:209
  2.4 0.8 pad_maximum_fusion.25
  3.2 3.7 %collective-permute-start.6 = (f32[8,1024]{1,0:T(8,128)S(1)}, f32[8,1024]{1,0:T(8,128)S(1)}, u32[]{:S(2)}, u32[]{:S(2)}) collective-permute-start(f32[8,1024]{1,0:T(8,128)S(1)} %pad_maximum_fusion.25), channel_id=1, source_target_pairs={{0,3},{1,0},{2,1},{3,2},{4,7},{5,4},{6,5},{7,6},{8,11},{9,8},{10,9... | collective-permute-start | bytes 98312 | tf_op jit(solution)/shard_map/ppermute | solution.py:224
  6.9 0.0 collective-permute-start.5
  6.9 1.0 collective-permute-start.4
  7.9 1.0 fusion.63
  8.8 1.9 %collective-permute-start = (f32[3,2,16,256]{3,2,1,0:T(8,128)S(1)}, f32[3,2,16,256]{3,2,1,0:T(8,128)S(1)}, u32[]{:S(2)}, u32[]{:S(2)}) collective-permute-start(f32[3,2,16,256]{3,2,1,0:T(8,128)S(1)} %get-tuple-element.18), channel_id=1, source_target_pairs={{4,0},{8,4},{12,8},{16,12},{20,16},{24,20},{28,24},{5,1},{9,5},{13... | collective-permute-start | bytes 294920 | tf_op jit(solution)/shard_map/ppermute | solution.py:166
  10.8 2.4 %collective-permute-start.1 = (f32[3,2,16,256]{3,2,1,0:T(8,128)S(1)}, f32[3,2,16,256]{3,2,1,0:T(8,128)S(1)}, u32[]{:S(2)}, u32[]{:S(2)}) collective-permute-start(f32[3,2,16,256]{3,2,1,0:T(8,128)S(1)} %get-tuple-element.19), channel_id=1, source_target_pairs={{0,4},{4,8},{8,12},{12,16},{16,20},{20,24},{24,28},{1,5},{5,9},{9,... | collective-permute-start | bytes 294920 | tf_op jit(solution)/shard_map/ppermute | solution.py:163
  13.2 0.0 collective-permute-done.6
  13.2 0.0 collective-permute-done.5
  13.2 0.0 collective-permute-done.4
  13.2 1.4 %pad_maximum_fusion.18.refs_0_ = f32[8,4096]{1,0:T(8,128)} fusion(f32[8,1024]{1,0:T(8,128)S(1)} %collective-permute-done.6, f32[8,1024]{1,0:T(8,128)S(1)} %collective-permute-done.5, f32[8,1024]{1,0:T(8,128)S(1)} %collective-permute-done.4, f32[1,1024]{1,0:T(1,128)S(1)} %fusion.1, f32[3,1024]{1,0:T(4,128)} %param.21, f32[1,1024]{1,0:T(1,128)} %bitcast.14, ...), kind=kLoop, calls=%fused_computation.109 | loop fusion | flops 196608 | bytes 262144 | tf_op jit(solution)/shard_map/concatenate | solution.py:225
  14.6 23.2 %incident.1 = f32[32,8,128]{2,1,0:T(8,128)} custom-call(f32[8,4096]{1,0:T(8,128)} %pad_maximum_fusion.18.refs_0_, f32[3,1024]{1,0:T(4,128)} %refs_1_.1, s32[1,1024]{1,0:T(1,128)} %bitcast.15, s32[1,1024]{1,0:T(1,128)} %bitcast.16), custom_call_target="tpu_custom_call" | custom-call | tf_op jit(solution)/shard_map/incident/pallas_call | solution.py:227
  37.9 5.4 %all-to-all-start = ((f32[32,8,128]{2,1,0:T(8,128)}), f32[32,8,128]{2,1,0:T(8,128)}, u32[]{:S(2)}, u32[]{:S(2)}) async-start(f32[32,8,128]{2,1,0:T(8,128)} %incident.1), calls=%async_computation | async-start | bytes 262144 | tf_op jit(solution)/shard_map/all_to_all | solution.py:233
  43.3 0.0 collective-permute-done.1
  43.3 0.0 copy-done.2
  43.3 0.1 constant_dynamic-update-slice_fusion.1
  43.5 0.0 collective-permute-done
  43.5 0.1 fusion.60
  43.6 3.4 %collective-permute-start.3 = (f32[3,12,2,256]{3,2,1,0:T(2,128)S(1)}, f32[3,12,2,256]{3,2,1,0:T(2,128)S(1)}, u32[]{:S(2)}, u32[]{:S(2)}) collective-permute-start(f32[3,12,2,256]{3,2,1,0:T(2,128)S(1)} %get-tuple-element.9), channel_id=1, source_target_pairs={{0,1},{1,2},{2,3},{4,5},{5,6},{6,7},{8,9},{9,10},{10,11},{12,13},{... | collective-permute-start | bytes 221192 | tf_op jit(solution)/shard_map/ppermute | solution.py:163
  46.9 1.3 %collective-permute-start.2 = (f32[3,12,2,256]{3,2,1,0:T(2,128)S(1)}, f32[3,12,2,256]{3,2,1,0:T(2,128)S(1)}, u32[]{:S(2)}, u32[]{:S(2)}) collective-permute-start(f32[3,12,2,256]{3,2,1,0:T(2,128)S(1)} %get-tuple-element.10), channel_id=1, source_target_pairs={{1,0},{2,1},{3,2},{5,4},{6,5},{7,6},{9,8},{10,9},{11,10},{13,12},{... | collective-permute-start | bytes 221192 | tf_op jit(solution)/shard_map/ppermute | solution.py:166
  48.2 0.0 copy-done.7
  48.3 0.6 collective-permute-done.3
  48.9 4.3 %collective-permute-done.2 = f32[3,12,2,256]{3,2,1,0:T(2,128)S(1)} collective-permute-done((f32[3,12,2,256]{3,2,1,0:T(2,128)S(1)}, f32[3,12,2,256]{3,2,1,0:T(2,128)S(1)}, u32[]{:S(2)}, u32[]{:S(2)}) %collective-permute-start.2) | collective-permute-done | bytes 73760 | tf_op jit(solution)/shard_map/ppermute | solution.py:166
  53.2 0.0 copy-start.5
  53.2 0.6 copy-done.5
  53.8 0.7 select_maximum_fusion.8
  54.5 0.0 all-to-all-done.refs_0_
  54.5 6.7 %scatter.1 = f32[9,128,256]{2,1,0:T(8,128)} custom-call(f32[32,8,128]{2,1,0:T(8,128)} %all-to-all-done.refs_0_), custom_call_target="tpu_custom_call" | custom-call | tf_op jit(solution)/shard_map/scatter/pallas_call | solution.py:235
  61.3 0.0 copy-start.3
  61.3 0.0 copy-start.4
  61.3 0.0 copy-start.6
  61.3 1.4 %fusion.59 = (f32[3,128,256]{2,1,0:T(8,128)S(1)}, f32[3,128,256]{2,1,0:T(8,128)S(1)}, f32[3,128,256]{2,1,0:T(8,128)S(1)}) fusion(f32[9,128,256]{2,1,0:T(8,128)} %scatter.1), kind=kLoop, calls=%fused_computation.125 | loop fusion | bytes 2359296 | tf_op jit(solution)/shard_map/slice | solution.py:247
  62.7 0.0 copy-done.3
  62.7 0.0 copy-done.4
  62.7 0.0 copy-done.6
  62.7 0.6 fusion.47
  63.4 1.9 %collective-permute-start.7 = (f32[3,2,16,256]{3,2,1,0:T(8,128)S(1)}, f32[3,2,16,256]{3,2,1,0:T(8,128)S(1)}, u32[]{:S(2)}, u32[]{:S(2)}) collective-permute-start(f32[3,2,16,256]{3,2,1,0:T(8,128)S(1)} %get-tuple-element.13), channel_id=1, source_target_pairs={{4,0},{8,4},{12,8},{16,12},{20,16},{24,20},{28,24},{5,1},{9,5},{13... | collective-permute-start | bytes 294920 | tf_op jit(solution)/shard_map/ppermute | solution.py:166
  65.3 2.4 %collective-permute-start.8 = (f32[3,2,16,256]{3,2,1,0:T(8,128)S(1)}, f32[3,2,16,256]{3,2,1,0:T(8,128)S(1)}, u32[]{:S(2)}, u32[]{:S(2)}) collective-permute-start(f32[3,2,16,256]{3,2,1,0:T(8,128)S(1)} %get-tuple-element.14), channel_id=1, source_target_pairs={{0,4},{4,8},{8,12},{12,16},{16,20},{20,24},{24,28},{1,5},{5,9},{9,... | collective-permute-start | bytes 294920 | tf_op jit(solution)/shard_map/ppermute | solution.py:163
  67.7 0.0 collective-permute-done.7
  67.7 4.4 %collective-permute-done.8 = f32[3,2,16,256]{3,2,1,0:T(8,128)S(1)} collective-permute-done((f32[3,2,16,256]{3,2,1,0:T(8,128)S(1)}, f32[3,2,16,256]{3,2,1,0:T(8,128)S(1)}, u32[]{:S(2)}, u32[]{:S(2)}) %collective-permute-start.8) | collective-permute-done | bytes 98336 | tf_op jit(solution)/shard_map/ppermute | solution.py:163
  72.1 0.1 pad_maximum_fusion.22
  72.2 3.4 %collective-permute-start.10 = (f32[3,12,2,256]{3,2,1,0:T(2,128)S(1)}, f32[3,12,2,256]{3,2,1,0:T(2,128)S(1)}, u32[]{:S(2)}, u32[]{:S(2)}) collective-permute-start(f32[3,12,2,256]{3,2,1,0:T(2,128)S(1)} %get-tuple-element.7), channel_id=1, source_target_pairs={{0,1},{1,2},{2,3},{4,5},{5,6},{6,7},{8,9},{9,10},{10,11},{12,13},{... | collective-permute-start | bytes 221192 | tf_op jit(solution)/shard_map/ppermute | solution.py:163
  75.6 1.3 %collective-permute-start.9 = (f32[3,12,2,256]{3,2,1,0:T(2,128)S(1)}, f32[3,12,2,256]{3,2,1,0:T(2,128)S(1)}, u32[]{:S(2)}, u32[]{:S(2)}) collective-permute-start(f32[3,12,2,256]{3,2,1,0:T(2,128)S(1)} %get-tuple-element.8), channel_id=1, source_target_pairs={{1,0},{2,1},{3,2},{5,4},{6,5},{7,6},{9,8},{10,9},{11,10},{13,12},{... | collective-permute-start | bytes 221192 | tf_op jit(solution)/shard_map/ppermute | solution.py:166
  76.9 0.7 collective-permute-done.10
  77.5 4.3 %collective-permute-done.9 = f32[3,12,2,256]{3,2,1,0:T(2,128)S(1)} collective-permute-done((f32[3,12,2,256]{3,2,1,0:T(2,128)S(1)}, f32[3,12,2,256]{3,2,1,0:T(2,128)S(1)}, u32[]{:S(2)}, u32[]{:S(2)}) %collective-permute-start.9) | collective-permute-done | bytes 73760 | tf_op jit(solution)/shard_map/ppermute | solution.py:166
  81.8 0.7 select_maximum_fusion.4
  82.5 0.6 fusion.27
  83.2 0.0 copy-start.1
  83.2 1.9 %collective-permute-start.11 = (f32[3,2,16,256]{3,2,1,0:T(8,128)S(1)}, f32[3,2,16,256]{3,2,1,0:T(8,128)S(1)}, u32[]{:S(2)}, u32[]{:S(2)}) collective-permute-start(f32[3,2,16,256]{3,2,1,0:T(8,128)S(1)} %get-tuple-element.11), channel_id=1, source_target_pairs={{4,0},{8,4},{12,8},{16,12},{20,16},{24,20},{28,24},{5,1},{9,5},{13... | collective-permute-start | bytes 294920 | tf_op jit(solution)/shard_map/ppermute | solution.py:166
  85.1 2.4 %collective-permute-start.12 = (f32[3,2,16,256]{3,2,1,0:T(8,128)S(1)}, f32[3,2,16,256]{3,2,1,0:T(8,128)S(1)}, u32[]{:S(2)}, u32[]{:S(2)}) collective-permute-start(f32[3,2,16,256]{3,2,1,0:T(8,128)S(1)} %get-tuple-element.12), channel_id=1, source_target_pairs={{0,4},{4,8},{8,12},{12,16},{16,20},{20,24},{24,28},{1,5},{5,9},{9,... | collective-permute-start | bytes 294920 | tf_op jit(solution)/shard_map/ppermute | solution.py:163
  87.5 0.0 collective-permute-done.11
  87.5 4.4 %collective-permute-done.12 = f32[3,2,16,256]{3,2,1,0:T(8,128)S(1)} collective-permute-done((f32[3,2,16,256]{3,2,1,0:T(8,128)S(1)}, f32[3,2,16,256]{3,2,1,0:T(8,128)S(1)}, u32[]{:S(2)}, u32[]{:S(2)}) %collective-permute-start.12) | collective-permute-done | bytes 98336 | tf_op jit(solution)/shard_map/ppermute | solution.py:163
  92.0 0.1 pad_maximum_fusion.19
  92.0 3.4 %collective-permute-start.14 = (f32[3,12,2,256]{3,2,1,0:T(2,128)S(1)}, f32[3,12,2,256]{3,2,1,0:T(2,128)S(1)}, u32[]{:S(2)}, u32[]{:S(2)}) collective-permute-start(f32[3,12,2,256]{3,2,1,0:T(2,128)S(1)} %get-tuple-element.5), channel_id=1, source_target_pairs={{0,1},{1,2},{2,3},{4,5},{5,6},{6,7},{8,9},{9,10},{10,11},{12,13},{... | collective-permute-start | bytes 221192 | tf_op jit(solution)/shard_map/ppermute | solution.py:163
  95.5 1.3 %collective-permute-start.13 = (f32[3,12,2,256]{3,2,1,0:T(2,128)S(1)}, f32[3,12,2,256]{3,2,1,0:T(2,128)S(1)}, u32[]{:S(2)}, u32[]{:S(2)}) collective-permute-start(f32[3,12,2,256]{3,2,1,0:T(2,128)S(1)} %get-tuple-element.6), channel_id=1, source_target_pairs={{1,0},{2,1},{3,2},{5,4},{6,5},{7,6},{9,8},{10,9},{11,10},{13,12},{... | collective-permute-start | bytes 221192 | tf_op jit(solution)/shard_map/ppermute | solution.py:166
  96.8 0.7 collective-permute-done.14
  97.4 4.3 %collective-permute-done.13 = f32[3,12,2,256]{3,2,1,0:T(2,128)S(1)} collective-permute-done((f32[3,12,2,256]{3,2,1,0:T(2,128)S(1)}, f32[3,12,2,256]{3,2,1,0:T(2,128)S(1)}, u32[]{:S(2)}, u32[]{:S(2)}) %collective-permute-start.13) | collective-permute-done | bytes 73760 | tf_op jit(solution)/shard_map/ppermute | solution.py:166
  101.7 0.7 select_maximum_fusion
  102.4 0.0 copy-done.1
  102.4 1.4 %fusion.14 = f32[3,8,16,256]{3,2,1,0:T(8,128)} fusion(f32[3,2,16,256]{3,2,1,0:T(8,128)S(1)} %collective-permute-done.12, f32[3,8,16,256]{3,2,1,0:T(8,128)S(1)} %fusion.27, f32[3,2,16,256]{3,2,1,0:T(8,128)S(1)} %collective-permute-done.11, f32[3,12,20,260]{3,2,1,0:T(8,128)S(1)} %select_maximum_fusion, f32[3,12,2,256]{3,2,1,0:T(2,128)S(1)} %collective-permute-done.14, ...), kind=kLoop, calls=%fused_computation.35 | loop fusion | flops 4030464 | bytes 3751936 | tf_op jit(solution)/shard_map/add | solution.py:249
  (6 shorter events, 0.1 us)
Async XLA Ops:
  0.6 0.7 copy-start
  0.6 42.7 %copy-start.2 = (f32[3,8,16,256]{3,2,1,0:T(8,128)S(1)}, f32[3,8,16,256]{3,2,1,0:T(8,128)}, u32[]{:S(2)}) copy-start(f32[3,8,16,256]{3,2,1,0:T(8,128)} %param.12) | copy-start | bytes 1179652
  3.2 10.0 %collective-permute-start.6 = (f32[8,1024]{1,0:T(8,128)S(1)}, f32[8,1024]{1,0:T(8,128)S(1)}, u32[]{:S(2)}, u32[]{:S(2)}) collective-permute-start(f32[8,1024]{1,0:T(8,128)S(1)} %pad_maximum_fusion.25), channel_id=1, source_target_pairs={{0,3},{1,0},{2,1},{3,2},{4,7},{5,4},{6,5},{7,6},{8,11},{9,8},{10,9... | collective-permute-start | bytes 98312 | tf_op jit(solution)/shard_map/ppermute | solution.py:224
  6.9 6.3 %collective-permute-start.5 = (f32[8,1024]{1,0:T(8,128)S(1)}, f32[8,1024]{1,0:T(8,128)S(1)}, u32[]{:S(2)}, u32[]{:S(2)}) collective-permute-start(f32[8,1024]{1,0:T(8,128)S(1)} %pad_maximum_fusion.25), channel_id=1, source_target_pairs={{0,2},{1,3},{2,0},{3,1},{4,6},{5,7},{6,4},{7,5},{8,10},{9,11},{10,... | collective-permute-start | bytes 98312 | tf_op jit(solution)/shard_map/ppermute | solution.py:224
  6.9 6.3 %collective-permute-start.4 = (f32[8,1024]{1,0:T(8,128)S(1)}, f32[8,1024]{1,0:T(8,128)S(1)}, u32[]{:S(2)}, u32[]{:S(2)}) collective-permute-start(f32[8,1024]{1,0:T(8,128)S(1)} %pad_maximum_fusion.25), channel_id=1, source_target_pairs={{0,1},{1,2},{2,3},{3,0},{4,5},{5,6},{6,7},{7,4},{8,9},{9,10},{10,1... | collective-permute-start | bytes 98312 | tf_op jit(solution)/shard_map/ppermute | solution.py:224
  8.8 34.6 %collective-permute-start = (f32[3,2,16,256]{3,2,1,0:T(8,128)S(1)}, f32[3,2,16,256]{3,2,1,0:T(8,128)S(1)}, u32[]{:S(2)}, u32[]{:S(2)}) collective-permute-start(f32[3,2,16,256]{3,2,1,0:T(8,128)S(1)} %get-tuple-element.18), channel_id=1, source_target_pairs={{4,0},{8,4},{12,8},{16,12},{20,16},{24,20},{28,24},{5,1},{9,5},{13... | collective-permute-start | bytes 294920 | tf_op jit(solution)/shard_map/ppermute | solution.py:166
  10.8 32.5 %collective-permute-start.1 = (f32[3,2,16,256]{3,2,1,0:T(8,128)S(1)}, f32[3,2,16,256]{3,2,1,0:T(8,128)S(1)}, u32[]{:S(2)}, u32[]{:S(2)}) collective-permute-start(f32[3,2,16,256]{3,2,1,0:T(8,128)S(1)} %get-tuple-element.19), channel_id=1, source_target_pairs={{0,4},{4,8},{8,12},{12,16},{16,20},{20,24},{24,28},{1,5},{5,9},{9,... | collective-permute-start | bytes 294920 | tf_op jit(solution)/shard_map/ppermute | solution.py:163
  37.9 10.4 %copy-start.7 = (s32[8,16,256]{2,1,0:T(8,128)S(1)}, s32[8,16,256]{2,1,0:T(8,128)}, u32[]{:S(2)}) copy-start(s32[8,16,256]{2,1,0:T(8,128)} %param.15) | copy-start | bytes 393220
  37.9 16.7 %all-to-all-start = ((f32[32,8,128]{2,1,0:T(8,128)}), f32[32,8,128]{2,1,0:T(8,128)}, u32[]{:S(2)}, u32[]{:S(2)}) async-start(f32[32,8,128]{2,1,0:T(8,128)} %incident.1), calls=%async_computation | async-start | bytes 262144 | tf_op jit(solution)/shard_map/all_to_all | solution.py:233
  43.6 5.3 %collective-permute-start.3 = (f32[3,12,2,256]{3,2,1,0:T(2,128)S(1)}, f32[3,12,2,256]{3,2,1,0:T(2,128)S(1)}, u32[]{:S(2)}, u32[]{:S(2)}) collective-permute-start(f32[3,12,2,256]{3,2,1,0:T(2,128)S(1)} %get-tuple-element.9), channel_id=1, source_target_pairs={{0,1},{1,2},{2,3},{4,5},{5,6},{6,7},{8,9},{9,10},{10,11},{12,13},{... | collective-permute-start | bytes 221192 | tf_op jit(solution)/shard_map/ppermute | solution.py:163
  46.9 6.2 %collective-permute-start.2 = (f32[3,12,2,256]{3,2,1,0:T(2,128)S(1)}, f32[3,12,2,256]{3,2,1,0:T(2,128)S(1)}, u32[]{:S(2)}, u32[]{:S(2)}) collective-permute-start(f32[3,12,2,256]{3,2,1,0:T(2,128)S(1)} %get-tuple-element.10), channel_id=1, source_target_pairs={{1,0},{2,1},{3,2},{5,4},{6,5},{7,6},{9,8},{10,9},{11,10},{13,12},{... | collective-permute-start | bytes 221192 | tf_op jit(solution)/shard_map/ppermute | solution.py:166
  53.2 0.6 copy-start.5
  61.3 1.4 %copy-start.3 = (f32[8,16,256]{2,1,0:T(8,128)S(1)}, f32[8,16,256]{2,1,0:T(8,128)}, u32[]{:S(2)}) copy-start(f32[8,16,256]{2,1,0:T(8,128)} %param.14) | copy-start | bytes 393220
  61.3 1.4 %copy-start.4 = (f32[3,8,16,256]{3,2,1,0:T(8,128)S(1)}, f32[3,8,16,256]{3,2,1,0:T(8,128)}, u32[]{:S(2)}) copy-start(f32[3,8,16,256]{3,2,1,0:T(8,128)} %param.13) | copy-start | bytes 1179652
  61.3 1.4 %copy-start.6 = (f32[3,12,2,256]{3,2,1,0:T(2,128)S(1)}, f32[3,12,2,256]{3,2,1,0:T(2,128)}, u32[]{:S(2)}) copy-start(f32[3,12,2,256]{3,2,1,0:T(2,128)} %copy-done.5) | copy-start | bytes 221188
  63.4 4.3 %collective-permute-start.7 = (f32[3,2,16,256]{3,2,1,0:T(8,128)S(1)}, f32[3,2,16,256]{3,2,1,0:T(8,128)S(1)}, u32[]{:S(2)}, u32[]{:S(2)}) collective-permute-start(f32[3,2,16,256]{3,2,1,0:T(8,128)S(1)} %get-tuple-element.13), channel_id=1, source_target_pairs={{4,0},{8,4},{12,8},{16,12},{20,16},{24,20},{28,24},{5,1},{9,5},{13... | collective-permute-start | bytes 294920 | tf_op jit(solution)/shard_map/ppermute | solution.py:166
  65.3 6.8 %collective-permute-start.8 = (f32[3,2,16,256]{3,2,1,0:T(8,128)S(1)}, f32[3,2,16,256]{3,2,1,0:T(8,128)S(1)}, u32[]{:S(2)}, u32[]{:S(2)}) collective-permute-start(f32[3,2,16,256]{3,2,1,0:T(8,128)S(1)} %get-tuple-element.14), channel_id=1, source_target_pairs={{0,4},{4,8},{8,12},{12,16},{16,20},{20,24},{24,28},{1,5},{5,9},{9,... | collective-permute-start | bytes 294920 | tf_op jit(solution)/shard_map/ppermute | solution.py:163
  72.2 5.4 %collective-permute-start.10 = (f32[3,12,2,256]{3,2,1,0:T(2,128)S(1)}, f32[3,12,2,256]{3,2,1,0:T(2,128)S(1)}, u32[]{:S(2)}, u32[]{:S(2)}) collective-permute-start(f32[3,12,2,256]{3,2,1,0:T(2,128)S(1)} %get-tuple-element.7), channel_id=1, source_target_pairs={{0,1},{1,2},{2,3},{4,5},{5,6},{6,7},{8,9},{9,10},{10,11},{12,13},{... | collective-permute-start | bytes 221192 | tf_op jit(solution)/shard_map/ppermute | solution.py:163
  75.6 6.2 %collective-permute-start.9 = (f32[3,12,2,256]{3,2,1,0:T(2,128)S(1)}, f32[3,12,2,256]{3,2,1,0:T(2,128)S(1)}, u32[]{:S(2)}, u32[]{:S(2)}) collective-permute-start(f32[3,12,2,256]{3,2,1,0:T(2,128)S(1)} %get-tuple-element.8), channel_id=1, source_target_pairs={{1,0},{2,1},{3,2},{5,4},{6,5},{7,6},{9,8},{10,9},{11,10},{13,12},{... | collective-permute-start | bytes 221192 | tf_op jit(solution)/shard_map/ppermute | solution.py:166
  83.2 19.3 %copy-start.1 = (f32[3,8,16,256]{3,2,1,0:T(8,128)}, f32[3,8,16,256]{3,2,1,0:T(8,128)S(1)}, u32[]{:S(2)}) copy-start(f32[3,8,16,256]{3,2,1,0:T(8,128)S(1)} %fusion.27) | copy-start | bytes 1179652
  83.2 4.3 %collective-permute-start.11 = (f32[3,2,16,256]{3,2,1,0:T(8,128)S(1)}, f32[3,2,16,256]{3,2,1,0:T(8,128)S(1)}, u32[]{:S(2)}, u32[]{:S(2)}) collective-permute-start(f32[3,2,16,256]{3,2,1,0:T(8,128)S(1)} %get-tuple-element.11), channel_id=1, source_target_pairs={{4,0},{8,4},{12,8},{16,12},{20,16},{24,20},{28,24},{5,1},{9,5},{13... | collective-permute-start | bytes 294920 | tf_op jit(solution)/shard_map/ppermute | solution.py:166
  85.1 6.8 %collective-permute-start.12 = (f32[3,2,16,256]{3,2,1,0:T(8,128)S(1)}, f32[3,2,16,256]{3,2,1,0:T(8,128)S(1)}, u32[]{:S(2)}, u32[]{:S(2)}) collective-permute-start(f32[3,2,16,256]{3,2,1,0:T(8,128)S(1)} %get-tuple-element.12), channel_id=1, source_target_pairs={{0,4},{4,8},{8,12},{12,16},{16,20},{20,24},{24,28},{1,5},{5,9},{9,... | collective-permute-start | bytes 294920 | tf_op jit(solution)/shard_map/ppermute | solution.py:163
  92.0 5.4 %collective-permute-start.14 = (f32[3,12,2,256]{3,2,1,0:T(2,128)S(1)}, f32[3,12,2,256]{3,2,1,0:T(2,128)S(1)}, u32[]{:S(2)}, u32[]{:S(2)}) collective-permute-start(f32[3,12,2,256]{3,2,1,0:T(2,128)S(1)} %get-tuple-element.5), channel_id=1, source_target_pairs={{0,1},{1,2},{2,3},{4,5},{5,6},{6,7},{8,9},{9,10},{10,11},{12,13},{... | collective-permute-start | bytes 221192 | tf_op jit(solution)/shard_map/ppermute | solution.py:163
  95.5 6.2 %collective-permute-start.13 = (f32[3,12,2,256]{3,2,1,0:T(2,128)S(1)}, f32[3,12,2,256]{3,2,1,0:T(2,128)S(1)}, u32[]{:S(2)}, u32[]{:S(2)}) collective-permute-start(f32[3,12,2,256]{3,2,1,0:T(2,128)S(1)} %get-tuple-element.6), channel_id=1, source_target_pairs={{1,0},{2,1},{3,2},{5,4},{6,5},{7,6},{9,8},{10,9},{11,10},{13,12},{... | collective-permute-start | bytes 221192 | tf_op jit(solution)/shard_map/ppermute | solution.py:166

commit v3 on v2

--- a/solution.py
+++ b/solution.py
@@ -46,24 +46,21 @@
     return lax.broadcasted_iota(jnp.int32, shape, 0)
 
 
-def incident_kernel(slot_stride, par_ref, xyz_ref, own_ref, off_ref, out_ref, x8_ref, acc_ref):
-    comps = par_ref.shape[1]
+def add_components(par_refs, xyz_ref, x8_ref, acc_ref):
     points = xyz_ref.shape[1]
-    owners = out_ref.shape[0]
     kc = 256
     tile = 256
     x8_ref[...] = jnp.zeros(x8_ref.shape, F32)
     x8_ref[0:3, :] = xyz_ref[...]
     xhi, xmid, xlo = split_three(x8_ref[...])
     right = jnp.concatenate([xhi, xmid, xlo, xhi, xmid, xhi], axis=0).astype(BF16)
-    acc_ref[...] = jnp.zeros(acc_ref.shape, F32)
     rows8 = row_ids((8, kc))
     times = step_size * (rows8 + 1).astype(F32)
     rows16 = row_ids((16, kc))
     comp_row = jnp.where(rows16 < 6, rows16 % 3, (rows16 + 2) % 3)
     valued = (rows16 < 10) & (rows16 != 6)
 
-    def body(step, total):
+    def body(par_ref, step, total):
         blk = par_ref[:, pl.ds(pl.multiple_of(step * kc, kc), kc)]
         kv = jnp.where(rows8 < 3, blk * inv_two_pi, 0.0)
         khi, kmid, klo = split_three(kv)
@@ -97,7 +94,26 @@
             acc_ref[:, cols] += part
         return total - wc
 
-    total = lax.fori_loop(0, comps // kc, body, jnp.zeros((16, kc), F32))
+    total = jnp.zeros((16, kc), F32)
+    for par_ref in par_refs:
+        steps = par_ref.shape[1] // kc
+        total = lax.fori_loop(0, steps, lambda step, t, ref=par_ref: body(ref, step, t), total)
+    return total
+
+
+def first_incident_kernel(count, *refs):
+    par_refs, (xyz_ref, acc_ref, total_ref, x8_ref) = refs[:count], refs[count:]
+    acc_ref[...] = jnp.zeros(acc_ref.shape, F32)
+    total_ref[...] = add_components(par_refs, xyz_ref, x8_ref, acc_ref)
+
+
+def last_incident_kernel(count, slot_stride, *refs):
+    par_refs, refs = refs[:count], refs[count:]
+    first_ref, first_total_ref, xyz_ref, own_ref, off_ref, out_ref, x8_ref, acc_ref = refs
+    points = xyz_ref.shape[1]
+    owners = out_ref.shape[0]
+    acc_ref[...] = first_ref[...]
+    total = add_components(par_refs, xyz_ref, x8_ref, acc_ref) + first_total_ref[...]
     vals = acc_ref[0:16, :] + acc_ref[16:32, :] + jnp.sum(total, axis=1, keepdims=True)
     vals = jnp.where(row_ids((16, points)) == 6, off_ref[...].astype(F32), vals)
     v1, v2, v3 = split_three(vals)
@@ -122,13 +138,24 @@
             out_ref[8 * t + 2 * pair + 1] = jnp.where(left_half, pltpu.roll(low, slot_stride, 1), high)
 
 
-def scatter_kernel(nz, val_ref, out_ref):
+TILE = 8
+DEEP = 6
+MID = 4
+NEAR = 2
+
+
+def half_turn(tile):
+    return pltpu.roll(tile, TILE // 2, 0)
+
+
+def scatter_kernel(par_ref, val_ref, mask_ref, out_ref, face_ref, acc_ref):
     sources = val_ref.shape[0]
-    rows = out_ref.shape[1]
+    cx, cy, nz = mask_ref.shape
+    rows = cx * cy
     chunk = 256
     lanes = val_ref.shape[2]
     left_half = lax.broadcasted_iota(jnp.int32, (8, lanes), 1) < lanes // 2
-    out_ref[...] = jnp.zeros(out_ref.shape, F32)
+    acc_ref[...] = jnp.zeros(acc_ref.shape, F32)
 
     def body(step, carry):
         lows, highs = [], []
@@ -149,45 +176,237 @@
             r = i if i < 6 else i + 1
             left = jnp.concatenate([mask * hi[r : r + 1, :], mask * lo[r : r + 1, :]], axis=0)
             got = lax.dot_general(left, zt, (((1,), (1,)), ((), ())), preferred_element_type=F32)
-            out_ref[i] += got[0:rows] + got[rows:]
+            acc_ref[i] += got[0:rows] + got[rows:]
         return carry
 
     lax.fori_loop(0, sources // 4, body, 0)
-
-
-def with_halo(block, sides, width):
-    for axis, dim in sides:
-        count = lax.axis_size(axis)
-        forward = [(i, i + 1) for i in range(count - 1)]
-        backward = [(target, source) for source, target in forward]
-        low = lax.ppermute(
-            lax.slice_in_dim(block, block.shape[dim] - width, None, axis=dim), axis, forward
-        )
-        high = lax.ppermute(lax.slice_in_dim(block, 0, width, axis=dim), axis, backward)
-        block = jnp.concatenate([low, block, high], axis=dim)
-    return block
-
-
-def shifted(padded, axis_pos, offset):
-    result = padded
-    for dim_pos in (1, 2, 3):
-        first_cell = 2 + offset if dim_pos == axis_pos else 2
-        result = lax.slice_in_dim(
-            result, first_cell, first_cell + padded.shape[dim_pos] - 4, axis=dim_pos
-        )
-    return result
-
-
-def laplace_four(padded):
-    summed = centre_weight * shifted(padded, 0, 0)
-    for axis_pos in (1, 2, 3):
-        summed = summed + near_weight * (
-            shifted(padded, axis_pos, 1) + shifted(padded, axis_pos, -1)
-        )
-        summed = summed + far_weight * (
-            shifted(padded, axis_pos, 2) + shifted(padded, axis_pos, -2)
-        )
-    return summed
+    sign = (mask_ref[...] == 1).astype(F32) - (mask_ref[...] == 2).astype(F32)
+    for i in range(9):
+        out_ref[i] = acc_ref[i].reshape(cx, cy, nz) * sign
+    parity = par_ref[0]
+    upper = row_ids((TILE, nz)) >= TILE // 2
+    for high, place in ((True, parity), (False, 1 - parity)):
+        ys = slice(cy - TILE, cy) if high else slice(0, TILE)
+        keep = upper if high else ~upper
+        for i in range(3):
+            for x in range(cx):
+                face_ref[place, i, x] = jnp.where(keep, out_ref[i, x, ys], half_turn(out_ref[3 + i, x, ys]))
+
+
+def pair_list(count, odd):
+    first = 1 if odd else 0
+    pairs = [(i, i + 1) for i in range(first, count - 1, 2)]
+    return pairs + [(j, i) for i, j in pairs]
+
+
+def swap_faces(faces, axis):
+    count = lax.axis_size(axis)
+    return [lax.ppermute(faces[k], axis, pair_list(count, k)) for k in (0, 1)]
+
+
+def field_face_kernel(par_ref, cur_ref, ear_ref, coef_ref, out_ref):
+    _, cx, cy, nz = cur_ref.shape
+    parity = par_ref[0]
+    upper = row_ids((TILE, nz)) >= TILE // 2
+    for high, place in ((True, parity), (False, 1 - parity)):
+        ys = slice(cy - TILE, cy) if high else slice(0, TILE)
+        keep = upper if high else ~upper
+        for x in range(cx):
+            for i in range(3):
+                out_ref[place, i, x] = cur_ref[i, x, ys]
+            out_ref[place, 3, x] = jnp.where(keep, ear_ref[0, x, ys], half_turn(ear_ref[1, x, ys]))
+            out_ref[place, 4, x] = jnp.where(keep, ear_ref[2, x, ys], half_turn(coef_ref[x, ys]))
+
+
+def face_tile(ref, name, x):
+    if name < 3:
+        return ref[name, x]
+    tile = ref[3 + (name - 3) // 2, x]
+    return half_turn(tile) if name in (4, 6) else tile
+
+
+def select_side(parity, even_ref, odd_ref, high):
+    from_even = (parity == 0) if high else (parity == 1)
+
+    def read(get):
+        return jnp.where(from_even, get(even_ref), get(odd_ref))
+
+    return read
+
+
+FIELD_PLAN = [(DEEP, MID)] * 3 + [(MID, NEAR)] * 4
+FORCE_PLAN = [(MID, NEAR)] * 3 + [(NEAR, 0)] * 3
+
+
+def plan_tiles(plan, cy):
+    out = []
+    for name, (planes, corners) in enumerate(plan):
+        for dist in range(1, planes + 1):
+            for part in list(range(cy // TILE)) + ([-1] if dist <= corners else []):
+                out.append((name, dist, part, len(out)))
+    return out
+
+
+def side_kernel(plan, own_tile, halo_tile, cx, cy, nz, px_ref, py_ref, even_ref, odd_ref, out_ref):
+    upper = row_ids((TILE, nz)) >= TILE // 2
+    low = select_side(py_ref[0], even_ref, odd_ref, False)
+    high = select_side(py_ref[0], even_ref, odd_ref, True)
+    parity = px_ref[0]
+    for is_high, place in ((True, parity), (False, 1 - parity)):
+        for name, dist, part, at in plan_tiles(plan, cy):
+            x = cx - dist if is_high else dist - 1
+            if part >= 0:
+                tile = own_tile(name, x, slice(part * TILE, (part + 1) * TILE))
+            else:
+                tile = jnp.where(
+                    upper,
+                    low(lambda ref: halo_tile(ref, name, x)),
+                    high(lambda ref: halo_tile(ref, name, x)),
+                )
+            out_ref[place, at] = tile
+
+
+def field_side_kernel(px_ref, py_ref, cur_ref, ear_ref, coef_ref, even_ref, odd_ref, out_ref):
+    _, cx, cy, nz = cur_ref.shape
+
+    def own_tile(name, x, ys):
+        if name < 3:
+            return cur_ref[name, x, ys]
+        return ear_ref[name - 3, x, ys] if name < 6 else coef_ref[x, ys]
+
+    side_kernel(FIELD_PLAN, own_tile, face_tile, cx, cy, nz, px_ref, py_ref, even_ref, odd_ref, out_ref)
+
+
+def force_side_kernel(px_ref, py_ref, force_ref, even_ref, odd_ref, out_ref):
+    _, cx, cy, nz = force_ref.shape
+    side_kernel(
+        FORCE_PLAN,
+        lambda name, x, ys: force_ref[name, x, ys],
+        lambda ref, name, x: ref[name, x],
+        cx, cy, nz, px_ref, py_ref, even_ref, odd_ref, out_ref,
+    )
+
+
+def laplacian(plane, x_near, x_far):
+    rows, nz = plane.shape
+    lane = lax.broadcasted_iota(jnp.int32, (rows, nz), 1)
+
+    def along_z(k):
+        below = jnp.where(lane >= k, pltpu.roll(plane, k, 1), 0.0)
+        return below + jnp.where(lane < nz - k, pltpu.roll(plane, nz - k, 1), 0.0)
+
+    def along_y(k):
+        return pltpu.roll(plane, k, 0) + pltpu.roll(plane, rows - k, 0)
+
+    near = x_near + along_y(1) + along_z(1)
+    far = x_far + along_y(2) + along_z(2)
+    return centre_weight * plane + near_weight * near + far_weight * far
+
+
+def laplacian_at(ref, i, x):
+    return laplacian(ref[i, x], ref[i, x - 1] + ref[i, x + 1], ref[i, x - 2] + ref[i, x + 2])
+
+
+def first_wave_kernel(
+    px_ref, py_ref, cur_ref, ear_ref, coef_ref, ye_ref, yo_ref, xe_ref, xo_ref,
+    next_ref, now_ref, wide_coef_ref, u_ref, e_ref, c_ref,
+):
+    _, cx, cy, nz = cur_ref.shape
+    own = slice(TILE, TILE + cy)
+    lower, higher = slice(0, TILE), slice(TILE + cy, 2 * TILE + cy)
+    low = select_side(py_ref[0], ye_ref, yo_ref, False)
+    high = select_side(py_ref[0], ye_ref, yo_ref, True)
+
+    def put(name, x, rows, value):
+        if name < 3:
+            u_ref[name, DEEP + x, rows] = value
+        elif name < 6:
+            e_ref[name - 3, MID + x, rows] = value
+        else:
+            c_ref[MID + x, rows] = value
+
+    for x in range(cx):
+        for name in range(7):
+            value = cur_ref[name, x] if name < 3 else ear_ref[name - 3, x] if name < 6 else coef_ref[x]
+            put(name, x, own, value)
+            put(name, x, lower, low(lambda ref: face_tile(ref, name, x)))
+            put(name, x, higher, high(lambda ref: face_tile(ref, name, x)))
+    for is_high in (False, True):
+        read = select_side(px_ref[0], xe_ref, xo_ref, is_high)
+        for name, dist, part, at in plan_tiles(FIELD_PLAN, cy):
+            x = cx - 1 + dist if is_high else -dist
+            tile = read(lambda ref: ref[at])
+            if part >= 0:
+                put(name, x, slice(TILE * (part + 1), TILE * (part + 2)), tile)
+            else:
+                put(name, x, lower, tile)
+                put(name, x, higher, tile)
+
+    def plane(x, carry):
+        coef = c_ref[x]
+        for i in range(3):
+            at = x + DEEP - MID
+            next_ref[i, x] = 2.0 * u_ref[i, at] - e_ref[i, x] + coef * laplacian_at(u_ref, i, at)
+        return carry
+
+    lax.fori_loop(0, cx + 2 * MID, plane, 0)
+    for i in range(3):
+        now_ref[i] = u_ref[i, DEEP - NEAR : DEEP + cx + NEAR]
+    wide_coef_ref[...] = c_ref[MID - NEAR : MID + cx + NEAR]
+
+
+def last_wave_kernel(
+    px_ref, py_ref, next_ref, now_ref, coef_ref, force_ref, ye_ref, yo_ref, xe_ref, xo_ref,
+    final_ref, prior_ref, one_ref, two_ref,
+):
+    _, cx, cy, nz = force_ref.shape
+    own = slice(TILE, TILE + cy)
+    lower, higher = slice(0, TILE), slice(TILE + cy, 2 * TILE + cy)
+    low = select_side(py_ref[0], ye_ref, yo_ref, False)
+    high = select_side(py_ref[0], ye_ref, yo_ref, True)
+    one_ref[...] = next_ref[...]
+    for i in range(3):
+        for x in range(cx):
+            one_ref[i, MID + x, own] += force_ref[i, x]
+            two_ref[i, NEAR + x, own] = force_ref[3 + i, x]
+            for rows, read in ((lower, low), (higher, high)):
+                tile = read(lambda ref: ref[i, x])
+                one_ref[i, MID + x, rows] += tile
+                two_ref[i, NEAR + x, rows] = half_turn(tile)
+    for is_high in (False, True):
+        read = select_side(px_ref[0], xe_ref, xo_ref, is_high)
+        for name, dist, part, at in plan_tiles(FORCE_PLAN, cy):
+            x = cx - 1 + dist if is_high else -dist
+            tile = read(lambda ref: ref[at])
+            if name >= 3:
+                two_ref[name - 3, NEAR + x, slice(TILE * (part + 1), TILE * (part + 2))] = tile
+            elif part >= 0:
+                one_ref[name, MID + x, slice(TILE * (part + 1), TILE * (part + 2))] += tile
+            else:
+                one_ref[name, MID + x, lower] += tile
+                one_ref[name, MID + x, higher] += tile
+
+    def second(x, carry):
+        coef = coef_ref[x]
+        for i in range(3):
+            at = x + MID - NEAR
+            lap = laplacian_at(one_ref, i, at)
+            two_ref[i, x] = 2.0 * one_ref[i, at] - now_ref[i, x] + coef * lap + two_ref[i, x]
+        return carry
+
+    lax.fori_loop(0, cx + 2 * NEAR, second, 0)
+
+    def third(x, carry):
+        coef = coef_ref[x + NEAR]
+        for i in range(3):
+            at = x + NEAR
+            plane = two_ref[i, at]
+            moved = 2.0 * plane - one_ref[i, x + MID] + coef * laplacian_at(two_ref, i, at)
+            final_ref[i, x] = moved[TILE : TILE + cy] + force_ref[6 + i, x]
+            prior_ref[i, x] = plane[TILE : TILE + cy]
+        return carry
+
+    lax.fori_loop(0, cx, third, 0)
 
 
 def local(
@@ -217,40 +436,95 @@
     comp_count = lax.axis_size("comp")
     device_count = slab_count * comp_count
     slot_count = max(2, 2 * point_count // device_count)
-    rows_out = STEPS * 3
-    blocks = [own_block]
-    for shift in range(1, comp_count):
-        ring = [(i, (i + shift) % comp_count) for i in range(comp_count)]
-        blocks.append(lax.ppermute(own_block, "comp", ring))
-    params = jnp.concatenate(blocks, axis=1)
+    _, cx, cy, nz = current_field.shape
     assert slot_count <= HALF and device_count % 8 == 0
-    packed = pl.pallas_call(
-        lambda *refs: incident_kernel(HALF, *refs),
-        out_shape=jax.ShapeDtypeStruct((device_count, 8, 2 * HALF), F32),
-        scratch_shapes=[pltpu.VMEM((8, point_count), F32), pltpu.VMEM((32, point_count), F32)],
-        name="incident",
-    )(params, point_xyz, point_owner.reshape(1, point_count), cell_offset.reshape(1, point_count))
+    assert cx >= DEEP and cy >= 2 * TILE and cy % TILE == 0
+    wide = cy + 2 * TILE
+    smem = pl.BlockSpec(memory_space=pltpu.SMEM)
+    vmem = pl.BlockSpec(memory_space=pltpu.VMEM)
+
+    def call(kernel, name, operands, shapes, scratch=(), scalars=0):
+        shapes = [jax.ShapeDtypeStruct(shape, F32) for shape in shapes]
+        return pl.pallas_call(
+            kernel,
+            out_shape=shapes,
+            in_specs=[smem] * scalars + [vmem] * (len(operands) - scalars),
+            out_specs=[vmem] * len(shapes),
+            scratch_shapes=[pltpu.VMEM(shape, F32) for shape in scratch],
+            name=name,
+        )(*operands)
+
+    px = (lax.axis_index("slab") % 2).astype(jnp.int32).reshape(1)
+    py = (lax.axis_index("comp") % 2).astype(jnp.int32).reshape(1)
+    if comp_count == 4:
+        near_block = lax.ppermute(own_block, "comp", pair_list(4, 0))
+        first_blocks = [own_block, near_block]
+        ring = pair_list(4, 1) + [(0, 3), (3, 0)]
+        far_block = lax.ppermute(jnp.concatenate(first_blocks, axis=1), "comp", ring)
+        last_blocks = [far_block]
+    else:
+        first_blocks = [own_block]
+        last_blocks = [
+            lax.ppermute(own_block, "comp", [(i, (i + k) % comp_count) for i in range(comp_count)])
+            for k in range(1, comp_count)
+        ]
+    fields = (current_field, earlier_field, wave_coef)
+    (faces,) = call(field_face_kernel, "field_faces", (py, *fields), [(2, 5, cx, TILE, nz)], scalars=1)
+    ye, yo = swap_faces(faces, "comp")
+    (sum_one, total_one) = call(
+        lambda *refs: first_incident_kernel(len(first_blocks), *refs),
+        "incident_first",
+        (*first_blocks, point_xyz),
+        [(32, point_count), (16, 256)],
+        [(8, point_count)],
+    )
+    field_tiles = len(plan_tiles(FIELD_PLAN, cy))
+    (sides,) = call(
+        field_side_kernel, "field_sides", (px, py, *fields, ye, yo), [(2, field_tiles, TILE, nz)], scalars=2
+    )
+    xe, xo = swap_faces(sides, "slab")
+    (packed,) = call(
+        lambda *refs: last_incident_kernel(len(last_blocks), HALF, *refs),
+        "incident_last",
+        (
+            *last_blocks, sum_one, total_one, point_xyz,
+            point_owner.reshape(1, point_count), cell_offset.reshape(1, point_count),
+        ),
+        [(device_count, 8, 2 * HALF)],
+        [(8, point_count), (32, point_count)],
+    )
     arrived = lax.all_to_all(packed, ("slab", "comp"), split_axis=0, concat_axis=0, tiled=True)
-    cx, cy, nz = current_field.shape[1:]
-    forcing = pl.pallas_call(
-        lambda *refs: scatter_kernel(nz, *refs),
-        out_shape=jax.ShapeDtypeStruct((rows_out, cx * cy, nz), F32),
-        name="scatter",
-    )(arrived)
-    forcing = forcing.reshape(rows_out, cx, cy, nz)
-    sign_field = ((layer_mask == 1).astype(F32) - (layer_mask == 2).astype(F32))[None]
-    current = current_field
-    earlier = earlier_field
-    for step_index in range(STEPS):
-        widened = with_halo(current, (("slab", 1), ("comp", 2)), 2)
-        padded = jnp.pad(widened, ((0, 0), (0, 0), (0, 0), (2, 2)))
-        source = forcing[3 * step_index : 3 * step_index + 3]
-        following = (
-            2.0 * current - earlier + wave_coef[None] * laplace_four(padded) + sign_field * source
-        )
-        earlier = current
-        current = following
-    return (current, earlier)
+    force, force_faces = call(
+        scatter_kernel,
+        "scatter",
+        (py, arrived, layer_mask),
+        [(9, cx, cy, nz), (2, 3, cx, TILE, nz)],
+        [(9, cx * cy, nz)],
+        scalars=1,
+    )
+    fye, fyo = swap_faces(force_faces, "comp")
+    force_tiles = len(plan_tiles(FORCE_PLAN, cy))
+    (force_sides,) = call(
+        force_side_kernel, "force_sides", (px, py, force, fye, fyo), [(2, force_tiles, TILE, nz)], scalars=2
+    )
+    fxe, fxo = swap_faces(force_sides, "slab")
+    following, now, wide_coef = call(
+        first_wave_kernel,
+        "first_wave",
+        (px, py, *fields, ye, yo, xe, xo),
+        [(3, cx + 2 * MID, wide, nz), (3, cx + 2 * NEAR, wide, nz), (cx + 2 * NEAR, wide, nz)],
+        [(3, cx + 2 * DEEP, wide, nz), (3, cx + 2 * MID, wide, nz), (cx + 2 * MID, wide, nz)],
+        scalars=2,
+    )
+    final, prior = call(
+        last_wave_kernel,
+        "last_wave",
+        (px, py, following, now, wide_coef, force, fye, fyo, fxe, fxo),
+        [current_field.shape, current_field.shape],
+        [(3, cx + 2 * MID, wide, nz), (3, cx + 2 * NEAR, wide, nz)],
+        scalars=2,
+    )
+    return (final, prior)
 
 
 def solution(mesh):

time: 105 us -> 103 us (0.981)
  Pallas kernels: 29.9 us -> 52.2 us
  starting transfers between devices: 37.1 us -> 22.2 us
  waiting for transfers between devices: 23.6 us -> 14.1 us
  local copies, waits for them, and re-layouts: 3.93 us -> 10.7 us
  other arithmetic: 7.07 us -> 0.8 us
    pallas_call x2 -> x8, Pallas kernels: 29.9 us -> 52.2 us  [call(): pl.pallas_call(kernel, out_shape=shapes, in_specs=[smem] * scalars + [vme...]
    ppermute x15 -> x10, starting transfers between devices: 31.7 us -> 16.8 us  [the longest x8 14.2 us: swap_faces(): return [lax.ppermute(faces[k], axis, pair_list(count, k)) for k in (0, 1)]]
    ppermute x15 -> x10, waiting for transfers between devices: 23.6 us -> 10.2 us  [the longest x8 10.2 us: swap_faces(): return [lax.ppermute(faces[k], axis, pair_list(count, k)) for k in (0, 1)]]
    squeeze x0 -> x4, local copies, waits for them, and re-layouts: none -> 5.45 us  [swap_faces(): return [lax.ppermute(faces[k], axis, pair_list(count, k)) for k in (0, 1)]]
    all_to_all x1, waiting for transfers between devices: 0.01 us -> 3.98 us  [local(): lax.all_to_all(packed, ('slab', 'comp'), split_axis=0, concat_axis=0, til...]
    unnamed x18 -> x28, local copies, waits for them, and re-layouts: 1.51 us -> 5.23 us
    concatenate x6 -> x1, other arithmetic: 3.64 us -> 0.02 us  [local(): jnp.concatenate(first_blocks, axis=1)]
    add x3 -> x0, other arithmetic: 2.63 us -> none  [local(): 2.0 * current - earlier + wave_coef[None] * laplace_four(padded)]
  transfers between devices with their start and end apart: 16 -> 11, of which waited for: 8 -> 3; matrix products, arithmetic and copies ran while one was open for 3% -> 4% of each run, Pallas kernels for 22% -> 38%
where the time goes in v3:
time: 103 us; the launch traced here: 102 us
  Pallas kernels  52.2 us (51%)
  starting transfers between devices  22.2 us (22%)
  waiting for transfers between devices  14.1 us (14%)
  local copies, waits for them, and re-layouts  10.7 us (10%)
  matrix products  1.12 us (1%)
    pallas_call x8, Pallas kernels, call(): pl.pallas_call(kernel, out_shape=shapes, in_specs=[smem] * scalars + [vme...  52.2 us
    ppermute x8, starting transfers between devices, swap_faces(): return [lax.ppermute(faces[k], axis, pair_list(count, k)) for k in (0, 1)]  14.2 us
    ppermute x8, waiting for transfers between devices, swap_faces(): return [lax.ppermute(faces[k], axis, pair_list(count, k)) for k in (0, 1)]  10.2 us
    squeeze x4, local copies, waits for them, and re-layouts, swap_faces(): return [lax.ppermute(faces[k], axis, pair_list(count, k)) for k in (0, 1)]  5.45 us
    all_to_all x1, starting transfers between devices, local(): lax.all_to_all(packed, ('slab', 'comp'), split_axis=0, concat_axis=0, til...  5.41 us
    unnamed x28, local copies, waits for them, and re-layouts  5.23 us
    all_to_all x1, waiting for transfers between devices, local(): lax.all_to_all(packed, ('slab', 'comp'), split_axis=0, concat_axis=0, til...  3.98 us
  transfers between devices with their start and end apart: 11, of which 3 were waited for; matrix products, arithmetic and copies ran while one was open for 4% of the time, Pallas kernels for 38%

profile of v3, /device:TPU:4, one launch (start us, length us, event | category | flops | bytes accessed | tf_op | source)
XLA Modules:
  0.0 102.0 jit_solution(6383363966810459183)
XLA Ops:
  0.6 0.0 copy-start
  0.6 0.7 copy-done
  1.3 1.1 %fusion = f32[1,1024]{1,0:T(1,128)S(1)} fusion(f32[256,1]{0,1:T(1,128)S(1)} %bitcast.24, s32[1024]{0:T(1024)} %param.22), kind=kOutput, calls=%fused_computation.1 | convolution fusion | flops 3407872 | bytes 9216 | tf_op jit(solution)/shard_map/dot_general | solution.py:428
  2.4 0.8 pad_maximum_fusion.1.refs_0_
  3.2 0.0 copy-start.9
  3.2 1.6 %collective-permute-start.4 = (f32[8,1024]{1,0:T(8,128)S(1)}, f32[8,1024]{1,0:T(8,128)S(1)}, u32[]{:S(2)}, u32[]{:S(2)}) collective-permute-start(f32[8,1024]{1,0:T(8,128)S(1)} %pad_maximum_fusion.1.refs_0_), channel_id=1, source_target_pairs={{0,1},{2,3},{1,0},{3,2},{4,5},{6,7},{5,4},{7,6},{8,9},{10,11},{9,8... | collective-permute-start | bytes 98312 | tf_op jit(solution)/shard_map/ppermute | solution.py:460
  4.9 0.0 copy-start.10
  4.9 0.0 copy-start.11
  4.9 0.0 copy-start.13
  4.9 2.1 %field_faces.1 = f32[2,5,8,8,256]{4,3,2,1,0:T(8,128)} custom-call(s32[1]{0:T(128)} %bitcast.1.par_ref.py_ref, f32[3,8,16,256]{3,2,1,0:T(8,128)} %cur_ref.5, f32[3,8,16,256]{3,2,1,0:T(8,128)} %ear_ref.5, f32[8,16,256]{2,1,0:T(8,128)} %coef_ref.5), custom_call_target="tpu_custom_call" | custom-call | tf_op jit(solution)/shard_map/field_faces/pallas_call | solution.py:448
  6.9 1.1 %slice_bitcast_fusion.4 = (f32[5,8,8,256]{3,2,1,0:T(8,128)S(1)}, f32[5,8,8,256]{3,2,1,0:T(8,128)S(1)}) fusion(f32[2,5,8,8,256]{4,3,2,1,0:T(8,128)} %field_faces.1), kind=kLoop, calls=%fused_computation.7 | loop fusion | bytes 1310720 | tf_op jit(solution)/shard_map/squeeze | solution.py:204
  8.1 0.0 copy-done.9
  8.1 0.7 collective-permute-start.1
  8.8 4.4 %collective-permute-start = (f32[5,8,8,256]{3,2,1,0:T(8,128)S(1)}, f32[5,8,8,256]{3,2,1,0:T(8,128)S(1)}, u32[]{:S(2)}, u32[]{:S(2)}) collective-permute-start(f32[5,8,8,256]{3,2,1,0:T(8,128)S(1)} %get-tuple-element.21), channel_id=1, source_target_pairs={{0,1},{2,3},{1,0},{3,2},{4,5},{6,7},{5,4},{7,6},{8,9},{10,11},{9,8... | collective-permute-start | bytes 983048 | tf_op jit(solution)/shard_map/ppermute | solution.py:204
  13.2 0.0 collective-permute-done.4.refs_1_
  13.2 0.0 copy-done.10
  13.2 0.0 copy-done.11
  13.2 0.0 copy-done.13
  13.3 0.0 copy-start.8
  13.3 1.0 collective-permute-start.5
  14.3 0.0 copy-done.8
  14.3 11.4 %incident_first.1 = (f32[32,1024]{1,0:T(8,128)}, f32[16,256]{1,0:T(8,128)}) custom-call(f32[8,1024]{1,0:T(8,128)} %copy-done.9, f32[8,1024]{1,0:T(8,128)} %copy-done.8, f32[3,1024]{1,0:T(4,128)} %refs_3_.1), custom_call_target="tpu_custom_call" | custom-call | tf_op jit(solution)/shard_map/incident_first/pallas_call | solution.py:448
  25.7 0.0 collective-permute-done.5.refs_0_
  25.7 0.0 copy-start.12
  25.7 0.6 copy-done.12
  26.4 13.2 %incident_last.1 = f32[32,8,128]{2,1,0:T(8,128)} custom-call(f32[8,2048]{1,0:T(8,128)} %copy-done.12, f32[32,1024]{1,0:T(8,128)} %get-tuple-element.12.refs_1_, f32[16,256]{1,0:T(8,128)} %get-tuple-element.13.refs_2_, f32[3,1024]{1,0:T(4,128)} %refs_3_.1, s32[1,1024]{1,0:T(1,128)} %bitcast.27, s32[1,1024]{1,0:T(1,128)} %bitcast.28), custom_call_target="tpu_custom_call" | custom-call | tf_op jit(solution)/shard_map/incident_last/pallas_call | solution.py:448
  39.6 5.4 %all-to-all-start = ((f32[32,8,128]{2,1,0:T(8,128)}), f32[32,8,128]{2,1,0:T(8,128)S(1)}, u32[]{:S(2)}, u32[]{:S(2)}) async-start(f32[32,8,128]{2,1,0:T(8,128)} %incident_last.1), calls=%async_computation | async-start | bytes 262144 | tf_op jit(solution)/shard_map/all_to_all | solution.py:496
  45.0 0.0 collective-permute-done.1.odd_ref.yo_ref
  45.0 0.0 copy-start.1
  45.0 0.0 collective-permute-done.even_ref.ye_ref
  45.0 0.0 copy-start.2
  45.0 0.7 copy-done.1
  45.7 0.1 copy-done.2
  45.8 2.6 %field_sides.1 = f32[2,88,8,256]{3,2,1,0:T(8,128)} custom-call(s32[1]{0:T(128)} %bitcast.px_ref, s32[1]{0:T(128)} %bitcast.1.par_ref.py_ref, f32[3,8,16,256]{3,2,1,0:T(8,128)} %cur_ref.5, f32[3,8,16,256]{3,2,1,0:T(8,128)} %ear_ref.5, f32[8,16,256]{2,1,0:T(8,128)} %coef_ref.5, f32[5,8,8,256]{3,2,1,0:T(8,128)} %copy-done.2, f32[5,8,8,256]{3,2,1,0:T(8,128)} %copy-done.1), custom_call_target="tpu_custom_call" | custom-call | tf_op jit(solution)/shard_map/field_sides/pallas_call | solution.py:448
  48.4 4.0 %all-to-all-done.val_ref = f32[32,8,128]{2,1,0:T(8,128)S(1)} async-done(((f32[32,8,128]{2,1,0:T(8,128)}), f32[32,8,128]{2,1,0:T(8,128)S(1)}, u32[]{:S(2)}, u32[]{:S(2)}) %all-to-all-start) | async-done | bytes 131104 | tf_op jit(solution)/shard_map/all_to_all | solution.py:496
  52.4 0.0 copy-start.7
  52.4 0.7 copy-done.7
  53.0 7.0 %scatter.1 = (f32[9,8,16,256]{3,2,1,0:T(8,128)}, f32[2,3,8,8,256]{4,3,2,1,0:T(8,128)}) custom-call(s32[1]{0:T(128)} %bitcast.1.par_ref.py_ref, f32[32,8,128]{2,1,0:T(8,128)} %copy-done.7, s32[8,16,256]{2,1,0:T(8,128)} %mask_ref.1), custom_call_target="tpu_custom_call" | custom-call | tf_op jit(solution)/shard_map/scatter/pallas_call | solution.py:448
  60.0 1.0 %slice_bitcast_fusion.6 = (f32[3,8,8,256]{3,2,1,0:T(8,128)S(1)}, f32[3,8,8,256]{3,2,1,0:T(8,128)S(1)}) fusion(f32[2,3,8,8,256]{4,3,2,1,0:T(8,128)} %get-tuple-element.15), kind=kLoop, calls=%fused_computation.9 | loop fusion | bytes 786432 | tf_op jit(solution)/shard_map/squeeze | solution.py:204
  61.1 0.7 collective-permute-start.7
  61.7 2.2 %collective-permute-start.6 = (f32[3,8,8,256]{3,2,1,0:T(8,128)S(1)}, f32[3,8,8,256]{3,2,1,0:T(8,128)S(1)}, u32[]{:S(2)}, u32[]{:S(2)}) collective-permute-start(f32[3,8,8,256]{3,2,1,0:T(8,128)S(1)} %get-tuple-element.23), channel_id=1, source_target_pairs={{0,1},{2,3},{1,0},{3,2},{4,5},{6,7},{5,4},{7,6},{8,9},{10,11},{9,8... | collective-permute-start | bytes 589832 | tf_op jit(solution)/shard_map/ppermute | solution.py:204
  63.9 1.4 %slice_bitcast_fusion = (f32[88,8,256]{2,1,0:T(8,128)S(1)}, f32[88,8,256]{2,1,0:T(8,128)S(1)}) fusion(f32[2,88,8,256]{3,2,1,0:T(8,128)} %field_sides.1), kind=kLoop, calls=%fused_computation.2 | loop fusion | bytes 2883584 | tf_op jit(solution)/shard_map/squeeze | solution.py:204
  65.3 2.5 %collective-permute-start.3 = (f32[88,8,256]{2,1,0:T(8,128)S(1)}, f32[88,8,256]{2,1,0:T(8,128)S(1)}, u32[]{:S(2)}, u32[]{:S(2)}) collective-permute-start(f32[88,8,256]{2,1,0:T(8,128)S(1)} %get-tuple-element.16), channel_id=1, source_target_pairs={{4,8},{12,16},{20,24},{8,4},{16,12},{24,20},{5,9},{13,17},{21,25},... | collective-permute-start | bytes 2162696 | tf_op jit(solution)/shard_map/ppermute | solution.py:204
  67.9 0.3 collective-permute-start.2
  68.1 0.0 collective-permute-done.7.odd_ref.yo_ref
  68.1 0.0 copy-start.3
  68.1 0.5 collective-permute-done.6.even_ref.ye_ref
  68.6 0.0 copy-start.4
  68.6 0.2 copy-done.3
  68.8 0.5 copy-done.4
  69.3 2.3 %force_sides.1 = f32[2,42,8,256]{3,2,1,0:T(8,128)} custom-call(s32[1]{0:T(128)} %bitcast.px_ref, s32[1]{0:T(128)} %bitcast.1.par_ref.py_ref, f32[9,8,16,256]{3,2,1,0:T(8,128)} %get-tuple-element.14.force_ref, f32[3,8,8,256]{3,2,1,0:T(8,128)} %copy-done.4, f32[3,8,8,256]{3,2,1,0:T(8,128)} %copy-done.3), custom_call_target="tpu_custom_call" | custom-call | tf_op jit(solution)/shard_map/force_sides/pallas_call | solution.py:448
  71.6 1.9 %slice_bitcast_fusion.2 = (f32[42,8,256]{2,1,0:T(8,128)}, f32[42,8,256]{2,1,0:T(8,128)S(1)}) fusion(f32[2,42,8,256]{3,2,1,0:T(8,128)} %force_sides.1), kind=kLoop, calls=%fused_computation.5 | loop fusion | bytes 1376256 | tf_op jit(solution)/shard_map/squeeze | solution.py:204
  73.4 3.4 %collective-permute-start.9 = (f32[42,8,256]{2,1,0:T(8,128)}, f32[42,8,256]{2,1,0:T(8,128)}, u32[]{:S(2)}, u32[]{:S(2)}) collective-permute-start(f32[42,8,256]{2,1,0:T(8,128)} %get-tuple-element.18), channel_id=1, source_target_pairs={{4,8},{12,16},{20,24},{8,4},{16,12},{24,20},{5,9},{13,17},{21,25},... | collective-permute-start | bytes 1032200 | tf_op jit(solution)/shard_map/ppermute | solution.py:204
  76.8 0.1 collective-permute-start.8
  76.9 9.7 %collective-permute-done.3.xo_ref = f32[88,8,256]{2,1,0:T(8,128)S(1)} collective-permute-done((f32[88,8,256]{2,1,0:T(8,128)S(1)}, f32[88,8,256]{2,1,0:T(8,128)S(1)}, u32[]{:S(2)}, u32[]{:S(2)}) %collective-permute-start.3) | collective-permute-done | bytes 720928 | tf_op jit(solution)/shard_map/ppermute | solution.py:204
  86.6 0.0 copy-start.5
  86.6 0.0 collective-permute-done.2.xe_ref
  86.6 0.9 copy-done.5
  87.5 0.0 copy-start.6
  87.5 0.9 copy-done.6
  88.3 6.8 %first_wave.1 = (f32[3,16,32,256]{3,2,1,0:T(8,128)}, f32[3,12,32,256]{3,2,1,0:T(8,128)}, f32[12,32,256]{2,1,0:T(8,128)}) custom-call(s32[1]{0:T(128)} %bitcast.px_ref, s32[1]{0:T(128)} %bitcast.1.par_ref.py_ref, f32[3,8,16,256]{3,2,1,0:T(8,128)} %cur_ref.5, f32[3,8,16,256]{3,2,1,0:T(8,128)} %ear_ref.5, f32[8,16,256]{2,1,0:T(8,128)} %coef_ref.5, ...), custom_call_target="tpu_custom_call" | custom-call | tf_op jit(solution)/shard_map/first_wave/pallas_call | solution.py:448
  95.1 0.0 collective-permute-done.9.xo_ref
  95.1 0.0 collective-permute-done.8.xe_ref
  95.1 6.9 %last_wave.1 = (f32[3,8,16,256]{3,2,1,0:T(8,128)}, f32[3,8,16,256]{3,2,1,0:T(8,128)}) custom-call(s32[1]{0:T(128)} %bitcast.px_ref, s32[1]{0:T(128)} %bitcast.1.par_ref.py_ref, f32[3,16,32,256]{3,2,1,0:T(8,128)} %get-tuple-element.9.next_ref, f32[3,12,32,256]{3,2,1,0:T(8,128)} %get-tuple-element.10.now_ref, f32[12,32,256]{2,1,0:T(8,128)} %get-tuple-element.11.coef_ref, ...), custom_call_target="tpu_custom_call" | custom-call | tf_op jit(solution)/shard_map/last_wave/pallas_call | solution.py:448
  (1 shorter events, 0.0 us)
Async XLA Ops:
  0.6 0.7 copy-start
  3.2 4.9 %copy-start.9 = (f32[8,1024]{1,0:T(8,128)}, f32[8,1024]{1,0:T(8,128)S(1)}, u32[]{:S(2)}) copy-start(f32[8,1024]{1,0:T(8,128)S(1)} %pad_maximum_fusion.1.refs_0_) | copy-start | bytes 98308
  3.2 10.0 %collective-permute-start.4 = (f32[8,1024]{1,0:T(8,128)S(1)}, f32[8,1024]{1,0:T(8,128)S(1)}, u32[]{:S(2)}, u32[]{:S(2)}) collective-permute-start(f32[8,1024]{1,0:T(8,128)S(1)} %pad_maximum_fusion.1.refs_0_), channel_id=1, source_target_pairs={{0,1},{2,3},{1,0},{3,2},{4,5},{6,7},{5,4},{7,6},{8,9},{10,11},{9,8... | collective-permute-start | bytes 98312 | tf_op jit(solution)/shard_map/ppermute | solution.py:460
  4.9 8.4 %copy-start.10 = (f32[3,1024]{1,0:T(4,128)S(1)}, f32[3,1024]{1,0:T(4,128)}, u32[]{:S(2)}) copy-start(f32[3,1024]{1,0:T(4,128)} %param.21) | copy-start | bytes 36868
  4.9 8.4 %copy-start.11 = (f32[3,1024]{1,0:T(4,128)S(1)}, f32[3,1024]{1,0:T(4,128)}, u32[]{:S(2)}) copy-start(f32[3,1024]{1,0:T(4,128)} %param.19) | copy-start | bytes 36868
  4.9 8.4 %copy-start.13 = (f32[1024]{0:T(1024)S(1)}, f32[1024]{0:T(1024)}, u32[]{:S(2)}) copy-start(f32[1024]{0:T(1024)} %param.20) | copy-start | bytes 12292
  8.1 36.9 %collective-permute-start.1 = (f32[5,8,8,256]{3,2,1,0:T(8,128)S(1)}, f32[5,8,8,256]{3,2,1,0:T(8,128)S(1)}, u32[]{:S(2)}, u32[]{:S(2)}) collective-permute-start(f32[5,8,8,256]{3,2,1,0:T(8,128)S(1)} %get-tuple-element.20), channel_id=1, source_target_pairs={{1,2},{2,1},{5,6},{6,5},{9,10},{10,9},{13,14},{14,13},{17,18},{18,... | collective-permute-start | bytes 983048 | tf_op jit(solution)/shard_map/ppermute | solution.py:204
  8.8 36.2 %collective-permute-start = (f32[5,8,8,256]{3,2,1,0:T(8,128)S(1)}, f32[5,8,8,256]{3,2,1,0:T(8,128)S(1)}, u32[]{:S(2)}, u32[]{:S(2)}) collective-permute-start(f32[5,8,8,256]{3,2,1,0:T(8,128)S(1)} %get-tuple-element.21), channel_id=1, source_target_pairs={{0,1},{2,3},{1,0},{3,2},{4,5},{6,7},{5,4},{7,6},{8,9},{10,11},{9,8... | collective-permute-start | bytes 983048 | tf_op jit(solution)/shard_map/ppermute | solution.py:204
  13.3 1.0 copy-start.8
  13.3 12.4 %collective-permute-start.5 = (f32[8,2048]{1,0:T(8,128)S(1)}, f32[8,2048]{1,0:T(8,128)S(1)}, u32[]{:S(2)}, u32[]{:S(2)}) collective-permute-start(f32[8,2048]{1,0:T(8,128)S(1)} %pad_maximum_fusion), channel_id=1, source_target_pairs={{1,2},{2,1},{0,3},{3,0},{5,6},{6,5},{4,7},{7,4},{9,10},{10,9},{8,1... | collective-permute-start | bytes 196616 | tf_op jit(solution)/shard_map/ppermute | solution.py:463
  25.7 0.6 copy-start.12
  39.6 12.8 %all-to-all-start = ((f32[32,8,128]{2,1,0:T(8,128)}), f32[32,8,128]{2,1,0:T(8,128)S(1)}, u32[]{:S(2)}, u32[]{:S(2)}) async-start(f32[32,8,128]{2,1,0:T(8,128)} %incident_last.1), calls=%async_computation | async-start | bytes 262144 | tf_op jit(solution)/shard_map/all_to_all | solution.py:496
  45.0 0.7 copy-start.1
  45.0 0.8 copy-start.2
  52.4 0.7 copy-start.7
  61.1 7.1 %collective-permute-start.7 = (f32[3,8,8,256]{3,2,1,0:T(8,128)S(1)}, f32[3,8,8,256]{3,2,1,0:T(8,128)S(1)}, u32[]{:S(2)}, u32[]{:S(2)}) collective-permute-start(f32[3,8,8,256]{3,2,1,0:T(8,128)S(1)} %get-tuple-element.22), channel_id=1, source_target_pairs={{1,2},{2,1},{5,6},{6,5},{9,10},{10,9},{13,14},{14,13},{17,18},{18,... | collective-permute-start | bytes 589832 | tf_op jit(solution)/shard_map/ppermute | solution.py:204
  61.7 6.9 %collective-permute-start.6 = (f32[3,8,8,256]{3,2,1,0:T(8,128)S(1)}, f32[3,8,8,256]{3,2,1,0:T(8,128)S(1)}, u32[]{:S(2)}, u32[]{:S(2)}) collective-permute-start(f32[3,8,8,256]{3,2,1,0:T(8,128)S(1)} %get-tuple-element.23), channel_id=1, source_target_pairs={{0,1},{2,3},{1,0},{3,2},{4,5},{6,7},{5,4},{7,6},{8,9},{10,11},{9,8... | collective-permute-start | bytes 589832 | tf_op jit(solution)/shard_map/ppermute | solution.py:204
  65.3 21.2 %collective-permute-start.3 = (f32[88,8,256]{2,1,0:T(8,128)S(1)}, f32[88,8,256]{2,1,0:T(8,128)S(1)}, u32[]{:S(2)}, u32[]{:S(2)}) collective-permute-start(f32[88,8,256]{2,1,0:T(8,128)S(1)} %get-tuple-element.16), channel_id=1, source_target_pairs={{4,8},{12,16},{20,24},{8,4},{16,12},{24,20},{5,9},{13,17},{21,25},... | collective-permute-start | bytes 2162696 | tf_op jit(solution)/shard_map/ppermute | solution.py:204
  67.9 18.7 %collective-permute-start.2 = (f32[88,8,256]{2,1,0:T(8,128)S(1)}, f32[88,8,256]{2,1,0:T(8,128)S(1)}, u32[]{:S(2)}, u32[]{:S(2)}) collective-permute-start(f32[88,8,256]{2,1,0:T(8,128)S(1)} %get-tuple-element.17), channel_id=1, source_target_pairs={{0,4},{8,12},{16,20},{24,28},{4,0},{12,8},{20,16},{28,24},{1,5},{9... | collective-permute-start | bytes 2162696 | tf_op jit(solution)/shard_map/ppermute | solution.py:204
  68.1 0.7 copy-start.3
  68.6 0.7 copy-start.4
  73.4 21.7 %collective-permute-start.9 = (f32[42,8,256]{2,1,0:T(8,128)}, f32[42,8,256]{2,1,0:T(8,128)}, u32[]{:S(2)}, u32[]{:S(2)}) collective-permute-start(f32[42,8,256]{2,1,0:T(8,128)} %get-tuple-element.18), channel_id=1, source_target_pairs={{4,8},{12,16},{20,24},{8,4},{16,12},{24,20},{5,9},{13,17},{21,25},... | collective-permute-start | bytes 1032200 | tf_op jit(solution)/shard_map/ppermute | solution.py:204
  76.8 18.3 %collective-permute-start.8 = (f32[42,8,256]{2,1,0:T(8,128)S(1)}, f32[42,8,256]{2,1,0:T(8,128)}, u32[]{:S(2)}, u32[]{:S(2)}) collective-permute-start(f32[42,8,256]{2,1,0:T(8,128)S(1)} %get-tuple-element.19), channel_id=1, source_target_pairs={{0,4},{8,12},{16,20},{24,28},{4,0},{12,8},{20,16},{28,24},{1,5},{9... | collective-permute-start | bytes 1032200 | tf_op jit(solution)/shard_map/ppermute | solution.py:204
  86.6 0.9 copy-start.5
  87.5 0.9 copy-start.6

commit v4 on v3

--- a/solution.py
+++ b/solution.py
@@ -5,16 +5,15 @@
 from jax.experimental.pallas import tpu as pltpu
 from jax.sharding import PartitionSpec as P
 
-STEPS = 3
 step_size = 0.05
 near_weight = 4.0 / 3.0
 far_weight = -1.0 / 12.0
 centre_weight = -7.5
 inv_two_pi = 0.15915494309189535
-round_magic = 12582912.0
 
 SIN_C = (4.442834854125977, -7.306587219238281, 3.588636875152588, -0.7713118195533752)
 HALF = 64
+VMEM_GRANT = 16 * 2**20
 
 F32 = jnp.float32
 BF16 = jnp.bfloat16
@@ -148,7 +147,7 @@
     return pltpu.roll(tile, TILE // 2, 0)
 
 
-def scatter_kernel(par_ref, val_ref, mask_ref, out_ref, face_ref, acc_ref):
+def scatter_kernel(par_ref, val_ref, mask_ref, out_ref, even_out, odd_out, acc_ref):
     sources = val_ref.shape[0]
     cx, cy, nz = mask_ref.shape
     rows = cx * cy
@@ -183,14 +182,28 @@
     sign = (mask_ref[...] == 1).astype(F32) - (mask_ref[...] == 2).astype(F32)
     for i in range(9):
         out_ref[i] = acc_ref[i].reshape(cx, cy, nz) * sign
-    parity = par_ref[0]
     upper = row_ids((TILE, nz)) >= TILE // 2
-    for high, place in ((True, parity), (False, 1 - parity)):
+
+    def write(high, face_ref):
         ys = slice(cy - TILE, cy) if high else slice(0, TILE)
         keep = upper if high else ~upper
         for i in range(3):
             for x in range(cx):
-                face_ref[place, i, x] = jnp.where(keep, out_ref[i, x, ys], half_turn(out_ref[3 + i, x, ys]))
+                face_ref[i, x] = jnp.where(keep, out_ref[i, x, ys], half_turn(out_ref[3 + i, x, ys]))
+
+    write_faces(par_ref[0], write, even_out, odd_out)
+
+
+def write_faces(parity, write, even_out, odd_out):
+    @pl.when(parity == 0)
+    def _():
+        write(True, even_out)
+        write(False, odd_out)
+
+    @pl.when(parity != 0)
+    def _():
+        write(False, even_out)
+        write(True, odd_out)
 
 
 def pair_list(count, odd):
@@ -201,21 +214,26 @@
 
 def swap_faces(faces, axis):
     count = lax.axis_size(axis)
-    return [lax.ppermute(faces[k], axis, pair_list(count, k)) for k in (0, 1)]
-
-
-def field_face_kernel(par_ref, cur_ref, ear_ref, coef_ref, out_ref):
+    out = []
+    for k in (0, 1):
+        out.append(lax.ppermute(faces[k], axis, pair_list(count, k)))
+    return out
+
+
+def field_face_kernel(par_ref, cur_ref, ear_ref, coef_ref, even_out, odd_out):
     _, cx, cy, nz = cur_ref.shape
-    parity = par_ref[0]
     upper = row_ids((TILE, nz)) >= TILE // 2
-    for high, place in ((True, parity), (False, 1 - parity)):
+
+    def write(high, face_ref):
         ys = slice(cy - TILE, cy) if high else slice(0, TILE)
         keep = upper if high else ~upper
         for x in range(cx):
             for i in range(3):
-                out_ref[place, i, x] = cur_ref[i, x, ys]
-            out_ref[place, 3, x] = jnp.where(keep, ear_ref[0, x, ys], half_turn(ear_ref[1, x, ys]))
-            out_ref[place, 4, x] = jnp.where(keep, ear_ref[2, x, ys], half_turn(coef_ref[x, ys]))
+                face_ref[i, x] = cur_ref[i, x, ys]
+            face_ref[3, x] = jnp.where(keep, ear_ref[0, x, ys], half_turn(ear_ref[1, x, ys]))
+            face_ref[4, x] = jnp.where(keep, ear_ref[2, x, ys], half_turn(coef_ref[x, ys]))
+
+    write_faces(par_ref[0], write, even_out, odd_out)
 
 
 def face_tile(ref, name, x):
@@ -247,12 +265,12 @@
     return out
 
 
-def side_kernel(plan, own_tile, halo_tile, cx, cy, nz, px_ref, py_ref, even_ref, odd_ref, out_ref):
+def side_kernel(plan, own_tile, halo_tile, cx, cy, nz, px_ref, py_ref, even_ref, odd_ref, even_out, odd_out):
     upper = row_ids((TILE, nz)) >= TILE // 2
     low = select_side(py_ref[0], even_ref, odd_ref, False)
     high = select_side(py_ref[0], even_ref, odd_ref, True)
-    parity = px_ref[0]
-    for is_high, place in ((True, parity), (False, 1 - parity)):
+
+    def write(is_high, face_ref):
         for name, dist, part, at in plan_tiles(plan, cy):
             x = cx - dist if is_high else dist - 1
             if part >= 0:
@@ -263,10 +281,12 @@
                     low(lambda ref: halo_tile(ref, name, x)),
                     high(lambda ref: halo_tile(ref, name, x)),
                 )
-            out_ref[place, at] = tile
-
-
-def field_side_kernel(px_ref, py_ref, cur_ref, ear_ref, coef_ref, even_ref, odd_ref, out_ref):
+            face_ref[at] = tile
+
+    write_faces(px_ref[0], write, even_out, odd_out)
+
+
+def field_side_kernel(px_ref, py_ref, cur_ref, ear_ref, coef_ref, *refs):
     _, cx, cy, nz = cur_ref.shape
 
     def own_tile(name, x, ys):
@@ -274,16 +294,16 @@
             return cur_ref[name, x, ys]
         return ear_ref[name - 3, x, ys] if name < 6 else coef_ref[x, ys]
 
-    side_kernel(FIELD_PLAN, own_tile, face_tile, cx, cy, nz, px_ref, py_ref, even_ref, odd_ref, out_ref)
-
-
-def force_side_kernel(px_ref, py_ref, force_ref, even_ref, odd_ref, out_ref):
+    side_kernel(FIELD_PLAN, own_tile, face_tile, cx, cy, nz, px_ref, py_ref, *refs)
+
+
+def force_side_kernel(px_ref, py_ref, force_ref, *refs):
     _, cx, cy, nz = force_ref.shape
     side_kernel(
         FORCE_PLAN,
         lambda name, x, ys: force_ref[name, x, ys],
         lambda ref, name, x: ref[name, x],
-        cx, cy, nz, px_ref, py_ref, even_ref, odd_ref, out_ref,
+        cx, cy, nz, px_ref, py_ref, *refs,
     )
 
 
@@ -311,7 +331,7 @@
     px_ref, py_ref, cur_ref, ear_ref, coef_ref, ye_ref, yo_ref, xe_ref, xo_ref,
     next_ref, now_ref, wide_coef_ref, u_ref, e_ref, c_ref,
 ):
-    _, cx, cy, nz = cur_ref.shape
+    _, cx, cy, _ = cur_ref.shape
     own = slice(TILE, TILE + cy)
     lower, higher = slice(0, TILE), slice(TILE + cy, 2 * TILE + cy)
     low = select_side(py_ref[0], ye_ref, yo_ref, False)
@@ -359,7 +379,7 @@
     px_ref, py_ref, next_ref, now_ref, coef_ref, force_ref, ye_ref, yo_ref, xe_ref, xo_ref,
     final_ref, prior_ref, one_ref, two_ref,
 ):
-    _, cx, cy, nz = force_ref.shape
+    _, cx, cy, _ = force_ref.shape
     own = slice(TILE, TILE + cy)
     lower, higher = slice(0, TILE), slice(TILE + cy, 2 * TILE + cy)
     low = select_side(py_ref[0], ye_ref, yo_ref, False)
@@ -443,7 +463,7 @@
     smem = pl.BlockSpec(memory_space=pltpu.SMEM)
     vmem = pl.BlockSpec(memory_space=pltpu.VMEM)
 
-    def call(kernel, name, operands, shapes, scratch=(), scalars=0):
+    def call(kernel, operands, shapes, scratch=(), scalars=0):
         shapes = [jax.ShapeDtypeStruct(shape, F32) for shape in shapes]
         return pl.pallas_call(
             kernel,
@@ -451,7 +471,7 @@
             in_specs=[smem] * scalars + [vmem] * (len(operands) - scalars),
             out_specs=[vmem] * len(shapes),
             scratch_shapes=[pltpu.VMEM(shape, F32) for shape in scratch],
-            name=name,
+            compiler_params=pltpu.CompilerParams(vmem_limit_bytes=VMEM_GRANT),
         )(*operands)
 
     px = (lax.axis_index("slab") % 2).astype(jnp.int32).reshape(1)
@@ -469,23 +489,19 @@
             for k in range(1, comp_count)
         ]
     fields = (current_field, earlier_field, wave_coef)
-    (faces,) = call(field_face_kernel, "field_faces", (py, *fields), [(2, 5, cx, TILE, nz)], scalars=1)
+    faces = call(field_face_kernel, (py, *fields), [(5, cx, TILE, nz)] * 2, scalars=1)
     ye, yo = swap_faces(faces, "comp")
     (sum_one, total_one) = call(
         lambda *refs: first_incident_kernel(len(first_blocks), *refs),
-        "incident_first",
         (*first_blocks, point_xyz),
         [(32, point_count), (16, 256)],
         [(8, point_count)],
     )
     field_tiles = len(plan_tiles(FIELD_PLAN, cy))
-    (sides,) = call(
-        field_side_kernel, "field_sides", (px, py, *fields, ye, yo), [(2, field_tiles, TILE, nz)], scalars=2
-    )
+    sides = call(field_side_kernel, (px, py, *fields, ye, yo), [(field_tiles, TILE, nz)] * 2, scalars=2)
     xe, xo = swap_faces(sides, "slab")
     (packed,) = call(
         lambda *refs: last_incident_kernel(len(last_blocks), HALF, *refs),
-        "incident_last",
         (
             *last_blocks, sum_one, total_one, point_xyz,
             point_owner.reshape(1, point_count), cell_offset.reshape(1, point_count),
@@ -494,23 +510,19 @@
         [(8, point_count), (32, point_count)],
     )
     arrived = lax.all_to_all(packed, ("slab", "comp"), split_axis=0, concat_axis=0, tiled=True)
-    force, force_faces = call(
+    force, *force_faces = call(
         scatter_kernel,
-        "scatter",
         (py, arrived, layer_mask),
-        [(9, cx, cy, nz), (2, 3, cx, TILE, nz)],
+        [(9, cx, cy, nz)] + [(3, cx, TILE, nz)] * 2,
         [(9, cx * cy, nz)],
         scalars=1,
     )
     fye, fyo = swap_faces(force_faces, "comp")
     force_tiles = len(plan_tiles(FORCE_PLAN, cy))
-    (force_sides,) = call(
-        force_side_kernel, "force_sides", (px, py, force, fye, fyo), [(2, force_tiles, TILE, nz)], scalars=2
-    )
+    force_sides = call(force_side_kernel, (px, py, force, fye, fyo), [(force_tiles, TILE, nz)] * 2, scalars=2)
     fxe, fxo = swap_faces(force_sides, "slab")
     following, now, wide_coef = call(
         first_wave_kernel,
-        "first_wave",
         (px, py, *fields, ye, yo, xe, xo),
         [(3, cx + 2 * MID, wide, nz), (3, cx + 2 * NEAR, wide, nz), (cx + 2 * NEAR, wide, nz)],
         [(3, cx + 2 * DEEP, wide, nz), (3, cx + 2 * MID, wide, nz), (cx + 2 * MID, wide, nz)],
@@ -518,7 +530,6 @@
     )
     final, prior = call(
         last_wave_kernel,
-        "last_wave",
         (px, py, following, now, wide_coef, force, fye, fyo, fxe, fxo),
         [current_field.shape, current_field.shape],
         [(3, cx + 2 * MID, wide, nz), (3, cx + 2 * NEAR, wide, nz)],

time: 103 us -> 78.9 us (0.77)
  the two profiles are of different devices: /device:TPU:4 before, /device:TPU:9 now
where the time goes in v4:
time: 78.9 us; the launch traced here: 78.5 us
  Pallas kernels  36.3 us (46%)
  starting transfers between devices  23 us (29%)
  waiting for transfers between devices  12.8 us (16%)
  local copies, waits for them, and re-layouts  3.54 us (4%)
  matrix products  1.12 us (1%)
  between operations  0.95 us (1%)
  other arithmetic  0.8 us (1%)
    pallas_call x8, Pallas kernels, call(): pl.pallas_call(kernel, out_shape=shapes, in_specs=[smem] * scalars + [vme...  36.3 us
    ppermute x8, starting transfers between devices, swap_faces(): out.append(lax.ppermute(faces[k], axis, pair_list(count, k)))  16.2 us
    ppermute x8, waiting for transfers between devices, swap_faces(): out.append(lax.ppermute(faces[k], axis, pair_list(count, k)))  10.8 us
    all_to_all x1, starting transfers between devices, local(): lax.all_to_all(packed, ('slab', 'comp'), split_axis=0, concat_axis=0, til...  6.43 us
    unnamed x28, local copies, waits for them, and re-layouts  3.54 us
    all_to_all x1, waiting for transfers between devices, local(): lax.all_to_all(packed, ('slab', 'comp'), split_axis=0, concat_axis=0, til...  2.01 us
  transfers between devices with their start and end apart: 11, of which 4 were waited for; matrix products, arithmetic and copies ran while one was open for 0% of the time, Pallas kernels for 41%

profile of v4, /device:TPU:9, one launch (start us, length us, event | category | flops | bytes accessed | tf_op | source)
XLA Modules:
  0.0 78.5 jit_solution(9934042041052519367)
XLA Ops:
  0.6 0.0 copy-start
  0.6 0.0 copy-start.11
  0.7 0.0 copy-start.13
  0.7 0.0 copy-start.12
  0.7 0.0 copy-start.6
  0.7 0.0 copy-start.8
  0.7 0.0 copy-start.9
  0.7 0.0 copy-start.10
  0.7 0.6 copy-done
  1.3 1.1 %fusion = f32[1,1024]{1,0:T(1,128)S(1)} fusion(f32[256,1]{0,1:T(1,128)S(1)} %bitcast.8, s32[1024]{0:T(1024)} %param.22), kind=kOutput, calls=%fused_computation.1 | convolution fusion | flops 3407872 | bytes 9216 | tf_op jit(solution)/shard_map/dot_general | solution.py:448
  2.4 0.8 pad_maximum_fusion.1.refs_0_
  3.2 0.1 collective-permute-start.4
  3.3 0.0 copy-start.1
  3.3 1.0 %copy-done.1 = f32[3,8,16,256]{3,2,1,0:T(8,128)S(1)} copy-done((f32[3,8,16,256]{3,2,1,0:T(8,128)S(1)}, f32[3,8,16,256]{3,2,1,0:T(8,128)}, u32[]{:S(2)}) %copy-start.1) | copy-done | bytes 393240
  4.3 0.0 copy-start.3
  4.3 1.0 %copy-done.3 = f32[3,8,16,256]{3,2,1,0:T(8,128)S(1)} copy-done((f32[3,8,16,256]{3,2,1,0:T(8,128)S(1)}, f32[3,8,16,256]{3,2,1,0:T(8,128)}, u32[]{:S(2)}) %copy-start.3) | copy-done | bytes 393240
  5.3 0.0 copy-start.5
  5.3 0.9 %copy-done.5 = f32[8,16,256]{2,1,0:T(8,128)S(1)} copy-done((f32[8,16,256]{2,1,0:T(8,128)S(1)}, f32[8,16,256]{2,1,0:T(8,128)}, u32[]{:S(2)}) %copy-start.5) | copy-done | bytes 131096
  6.2 0.0 copy-start.2
  6.2 0.0 copy-start.4
  6.2 0.1 shard_map.131
  6.3 1.5 %collective-permute-start = (f32[5,8,8,256]{3,2,1,0:T(8,128)S(1)}, f32[5,8,8,256]{3,2,1,0:T(8,128)S(1)}, u32[]{:S(2)}, u32[]{:S(2)}) collective-permute-start(f32[5,8,8,256]{3,2,1,0:T(8,128)S(1)} %get-tuple-element.16), channel_id=1, source_target_pairs={{0,1},{2,3},{1,0},{3,2},{4,5},{6,7},{5,4},{7,6},{8,9},{10,11},{9,8... | collective-permute-start | bytes 983048 | tf_op jit(solution)/shard_map/ppermute | solution.py:219
  7.8 3.2 %collective-permute-start.1 = (f32[5,8,8,256]{3,2,1,0:T(8,128)S(1)}, f32[5,8,8,256]{3,2,1,0:T(8,128)S(1)}, u32[]{:S(2)}, u32[]{:S(2)}) collective-permute-start(f32[5,8,8,256]{3,2,1,0:T(8,128)S(1)} %get-tuple-element.17), channel_id=1, source_target_pairs={{1,2},{2,1},{5,6},{6,5},{9,10},{10,9},{13,14},{14,13},{17,18},{18,... | collective-permute-start | bytes 983048 | tf_op jit(solution)/shard_map/ppermute | solution.py:219
  11.0 0.0 collective-permute-done.4.refs_1_
  11.0 0.0 copy-done.11
  11.0 0.0 copy-done.13
  11.0 0.0 copy-done.12
  11.0 0.0 copy-start.7
  11.1 0.2 collective-permute-start.5
  11.3 0.0 copy-done.8
  11.3 10.0 %shard_map.134 = (f32[32,1024]{1,0:T(8,128)S(1)}, f32[16,256]{1,0:T(8,128)S(1)}) custom-call(f32[8,1024]{1,0:T(8,128)S(1)} %pad_maximum_fusion.1.refs_0_, f32[8,1024]{1,0:T(8,128)S(1)} %collective-permute-done.4.refs_1_, f32[3,1024]{1,0:T(4,128)S(1)} %copy-done.8), custom_call_target="tpu_custom_call" | custom-call | tf_op jit(solution)/shard_map/pallas_call | solution.py:468
  21.3 0.0 collective-permute-done.5.refs_0_
  21.3 0.0 copy-done.9
  21.3 0.0 copy-done.10
  21.4 12.3 %shard_map.135 = f32[32,8,128]{2,1,0:T(8,128)} custom-call(f32[8,2048]{1,0:T(8,128)S(1)} %collective-permute-done.5.refs_0_, f32[32,1024]{1,0:T(8,128)S(1)} %get-tuple-element.23.refs_1_, f32[16,256]{1,0:T(8,128)S(1)} %get-tuple-element.24.refs_2_, f32[3,1024]{1,0:T(4,128)S(1)} %copy-done.8, s32[1,1024]{1,0:T(1,128)S(1)} %bitcast.9, s32[1,1024]{1,0:T(1,128)S(1)} %bitcast.10), custom_call_target="tpu_custom_call" | custom-call | tf_op jit(solution)/shard_map/pallas_call | solution.py:468
  33.6 6.4 %all-to-all-start = ((f32[32,8,128]{2,1,0:T(8,128)}), f32[32,8,128]{2,1,0:T(8,128)S(1)}, u32[]{:S(2)}, u32[]{:S(2)}) async-start(f32[32,8,128]{2,1,0:T(8,128)} %shard_map.135), calls=%async_computation | async-start | bytes 262144 | tf_op jit(solution)/shard_map/all_to_all | solution.py:512
  40.1 0.0 collective-permute-done.refs_0_.ye_ref
  40.1 0.0 collective-permute-done.1.refs_1_.yo_ref
  40.1 0.0 copy-done.6
  40.1 0.0 copy-done.2
  40.1 0.0 copy-done.4
  40.1 1.2 %shard_map.132 = (f32[88,8,256]{2,1,0:T(8,128)}, f32[88,8,256]{2,1,0:T(8,128)}) custom-call(s32[1]{0:T(128)} %bitcast.px_ref, s32[1]{0:T(128)} %bitcast.1.par_ref.py_ref, f32[3,8,16,256]{3,2,1,0:T(8,128)S(1)} %copy-done.2, f32[3,8,16,256]{3,2,1,0:T(8,128)S(1)} %copy-done.4, f32[8,16,256]{2,1,0:T(8,128)S(1)} %copy-done.6, ...), custom_call_target="tpu_custom_call" | custom-call | tf_op jit(solution)/shard_map/pallas_call | solution.py:468
  41.4 0.4 collective-permute-start.2
  41.8 3.1 %collective-permute-start.3 = (f32[88,8,256]{2,1,0:T(8,128)}, f32[88,8,256]{2,1,0:T(8,128)S(1)}, u32[]{:S(2)}, u32[]{:S(2)}) collective-permute-start(f32[88,8,256]{2,1,0:T(8,128)} %get-tuple-element.19), channel_id=1, source_target_pairs={{4,8},{12,16},{20,24},{8,4},{16,12},{24,20},{5,9},{13,17},{21,25},... | collective-permute-start | bytes 2162696 | tf_op jit(solution)/shard_map/ppermute | solution.py:219
  44.9 2.0 %all-to-all-done.val_ref = f32[32,8,128]{2,1,0:T(8,128)S(1)} async-done(((f32[32,8,128]{2,1,0:T(8,128)}), f32[32,8,128]{2,1,0:T(8,128)S(1)}, u32[]{:S(2)}, u32[]{:S(2)}) %all-to-all-start) | async-done | bytes 131104 | tf_op jit(solution)/shard_map/all_to_all | solution.py:512
  46.9 0.0 copy-done.7
  46.9 4.9 %shard_map.136 = (f32[9,8,16,256]{3,2,1,0:T(8,128)S(1)}, f32[3,8,8,256]{3,2,1,0:T(8,128)S(1)}, f32[3,8,8,256]{3,2,1,0:T(8,128)S(1)}) custom-call(s32[1]{0:T(128)} %bitcast.1.par_ref.py_ref, f32[32,8,128]{2,1,0:T(8,128)S(1)} %all-to-all-done.val_ref, s32[8,16,256]{2,1,0:T(8,128)S(1)} %copy-done.7), custom_call_target="tpu_custom_call" | custom-call | tf_op jit(solution)/shard_map/pallas_call | solution.py:468
  51.8 0.8 collective-permute-start.6
  52.6 2.1 %collective-permute-start.7 = (f32[3,8,8,256]{3,2,1,0:T(8,128)S(1)}, f32[3,8,8,256]{3,2,1,0:T(8,128)S(1)}, u32[]{:S(2)}, u32[]{:S(2)}) collective-permute-start(f32[3,8,8,256]{3,2,1,0:T(8,128)S(1)} %get-tuple-element.27), channel_id=1, source_target_pairs={{1,2},{2,1},{5,6},{6,5},{9,10},{10,9},{13,14},{14,13},{17,18},{18,... | collective-permute-start | bytes 589832 | tf_op jit(solution)/shard_map/ppermute | solution.py:219
  54.6 3.4 %collective-permute-done.6.refs_0_.ye_ref = f32[3,8,8,256]{3,2,1,0:T(8,128)S(1)} collective-permute-done((f32[3,8,8,256]{3,2,1,0:T(8,128)S(1)}, f32[3,8,8,256]{3,2,1,0:T(8,128)S(1)}, u32[]{:S(2)}, u32[]{:S(2)}) %collective-permute-start.6) | collective-permute-done | bytes 196640 | tf_op jit(solution)/shard_map/ppermute | solution.py:219
  58.0 1.0 %collective-permute-done.7.refs_1_.yo_ref = f32[3,8,8,256]{3,2,1,0:T(8,128)S(1)} collective-permute-done((f32[3,8,8,256]{3,2,1,0:T(8,128)S(1)}, f32[3,8,8,256]{3,2,1,0:T(8,128)S(1)}, u32[]{:S(2)}, u32[]{:S(2)}) %collective-permute-start.7) | collective-permute-done | bytes 196640 | tf_op jit(solution)/shard_map/ppermute | solution.py:219
  59.0 0.1 shard_map.137
  59.0 2.9 %collective-permute-start.8 = (f32[42,8,256]{2,1,0:T(8,128)S(1)}, f32[42,8,256]{2,1,0:T(8,128)S(1)}, u32[]{:S(2)}, u32[]{:S(2)}) collective-permute-start(f32[42,8,256]{2,1,0:T(8,128)S(1)} %get-tuple-element.28), channel_id=1, source_target_pairs={{0,4},{8,12},{16,20},{24,28},{4,0},{12,8},{20,16},{28,24},{1,5},{9... | collective-permute-start | bytes 1032200 | tf_op jit(solution)/shard_map/ppermute | solution.py:219
  61.9 2.4 %collective-permute-start.9 = (f32[42,8,256]{2,1,0:T(8,128)S(1)}, f32[42,8,256]{2,1,0:T(8,128)S(1)}, u32[]{:S(2)}, u32[]{:S(2)}) collective-permute-start(f32[42,8,256]{2,1,0:T(8,128)S(1)} %get-tuple-element.29), channel_id=1, source_target_pairs={{4,8},{12,16},{20,24},{8,4},{16,12},{24,20},{5,9},{13,17},{21,25},... | collective-permute-start | bytes 1032200 | tf_op jit(solution)/shard_map/ppermute | solution.py:219
  64.3 0.0 collective-permute-done.2.xe_ref
  64.3 0.0 collective-permute-done.3.xo_ref
  64.3 3.3 %shard_map.133 = (f32[3,16,32,256]{3,2,1,0:T(8,128)S(1)}, f32[3,12,32,256]{3,2,1,0:T(8,128)S(1)}, f32[12,32,256]{2,1,0:T(8,128)S(1)}) custom-call(s32[1]{0:T(128)} %bitcast.px_ref, s32[1]{0:T(128)} %bitcast.1.par_ref.py_ref, f32[3,8,16,256]{3,2,1,0:T(8,128)S(1)} %copy-done.2, f32[3,8,16,256]{3,2,1,0:T(8,128)S(1)} %copy-done.4, f32[8,16,256]{2,1,0:T(8,128)S(1)} %copy-done.6, ...), custom_call_target="tpu_custom_call" | custom-call | tf_op jit(solution)/shard_map/pallas_call | solution.py:468
  67.6 0.0 collective-permute-done.8.xe_ref
  67.6 6.4 %collective-permute-done.9.xo_ref = f32[42,8,256]{2,1,0:T(8,128)S(1)} collective-permute-done((f32[42,8,256]{2,1,0:T(8,128)S(1)}, f32[42,8,256]{2,1,0:T(8,128)S(1)}, u32[]{:S(2)}, u32[]{:S(2)}) %collective-permute-start.9) | collective-permute-done | bytes 344096 | tf_op jit(solution)/shard_map/ppermute | solution.py:219
  74.1 4.4 %shard_map.138 = (f32[3,8,16,256]{3,2,1,0:T(8,128)}, f32[3,8,16,256]{3,2,1,0:T(8,128)}) custom-call(s32[1]{0:T(128)} %bitcast.px_ref, s32[1]{0:T(128)} %bitcast.1.par_ref.py_ref, f32[3,16,32,256]{3,2,1,0:T(8,128)S(1)} %get-tuple-element.20.next_ref, f32[3,12,32,256]{3,2,1,0:T(8,128)S(1)} %get-tuple-element.21.now_ref, ...), custom_call_target="tpu_custom_call" | custom-call | tf_op jit(solution)/shard_map/pallas_call | solution.py:468
  (1 shorter events, 0.0 us)
Async XLA Ops:
  0.6 0.7 copy-start
  0.6 10.3 %copy-start.11 = (f32[3,1024]{1,0:T(4,128)S(1)}, f32[3,1024]{1,0:T(4,128)}, u32[]{:S(2)}) copy-start(f32[3,1024]{1,0:T(4,128)} %param.21) | copy-start | bytes 36868
  0.7 10.3 %copy-start.13 = (f32[1024]{0:T(1024)S(1)}, f32[1024]{0:T(1024)}, u32[]{:S(2)}) copy-start(f32[1024]{0:T(1024)} %param.20) | copy-start | bytes 12292
  0.7 10.3 %copy-start.12 = (f32[3,1024]{1,0:T(4,128)S(1)}, f32[3,1024]{1,0:T(4,128)}, u32[]{:S(2)}) copy-start(f32[3,1024]{1,0:T(4,128)} %param.19) | copy-start | bytes 36868
  0.7 39.4 %copy-start.6 = (f32[8,16,256]{2,1,0:T(8,128)S(1)}, f32[8,16,256]{2,1,0:T(8,128)}, u32[]{:S(2)}) copy-start(f32[8,16,256]{2,1,0:T(8,128)} %coef_ref.5) | copy-start | bytes 393220
  0.7 10.6 %copy-start.8 = (f32[3,1024]{1,0:T(4,128)S(1)}, f32[3,1024]{1,0:T(4,128)}, u32[]{:S(2)}) copy-start(f32[3,1024]{1,0:T(4,128)} %refs_3_.1) | copy-start | bytes 36868
  0.7 20.6 %copy-start.9 = (s32[1024,1]{0,1:T(1,128)S(1)}, s32[1024,1]{0,1:T(1,128)}, u32[]{:S(2)}) copy-start(s32[1024,1]{0,1:T(1,128)} %param.17) | copy-start | bytes 12292
  0.7 20.6 %copy-start.10 = (s32[1024]{0:T(1024)S(1)}, s32[1024]{0:T(1024)}, u32[]{:S(2)}) copy-start(s32[1024]{0:T(1024)} %param.18) | copy-start | bytes 12292
  3.2 7.8 %collective-permute-start.4 = (f32[8,1024]{1,0:T(8,128)S(1)}, f32[8,1024]{1,0:T(8,128)S(1)}, u32[]{:S(2)}, u32[]{:S(2)}) collective-permute-start(f32[8,1024]{1,0:T(8,128)S(1)} %pad_maximum_fusion.1.refs_0_), channel_id=1, source_target_pairs={{0,1},{2,3},{1,0},{3,2},{4,5},{6,7},{5,4},{7,6},{8,9},{10,11},{9,8... | collective-permute-start | bytes 98312 | tf_op jit(solution)/shard_map/ppermute | solution.py:480
  3.3 1.0 %copy-start.1 = (f32[3,8,16,256]{3,2,1,0:T(8,128)S(1)}, f32[3,8,16,256]{3,2,1,0:T(8,128)}, u32[]{:S(2)}) copy-start(f32[3,8,16,256]{3,2,1,0:T(8,128)} %cur_ref.5) | copy-start | bytes 1179652
  4.3 1.0 %copy-start.3 = (f32[3,8,16,256]{3,2,1,0:T(8,128)S(1)}, f32[3,8,16,256]{3,2,1,0:T(8,128)}, u32[]{:S(2)}) copy-start(f32[3,8,16,256]{3,2,1,0:T(8,128)} %ear_ref.5) | copy-start | bytes 1179652
  5.3 0.9 %copy-start.5 = (f32[8,16,256]{2,1,0:T(8,128)S(1)}, f32[8,16,256]{2,1,0:T(8,128)}, u32[]{:S(2)}) copy-start(f32[8,16,256]{2,1,0:T(8,128)} %coef_ref.5) | copy-start | bytes 393220
  6.2 33.9 %copy-start.2 = (f32[3,8,16,256]{3,2,1,0:T(8,128)S(1)}, f32[3,8,16,256]{3,2,1,0:T(8,128)}, u32[]{:S(2)}) copy-start(f32[3,8,16,256]{3,2,1,0:T(8,128)} %cur_ref.5) | copy-start | bytes 1179652
  6.2 33.9 %copy-start.4 = (f32[3,8,16,256]{3,2,1,0:T(8,128)S(1)}, f32[3,8,16,256]{3,2,1,0:T(8,128)}, u32[]{:S(2)}) copy-start(f32[3,8,16,256]{3,2,1,0:T(8,128)} %ear_ref.5) | copy-start | bytes 1179652
  6.3 33.8 %collective-permute-start = (f32[5,8,8,256]{3,2,1,0:T(8,128)S(1)}, f32[5,8,8,256]{3,2,1,0:T(8,128)S(1)}, u32[]{:S(2)}, u32[]{:S(2)}) collective-permute-start(f32[5,8,8,256]{3,2,1,0:T(8,128)S(1)} %get-tuple-element.16), channel_id=1, source_target_pairs={{0,1},{2,3},{1,0},{3,2},{4,5},{6,7},{5,4},{7,6},{8,9},{10,11},{9,8... | collective-permute-start | bytes 983048 | tf_op jit(solution)/shard_map/ppermute | solution.py:219
  7.8 32.3 %collective-permute-start.1 = (f32[5,8,8,256]{3,2,1,0:T(8,128)S(1)}, f32[5,8,8,256]{3,2,1,0:T(8,128)S(1)}, u32[]{:S(2)}, u32[]{:S(2)}) collective-permute-start(f32[5,8,8,256]{3,2,1,0:T(8,128)S(1)} %get-tuple-element.17), channel_id=1, source_target_pairs={{1,2},{2,1},{5,6},{6,5},{9,10},{10,9},{13,14},{14,13},{17,18},{18,... | collective-permute-start | bytes 983048 | tf_op jit(solution)/shard_map/ppermute | solution.py:219
  11.0 35.8 %copy-start.7 = (s32[8,16,256]{2,1,0:T(8,128)S(1)}, s32[8,16,256]{2,1,0:T(8,128)}, u32[]{:S(2)}) copy-start(s32[8,16,256]{2,1,0:T(8,128)} %mask_ref.1) | copy-start | bytes 393220
  11.1 10.3 %collective-permute-start.5 = (f32[8,2048]{1,0:T(8,128)S(1)}, f32[8,2048]{1,0:T(8,128)S(1)}, u32[]{:S(2)}, u32[]{:S(2)}) collective-permute-start(f32[8,2048]{1,0:T(8,128)S(1)} %pad_maximum_fusion), channel_id=1, source_target_pairs={{1,2},{2,1},{0,3},{3,0},{5,6},{6,5},{4,7},{7,4},{9,10},{10,9},{8,1... | collective-permute-start | bytes 196616 | tf_op jit(solution)/shard_map/ppermute | solution.py:483
  33.6 13.2 %all-to-all-start = ((f32[32,8,128]{2,1,0:T(8,128)}), f32[32,8,128]{2,1,0:T(8,128)S(1)}, u32[]{:S(2)}, u32[]{:S(2)}) async-start(f32[32,8,128]{2,1,0:T(8,128)} %shard_map.135), calls=%async_computation | async-start | bytes 262144 | tf_op jit(solution)/shard_map/all_to_all | solution.py:512
  41.4 22.9 %collective-permute-start.2 = (f32[88,8,256]{2,1,0:T(8,128)}, f32[88,8,256]{2,1,0:T(8,128)S(1)}, u32[]{:S(2)}, u32[]{:S(2)}) collective-permute-start(f32[88,8,256]{2,1,0:T(8,128)} %get-tuple-element.18), channel_id=1, source_target_pairs={{0,4},{8,12},{16,20},{24,28},{4,0},{12,8},{20,16},{28,24},{1,5},{9... | collective-permute-start | bytes 2162696 | tf_op jit(solution)/shard_map/ppermute | solution.py:219
  41.8 22.5 %collective-permute-start.3 = (f32[88,8,256]{2,1,0:T(8,128)}, f32[88,8,256]{2,1,0:T(8,128)S(1)}, u32[]{:S(2)}, u32[]{:S(2)}) collective-permute-start(f32[88,8,256]{2,1,0:T(8,128)} %get-tuple-element.19), channel_id=1, source_target_pairs={{4,8},{12,16},{20,24},{8,4},{16,12},{24,20},{5,9},{13,17},{21,25},... | collective-permute-start | bytes 2162696 | tf_op jit(solution)/shard_map/ppermute | solution.py:219
  51.8 6.2 %collective-permute-start.6 = (f32[3,8,8,256]{3,2,1,0:T(8,128)S(1)}, f32[3,8,8,256]{3,2,1,0:T(8,128)S(1)}, u32[]{:S(2)}, u32[]{:S(2)}) collective-permute-start(f32[3,8,8,256]{3,2,1,0:T(8,128)S(1)} %get-tuple-element.26), channel_id=1, source_target_pairs={{0,1},{2,3},{1,0},{3,2},{4,5},{6,7},{5,4},{7,6},{8,9},{10,11},{9,8... | collective-permute-start | bytes 589832 | tf_op jit(solution)/shard_map/ppermute | solution.py:219
  52.6 6.4 %collective-permute-start.7 = (f32[3,8,8,256]{3,2,1,0:T(8,128)S(1)}, f32[3,8,8,256]{3,2,1,0:T(8,128)S(1)}, u32[]{:S(2)}, u32[]{:S(2)}) collective-permute-start(f32[3,8,8,256]{3,2,1,0:T(8,128)S(1)} %get-tuple-element.27), channel_id=1, source_target_pairs={{1,2},{2,1},{5,6},{6,5},{9,10},{10,9},{13,14},{14,13},{17,18},{18,... | collective-permute-start | bytes 589832 | tf_op jit(solution)/shard_map/ppermute | solution.py:219
  59.0 8.6 %collective-permute-start.8 = (f32[42,8,256]{2,1,0:T(8,128)S(1)}, f32[42,8,256]{2,1,0:T(8,128)S(1)}, u32[]{:S(2)}, u32[]{:S(2)}) collective-permute-start(f32[42,8,256]{2,1,0:T(8,128)S(1)} %get-tuple-element.28), channel_id=1, source_target_pairs={{0,4},{8,12},{16,20},{24,28},{4,0},{12,8},{20,16},{28,24},{1,5},{9... | collective-permute-start | bytes 1032200 | tf_op jit(solution)/shard_map/ppermute | solution.py:219
  61.9 12.2 %collective-permute-start.9 = (f32[42,8,256]{2,1,0:T(8,128)S(1)}, f32[42,8,256]{2,1,0:T(8,128)S(1)}, u32[]{:S(2)}, u32[]{:S(2)}) collective-permute-start(f32[42,8,256]{2,1,0:T(8,128)S(1)} %get-tuple-element.29), channel_id=1, source_target_pairs={{4,8},{12,16},{20,24},{8,4},{16,12},{24,20},{5,9},{13,17},{21,25},... | collective-permute-start | bytes 1032200 | tf_op jit(solution)/shard_map/ppermute | solution.py:219

commit v5 on v4

v5 whole, which is shorter than its diff:
```python
import jax
import jax.numpy as jnp
from jax import lax
from jax.experimental import pallas as pl
from jax.experimental.pallas import tpu as pltpu
from jax.sharding import PartitionSpec as P

step_size = 0.05
near_weight = 4.0 / 3.0
far_weight = -1.0 / 12.0
centre_weight = -7.5
inv_two_pi = 0.15915494309189535

LEAD = -0.7713118195533752
SIN_C = (4.442834854125977 / LEAD, -7.306587219238281 / LEAD, 3.588636875152588 / LEAD)
SIN_SCALE = LEAD * abs(LEAD)
VER_SCALE = LEAD * LEAD
HALF = 64
OWN_TILES = 5
SIDE_TILES = 4
HIGH_LIST = OWN_TILES
LOW_LIST = OWN_TILES + SIDE_TILES
LIST_ROWS = 16
VMEM_GRANT = 16 * 2**20

F32 = jnp.float32
BF16 = jnp.bfloat16


def sin_versine(u):
    r = u - jnp.round(u)
    z = r * r
    s = r * (((z + SIN_C[2]) * z + SIN_C[1]) * z + SIN_C[0])
    q = s * s
    w = 2.0 / VER_SCALE - q
    return s * (w * lax.rsqrt(w)), q


def split_three(x):
    hi = x.astype(BF16).astype(F32)
    rest = x - hi
    mid = rest.astype(BF16).astype(F32)
    return hi, mid, rest - mid


def row_ids(shape):
    return lax.broadcasted_iota(jnp.int32, shape, 0)


def add_components(par_refs, xyz_ref, x8_ref, acc_ref):
    points = xyz_ref.shape[1]
    kc = 256
    tile = 256
    x8_ref[...] = jnp.zeros(x8_ref.shape, F32)
    x8_ref[0:3, :] = xyz_ref[...]
    xhi, xmid, xlo = split_three(x8_ref[...])
    right = jnp.concatenate([xhi, xmid, xlo, xhi, xmid, xhi], axis=0).astype(BF16)
    rows8 = row_ids((8, kc))
    times = step_size * (rows8 + 1).astype(F32)
    rows16 = row_ids((16, kc))
    comp_row = jnp.where(rows16 < 6, rows16 % 3, (rows16 + 2) % 3)
    valued = (rows16 < 10) & (rows16 != 6)

    def body(par_ref, step, total):
        blk = par_ref[:, pl.ds(pl.multiple_of(step * kc, kc), kc)]
        kv = jnp.where(rows8 < 3, blk * inv_two_pi, 0.0)
        khi, kmid, klo = split_three(kv)
        left = jnp.concatenate([khi, khi, khi, kmid, kmid, klo], axis=0).astype(BF16)
        delays = times * blk[3:4, :] - blk[7:8, :]
        sd, qd = sin_versine(delays * inv_two_pi)
        sd, cd = SIN_SCALE * sd, 1.0 - VER_SCALE * qd
        amp = jnp.where(comp_row == 0, blk[4:5, :], jnp.where(comp_row == 1, blk[5:6, :], blk[6:7, :]))
        amp = jnp.where(valued, amp, 0.0)

        def rows_of(t):
            w = amp * jnp.where(rows16 < 3, t[0:1, :], jnp.where(rows16 < 6, t[1:2, :], t[2:3, :]))
            hi = w.astype(BF16)
            lo = (w - hi.astype(F32)).astype(BF16)
            return w, jnp.concatenate([hi, lo], axis=0)

        wc = rows_of(cd)[0]
        lc = rows_of(-VER_SCALE * cd)[1]
        ls = rows_of(SIN_SCALE * sd)[1]
        for t in range(points // tile):
            cols = slice(t * tile, (t + 1) * tile)
            u = lax.dot_general(left, right[:, cols], (((0,), (0,)), ((), ())), preferred_element_type=F32)
            highs, lows = [], []
            for j in range(kc // 32):
                for value in sin_versine(u[32 * j : 32 * j + 32]):
                    high = value.astype(BF16)
                    highs.append(high)
                    lows.append((value - high.astype(F32)).astype(BF16))
            part = jnp.dot(ls, jnp.concatenate(highs[0::2], axis=0), preferred_element_type=F32)
            part += jnp.dot(lc, jnp.concatenate(highs[1::2], axis=0), preferred_element_type=F32)
            part += jnp.dot(ls, jnp.concatenate(lows[0::2], axis=0), preferred_element_type=F32)
            part += jnp.dot(lc, jnp.concatenate(lows[1::2], axis=0), preferred_element_type=F32)
            acc_ref[:, cols] += part
        return total + wc

    total = jnp.zeros((16, kc), F32)
    for par_ref in par_refs:
        steps = par_ref.shape[1] // kc
        total = lax.fori_loop(0, steps, lambda step, t, ref=par_ref: body(ref, step, t), total)
    return total


def first_incident_kernel(count, *refs):
    par_refs, (xyz_ref, acc_ref, total_ref, x8_ref) = refs[:count], refs[count:]
    acc_ref[...] = jnp.zeros(acc_ref.shape, F32)
    total_ref[...] = add_components(par_refs, xyz_ref, x8_ref, acc_ref)


def last_incident_kernel(count, step, *refs):
    par_refs, refs = refs[:count], refs[count:]
    first_ref, first_total_ref, xyz_ref, own_ref, off_ref, out_ref, x8_ref, acc_ref = refs
    points = xyz_ref.shape[1]
    owners = out_ref.shape[0]
    acc_ref[...] = first_ref[...]
    total = add_components(par_refs, xyz_ref, x8_ref, acc_ref) + first_total_ref[...]
    vals = acc_ref[0:16, :] + acc_ref[16:32, :] + jnp.sum(total, axis=1, keepdims=True)
    vals = jnp.where(row_ids((16, points)) == 6, off_ref[...].astype(F32), vals)
    v1, v2, v3 = split_three(vals)
    named = own_ref[...] == row_ids((owners, points))
    named_one = named.astype(F32).astype(BF16)
    earlier = row_ids((points, points)) < lax.broadcasted_iota(jnp.int32, (points, points), 1)
    before = jnp.dot(named_one, earlier.astype(F32).astype(BF16), preferred_element_type=F32)
    rank = jnp.sum(jnp.where(named, before, 0.0), axis=0, keepdims=True).astype(jnp.int32)
    terms = [v.astype(BF16) for v in (v1, v2, v3)]
    tiles = 0.0
    for odd in (0, 1):
        left = jnp.concatenate(
            [named_one * t[2 * j + odd : 2 * j + odd + 1, :] for t in terms for j in range(OWN_TILES)], axis=0
        )
        spots = (row_ids((2 * HALF, points)) == rank + odd * HALF).astype(F32).astype(BF16)
        got = lax.dot_general(left, spots, (((1,), (1,)), ((), ())), preferred_element_type=F32)
        size = OWN_TILES * owners
        tiles = tiles + (got[0:size] + got[size : 2 * size] + got[2 * size :])
    owner_row = row_ids((owners, 2 * HALF))
    for j in range(OWN_TILES):
        tile = tiles[j * owners : (j + 1) * owners]
        out_ref[:, j, :] = tile
        if j < SIDE_TILES:
            above = pltpu.roll(tile, owners - step, 0)
            out_ref[:, HIGH_LIST + j, :] = jnp.where(owner_row < owners - step, above, 0.0)
            out_ref[:, LOW_LIST + j, :] = jnp.where(owner_row >= step, pltpu.roll(tile, step, 0), 0.0)
    for j in range(LOW_LIST + SIDE_TILES, LIST_ROWS):
        out_ref[:, j, :] = jnp.zeros((owners, 2 * HALF), F32)


TILE = 8
DEEP = 6
MID = 4
NEAR = 2


def half_turn(tile):
    return pltpu.roll(tile, TILE // 2, 0)


def scatter_kernel(par_ref, val_ref, sign_ref, zero_out, one_out, two_out, even_out, odd_out, zero_ref, one_ref, two_ref):
    sources, _, lanes = val_ref.shape
    _, cx, cy, nz = two_out.shape
    rows, mid, near = cx * cy, MID * cy, NEAR * cy
    chunk = 2 * lanes
    left_half = lax.broadcasted_iota(jnp.int32, (LIST_ROWS, lanes), 1) < lanes // 2
    for ref in (zero_ref, one_ref, two_ref):
        ref[...] = jnp.zeros(ref.shape, F32)

    def body(step, carry):
        evens, odds = [], []
        for pair in range(2):
            first, second = val_ref[4 * step + 2 * pair], val_ref[4 * step + 2 * pair + 1]
            evens.append(jnp.where(left_half, first, pltpu.roll(second, lanes // 2, 1)))
            odds.append(jnp.where(left_half, pltpu.roll(first, lanes // 2, 1), second))
        values = [jnp.concatenate(evens, axis=1), jnp.concatenate(odds, axis=1)]
        high = [v.astype(BF16) for v in values]
        low = [(v - h.astype(F32)).astype(BF16) for v, h in zip(values, high)]

        def spread(base, r, mask, zt, ref, i, start):
            at = base + r // 2
            left = jnp.concatenate([mask * t[r % 2][at : at + 1, :] for t in (high, low)], axis=0)
            got = lax.dot_general(left, zt, (((1,), (1,)), ((), ())), preferred_element_type=F32)
            size = mask.shape[0]
            ref[i, start : start + size] += got[0:size] + got[size:]

        for base, count, shift in ((0, rows, 0), (HIGH_LIST, mid, 0), (LOW_LIST, mid, rows - mid)):
            off = values[0][base + 3 : base + 4, :].astype(jnp.int32)
            row = off // nz
            zt = (row_ids((nz, chunk)) == off - row * nz).astype(F32).astype(BF16)
            mask = (row_ids((count, chunk)) == row - shift).astype(F32).astype(BF16)
            for i in range(3):
                if base == 0:
                    spread(base, i, mask, zt, zero_ref, i, mid)
                    spread(base, 3 + i, mask, zt, one_ref, i, near)
                    spread(base, 7 + i, mask, zt, two_ref, i, 0)
                elif base == HIGH_LIST:
                    spread(base, i, mask, zt, zero_ref, i, mid + rows)
                    spread(base, 3 + i, mask[0:near], zt, one_ref, i, near + rows)
                else:
                    spread(base, i, mask, zt, zero_ref, i, 0)
                    spread(base, 3 + i, mask[mid - near :], zt, one_ref, i, 0)
        return carry

    lax.fori_loop(0, sources // 4, body, 0)
    sign = sign_ref[...]
    for i in range(3):
        zero_out[i] = zero_ref[i].reshape(zero_out.shape[1:]) * sign
        one_out[i] = one_ref[i].reshape(one_out.shape[1:]) * sign[MID - NEAR : MID + cx + NEAR]
        two_out[i] = two_ref[i].reshape(two_out.shape[1:]) * sign[MID : MID + cx]
    at = row_ids((TILE, nz))

    def write(is_high, face_ref):
        ys = slice(cy - TILE, cy) if is_high else slice(0, TILE)
        half = at >= TILE // 2 if is_high else at < TILE // 2
        corner = at < NEAR if is_high else at >= TILE - NEAR
        for i in range(3):
            for x in range(cx):
                tile = jnp.where(half, zero_out[i, MID + x, ys], half_turn(one_out[i, NEAR + x, ys]))
                if x < 2 * NEAR:
                    moved = pltpu.roll(zero_out[i, MID + corner_plane(x, cx), ys], NEAR if is_high else TILE - NEAR, 0)
                    tile = jnp.where(corner, moved, tile)
                face_ref[i, x] = tile

    write_faces(par_ref[0], write, even_out, odd_out)


def corner_plane(x, cx):
    return x - NEAR if x < NEAR else cx + x - NEAR


def write_faces(parity, write, even_out, odd_out):
    @pl.when(parity == 0)
    def _():
        write(True, even_out)
        write(False, odd_out)

    @pl.when(parity != 0)
    def _():
        write(False, even_out)
        write(True, odd_out)


def pair_list(count, odd):
    first = 1 if odd else 0
    pairs = [(i, i + 1) for i in range(first, count - 1, 2)]
    return pairs + [(j, i) for i, j in pairs]


def swap_faces(faces, axis):
    count = lax.axis_size(axis)
    out = []
    for k in (0, 1):
        out.append(lax.ppermute(faces[k], axis, pair_list(count, k)))
    return out


def field_face_kernel(par_ref, cur_ref, ear_ref, coef_ref, even_out, odd_out):
    _, cx, cy, nz = cur_ref.shape
    upper = row_ids((TILE, nz)) >= TILE // 2

    def write(high, face_ref):
        ys = slice(cy - TILE, cy) if high else slice(0, TILE)
        keep = upper if high else ~upper
        for x in range(cx):
            for i in range(3):
                face_ref[i, x] = cur_ref[i, x, ys]
            face_ref[3, x] = jnp.where(keep, ear_ref[0, x, ys], half_turn(ear_ref[1, x, ys]))
            face_ref[4, x] = jnp.where(keep, ear_ref[2, x, ys], half_turn(coef_ref[x, ys]))

    write_faces(par_ref[0], write, even_out, odd_out)


def face_tile(ref, name, x):
    if name < 3:
        return ref[name, x]
    tile = ref[3 + (name - 3) // 2, x]
    return half_turn(tile) if name in (4, 6) else tile


def select_side(parity, even_ref, odd_ref, high):
    from_even = (parity == 0) if high else (parity == 1)

    def read(get):
        return jnp.where(from_even, get(even_ref), get(odd_ref))

    return read


FIELD_PLAN = [(DEEP, MID)] * 3 + [(MID, NEAR)] * 4 + [(MID, 0)]


def plan_tiles(plan, cy):
    out = []
    for name, (planes, corners) in enumerate(plan):
        for dist in range(1, planes + 1):
            for part in list(range(cy // TILE)) + ([-1] if dist <= corners else []):
                out.append((name, dist, part, len(out)))
    return out


def side_kernel(plan, own_tile, halo_tile, cx, cy, nz, px_ref, py_ref, even_ref, odd_ref, even_out, odd_out):
    upper = row_ids((TILE, nz)) >= TILE // 2
    low = select_side(py_ref[0], even_ref, odd_ref, False)
    high = select_side(py_ref[0], even_ref, odd_ref, True)

    def write(is_high, face_ref):
        for name, dist, part, at in plan_tiles(plan, cy):
            x = cx - dist if is_high else dist - 1
            if part >= 0:
                tile = own_tile(name, x, slice(part * TILE, (part + 1) * TILE))
            else:
                tile = jnp.where(
                    upper,
                    low(lambda ref: halo_tile(ref, name, x)),
                    high(lambda ref: halo_tile(ref, name, x)),
                )
            face_ref[at] = tile

    write_faces(px_ref[0], write, even_out, odd_out)


def sign_of(mask):
    return (mask == 1).astype(F32) - (mask == 2).astype(F32)


def field_side_kernel(px_ref, py_ref, cur_ref, ear_ref, coef_ref, mask_ref, *refs):
    _, cx, cy, nz = cur_ref.shape

    def own_tile(name, x, ys):
        if name < 3:
            return cur_ref[name, x, ys]
        if name < 6:
            return ear_ref[name - 3, x, ys]
        return coef_ref[x, ys] if name == 6 else sign_of(mask_ref[x, ys])

    side_kernel(FIELD_PLAN, own_tile, face_tile, cx, cy, nz, px_ref, py_ref, *refs)


def laplacian(plane, x_near, x_far):
    rows, nz = plane.shape
    width = 128
    lane = lax.broadcasted_iota(jnp.int32, (rows, width), 1)
    parts = [plane[:, k : k + width] for k in range(0, nz, width)]

    def along_z(k):
        up = [pltpu.roll(p, k, 1) for p in parts]
        down = [pltpu.roll(p, width - k, 1) for p in parts]
        out = []
        for j in range(len(parts)):
            below = jnp.where(lane >= k, up[j], up[j - 1] if j else 0.0)
            above = jnp.where(lane < width - k, down[j], down[j + 1] if j + 1 < len(parts) else 0.0)
            out.append(below + above)
        return jnp.concatenate(out, axis=1)

    def along_y(k):
        return pltpu.roll(plane, k, 0) + pltpu.roll(plane, rows - k, 0)

    near = x_near + along_y(1) + along_z(1)
    far = x_far + along_y(2) + along_z(2)
    return centre_weight * plane + near_weight * near + far_weight * far


def laplacian_at(ref, i, x):
    return laplacian(ref[i, x], ref[i, x - 1] + ref[i, x + 1], ref[i, x - 2] + ref[i, x + 2])


def first_wave_kernel(
    px_ref, py_ref, cur_ref, ear_ref, coef_ref, mask_ref, ye_ref, yo_ref, xe_ref, xo_ref,
    final_ref, prior_ref, wide_coef_ref, wide_sign_ref, u_ref, e_ref, c_ref, one_ref, two_ref,
):
    _, cx, cy, _ = cur_ref.shape
    own = slice(TILE, TILE + cy)
    lower, higher = slice(0, TILE), slice(TILE + cy, 2 * TILE + cy)
    low = select_side(py_ref[0], ye_ref, yo_ref, False)
    high = select_side(py_ref[0], ye_ref, yo_ref, True)

    def put(name, x, rows, value):
        if name < 3:
            u_ref[name, DEEP + x, rows] = value
        elif name < 6:
            e_ref[name - 3, MID + x, rows] = value
        elif name == 6:
            c_ref[MID + x, rows] = value
        else:
            wide_sign_ref[MID + x, slice(rows.start - TILE, rows.stop - TILE)] = value

    for x in range(cx):
        for name in range(7):
            value = cur_ref[name, x] if name < 3 else ear_ref[name - 3, x] if name < 6 else coef_ref[x]
            put(name, x, own, value)
            put(name, x, lower, low(lambda ref: face_tile(ref, name, x)))
            put(name, x, higher, high(lambda ref: face_tile(ref, name, x)))
        put(7, x, own, sign_of(mask_ref[x]))
    for is_high in (False, True):
        read = select_side(px_ref[0], xe_ref, xo_ref, is_high)
        for name, dist, part, at in plan_tiles(FIELD_PLAN, cy):
            x = cx - 1 + dist if is_high else -dist
            tile = read(lambda ref: ref[at])
            if part >= 0:
                put(name, x, slice(TILE * (part + 1), TILE * (part + 2)), tile)
            else:
                put(name, x, lower, tile)
                put(name, x, higher, tile)

    def first(x, carry):
        for i in range(3):
            at = x + DEEP - MID
            one_ref[i, x] = 2.0 * u_ref[i, at] - e_ref[i, x] + c_ref[x] * laplacian_at(u_ref, i, at)
        return carry

    def second(x, carry):
        at = x + MID - NEAR
        coef = c_ref[at]
        wide_coef_ref[x] = coef
        for i in range(3):
            lap = laplacian_at(one_ref, i, at)
            two_ref[i, x] = 2.0 * one_ref[i, at] - u_ref[i, x + DEEP - NEAR] + coef * lap
        return carry

    def third(x, carry):
        for i in range(3):
            at = x + NEAR
            plane = two_ref[i, at]
            moved = 2.0 * plane - one_ref[i, x + MID] + c_ref[x + MID] * laplacian_at(two_ref, i, at)
            final_ref[i, x] = moved[own]
            prior_ref[i, x] = plane[own]
        return carry

    lax.fori_loop(0, cx + 2 * MID, first, 0)
    lax.fori_loop(0, cx + 2 * NEAR, second, 0)
    lax.fori_loop(0, cx, third, 0)


def last_wave_kernel(
    py_ref, free_final_ref, free_prior_ref, coef_ref, zero_in, one_in, two_in, ye_ref, yo_ref,
    final_ref, prior_ref, one_ref, two_ref,
):
    _, cx, cy, _ = two_in.shape
    own = slice(TILE, TILE + cy)
    lower, higher = slice(0, TILE), slice(TILE + cy, 2 * TILE + cy)
    low = select_side(py_ref[0], ye_ref, yo_ref, False)
    high = select_side(py_ref[0], ye_ref, yo_ref, True)
    for i in range(3):
        for x in range(cx + 2 * MID):
            one_ref[i, x, own] = zero_in[i, x]
        for x in range(cx + 2 * NEAR):
            two_ref[i, x, own] = one_in[i, x]
        for x in range(cx):
            for rows, read, turn in ((lower, low, TILE - NEAR), (higher, high, NEAR)):
                tile = read(lambda ref: ref[i, x])
                one_ref[i, MID + x, rows] = tile
                two_ref[i, NEAR + x, rows] = half_turn(tile)
                if x < 2 * NEAR:
                    one_ref[i, MID + corner_plane(x, cx), rows] = pltpu.roll(tile, turn, 0)

    def second(x, carry):
        coef = coef_ref[x]
        for i in range(3):
            at = x + MID - NEAR
            two_ref[i, x] = 2.0 * one_ref[i, at] + coef * laplacian_at(one_ref, i, at) + two_ref[i, x]
        return carry

    lax.fori_loop(0, cx + 2 * NEAR, second, 0)

    def third(x, carry):
        coef = coef_ref[x + NEAR]
        for i in range(3):
            at = x + NEAR
            plane = two_ref[i, at]
            moved = 2.0 * plane - one_ref[i, x + MID] + coef * laplacian_at(two_ref, i, at)
            final_ref[i, x] = free_final_ref[i, x] + (moved[own] + two_in[i, x])
            prior_ref[i, x] = free_prior_ref[i, x] + plane[own]
        return carry

    lax.fori_loop(0, cx, third, 0)


def staged(kernel, positions, operand_count):
    def run(*refs):
        refs, stages, sems = refs[: -len(positions) - 1], refs[-len(positions) - 1 : -1], refs[-1]
        ins = list(refs[:operand_count])
        copies = []
        for k, (at, stage) in enumerate(zip(positions, stages)):
            copies.append(pltpu.make_async_copy(ins[at], stage, sems.at[k]))
            ins[at] = stage
        for copy in copies:
            copy.start()
        for copy in copies:
            copy.wait()
        kernel(*ins, *refs[operand_count:])

    return run


def local(
    current_field,
    earlier_field,
    wave_coef,
    layer_mask,
    point_xyz,
    point_owner,
    cell_offset,
    wave_vector,
    frequency,
    amplitude,
    phase_index,
    phase_table,
):
    table_size = phase_table.shape[0]
    matches = (phase_index[None, :] == jnp.arange(table_size)[:, None]).astype(F32)
    phases = jnp.dot(
        phase_table[None, :], matches, precision=lax.Precision.HIGHEST, preferred_element_type=F32
    )[0]
    own_block = jnp.concatenate(
        [wave_vector, frequency[None, :], amplitude, phases[None, :]], axis=0
    )
    point_count = point_xyz.shape[1]
    slab_count = lax.axis_size("slab")
    comp_count = lax.axis_size("comp")
    device_count = slab_count * comp_count
    slot_count = max(2, 2 * point_count // device_count)
    _, cx, cy, nz = current_field.shape
    assert slot_count <= HALF and device_count % 8 == 0
    assert cx >= DEEP and cy >= 2 * TILE and cy % TILE == 0
    wide = cy + 2 * TILE
    smem = pl.BlockSpec(memory_space=pltpu.SMEM)
    vmem = pl.BlockSpec(memory_space=pltpu.VMEM)

    def call(kernel, operands, shapes, scratch=(), scalars=0, from_hbm=(), to_hbm=False):
        shapes = [(pltpu.HBM if to_hbm else jax.ShapeDtypeStruct)(shape, F32) for shape in shapes]
        operands = list(operands)
        in_specs = [smem] * scalars + [vmem] * (len(operands) - scalars)
        scratch_shapes = [pltpu.VMEM(shape, F32) for shape in scratch]
        if from_hbm:
            for at in from_hbm:
                operands[at] = pltpu.with_memory_space_constraint(operands[at], pltpu.HBM)
                in_specs[at] = pl.BlockSpec(memory_space=pltpu.HBM)
                scratch_shapes.append(pltpu.VMEM(operands[at].shape, operands[at].dtype))
            scratch_shapes.append(pltpu.SemaphoreType.DMA((len(from_hbm),)))
            kernel = staged(kernel, from_hbm, len(operands))
        return pl.pallas_call(
            kernel,
            out_shape=shapes,
            in_specs=in_specs,
            out_specs=[vmem] * len(shapes),
            scratch_shapes=scratch_shapes,
            compiler_params=pltpu.CompilerParams(vmem_limit_bytes=VMEM_GRANT),
        )(*operands)

    px = (lax.axis_index("slab") % 2).astype(jnp.int32).reshape(1)
    py = (lax.axis_index("comp") % 2).astype(jnp.int32).reshape(1)
    if comp_count == 4:
        near_block = lax.ppermute(own_block, "comp", pair_list(4, 0))
        first_blocks = [own_block, near_block]
        ring = pair_list(4, 1) + [(0, 3), (3, 0)]
        far_block = lax.ppermute(jnp.concatenate(first_blocks, axis=1), "comp", ring)
        last_blocks = [far_block]
    else:
        first_blocks = [own_block]
        last_blocks = [
            lax.ppermute(own_block, "comp", [(i, (i + k) % comp_count) for i in range(comp_count)])
            for k in range(1, comp_count)
        ]
    fields = (current_field, earlier_field, wave_coef)
    faces = call(field_face_kernel, (py, *fields), [(5, cx, TILE, nz)] * 2, scalars=1, from_hbm=(1, 2, 3))
    ye, yo = swap_faces(faces, "comp")
    (sum_one, total_one) = call(
        lambda *refs: first_incident_kernel(len(first_blocks), *refs),
        (*first_blocks, point_xyz),
        [(32, point_count), (16, 256)],
        [(8, point_count)],
    )
    field_tiles = len(plan_tiles(FIELD_PLAN, cy))
    sides = call(
        field_side_kernel,
        (px, py, *fields, layer_mask, ye, yo),
        [(field_tiles, TILE, nz)] * 2,
        scalars=2,
        from_hbm=(2, 3, 4, 5),
    )
    xe, xo = swap_faces(sides, "slab")
    (packed,) = call(
        lambda *refs: last_incident_kernel(len(last_blocks), comp_count, *refs),
        (
            *last_blocks, sum_one, total_one, point_xyz,
            point_owner.reshape(1, point_count), cell_offset.reshape(1, point_count),
        ),
        [(device_count, LIST_ROWS, 2 * HALF)],
        [(8, point_count), (32, point_count)],
    )
    arrived = lax.all_to_all(packed, ("slab", "comp"), split_axis=0, concat_axis=0, tiled=True)
    free_final, free_prior, wide_coef, wide_sign = call(
        first_wave_kernel,
        (px, py, *fields, layer_mask, ye, yo, xe, xo),
        [current_field.shape, current_field.shape, (cx + 2 * NEAR, wide, nz), (cx + 2 * MID, cy, nz)],
        [
            (3, cx + 2 * DEEP, wide, nz), (3, cx + 2 * MID, wide, nz), (cx + 2 * MID, wide, nz),
            (3, cx + 2 * MID, wide, nz), (3, cx + 2 * NEAR, wide, nz),
        ],
        scalars=2,
        from_hbm=(2, 3, 4, 5),
        to_hbm=True,
    )
    *force, face_even, face_odd = call(
        scatter_kernel,
        (py, arrived, wide_sign),
        [(3, cx + 2 * MID, cy, nz), (3, cx + 2 * NEAR, cy, nz), (3, cx, cy, nz)] + [(3, cx, TILE, nz)] * 2,
        [(3, (cx + 2 * MID) * cy, nz), (3, (cx + 2 * NEAR) * cy, nz), (3, cx * cy, nz)],
        scalars=1,
        from_hbm=(2,),
    )
    fye, fyo = swap_faces((face_even, face_odd), "comp")
    final, prior = call(
        last_wave_kernel,
        (py, free_final, free_prior, wide_coef, *force, fye, fyo),
        [current_field.shape, current_field.shape],
        [(3, cx + 2 * MID, wide, nz), (3, cx + 2 * NEAR, wide, nz)],
        scalars=1,
        from_hbm=(1, 2, 3),
    )
    return (final, prior)


def solution(mesh):
    in_specs = (
        P(None, "slab", "comp", None),
        P(None, "slab", "comp", None),
        P("slab", "comp", None),
        P("slab", "comp", None),
        P(None, ("slab", "comp")),
        P(("slab", "comp"), None),
        P(("slab", "comp")),
        P(None, "comp"),
        P("comp"),
        P(None, "comp"),
        P("comp"),
        P(),
    )
    out_specs = (P(None, "slab", "comp", None), P(None, "slab", "comp", None))
    return jax.shard_map(local, mesh=mesh, in_specs=in_specs, out_specs=out_specs, check_vma=False)
```

time: 78.9 us -> 82.1 us (1.041)
  the two profiles are of different devices: /device:TPU:9 before, /device:TPU:8 now
where the time goes in v5:
time: 82.1 us; the launch traced here: 81.6 us
  Pallas kernels  48.3 us (59%)
  starting transfers between devices  18.1 us (22%)
  waiting for transfers between devices  12.9 us (16%)
  local copies, waits for them, and re-layouts  0.98 us (1%)
  between operations  0.86 us (1%)
    pallas_call x7, Pallas kernels, call(): pl.pallas_call(kernel, out_shape=shapes, in_specs=in_specs, out_specs=[vm...  48.3 us
    ppermute x6, waiting for transfers between devices, swap_faces(): out.append(lax.ppermute(faces[k], axis, pair_list(count, k)))  12.3 us
    ppermute x6, starting transfers between devices, swap_faces(): out.append(lax.ppermute(faces[k], axis, pair_list(count, k)))  10.3 us
    all_to_all x1, starting transfers between devices, local(): lax.all_to_all(packed, ('slab', 'comp'), split_axis=0, concat_axis=0, til...  5.96 us
    ppermute x1, starting transfers between devices, local(): lax.ppermute(jnp.concatenate(first_blocks, axis=1), 'comp', ring)  1.8 us
  transfers between devices with their start and end apart: 9, of which 5 were waited for; matrix products, arithmetic and copies ran while one was open for 1% of the time, Pallas kernels for 39%

profile of v5, /device:TPU:8, one launch (start us, length us, event | category | flops | bytes accessed | tf_op | source)
XLA Modules:
  0.0 81.6 jit_solution(493001669589503893)
XLA Ops:
  0.6 0.0 copy-start
  0.7 1.2 %shard_map.131 = (f32[5,8,8,256]{3,2,1,0:T(8,128)S(1)}, f32[5,8,8,256]{3,2,1,0:T(8,128)S(1)}) custom-call(s32[1]{0:T(128)} %bitcast.refs_0_.refs_1_, f32[3,8,16,256]{3,2,1,0:T(8,128)} %refs_2_.6, f32[3,8,16,256]{3,2,1,0:T(8,128)} %refs_3_.6, f32[8,16,256]{2,1,0:T(8,128)} %refs_4_.3), custom_call_target="tpu_custom_call" | custom-call | tf_op jit(solution)/shard_map/pallas_call | solution.py:541
  1.9 0.0 copy-start.7
  1.9 0.1 collective-permute-start
  2.0 5.0 %collective-permute-start.1 = (f32[5,8,8,256]{3,2,1,0:T(8,128)S(1)}, f32[5,8,8,256]{3,2,1,0:T(8,128)S(1)}, u32[]{:S(2)}, u32[]{:S(2)}) collective-permute-start(f32[5,8,8,256]{3,2,1,0:T(8,128)S(1)} %get-tuple-element.18), channel_id=1, source_target_pairs={{1,2},{2,1},{5,6},{6,5},{9,10},{10,9},{13,14},{14,13},{17,18},{18,... | collective-permute-start | bytes 983048 | tf_op jit(solution)/shard_map/ppermute | solution.py:253
  7.0 0.0 copy-done
  7.0 0.0 copy-done.7
  7.1 0.0 copy-start.4
  7.1 0.0 copy-start.5
  7.1 0.0 copy-start.6
  7.1 0.4 fusion
  7.5 0.3 copy-done.4
  7.8 0.0 copy-done.5
  7.8 0.0 copy-done.6
  7.8 0.1 collective-permute-start.4
  7.9 3.9 %collective-permute-done.refs_6_ = f32[5,8,8,256]{3,2,1,0:T(8,128)S(1)} collective-permute-done((f32[5,8,8,256]{3,2,1,0:T(8,128)S(1)}, f32[5,8,8,256]{3,2,1,0:T(8,128)S(1)}, u32[]{:S(2)}, u32[]{:S(2)}) %collective-permute-start) | collective-permute-done | bytes 327712 | tf_op jit(solution)/shard_map/ppermute | solution.py:253
  11.8 2.7 %collective-permute-done.1.refs_7_ = f32[5,8,8,256]{3,2,1,0:T(8,128)S(1)} collective-permute-done((f32[5,8,8,256]{3,2,1,0:T(8,128)S(1)}, f32[5,8,8,256]{3,2,1,0:T(8,128)S(1)}, u32[]{:S(2)}, u32[]{:S(2)}) %collective-permute-start.1) | collective-permute-done | bytes 327712 | tf_op jit(solution)/shard_map/ppermute | solution.py:253
  14.4 2.2 %shard_map.132 = (f32[96,8,256]{2,1,0:T(8,128)}, f32[96,8,256]{2,1,0:T(8,128)S(1)}) custom-call(s32[1]{0:T(128)} %bitcast.1.refs_0_, s32[1]{0:T(128)} %bitcast.refs_0_.refs_1_, f32[3,8,16,256]{3,2,1,0:T(8,128)} %refs_2_.6, f32[3,8,16,256]{3,2,1,0:T(8,128)} %refs_3_.6, f32[8,16,256]{2,1,0:T(8,128)} %refs_4_.3, s32[8,16,256]{2,1,0:T(8,128)} %refs_5_.3, ...), custom_call_target="tpu_custom_call" | custom-call | tf_op jit(solution)/shard_map/pallas_call | solution.py:541
  16.7 0.1 collective-permute-start.2
  16.8 0.0 copy-start.1
  16.8 0.7 collective-permute-start.3
  17.5 0.0 collective-permute-done.4.refs_1_
  17.5 1.8 %collective-permute-start.5 = (f32[8,2048]{1,0:T(8,128)S(1)}, f32[8,2048]{1,0:T(8,128)S(1)}, u32[]{:S(2)}, u32[]{:S(2)}) collective-permute-start(f32[8,2048]{1,0:T(8,128)S(1)} %pad_maximum_fusion), channel_id=1, source_target_pairs={{1,2},{2,1},{0,3},{3,0},{5,6},{6,5},{4,7},{7,4},{9,10},{10,9},{8,1... | collective-permute-start | bytes 196616 | tf_op jit(solution)/shard_map/ppermute | solution.py:556
  19.3 0.0 copy-done.1
  19.3 0.0 copy-start.3
  19.3 9.8 %shard_map.134 = (f32[32,1024]{1,0:T(8,128)S(1)}, f32[16,256]{1,0:T(8,128)S(1)}) custom-call(f32[8,1024]{1,0:T(8,128)S(1)} %pad_maximum_fusion.1.refs_0_, f32[8,1024]{1,0:T(8,128)S(1)} %collective-permute-done.4.refs_1_, f32[3,1024]{1,0:T(4,128)S(1)} %copy-done.1), custom_call_target="tpu_custom_call" | custom-call | tf_op jit(solution)/shard_map/pallas_call | solution.py:541
  29.2 0.0 copy-start.2
  29.2 0.0 collective-permute-done.5.refs_0_
  29.2 0.0 copy-done.3
  29.2 0.7 copy-done.2
  29.8 11.6 %shard_map.135 = f32[32,16,128]{2,1,0:T(8,128)} custom-call(f32[8,2048]{1,0:T(8,128)S(1)} %collective-permute-done.5.refs_0_, f32[32,1024]{1,0:T(8,128)S(1)} %get-tuple-element.24.refs_1_, f32[16,256]{1,0:T(8,128)S(1)} %get-tuple-element.25.refs_2_, f32[3,1024]{1,0:T(4,128)S(1)} %copy-done.1, s32[1,1024]{1,0:T(1,128)S(1)} %bitcast.9, s32[1,1024]{1,0:T(1,128)S(1)} %bitcast.10), custom_call_target="tpu_custom_call" | custom-call | tf_op jit(solution)/shard_map/pallas_call | solution.py:541
  41.4 6.0 %all-to-all-start = ((f32[32,16,128]{2,1,0:T(8,128)}), f32[32,16,128]{2,1,0:T(8,128)S(1)}, u32[]{:S(2)}, u32[]{:S(2)}) async-start(f32[32,16,128]{2,1,0:T(8,128)} %shard_map.135), calls=%async_computation | async-start | bytes 524288 | tf_op jit(solution)/shard_map/all_to_all | solution.py:591
  47.4 0.0 collective-permute-done.2.refs_8_
  47.4 0.0 collective-permute-done.3.refs_9_
  47.4 8.6 %shard_map.133 = (f32[3,8,16,256]{3,2,1,0:T(8,128)}, f32[3,8,16,256]{3,2,1,0:T(8,128)}, f32[12,32,256]{2,1,0:T(8,128)}, f32[16,16,256]{2,1,0:T(8,128)}) custom-call(s32[1]{0:T(128)} %bitcast.1.refs_0_, s32[1]{0:T(128)} %bitcast.refs_0_.refs_1_, f32[3,8,16,256]{3,2,1,0:T(8,128)} %refs_2_.6, f32[3,8,16,256]{3,2,1,0:T(8,128)} %refs_3_.6, ...), custom_call_target="tpu_custom_call" | custom-call | tf_op jit(solution)/shard_map/pallas_call | solution.py:541
  56.0 0.6 all-to-all-done.refs_1_
  56.5 9.5 %shard_map.136 = (f32[3,16,16,256]{3,2,1,0:T(8,128)S(1)}, f32[3,12,16,256]{3,2,1,0:T(8,128)S(1)}, f32[3,8,16,256]{3,2,1,0:T(8,128)S(1)}, f32[3,8,8,256]{3,2,1,0:T(8,128)S(1)}, f32[3,8,8,256]{3,2,1,0:T(8,128)S(1)}) custom-call(s32[1]{0:T(128)} %bitcast.refs_0_.refs_1_, f32[32,16,128]{2,1,0:T(8,128)S(1)} %all-to-all-done.refs_1_, ...), custom_call_target="tpu_custom_call" | custom-call | tf_op jit(solution)/shard_map/pallas_call | solution.py:541
  66.1 1.4 %collective-permute-start.6 = (f32[3,8,8,256]{3,2,1,0:T(8,128)S(1)}, f32[3,8,8,256]{3,2,1,0:T(8,128)S(1)}, u32[]{:S(2)}, u32[]{:S(2)}) collective-permute-start(f32[3,8,8,256]{3,2,1,0:T(8,128)S(1)} %get-tuple-element.30), channel_id=1, source_target_pairs={{0,1},{2,3},{1,0},{3,2},{4,5},{6,7},{5,4},{7,6},{8,9},{10,11},{9,8... | collective-permute-start | bytes 589832 | tf_op jit(solution)/shard_map/ppermute | solution.py:253
  67.5 3.0 %collective-permute-start.7 = (f32[3,8,8,256]{3,2,1,0:T(8,128)S(1)}, f32[3,8,8,256]{3,2,1,0:T(8,128)S(1)}, u32[]{:S(2)}, u32[]{:S(2)}) collective-permute-start(f32[3,8,8,256]{3,2,1,0:T(8,128)S(1)} %get-tuple-element.31), channel_id=1, source_target_pairs={{1,2},{2,1},{5,6},{6,5},{9,10},{10,9},{13,14},{14,13},{17,18},{18,... | collective-permute-start | bytes 589832 | tf_op jit(solution)/shard_map/ppermute | solution.py:253
  70.5 2.4 %collective-permute-done.6.refs_7_ = f32[3,8,8,256]{3,2,1,0:T(8,128)S(1)} collective-permute-done((f32[3,8,8,256]{3,2,1,0:T(8,128)S(1)}, f32[3,8,8,256]{3,2,1,0:T(8,128)S(1)}, u32[]{:S(2)}, u32[]{:S(2)}) %collective-permute-start.6) | collective-permute-done | bytes 196640 | tf_op jit(solution)/shard_map/ppermute | solution.py:253
  72.9 3.3 %collective-permute-done.7.refs_8_ = f32[3,8,8,256]{3,2,1,0:T(8,128)S(1)} collective-permute-done((f32[3,8,8,256]{3,2,1,0:T(8,128)S(1)}, f32[3,8,8,256]{3,2,1,0:T(8,128)S(1)}, u32[]{:S(2)}, u32[]{:S(2)}) %collective-permute-start.7) | collective-permute-done | bytes 196640 | tf_op jit(solution)/shard_map/ppermute | solution.py:253
  76.2 5.4 %shard_map.137 = (f32[3,8,16,256]{3,2,1,0:T(8,128)}, f32[3,8,16,256]{3,2,1,0:T(8,128)}) custom-call(s32[1]{0:T(128)} %bitcast.refs_0_.refs_1_, f32[3,8,16,256]{3,2,1,0:T(8,128)} %get-tuple-element.21.refs_1_, f32[3,8,16,256]{3,2,1,0:T(8,128)} %get-tuple-element.22.refs_2_, f32[12,32,256]{2,1,0:T(8,128)} %get-tuple-element.23.refs_3_, ...), custom_call_target="tpu_custom_call" | custom-call | tf_op jit(solution)/shard_map/pallas_call | solution.py:541
  (2 shorter events, 0.0 us)
Async XLA Ops:
  0.6 6.4 %copy-start = (f32[256]{0:T(256)S(1)}, f32[256]{0:T(256)}, u32[]{:S(2)}) copy-start(f32[256]{0:T(256)} %param.23) | copy-start | bytes 3076
  1.9 5.1 %copy-start.7 = (s32[1024]{0:T(1024)S(1)}, s32[1024]{0:T(1024)}, u32[]{:S(2)}) copy-start(s32[1024]{0:T(1024)} %param.22) | copy-start | bytes 12292
  1.9 9.9 %collective-permute-start = (f32[5,8,8,256]{3,2,1,0:T(8,128)S(1)}, f32[5,8,8,256]{3,2,1,0:T(8,128)S(1)}, u32[]{:S(2)}, u32[]{:S(2)}) collective-permute-start(f32[5,8,8,256]{3,2,1,0:T(8,128)S(1)} %get-tuple-element.17), channel_id=1, source_target_pairs={{0,1},{2,3},{1,0},{3,2},{4,5},{6,7},{5,4},{7,6},{8,9},{10,11},{9,8... | collective-permute-start | bytes 983048 | tf_op jit(solution)/shard_map/ppermute | solution.py:253
  2.0 12.5 %collective-permute-start.1 = (f32[5,8,8,256]{3,2,1,0:T(8,128)S(1)}, f32[5,8,8,256]{3,2,1,0:T(8,128)S(1)}, u32[]{:S(2)}, u32[]{:S(2)}) collective-permute-start(f32[5,8,8,256]{3,2,1,0:T(8,128)S(1)} %get-tuple-element.18), channel_id=1, source_target_pairs={{1,2},{2,1},{5,6},{6,5},{9,10},{10,9},{13,14},{14,13},{17,18},{18,... | collective-permute-start | bytes 983048 | tf_op jit(solution)/shard_map/ppermute | solution.py:253
  7.1 0.7 copy-start.4
  7.1 0.7 copy-start.5
  7.1 0.7 copy-start.6
  7.8 9.7 %collective-permute-start.4 = (f32[8,1024]{1,0:T(8,128)S(1)}, f32[8,1024]{1,0:T(8,128)S(1)}, u32[]{:S(2)}, u32[]{:S(2)}) collective-permute-start(f32[8,1024]{1,0:T(8,128)S(1)} %pad_maximum_fusion.1.refs_0_), channel_id=1, source_target_pairs={{0,1},{2,3},{1,0},{3,2},{4,5},{6,7},{5,4},{7,6},{8,9},{10,11},{9,8... | collective-permute-start | bytes 98312 | tf_op jit(solution)/shard_map/ppermute | solution.py:553
  16.7 30.7 %collective-permute-start.2 = (f32[96,8,256]{2,1,0:T(8,128)}, f32[96,8,256]{2,1,0:T(8,128)S(1)}, u32[]{:S(2)}, u32[]{:S(2)}) collective-permute-start(f32[96,8,256]{2,1,0:T(8,128)} %get-tuple-element.19), channel_id=1, source_target_pairs={{0,4},{8,12},{16,20},{24,28},{4,0},{12,8},{20,16},{28,24},{1,5},{9... | collective-permute-start | bytes 2359304 | tf_op jit(solution)/shard_map/ppermute | solution.py:253
  16.8 2.6 %copy-start.1 = (f32[3,1024]{1,0:T(4,128)S(1)}, f32[3,1024]{1,0:T(4,128)}, u32[]{:S(2)}) copy-start(f32[3,1024]{1,0:T(4,128)} %refs_3_.7) | copy-start | bytes 36868
  16.8 30.6 %collective-permute-start.3 = (f32[96,8,256]{2,1,0:T(8,128)S(1)}, f32[96,8,256]{2,1,0:T(8,128)S(1)}, u32[]{:S(2)}, u32[]{:S(2)}) collective-permute-start(f32[96,8,256]{2,1,0:T(8,128)S(1)} %get-tuple-element.20), channel_id=1, source_target_pairs={{4,8},{12,16},{20,24},{8,4},{16,12},{24,20},{5,9},{13,17},{21,25},... | collective-permute-start | bytes 2359304 | tf_op jit(solution)/shard_map/ppermute | solution.py:253
  17.5 11.6 %collective-permute-start.5 = (f32[8,2048]{1,0:T(8,128)S(1)}, f32[8,2048]{1,0:T(8,128)S(1)}, u32[]{:S(2)}, u32[]{:S(2)}) collective-permute-start(f32[8,2048]{1,0:T(8,128)S(1)} %pad_maximum_fusion), channel_id=1, source_target_pairs={{1,2},{2,1},{0,3},{3,0},{5,6},{6,5},{4,7},{7,4},{9,10},{10,9},{8,1... | collective-permute-start | bytes 196616 | tf_op jit(solution)/shard_map/ppermute | solution.py:556
  19.3 9.8 %copy-start.3 = (s32[1024]{0:T(1024)S(1)}, s32[1024]{0:T(1024)}, u32[]{:S(2)}) copy-start(s32[1024]{0:T(1024)} %param.18) | copy-start | bytes 12292
  29.2 0.7 copy-start.2
  41.4 15.1 %all-to-all-start = ((f32[32,16,128]{2,1,0:T(8,128)}), f32[32,16,128]{2,1,0:T(8,128)S(1)}, u32[]{:S(2)}, u32[]{:S(2)}) async-start(f32[32,16,128]{2,1,0:T(8,128)} %shard_map.135), calls=%async_computation | async-start | bytes 524288 | tf_op jit(solution)/shard_map/all_to_all | solution.py:591
  66.1 6.8 %collective-permute-start.6 = (f32[3,8,8,256]{3,2,1,0:T(8,128)S(1)}, f32[3,8,8,256]{3,2,1,0:T(8,128)S(1)}, u32[]{:S(2)}, u32[]{:S(2)}) collective-permute-start(f32[3,8,8,256]{3,2,1,0:T(8,128)S(1)} %get-tuple-element.30), channel_id=1, source_target_pairs={{0,1},{2,3},{1,0},{3,2},{4,5},{6,7},{5,4},{7,6},{8,9},{10,11},{9,8... | collective-permute-start | bytes 589832 | tf_op jit(solution)/shard_map/ppermute | solution.py:253
  67.5 8.8 %collective-permute-start.7 = (f32[3,8,8,256]{3,2,1,0:T(8,128)S(1)}, f32[3,8,8,256]{3,2,1,0:T(8,128)S(1)}, u32[]{:S(2)}, u32[]{:S(2)}) collective-permute-start(f32[3,8,8,256]{3,2,1,0:T(8,128)S(1)} %get-tuple-element.31), channel_id=1, source_target_pairs={{1,2},{2,1},{5,6},{6,5},{9,10},{10,9},{13,14},{14,13},{17,18},{18,... | collective-permute-start | bytes 589832 | tf_op jit(solution)/shard_map/ppermute | solution.py:253

commit v6 on v5

--- a/solution.py
+++ b/solution.py
@@ -157,13 +157,11 @@
     return pltpu.roll(tile, TILE // 2, 0)
 
 
-def scatter_kernel(par_ref, val_ref, sign_ref, zero_out, one_out, two_out, even_out, odd_out, zero_ref, one_ref, two_ref):
+def scatter_lists(val_ref, jobs, cy, nz):
     sources, _, lanes = val_ref.shape
-    _, cx, cy, nz = two_out.shape
-    rows, mid, near = cx * cy, MID * cy, NEAR * cy
     chunk = 2 * lanes
     left_half = lax.broadcasted_iota(jnp.int32, (LIST_ROWS, lanes), 1) < lanes // 2
-    for ref in (zero_ref, one_ref, two_ref):
+    for ref in {id(job[4]): job[4] for job in jobs}.values():
         ref[...] = jnp.zeros(ref.shape, F32)
 
     def body(step, carry):
@@ -175,38 +173,48 @@
         values = [jnp.concatenate(evens, axis=1), jnp.concatenate(odds, axis=1)]
         high = [v.astype(BF16) for v in values]
         low = [(v - h.astype(F32)).astype(BF16) for v, h in zip(values, high)]
-
-        def spread(base, r, mask, zt, ref, i, start):
-            at = base + r // 2
-            left = jnp.concatenate([mask * t[r % 2][at : at + 1, :] for t in (high, low)], axis=0)
-            got = lax.dot_general(left, zt, (((1,), (1,)), ((), ())), preferred_element_type=F32)
-            size = mask.shape[0]
-            ref[i, start : start + size] += got[0:size] + got[size:]
-
-        for base, count, shift in ((0, rows, 0), (HIGH_LIST, mid, 0), (LOW_LIST, mid, rows - mid)):
+        for base in (0, HIGH_LIST, LOW_LIST):
+            own_jobs = [job for job in jobs if job[0] == base]
             off = values[0][base + 3 : base + 4, :].astype(jnp.int32)
             row = off // nz
             zt = (row_ids((nz, chunk)) == off - row * nz).astype(F32).astype(BF16)
-            mask = (row_ids((count, chunk)) == row - shift).astype(F32).astype(BF16)
-            for i in range(3):
-                if base == 0:
-                    spread(base, i, mask, zt, zero_ref, i, mid)
-                    spread(base, 3 + i, mask, zt, one_ref, i, near)
-                    spread(base, 7 + i, mask, zt, two_ref, i, 0)
-                elif base == HIGH_LIST:
-                    spread(base, i, mask, zt, zero_ref, i, mid + rows)
-                    spread(base, 3 + i, mask[0:near], zt, one_ref, i, near + rows)
-                else:
-                    spread(base, i, mask, zt, zero_ref, i, 0)
-                    spread(base, 3 + i, mask[mid - near :], zt, one_ref, i, 0)
+            masks, left = {}, []
+            for _, ranks, plane, planes, ref, start in own_jobs:
+                if (plane, planes) not in masks:
+                    ids = row_ids((planes * cy, chunk)) + plane * cy
+                    masks[plane, planes] = (ids == row).astype(F32).astype(BF16)
+                for r in ranks:
+                    at = base + r // 2
+                    left += [masks[plane, planes] * t[r % 2][at : at + 1, :] for t in (high, low)]
+            left = jnp.concatenate(left, axis=0)
+            got = lax.dot_general(left, zt, (((1,), (1,)), ((), ())), preferred_element_type=F32)
+            at = 0
+            for _, ranks, _, planes, ref, start in own_jobs:
+                size = planes * cy
+                for i in range(len(ranks)):
+                    ref[i, start : start + size] += got[at : at + size] + got[at + size : at + 2 * size]
+                    at += 2 * size
         return carry
 
     lax.fori_loop(0, sources // 4, body, 0)
+
+
+STEP_ROWS = ((0, 1, 2), (3, 4, 5), (7, 8, 9))
+
+
+def near_scatter_kernel(par_ref, val_ref, sign_ref, zero_out, one_out, even_out, odd_out, zero_ref, one_ref):
+    _, cx, cy, nz = one_out.shape
+    jobs = (
+        (0, STEP_ROWS[0], 0, cx, zero_ref, NEAR * cy),
+        (0, STEP_ROWS[1], 0, cx, one_ref, 0),
+        (HIGH_LIST, STEP_ROWS[0], 0, NEAR, zero_ref, (NEAR + cx) * cy),
+        (LOW_LIST, STEP_ROWS[0], cx - NEAR, NEAR, zero_ref, 0),
+    )
+    scatter_lists(val_ref, jobs, cy, nz)
     sign = sign_ref[...]
     for i in range(3):
-        zero_out[i] = zero_ref[i].reshape(zero_out.shape[1:]) * sign
-        one_out[i] = one_ref[i].reshape(one_out.shape[1:]) * sign[MID - NEAR : MID + cx + NEAR]
-        two_out[i] = two_ref[i].reshape(two_out.shape[1:]) * sign[MID : MID + cx]
+        zero_out[i] = zero_ref[i].reshape(zero_out.shape[1:]) * sign[MID - NEAR : MID + cx + NEAR]
+        one_out[i] = one_ref[i].reshape(one_out.shape[1:]) * sign[MID : MID + cx]
     at = row_ids((TILE, nz))
 
     def write(is_high, face_ref):
@@ -215,13 +223,33 @@
         corner = at < NEAR if is_high else at >= TILE - NEAR
         for i in range(3):
             for x in range(cx):
-                tile = jnp.where(half, zero_out[i, MID + x, ys], half_turn(one_out[i, NEAR + x, ys]))
+                tile = jnp.where(half, zero_out[i, NEAR + x, ys], half_turn(one_out[i, x, ys]))
                 if x < 2 * NEAR:
-                    moved = pltpu.roll(zero_out[i, MID + corner_plane(x, cx), ys], NEAR if is_high else TILE - NEAR, 0)
+                    moved = pltpu.roll(zero_out[i, NEAR + corner_plane(x, cx), ys], NEAR if is_high else TILE - NEAR, 0)
                     tile = jnp.where(corner, moved, tile)
                 face_ref[i, x] = tile
 
     write_faces(par_ref[0], write, even_out, odd_out)
+
+
+def rest_scatter_kernel(val_ref, sign_ref, zero_out, one_out, two_out, zero_ref, one_ref, two_ref):
+    _, cx, cy, nz = two_out.shape
+    jobs = (
+        (0, STEP_ROWS[2], 0, cx, two_ref, 0),
+        (HIGH_LIST, STEP_ROWS[0], NEAR, MID - NEAR, zero_ref, NEAR * cy),
+        (LOW_LIST, STEP_ROWS[0], cx - MID, MID - NEAR, zero_ref, 0),
+        (HIGH_LIST, STEP_ROWS[1], 0, NEAR, one_ref, NEAR * cy),
+        (LOW_LIST, STEP_ROWS[1], cx - NEAR, NEAR, one_ref, 0),
+    )
+    scatter_lists(val_ref, jobs, cy, nz)
+    sign = sign_ref[...]
+    last = cx + 2 * MID
+    far = jnp.concatenate([sign[0 : MID - NEAR], sign[last - (MID - NEAR) :]], axis=0)
+    side = jnp.concatenate([sign[MID - NEAR : MID], sign[MID + cx : MID + cx + NEAR]], axis=0)
+    for i in range(3):
+        zero_out[i] = zero_ref[i].reshape(zero_out.shape[1:]) * far
+        one_out[i] = one_ref[i].reshape(one_out.shape[1:]) * side
+        two_out[i] = two_ref[i].reshape(two_out.shape[1:]) * sign[MID : MID + cx]
 
 
 def corner_plane(x, cx):
@@ -336,32 +364,36 @@
     side_kernel(FIELD_PLAN, own_tile, face_tile, cx, cy, nz, px_ref, py_ref, *refs)
 
 
-def laplacian(plane, x_near, x_far):
-    rows, nz = plane.shape
-    width = 128
-    lane = lax.broadcasted_iota(jnp.int32, (rows, width), 1)
-    parts = [plane[:, k : k + width] for k in range(0, nz, width)]
-
-    def along_z(k):
-        up = [pltpu.roll(p, k, 1) for p in parts]
-        down = [pltpu.roll(p, width - k, 1) for p in parts]
-        out = []
-        for j in range(len(parts)):
-            below = jnp.where(lane >= k, up[j], up[j - 1] if j else 0.0)
-            above = jnp.where(lane < width - k, down[j], down[j + 1] if j + 1 < len(parts) else 0.0)
-            out.append(below + above)
-        return jnp.concatenate(out, axis=1)
-
-    def along_y(k):
-        return pltpu.roll(plane, k, 0) + pltpu.roll(plane, rows - k, 0)
-
-    near = x_near + along_y(1) + along_z(1)
-    far = x_far + along_y(2) + along_z(2)
-    return centre_weight * plane + near_weight * near + far_weight * far
-
-
-def laplacian_at(ref, i, x):
-    return laplacian(ref[i, x], ref[i, x - 1] + ref[i, x + 1], ref[i, x - 2] + ref[i, x + 2])
+LANES = 128
+
+
+def put_rows(ref, index, rows, value):
+    for h in range(value.shape[1] // LANES):
+        ref[(*index, h, rows)] = value[:, h * LANES : (h + 1) * LANES]
+
+
+def laplacian_rows(ref, i, x, start, count):
+    tiles = ref.shape[2]
+    lane = lax.broadcasted_iota(jnp.int32, (count, LANES), 1)
+
+    def rows(h, dx, dy):
+        return ref[i, x + dx, h, pl.ds(start + dy, count)]
+
+    centre = [rows(h, 0, 0) for h in range(tiles)]
+    out = [centre_weight * c for c in centre]
+    for k, weight in ((1, near_weight), (2, far_weight)):
+        up = [pltpu.roll(c, k, 1) for c in centre]
+        down = [pltpu.roll(c, LANES - k, 1) for c in centre]
+        for h in range(tiles):
+            below = jnp.where(lane >= k, up[h], up[h - 1] if h else 0.0)
+            above = jnp.where(lane < LANES - k, down[h], down[h + 1] if h + 1 < tiles else 0.0)
+            across = (rows(h, -k, 0) + rows(h, k, 0)) + (rows(h, 0, -k) + rows(h, 0, k))
+            out[h] = out[h] + weight * (across + (below + above))
+    return centre, out
+
+
+def run_planes(first, last, body):
+    lax.fori_loop(first, last, lambda x, carry: (body(x), carry)[1], 0, unroll=2)
 
 
 def first_wave_kernel(
@@ -376,11 +408,13 @@
 
     def put(name, x, rows, value):
         if name < 3:
-            u_ref[name, DEEP + x, rows] = value
+            put_rows(u_ref, (name, DEEP + x), rows, value)
         elif name < 6:
-            e_ref[name - 3, MID + x, rows] = value
+            put_rows(e_ref, (name - 3, MID + x), rows, value)
         elif name == 6:
-            c_ref[MID + x, rows] = value
+            put_rows(c_ref, (MID + x,), rows, value)
+            if -NEAR <= x < cx + NEAR:
+                put_rows(wide_coef_ref, (NEAR + x,), rows, value)
         else:
             wide_sign_ref[MID + x, slice(rows.start - TILE, rows.stop - TILE)] = value
 
@@ -402,38 +436,51 @@
                 put(name, x, lower, tile)
                 put(name, x, higher, tile)
 
-    def first(x, carry):
+    begin = px_ref[1]
+    deep = cy + TILE
+
+    def first(start, count):
+        def body(x):
+            for i in range(3):
+                centre, lap = laplacian_rows(u_ref, i, x + DEEP - MID, start, count)
+                for h, (c, l) in enumerate(zip(centre, lap)):
+                    rows = pl.ds(start, count)
+                    one_ref[i, x, h, rows] = 2.0 * c - e_ref[i, x, h, rows] + c_ref[x, h, rows] * l
+
+        return body
+
+    def second(start, count):
+        def body(x):
+            for i in range(3):
+                centre, lap = laplacian_rows(one_ref, i, x + MID - NEAR, start, count)
+                for h, (c, l) in enumerate(zip(centre, lap)):
+                    rows = pl.ds(start, count)
+                    moved = 2.0 * c - u_ref[i, x + DEEP - NEAR, h, rows]
+                    two_ref[i, x, h, rows] = moved + c_ref[x + MID - NEAR, h, rows] * l
+
+        return body
+
+    def third(x):
         for i in range(3):
-            at = x + DEEP - MID
-            one_ref[i, x] = 2.0 * u_ref[i, at] - e_ref[i, x] + c_ref[x] * laplacian_at(u_ref, i, at)
-        return carry
-
-    def second(x, carry):
-        at = x + MID - NEAR
-        coef = c_ref[at]
-        wide_coef_ref[x] = coef
-        for i in range(3):
-            lap = laplacian_at(one_ref, i, at)
-            two_ref[i, x] = 2.0 * one_ref[i, at] - u_ref[i, x + DEEP - NEAR] + coef * lap
-        return carry
-
-    def third(x, carry):
-        for i in range(3):
-            at = x + NEAR
-            plane = two_ref[i, at]
-            moved = 2.0 * plane - one_ref[i, x + MID] + c_ref[x + MID] * laplacian_at(two_ref, i, at)
-            final_ref[i, x] = moved[own]
-            prior_ref[i, x] = plane[own]
-        return carry
-
-    lax.fori_loop(0, cx + 2 * MID, first, 0)
-    lax.fori_loop(0, cx + 2 * NEAR, second, 0)
-    lax.fori_loop(0, cx, third, 0)
+            centre, lap = laplacian_rows(two_ref, i, x + NEAR, TILE, cy)
+            for h, (c, l) in enumerate(zip(centre, lap)):
+                lanes = slice(h * LANES, (h + 1) * LANES)
+                moved = 2.0 * c - one_ref[i, x + MID, h, own]
+                final_ref[i, x, :, lanes] = moved + c_ref[x + MID, h, own] * l
+                prior_ref[i, x, :, lanes] = c
+
+    run_planes(0, NEAR, first(TILE, cy))
+    run_planes(NEAR, cx + 2 * MID - NEAR, first(begin, deep))
+    run_planes(cx + 2 * MID - NEAR, cx + 2 * MID, first(TILE, cy))
+    run_planes(0, NEAR, second(TILE, cy))
+    run_planes(NEAR, cx + NEAR, second(begin, deep))
+    run_planes(cx + NEAR, cx + 2 * NEAR, second(TILE, cy))
+    run_planes(0, cx, third)
 
 
 def last_wave_kernel(
-    py_ref, free_final_ref, free_prior_ref, coef_ref, zero_in, one_in, two_in, ye_ref, yo_ref,
-    final_ref, prior_ref, one_ref, two_ref,
+    px_ref, py_ref, free_final_ref, free_prior_ref, coef_ref, zero_in, zero_far_in, one_in, one_side_in, two_in,
+    ye_ref, yo_ref, final_ref, prior_ref, one_ref, two_ref,
 ):
     _, cx, cy, _ = two_in.shape
     own = slice(TILE, TILE + cy)
@@ -441,38 +488,45 @@
     low = select_side(py_ref[0], ye_ref, yo_ref, False)
     high = select_side(py_ref[0], ye_ref, yo_ref, True)
     for i in range(3):
-        for x in range(cx + 2 * MID):
-            one_ref[i, x, own] = zero_in[i, x]
         for x in range(cx + 2 * NEAR):
-            two_ref[i, x, own] = one_in[i, x]
+            put_rows(one_ref, (i, x + MID - NEAR), own, zero_in[i, x])
+        for k in range(NEAR):
+            put_rows(one_ref, (i, k), own, zero_far_in[i, k])
+            put_rows(one_ref, (i, cx + 2 * MID - NEAR + k), own, zero_far_in[i, NEAR + k])
+            put_rows(two_ref, (i, k), own, one_side_in[i, k])
+            put_rows(two_ref, (i, cx + NEAR + k), own, one_side_in[i, NEAR + k])
         for x in range(cx):
+            put_rows(two_ref, (i, NEAR + x), own, one_in[i, x])
             for rows, read, turn in ((lower, low, TILE - NEAR), (higher, high, NEAR)):
                 tile = read(lambda ref: ref[i, x])
-                one_ref[i, MID + x, rows] = tile
-                two_ref[i, NEAR + x, rows] = half_turn(tile)
+                put_rows(one_ref, (i, MID + x), rows, tile)
+                put_rows(two_ref, (i, NEAR + x), rows, half_turn(tile))
                 if x < 2 * NEAR:
-                    one_ref[i, MID + corner_plane(x, cx), rows] = pltpu.roll(tile, turn, 0)
-
-    def second(x, carry):
-        coef = coef_ref[x]
+                    put_rows(one_ref, (i, MID + corner_plane(x, cx)), rows, pltpu.roll(tile, turn, 0))
+
+    def second(start, count):
+        def body(x):
+            for i in range(3):
+                centre, lap = laplacian_rows(one_ref, i, x + MID - NEAR, start, count)
+                for h, (c, l) in enumerate(zip(centre, lap)):
+                    rows = pl.ds(start, count)
+                    two_ref[i, x, h, rows] = 2.0 * c + coef_ref[x, h, rows] * l + two_ref[i, x, h, rows]
+
+        return body
+
+    def third(x):
         for i in range(3):
-            at = x + MID - NEAR
-            two_ref[i, x] = 2.0 * one_ref[i, at] + coef * laplacian_at(one_ref, i, at) + two_ref[i, x]
-        return carry
-
-    lax.fori_loop(0, cx + 2 * NEAR, second, 0)
-
-    def third(x, carry):
-        coef = coef_ref[x + NEAR]
-        for i in range(3):
-            at = x + NEAR
-            plane = two_ref[i, at]
-            moved = 2.0 * plane - one_ref[i, x + MID] + coef * laplacian_at(two_ref, i, at)
-            final_ref[i, x] = free_final_ref[i, x] + (moved[own] + two_in[i, x])
-            prior_ref[i, x] = free_prior_ref[i, x] + plane[own]
-        return carry
-
-    lax.fori_loop(0, cx, third, 0)
+            centre, lap = laplacian_rows(two_ref, i, x + NEAR, TILE, cy)
+            for h, (c, l) in enumerate(zip(centre, lap)):
+                lanes = slice(h * LANES, (h + 1) * LANES)
+                moved = 2.0 * c - one_ref[i, x + MID, h, own] + coef_ref[x + NEAR, h, own] * l
+                final_ref[i, x, :, lanes] = free_final_ref[i, x, :, lanes] + (moved + two_in[i, x, :, lanes])
+                prior_ref[i, x, :, lanes] = free_prior_ref[i, x, :, lanes] + c
+
+    run_planes(0, NEAR, second(TILE, cy))
+    run_planes(NEAR, cx + NEAR, second(px_ref[1], cy + TILE))
+    run_planes(cx + NEAR, cx + 2 * NEAR, second(TILE, cy))
+    run_planes(0, cx, third)
 
 
 def staged(kernel, positions, operand_count):
@@ -523,6 +577,11 @@
     assert slot_count <= HALF and device_count % 8 == 0
     assert cx >= DEEP and cy >= 2 * TILE and cy % TILE == 0
     wide = cy + 2 * TILE
+    assert nz % LANES == 0 and MID == 2 * NEAR
+
+    def plane_stack(*lead):
+        return (*lead, nz // LANES, wide, LANES)
+
     smem = pl.BlockSpec(memory_space=pltpu.SMEM)
     vmem = pl.BlockSpec(memory_space=pltpu.VMEM)
 
@@ -547,7 +606,7 @@
             compiler_params=pltpu.CompilerParams(vmem_limit_bytes=VMEM_GRANT),
         )(*operands)
 
-    px = (lax.axis_index("slab") % 2).astype(jnp.int32).reshape(1)
+    px = jnp.stack([lax.axis_index("slab") % 2, TILE // 2]).astype(jnp.int32)
     py = (lax.axis_index("comp") % 2).astype(jnp.int32).reshape(1)
     if comp_count == 4:
         near_block = lax.ppermute(own_block, "comp", pair_list(4, 0))
@@ -592,31 +651,38 @@
     free_final, free_prior, wide_coef, wide_sign = call(
         first_wave_kernel,
         (px, py, *fields, layer_mask, ye, yo, xe, xo),
-        [current_field.shape, current_field.shape, (cx + 2 * NEAR, wide, nz), (cx + 2 * MID, cy, nz)],
+        [current_field.shape, current_field.shape, plane_stack(cx + 2 * NEAR), (cx + 2 * MID, cy, nz)],
         [
-            (3, cx + 2 * DEEP, wide, nz), (3, cx + 2 * MID, wide, nz), (cx + 2 * MID, wide, nz),
-            (3, cx + 2 * MID, wide, nz), (3, cx + 2 * NEAR, wide, nz),
+            plane_stack(3, cx + 2 * DEEP), plane_stack(3, cx + 2 * MID), plane_stack(cx + 2 * MID),
+            plane_stack(3, cx + 2 * MID), plane_stack(3, cx + 2 * NEAR),
         ],
         scalars=2,
         from_hbm=(2, 3, 4, 5),
         to_hbm=True,
     )
-    *force, face_even, face_odd = call(
-        scatter_kernel,
+    zero, one, face_even, face_odd = call(
+        near_scatter_kernel,
         (py, arrived, wide_sign),
-        [(3, cx + 2 * MID, cy, nz), (3, cx + 2 * NEAR, cy, nz), (3, cx, cy, nz)] + [(3, cx, TILE, nz)] * 2,
-        [(3, (cx + 2 * MID) * cy, nz), (3, (cx + 2 * NEAR) * cy, nz), (3, cx * cy, nz)],
+        [(3, cx + 2 * NEAR, cy, nz), (3, cx, cy, nz)] + [(3, cx, TILE, nz)] * 2,
+        [(3, (cx + 2 * NEAR) * cy, nz), (3, cx * cy, nz)],
         scalars=1,
         from_hbm=(2,),
     )
     fye, fyo = swap_faces((face_even, face_odd), "comp")
+    zero_far, one_side, two = call(
+        rest_scatter_kernel,
+        (arrived, wide_sign),
+        [(3, 2 * NEAR, cy, nz), (3, 2 * NEAR, cy, nz), (3, cx, cy, nz)],
+        [(3, 2 * NEAR * cy, nz), (3, 2 * NEAR * cy, nz), (3, cx * cy, nz)],
+        from_hbm=(1,),
+    )
     final, prior = call(
         last_wave_kernel,
-        (py, free_final, free_prior, wide_coef, *force, fye, fyo),
+        (px, py, free_final, free_prior, wide_coef, zero, zero_far, one, one_side, two, fye, fyo),
         [current_field.shape, current_field.shape],
-        [(3, cx + 2 * MID, wide, nz), (3, cx + 2 * NEAR, wide, nz)],
-        scalars=1,
-        from_hbm=(1, 2, 3),
+        [plane_stack(3, cx + 2 * MID), plane_stack(3, cx + 2 * NEAR)],
+        scalars=2,
+        from_hbm=(2, 3, 4),
     )
     return (final, prior)
 

time: 82.1 us -> 78.1 us (0.951)
  waiting for transfers between devices: 12.9 us -> 9.89 us
  Pallas kernels: 48.3 us -> 47.4 us
    ppermute x6, waiting for transfers between devices: 12.3 us -> 7.38 us  [swap_faces(): out.append(lax.ppermute(faces[k], axis, pair_list(count, k)))]
    all_to_all x1, waiting for transfers between devices: 0.56 us -> 2.51 us  [local(): lax.all_to_all(packed, ('slab', 'comp'), split_axis=0, concat_axis=0, til...]
    pallas_call x7 -> x8, Pallas kernels: 48.3 us -> 47.4 us  [call(): pl.pallas_call(kernel, out_shape=shapes, in_specs=in_specs, out_specs=[vm...]
  transfers between devices with their start and end apart: 9 -> 9, of which waited for: 5 -> 4; matrix products, arithmetic and copies ran while one was open for 1% -> 1% of each run, Pallas kernels for 39% -> 46%
where the time goes in v6:
time: 78.1 us; the launch traced here: 77.6 us
  Pallas kernels  47.4 us (61%)
  starting transfers between devices  17.8 us (23%)
  waiting for transfers between devices  9.89 us (13%)
  local copies, waits for them, and re-layouts  0.98 us (1%)
  between operations  0.88 us (1%)
    pallas_call x8, Pallas kernels, call(): pl.pallas_call(kernel, out_shape=shapes, in_specs=in_specs, out_specs=[vm...  47.4 us
    ppermute x6, starting transfers between devices, swap_faces(): out.append(lax.ppermute(faces[k], axis, pair_list(count, k)))  9.98 us
    ppermute x6, waiting for transfers between devices, swap_faces(): out.append(lax.ppermute(faces[k], axis, pair_list(count, k)))  7.38 us
    all_to_all x1, starting transfers between devices, local(): lax.all_to_all(packed, ('slab', 'comp'), split_axis=0, concat_axis=0, til...  5.96 us
    all_to_all x1, waiting for transfers between devices, local(): lax.all_to_all(packed, ('slab', 'comp'), split_axis=0, concat_axis=0, til...  2.51 us
    ppermute x1, starting transfers between devices, local(): lax.ppermute(jnp.concatenate(first_blocks, axis=1), 'comp', ring)  1.8 us
  transfers between devices with their start and end apart: 9, of which 4 were waited for; matrix products, arithmetic and copies ran while one was open for 1% of the time, Pallas kernels for 46%

profile of v6, /device:TPU:8, one launch (start us, length us, event | category | flops | bytes accessed | tf_op | source)
XLA Modules:
  0.0 77.6 jit_solution(15176721098369915679)
XLA Ops:
  0.6 0.0 copy-start
  0.7 1.2 %shard_map.131 = (f32[5,8,8,256]{3,2,1,0:T(8,128)S(1)}, f32[5,8,8,256]{3,2,1,0:T(8,128)S(1)}) custom-call(s32[1]{0:T(128)} %bitcast.1.refs_0_.refs_1_, f32[3,8,16,256]{3,2,1,0:T(8,128)} %refs_2_.6, f32[3,8,16,256]{3,2,1,0:T(8,128)} %refs_3_.6, f32[8,16,256]{2,1,0:T(8,128)} %refs_4_.3), custom_call_target="tpu_custom_call" | custom-call | tf_op jit(solution)/shard_map/pallas_call | solution.py:600
  1.9 0.0 copy-start.7
  1.9 0.1 collective-permute-start
  2.0 5.0 %collective-permute-start.1 = (f32[5,8,8,256]{3,2,1,0:T(8,128)S(1)}, f32[5,8,8,256]{3,2,1,0:T(8,128)S(1)}, u32[]{:S(2)}, u32[]{:S(2)}) collective-permute-start(f32[5,8,8,256]{3,2,1,0:T(8,128)S(1)} %get-tuple-element.20), channel_id=1, source_target_pairs={{1,2},{2,1},{5,6},{6,5},{9,10},{10,9},{13,14},{14,13},{17,18},{18,... | collective-permute-start | bytes 983048 | tf_op jit(solution)/shard_map/ppermute | solution.py:281
  7.0 0.0 copy-done
  7.0 0.0 copy-done.7
  7.1 0.0 copy-start.4
  7.1 0.0 copy-start.5
  7.1 0.0 copy-start.6
  7.1 0.4 fusion
  7.5 0.3 copy-done.4
  7.8 0.0 copy-done.5
  7.8 0.0 copy-done.6
  7.8 0.1 collective-permute-start.4
  7.9 0.1 pad_add_fusion.refs_0_
  8.0 3.8 %collective-permute-done.refs_6_ = f32[5,8,8,256]{3,2,1,0:T(8,128)S(1)} collective-permute-done((f32[5,8,8,256]{3,2,1,0:T(8,128)S(1)}, f32[5,8,8,256]{3,2,1,0:T(8,128)S(1)}, u32[]{:S(2)}, u32[]{:S(2)}) %collective-permute-start) | collective-permute-done | bytes 327712 | tf_op jit(solution)/shard_map/ppermute | solution.py:281
  11.8 2.7 %collective-permute-done.1.refs_7_ = f32[5,8,8,256]{3,2,1,0:T(8,128)S(1)} collective-permute-done((f32[5,8,8,256]{3,2,1,0:T(8,128)S(1)}, f32[5,8,8,256]{3,2,1,0:T(8,128)S(1)}, u32[]{:S(2)}, u32[]{:S(2)}) %collective-permute-start.1) | collective-permute-done | bytes 327712 | tf_op jit(solution)/shard_map/ppermute | solution.py:281
  14.4 2.8 %shard_map.132 = (f32[96,8,256]{2,1,0:T(8,128)}, f32[96,8,256]{2,1,0:T(8,128)S(1)}) custom-call(s32[2]{0:T(128)S(1)} %pad_add_fusion.refs_0_, s32[1]{0:T(128)} %bitcast.1.refs_0_.refs_1_, f32[3,8,16,256]{3,2,1,0:T(8,128)} %refs_2_.6, f32[3,8,16,256]{3,2,1,0:T(8,128)} %refs_3_.6, f32[8,16,256]{2,1,0:T(8,128)} %refs_4_.3, s32[8,16,256]{2,1,0:T(8,128)} %refs_5_.3, ...), custom_call_target="tpu_custom_call" | custom-call | tf_op jit(solution)/shard_map/pallas_call | solution.py:600
  17.2 0.1 collective-permute-start.2
  17.3 0.0 copy-start.1
  17.3 0.7 collective-permute-start.3
  18.0 0.0 collective-permute-done.4.refs_1_
  18.1 1.8 %collective-permute-start.5 = (f32[8,2048]{1,0:T(8,128)S(1)}, f32[8,2048]{1,0:T(8,128)S(1)}, u32[]{:S(2)}, u32[]{:S(2)}) collective-permute-start(f32[8,2048]{1,0:T(8,128)S(1)} %pad_maximum_fusion), channel_id=1, source_target_pairs={{1,2},{2,1},{0,3},{3,0},{5,6},{6,5},{4,7},{7,4},{9,10},{10,9},{8,1... | collective-permute-start | bytes 196616 | tf_op jit(solution)/shard_map/ppermute | solution.py:615
  19.9 0.0 copy-done.1
  19.9 0.0 copy-start.3
  19.9 9.8 %shard_map.134 = (f32[32,1024]{1,0:T(8,128)S(1)}, f32[16,256]{1,0:T(8,128)S(1)}) custom-call(f32[8,1024]{1,0:T(8,128)S(1)} %pad_maximum_fusion.1.refs_0_, f32[8,1024]{1,0:T(8,128)S(1)} %collective-permute-done.4.refs_1_, f32[3,1024]{1,0:T(4,128)S(1)} %copy-done.1), custom_call_target="tpu_custom_call" | custom-call | tf_op jit(solution)/shard_map/pallas_call | solution.py:600
  29.7 0.0 copy-start.2
  29.7 0.0 collective-permute-done.5.refs_0_
  29.7 0.0 copy-done.3
  29.7 0.7 copy-done.2
  30.4 11.6 %shard_map.135 = f32[32,16,128]{2,1,0:T(8,128)} custom-call(f32[8,2048]{1,0:T(8,128)S(1)} %collective-permute-done.5.refs_0_, f32[32,1024]{1,0:T(8,128)S(1)} %get-tuple-element.26.refs_1_, f32[16,256]{1,0:T(8,128)S(1)} %get-tuple-element.27.refs_2_, f32[3,1024]{1,0:T(4,128)S(1)} %copy-done.1, s32[1,1024]{1,0:T(1,128)S(1)} %bitcast.9, s32[1,1024]{1,0:T(1,128)S(1)} %bitcast.10), custom_call_target="tpu_custom_call" | custom-call | tf_op jit(solution)/shard_map/pallas_call | solution.py:600
  42.0 6.0 %all-to-all-start = ((f32[32,16,128]{2,1,0:T(8,128)}), f32[32,16,128]{2,1,0:T(8,128)S(1)}, u32[]{:S(2)}, u32[]{:S(2)}) async-start(f32[32,16,128]{2,1,0:T(8,128)} %shard_map.135), calls=%async_computation | async-start | bytes 524288 | tf_op jit(solution)/shard_map/all_to_all | solution.py:650
  47.9 0.0 collective-permute-done.2.refs_8_
  47.9 0.0 collective-permute-done.3.refs_9_
  48.0 6.6 %shard_map.133 = (f32[3,8,16,256]{3,2,1,0:T(8,128)}, f32[3,8,16,256]{3,2,1,0:T(8,128)}, f32[12,2,32,128]{3,2,1,0:T(8,128)}, f32[16,16,256]{2,1,0:T(8,128)}) custom-call(s32[2]{0:T(128)S(1)} %pad_add_fusion.refs_0_, s32[1]{0:T(128)} %bitcast.1.refs_0_.refs_1_, f32[3,8,16,256]{3,2,1,0:T(8,128)} %refs_2_.6, f32[3,8,16,256]{3,2,1,0:T(8,128)} %refs_3_.6, ...), custom_call_target="tpu_custom_call" | custom-call | tf_op jit(solution)/shard_map/pallas_call | solution.py:600
  54.6 2.5 %all-to-all-done.refs_1_.refs_0_ = f32[32,16,128]{2,1,0:T(8,128)S(1)} async-done(((f32[32,16,128]{2,1,0:T(8,128)}), f32[32,16,128]{2,1,0:T(8,128)S(1)}, u32[]{:S(2)}, u32[]{:S(2)}) %all-to-all-start) | async-done | bytes 262176 | tf_op jit(solution)/shard_map/all_to_all | solution.py:650
  57.1 5.6 %shard_map.136 = (f32[3,12,16,256]{3,2,1,0:T(8,128)S(1)}, f32[3,8,16,256]{3,2,1,0:T(8,128)S(1)}, f32[3,8,8,256]{3,2,1,0:T(8,128)S(1)}, f32[3,8,8,256]{3,2,1,0:T(8,128)S(1)}) custom-call(s32[1]{0:T(128)} %bitcast.1.refs_0_.refs_1_, f32[32,16,128]{2,1,0:T(8,128)S(1)} %all-to-all-done.refs_1_.refs_0_, f32[16,16,256]{2,1,0:T(8,128)} %get-tuple-element.28.refs_2_.refs_1_), custom_call_target="tpu_custom_call" | custom-call | tf_op jit(solution)/shard_map/pallas_call | solution.py:600
  62.7 1.4 %collective-permute-start.6 = (f32[3,8,8,256]{3,2,1,0:T(8,128)S(1)}, f32[3,8,8,256]{3,2,1,0:T(8,128)S(1)}, u32[]{:S(2)}, u32[]{:S(2)}) collective-permute-start(f32[3,8,8,256]{3,2,1,0:T(8,128)S(1)} %get-tuple-element.34), channel_id=1, source_target_pairs={{0,1},{2,3},{1,0},{3,2},{4,5},{6,7},{5,4},{7,6},{8,9},{10,11},{9,8... | collective-permute-start | bytes 589832 | tf_op jit(solution)/shard_map/ppermute | solution.py:281
  64.1 2.7 %collective-permute-start.7 = (f32[3,8,8,256]{3,2,1,0:T(8,128)S(1)}, f32[3,8,8,256]{3,2,1,0:T(8,128)S(1)}, u32[]{:S(2)}, u32[]{:S(2)}) collective-permute-start(f32[3,8,8,256]{3,2,1,0:T(8,128)S(1)} %get-tuple-element.35), channel_id=1, source_target_pairs={{1,2},{2,1},{5,6},{6,5},{9,10},{10,9},{13,14},{14,13},{17,18},{18,... | collective-permute-start | bytes 589832 | tf_op jit(solution)/shard_map/ppermute | solution.py:281
  66.8 5.1 %shard_map.137 = (f32[3,4,16,256]{3,2,1,0:T(8,128)S(1)}, f32[3,4,16,256]{3,2,1,0:T(8,128)S(1)}, f32[3,8,16,256]{3,2,1,0:T(8,128)S(1)}) custom-call(f32[32,16,128]{2,1,0:T(8,128)S(1)} %all-to-all-done.refs_1_.refs_0_, f32[16,16,256]{2,1,0:T(8,128)} %get-tuple-element.28.refs_2_.refs_1_), custom_call_target="tpu_custom_call" | custom-call | tf_op jit(solution)/shard_map/pallas_call | solution.py:600
  71.9 0.0 collective-permute-done.6.refs_10_
  71.9 0.9 %collective-permute-done.7.refs_11_ = f32[3,8,8,256]{3,2,1,0:T(8,128)S(1)} collective-permute-done((f32[3,8,8,256]{3,2,1,0:T(8,128)S(1)}, f32[3,8,8,256]{3,2,1,0:T(8,128)S(1)}, u32[]{:S(2)}, u32[]{:S(2)}) %collective-permute-start.7) | collective-permute-done | bytes 196640 | tf_op jit(solution)/shard_map/ppermute | solution.py:281
  72.8 4.7 %shard_map.138 = (f32[3,8,16,256]{3,2,1,0:T(8,128)}, f32[3,8,16,256]{3,2,1,0:T(8,128)}) custom-call(s32[2]{0:T(128)S(1)} %pad_add_fusion.refs_0_, s32[1]{0:T(128)} %bitcast.1.refs_0_.refs_1_, f32[3,8,16,256]{3,2,1,0:T(8,128)} %get-tuple-element.23.refs_2_, f32[3,8,16,256]{3,2,1,0:T(8,128)} %get-tuple-element.24.refs_3_, ...), custom_call_target="tpu_custom_call" | custom-call | tf_op jit(solution)/shard_map/pallas_call | solution.py:600
  (2 shorter events, 0.0 us)
Async XLA Ops:
  0.6 6.4 %copy-start = (f32[256]{0:T(256)S(1)}, f32[256]{0:T(256)}, u32[]{:S(2)}) copy-start(f32[256]{0:T(256)} %param.23) | copy-start | bytes 3076
  1.9 5.1 %copy-start.7 = (s32[1024]{0:T(1024)S(1)}, s32[1024]{0:T(1024)}, u32[]{:S(2)}) copy-start(s32[1024]{0:T(1024)} %param.22) | copy-start | bytes 12292
  1.9 9.9 %collective-permute-start = (f32[5,8,8,256]{3,2,1,0:T(8,128)S(1)}, f32[5,8,8,256]{3,2,1,0:T(8,128)S(1)}, u32[]{:S(2)}, u32[]{:S(2)}) collective-permute-start(f32[5,8,8,256]{3,2,1,0:T(8,128)S(1)} %get-tuple-element.19), channel_id=1, source_target_pairs={{0,1},{2,3},{1,0},{3,2},{4,5},{6,7},{5,4},{7,6},{8,9},{10,11},{9,8... | collective-permute-start | bytes 983048 | tf_op jit(solution)/shard_map/ppermute | solution.py:281
  2.0 12.5 %collective-permute-start.1 = (f32[5,8,8,256]{3,2,1,0:T(8,128)S(1)}, f32[5,8,8,256]{3,2,1,0:T(8,128)S(1)}, u32[]{:S(2)}, u32[]{:S(2)}) collective-permute-start(f32[5,8,8,256]{3,2,1,0:T(8,128)S(1)} %get-tuple-element.20), channel_id=1, source_target_pairs={{1,2},{2,1},{5,6},{6,5},{9,10},{10,9},{13,14},{14,13},{17,18},{18,... | collective-permute-start | bytes 983048 | tf_op jit(solution)/shard_map/ppermute | solution.py:281
  7.1 0.7 copy-start.4
  7.1 0.7 copy-start.5
  7.1 0.7 copy-start.6
  7.8 10.2 %collective-permute-start.4 = (f32[8,1024]{1,0:T(8,128)S(1)}, f32[8,1024]{1,0:T(8,128)S(1)}, u32[]{:S(2)}, u32[]{:S(2)}) collective-permute-start(f32[8,1024]{1,0:T(8,128)S(1)} %pad_maximum_fusion.1.refs_0_), channel_id=1, source_target_pairs={{0,1},{2,3},{1,0},{3,2},{4,5},{6,7},{5,4},{7,6},{8,9},{10,11},{9,8... | collective-permute-start | bytes 98312 | tf_op jit(solution)/shard_map/ppermute | solution.py:612
  17.2 30.7 %collective-permute-start.2 = (f32[96,8,256]{2,1,0:T(8,128)}, f32[96,8,256]{2,1,0:T(8,128)S(1)}, u32[]{:S(2)}, u32[]{:S(2)}) collective-permute-start(f32[96,8,256]{2,1,0:T(8,128)} %get-tuple-element.21), channel_id=1, source_target_pairs={{0,4},{8,12},{16,20},{24,28},{4,0},{12,8},{20,16},{28,24},{1,5},{9... | collective-permute-start | bytes 2359304 | tf_op jit(solution)/shard_map/ppermute | solution.py:281
  17.3 2.6 %copy-start.1 = (f32[3,1024]{1,0:T(4,128)S(1)}, f32[3,1024]{1,0:T(4,128)}, u32[]{:S(2)}) copy-start(f32[3,1024]{1,0:T(4,128)} %refs_3_.7) | copy-start | bytes 36868
  17.3 30.6 %collective-permute-start.3 = (f32[96,8,256]{2,1,0:T(8,128)S(1)}, f32[96,8,256]{2,1,0:T(8,128)S(1)}, u32[]{:S(2)}, u32[]{:S(2)}) collective-permute-start(f32[96,8,256]{2,1,0:T(8,128)S(1)} %get-tuple-element.22), channel_id=1, source_target_pairs={{4,8},{12,16},{20,24},{8,4},{16,12},{24,20},{5,9},{13,17},{21,25},... | collective-permute-start | bytes 2359304 | tf_op jit(solution)/shard_map/ppermute | solution.py:281
  18.1 11.6 %collective-permute-start.5 = (f32[8,2048]{1,0:T(8,128)S(1)}, f32[8,2048]{1,0:T(8,128)S(1)}, u32[]{:S(2)}, u32[]{:S(2)}) collective-permute-start(f32[8,2048]{1,0:T(8,128)S(1)} %pad_maximum_fusion), channel_id=1, source_target_pairs={{1,2},{2,1},{0,3},{3,0},{5,6},{6,5},{4,7},{7,4},{9,10},{10,9},{8,1... | collective-permute-start | bytes 196616 | tf_op jit(solution)/shard_map/ppermute | solution.py:615
  19.9 9.8 %copy-start.3 = (s32[1024]{0:T(1024)S(1)}, s32[1024]{0:T(1024)}, u32[]{:S(2)}) copy-start(s32[1024]{0:T(1024)} %param.18) | copy-start | bytes 12292
  29.7 0.7 copy-start.2
  42.0 15.1 %all-to-all-start = ((f32[32,16,128]{2,1,0:T(8,128)}), f32[32,16,128]{2,1,0:T(8,128)S(1)}, u32[]{:S(2)}, u32[]{:S(2)}) async-start(f32[32,16,128]{2,1,0:T(8,128)} %shard_map.135), calls=%async_computation | async-start | bytes 524288 | tf_op jit(solution)/shard_map/all_to_all | solution.py:650
  62.7 9.2 %collective-permute-start.6 = (f32[3,8,8,256]{3,2,1,0:T(8,128)S(1)}, f32[3,8,8,256]{3,2,1,0:T(8,128)S(1)}, u32[]{:S(2)}, u32[]{:S(2)}) collective-permute-start(f32[3,8,8,256]{3,2,1,0:T(8,128)S(1)} %get-tuple-element.34), channel_id=1, source_target_pairs={{0,1},{2,3},{1,0},{3,2},{4,5},{6,7},{5,4},{7,6},{8,9},{10,11},{9,8... | collective-permute-start | bytes 589832 | tf_op jit(solution)/shard_map/ppermute | solution.py:281
  64.1 8.8 %collective-permute-start.7 = (f32[3,8,8,256]{3,2,1,0:T(8,128)S(1)}, f32[3,8,8,256]{3,2,1,0:T(8,128)S(1)}, u32[]{:S(2)}, u32[]{:S(2)}) collective-permute-start(f32[3,8,8,256]{3,2,1,0:T(8,128)S(1)} %get-tuple-element.35), channel_id=1, source_target_pairs={{1,2},{2,1},{5,6},{6,5},{9,10},{10,9},{13,14},{14,13},{17,18},{18,... | collective-permute-start | bytes 589832 | tf_op jit(solution)/shard_map/ppermute | solution.py:281

commit v7 on v6

--- a/solution.py
+++ b/solution.py
@@ -20,7 +20,7 @@
 SIDE_TILES = 4
 HIGH_LIST = OWN_TILES
 LOW_LIST = OWN_TILES + SIDE_TILES
-LIST_ROWS = 16
+LIST_ROWS = OWN_TILES + 2 * SIDE_TILES
 VMEM_GRANT = 16 * 2**20
 
 F32 = jnp.float32
@@ -136,15 +136,17 @@
         size = OWN_TILES * owners
         tiles = tiles + (got[0:size] + got[size : 2 * size] + got[2 * size :])
     owner_row = row_ids((owners, 2 * HALF))
+
+    def put(j, tile):
+        out_ref[:, 0, 2 * HALF * j : 2 * HALF * (j + 1)] = tile
+
     for j in range(OWN_TILES):
         tile = tiles[j * owners : (j + 1) * owners]
-        out_ref[:, j, :] = tile
+        put(j, tile)
         if j < SIDE_TILES:
             above = pltpu.roll(tile, owners - step, 0)
-            out_ref[:, HIGH_LIST + j, :] = jnp.where(owner_row < owners - step, above, 0.0)
-            out_ref[:, LOW_LIST + j, :] = jnp.where(owner_row >= step, pltpu.roll(tile, step, 0), 0.0)
-    for j in range(LOW_LIST + SIDE_TILES, LIST_ROWS):
-        out_ref[:, j, :] = jnp.zeros((owners, 2 * HALF), F32)
+            put(HIGH_LIST + j, jnp.where(owner_row < owners - step, above, 0.0))
+            put(LOW_LIST + j, jnp.where(owner_row >= step, pltpu.roll(tile, step, 0), 0.0))
 
 
 TILE = 8
@@ -157,19 +159,30 @@
     return pltpu.roll(tile, TILE // 2, 0)
 
 
-def scatter_lists(val_ref, jobs, cy, nz):
-    sources, _, lanes = val_ref.shape
+ROWS_HELD = 16
+
+
+def scatter_lists(val_ref, even_ref, odd_ref, jobs, cy, nz):
+    lanes = 2 * HALF
+    sources = val_ref.shape[0]
+    groups = sources // 2
     chunk = 2 * lanes
-    left_half = lax.broadcasted_iota(jnp.int32, (LIST_ROWS, lanes), 1) < lanes // 2
+    left_half = lax.broadcasted_iota(jnp.int32, (groups, lanes), 1) < lanes // 2
     for ref in {id(job[4]): job[4] for job in jobs}.values():
         ref[...] = jnp.zeros(ref.shape, F32)
+    for j in range(LIST_ROWS):
+        rows = val_ref[:, 0, lanes * j : lanes * (j + 1)]
+        first, second = rows[0:groups], rows[groups:]
+        at = pl.ds(j, groups, stride=ROWS_HELD)
+        even_ref[at, :] = jnp.where(left_half, first, pltpu.roll(second, lanes // 2, 1))
+        odd_ref[at, :] = jnp.where(left_half, pltpu.roll(first, lanes // 2, 1), second)
 
     def body(step, carry):
         evens, odds = [], []
         for pair in range(2):
-            first, second = val_ref[4 * step + 2 * pair], val_ref[4 * step + 2 * pair + 1]
-            evens.append(jnp.where(left_half, first, pltpu.roll(second, lanes // 2, 1)))
-            odds.append(jnp.where(left_half, pltpu.roll(first, lanes // 2, 1), second))
+            at = pl.ds(pl.multiple_of((2 * step + pair) * ROWS_HELD, ROWS_HELD), ROWS_HELD)
+            evens.append(even_ref[at, :])
+            odds.append(odd_ref[at, :])
         values = [jnp.concatenate(evens, axis=1), jnp.concatenate(odds, axis=1)]
         high = [v.astype(BF16) for v in values]
         low = [(v - h.astype(F32)).astype(BF16) for v, h in zip(values, high)]
@@ -196,13 +209,15 @@
                     at += 2 * size
         return carry
 
-    lax.fori_loop(0, sources // 4, body, 0)
+    lax.fori_loop(0, groups // 2, body, 0)
 
 
 STEP_ROWS = ((0, 1, 2), (3, 4, 5), (7, 8, 9))
 
 
-def near_scatter_kernel(par_ref, val_ref, sign_ref, zero_out, one_out, even_out, odd_out, zero_ref, one_ref):
+def near_scatter_kernel(
+    ready, par_ref, val_ref, sign_ref, zero_out, one_out, even_out, odd_out, zero_ref, one_ref, even_ref, odd_ref
+):
     _, cx, cy, nz = one_out.shape
     jobs = (
         (0, STEP_ROWS[0], 0, cx, zero_ref, NEAR * cy),
@@ -210,7 +225,8 @@
         (HIGH_LIST, STEP_ROWS[0], 0, NEAR, zero_ref, (NEAR + cx) * cy),
         (LOW_LIST, STEP_ROWS[0], cx - NEAR, NEAR, zero_ref, 0),
     )
-    scatter_lists(val_ref, jobs, cy, nz)
+    scatter_lists(val_ref, even_ref, odd_ref, jobs, cy, nz)
+    ready()
     sign = sign_ref[...]
     for i in range(3):
         zero_out[i] = zero_ref[i].reshape(zero_out.shape[1:]) * sign[MID - NEAR : MID + cx + NEAR]
@@ -232,7 +248,9 @@
     write_faces(par_ref[0], write, even_out, odd_out)
 
 
-def rest_scatter_kernel(val_ref, sign_ref, zero_out, one_out, two_out, zero_ref, one_ref, two_ref):
+def rest_scatter_kernel(
+    ready, val_ref, sign_ref, zero_out, one_out, two_out, zero_ref, one_ref, two_ref, even_ref, odd_ref
+):
     _, cx, cy, nz = two_out.shape
     jobs = (
         (0, STEP_ROWS[2], 0, cx, two_ref, 0),
@@ -241,7 +259,8 @@
         (HIGH_LIST, STEP_ROWS[1], 0, NEAR, one_ref, NEAR * cy),
         (LOW_LIST, STEP_ROWS[1], cx - NEAR, NEAR, one_ref, 0),
     )
-    scatter_lists(val_ref, jobs, cy, nz)
+    scatter_lists(val_ref, even_ref, odd_ref, jobs, cy, nz)
+    ready()
     sign = sign_ref[...]
     last = cx + 2 * MID
     far = jnp.concatenate([sign[0 : MID - NEAR], sign[last - (MID - NEAR) :]], axis=0)
@@ -282,7 +301,20 @@
     return out
 
 
-def field_face_kernel(par_ref, cur_ref, ear_ref, coef_ref, even_out, odd_out):
+def prepare_kernel(
+    ready, par_ref, cur_ref, ear_ref, coef_ref, wave_ref, freq_ref, amp_ref, index_ref, table_ref,
+    block_out, even_out, odd_out,
+):
+    entries = table_ref.shape[1]
+    comps = index_ref.shape[1]
+    picked = (row_ids((entries, comps)) == index_ref[...]).astype(F32).astype(BF16)
+    terms = jnp.concatenate(list(split_three(jnp.broadcast_to(table_ref[...], (TILE, entries)))), axis=0).astype(BF16)
+    phase = jnp.dot(terms, picked, preferred_element_type=F32)
+    block_out[0:3, :] = wave_ref[...]
+    block_out[3:4, :] = freq_ref[...]
+    block_out[4:7, :] = amp_ref[...]
+    block_out[7:8, :] = phase[0:1] + phase[TILE : TILE + 1] + phase[2 * TILE : 2 * TILE + 1]
+    ready()
     _, cx, cy, nz = cur_ref.shape
     upper = row_ids((TILE, nz)) >= TILE // 2
 
@@ -351,8 +383,9 @@
     return (mask == 1).astype(F32) - (mask == 2).astype(F32)
 
 
-def field_side_kernel(px_ref, py_ref, cur_ref, ear_ref, coef_ref, mask_ref, *refs):
+def field_side_kernel(ready, px_ref, py_ref, cur_ref, ear_ref, coef_ref, mask_ref, *refs):
     _, cx, cy, nz = cur_ref.shape
+    ready()
 
     def own_tile(name, x, ys):
         if name < 3:
@@ -397,7 +430,7 @@
 
 
 def first_wave_kernel(
-    px_ref, py_ref, cur_ref, ear_ref, coef_ref, mask_ref, ye_ref, yo_ref, xe_ref, xo_ref,
+    ready, px_ref, py_ref, cur_ref, ear_ref, coef_ref, mask_ref, ye_ref, yo_ref, xe_ref, xo_ref,
     final_ref, prior_ref, wide_coef_ref, wide_sign_ref, u_ref, e_ref, c_ref, one_ref, two_ref,
 ):
     _, cx, cy, _ = cur_ref.shape
@@ -405,6 +438,7 @@
     lower, higher = slice(0, TILE), slice(TILE + cy, 2 * TILE + cy)
     low = select_side(py_ref[0], ye_ref, yo_ref, False)
     high = select_side(py_ref[0], ye_ref, yo_ref, True)
+    ready()
 
     def put(name, x, rows, value):
         if name < 3:
@@ -479,7 +513,7 @@
 
 
 def last_wave_kernel(
-    px_ref, py_ref, free_final_ref, free_prior_ref, coef_ref, zero_in, zero_far_in, one_in, one_side_in, two_in,
+    ready, px_ref, py_ref, free_final_ref, free_prior_ref, coef_ref, zero_in, zero_far_in, one_in, one_side_in, two_in,
     ye_ref, yo_ref, final_ref, prior_ref, one_ref, two_ref,
 ):
     _, cx, cy, _ = two_in.shape
@@ -523,6 +557,7 @@
                 final_ref[i, x, :, lanes] = free_final_ref[i, x, :, lanes] + (moved + two_in[i, x, :, lanes])
                 prior_ref[i, x, :, lanes] = free_prior_ref[i, x, :, lanes] + c
 
+    ready()
     run_planes(0, NEAR, second(TILE, cy))
     run_planes(NEAR, cx + NEAR, second(px_ref[1], cy + TILE))
     run_planes(cx + NEAR, cx + 2 * NEAR, second(TILE, cy))
@@ -539,9 +574,12 @@
             ins[at] = stage
         for copy in copies:
             copy.start()
-        for copy in copies:
-            copy.wait()
-        kernel(*ins, *refs[operand_count:])
+
+        def ready():
+            for copy in copies:
+                copy.wait()
+
+        kernel(ready, *ins, *refs[operand_count:])
 
     return run
 
@@ -560,14 +598,6 @@
     phase_index,
     phase_table,
 ):
-    table_size = phase_table.shape[0]
-    matches = (phase_index[None, :] == jnp.arange(table_size)[:, None]).astype(F32)
-    phases = jnp.dot(
-        phase_table[None, :], matches, precision=lax.Precision.HIGHEST, preferred_element_type=F32
-    )[0]
-    own_block = jnp.concatenate(
-        [wave_vector, frequency[None, :], amplitude, phases[None, :]], axis=0
-    )
     point_count = point_xyz.shape[1]
     slab_count = lax.axis_size("slab")
     comp_count = lax.axis_size("comp")
@@ -608,6 +638,18 @@
 
     px = jnp.stack([lax.axis_index("slab") % 2, TILE // 2]).astype(jnp.int32)
     py = (lax.axis_index("comp") % 2).astype(jnp.int32).reshape(1)
+    fields = (current_field, earlier_field, wave_coef)
+    local_comps = frequency.shape[0]
+    own_block, *faces = call(
+        prepare_kernel,
+        (
+            py, *fields, wave_vector, frequency.reshape(1, local_comps), amplitude,
+            phase_index.reshape(1, local_comps), phase_table.reshape(1, -1),
+        ),
+        [(8, local_comps)] + [(5, cx, TILE, nz)] * 2,
+        scalars=1,
+        from_hbm=(1, 2, 3),
+    )
     if comp_count == 4:
         near_block = lax.ppermute(own_block, "comp", pair_list(4, 0))
         first_blocks = [own_block, near_block]
@@ -620,8 +662,6 @@
             lax.ppermute(own_block, "comp", [(i, (i + k) % comp_count) for i in range(comp_count)])
             for k in range(1, comp_count)
         ]
-    fields = (current_field, earlier_field, wave_coef)
-    faces = call(field_face_kernel, (py, *fields), [(5, cx, TILE, nz)] * 2, scalars=1, from_hbm=(1, 2, 3))
     ye, yo = swap_faces(faces, "comp")
     (sum_one, total_one) = call(
         lambda *refs: first_incident_kernel(len(first_blocks), *refs),
@@ -644,7 +684,7 @@
             *last_blocks, sum_one, total_one, point_xyz,
             point_owner.reshape(1, point_count), cell_offset.reshape(1, point_count),
         ),
-        [(device_count, LIST_ROWS, 2 * HALF)],
+        [(device_count, 1, LIST_ROWS * 2 * HALF)],
         [(8, point_count), (32, point_count)],
     )
     arrived = lax.all_to_all(packed, ("slab", "comp"), split_axis=0, concat_axis=0, tiled=True)
@@ -660,11 +700,12 @@
         from_hbm=(2, 3, 4, 5),
         to_hbm=True,
     )
+    held = (device_count // 2 * ROWS_HELD, 2 * HALF)
     zero, one, face_even, face_odd = call(
         near_scatter_kernel,
         (py, arrived, wide_sign),
         [(3, cx + 2 * NEAR, cy, nz), (3, cx, cy, nz)] + [(3, cx, TILE, nz)] * 2,
-        [(3, (cx + 2 * NEAR) * cy, nz), (3, cx * cy, nz)],
+        [(3, (cx + 2 * NEAR) * cy, nz), (3, cx * cy, nz), held, held],
         scalars=1,
         from_hbm=(2,),
     )
@@ -673,7 +714,7 @@
         rest_scatter_kernel,
         (arrived, wide_sign),
         [(3, 2 * NEAR, cy, nz), (3, 2 * NEAR, cy, nz), (3, cx, cy, nz)],
-        [(3, 2 * NEAR * cy, nz), (3, 2 * NEAR * cy, nz), (3, cx * cy, nz)],
+        [(3, 2 * NEAR * cy, nz), (3, 2 * NEAR * cy, nz), (3, cx * cy, nz), held, held],
         from_hbm=(1,),
     )
     final, prior = call(

time: 78.1 us -> 81.4 us (1.042)
  waiting for transfers between devices: 9.89 us -> 14.4 us
  Pallas kernels: 47.4 us -> 44.5 us
  local copies, waits for them, and re-layouts: 0.98 us -> 2.77 us
    ppermute x1, waiting for transfers between devices: 0.01 us -> 3.9 us  [local(): near_block = lax.ppermute(own_block, 'comp', pair_list(4, 0))]
    pallas_call x8, Pallas kernels: 47.4 us -> 44.5 us  [call(): pl.pallas_call(kernel, out_shape=shapes, in_specs=in_specs, out_specs=[vm...]
    ppermute x6, waiting for transfers between devices: 7.38 us -> 9.42 us  [swap_faces(): out.append(lax.ppermute(faces[k], axis, pair_list(count, k)))]
    unnamed x16, local copies, waits for them, and re-layouts: 0.98 us -> 2.77 us
    all_to_all x1, waiting for transfers between devices: 2.51 us -> 1.05 us  [local(): lax.all_to_all(packed, ('slab', 'comp'), split_axis=0, concat_axis=0, til...]
  transfers between devices with their start and end apart: 9 -> 9, of which waited for: 4 -> 5; matrix products, arithmetic and copies ran while one was open for 1% -> 0% of each run, Pallas kernels for 46% -> 39%
where the time goes in v7:
time: 81.4 us; the launch traced here: 81 us
  Pallas kernels  44.5 us (55%)
  starting transfers between devices  18.4 us (23%)
  waiting for transfers between devices  14.4 us (18%)
  local copies, waits for them, and re-layouts  2.77 us (3%)
  between operations  0.83 us (1%)
    pallas_call x8, Pallas kernels, call(): pl.pallas_call(kernel, out_shape=shapes, in_specs=in_specs, out_specs=[vm...  44.5 us
    ppermute x6, starting transfers between devices, swap_faces(): out.append(lax.ppermute(faces[k], axis, pair_list(count, k)))  10.6 us
    ppermute x6, waiting for transfers between devices, swap_faces(): out.append(lax.ppermute(faces[k], axis, pair_list(count, k)))  9.42 us
    all_to_all x1, starting transfers between devices, local(): lax.all_to_all(packed, ('slab', 'comp'), split_axis=0, concat_axis=0, til...  5.98 us
    ppermute x1, waiting for transfers between devices, local(): near_block = lax.ppermute(own_block, 'comp', pair_list(4, 0))  3.9 us
    unnamed x16, local copies, waits for them, and re-layouts  2.77 us
    ppermute x1, starting transfers between devices, local(): lax.ppermute(jnp.concatenate(first_blocks, axis=1), 'comp', ring)  1.73 us
  transfers between devices with their start and end apart: 9, of which 5 were waited for; matrix products, arithmetic and copies ran while one was open for 0% of the time, Pallas kernels for 39%

profile of v7, /device:TPU:8, one launch (start us, length us, event | category | flops | bytes accessed | tf_op | source)
XLA Modules:
  0.0 81.0 jit_solution(17011605687102831879)
XLA Ops:
  0.6 0.0 copy-start.7
  0.6 0.0 copy-start.1
  0.7 0.0 copy-start.2
  0.7 0.6 copy-done.7
  1.3 0.1 copy-done.1
  1.4 0.0 copy-done.2
  1.4 0.0 copy-start.3
  1.4 0.7 copy-done.3
  2.1 0.0 copy-start.4
  2.1 0.7 copy-done.4
  2.8 1.3 %shard_map.131 = (f32[8,1024]{1,0:T(8,128)S(1)}, f32[5,8,8,256]{3,2,1,0:T(8,128)S(1)}, f32[5,8,8,256]{3,2,1,0:T(8,128)S(1)}) custom-call(s32[1]{0:T(128)} %bitcast.1.refs_0_.refs_1_, f32[3,8,16,256]{3,2,1,0:T(8,128)} %refs_2_.6, f32[3,8,16,256]{3,2,1,0:T(8,128)} %refs_3_.6, f32[8,16,256]{2,1,0:T(8,128)} %refs_4_.5, f32[3,1024]{1,0:T(4,128)S(1)} %copy-done.1, ...), custom_call_target="tpu_custom_call" | custom-call | tf_op jit(solution)/shard_map/pallas_call | solution.py:630
  4.0 0.1 collective-permute-start
  4.1 5.0 %collective-permute-start.1 = (f32[5,8,8,256]{3,2,1,0:T(8,128)S(1)}, f32[5,8,8,256]{3,2,1,0:T(8,128)S(1)}, u32[]{:S(2)}, u32[]{:S(2)}) collective-permute-start(f32[5,8,8,256]{3,2,1,0:T(8,128)S(1)} %get-tuple-element.21), channel_id=1, source_target_pairs={{1,2},{2,1},{5,6},{6,5},{9,10},{10,9},{13,14},{14,13},{17,18},{18,... | collective-permute-start | bytes 983048 | tf_op jit(solution)/shard_map/ppermute | solution.py:300
  9.2 0.1 pad_add_fusion.refs_0_
  9.2 4.3 %collective-permute-done.refs_6_ = f32[5,8,8,256]{3,2,1,0:T(8,128)S(1)} collective-permute-done((f32[5,8,8,256]{3,2,1,0:T(8,128)S(1)}, f32[5,8,8,256]{3,2,1,0:T(8,128)S(1)}, u32[]{:S(2)}, u32[]{:S(2)}) %collective-permute-start) | collective-permute-done | bytes 327712 | tf_op jit(solution)/shard_map/ppermute | solution.py:300
  13.5 3.0 %collective-permute-done.1.refs_7_ = f32[5,8,8,256]{3,2,1,0:T(8,128)S(1)} collective-permute-done((f32[5,8,8,256]{3,2,1,0:T(8,128)S(1)}, f32[5,8,8,256]{3,2,1,0:T(8,128)S(1)}, u32[]{:S(2)}, u32[]{:S(2)}) %collective-permute-start.1) | collective-permute-done | bytes 327712 | tf_op jit(solution)/shard_map/ppermute | solution.py:300
  16.6 2.8 %shard_map.132 = (f32[96,8,256]{2,1,0:T(8,128)}, f32[96,8,256]{2,1,0:T(8,128)S(1)}) custom-call(s32[2]{0:T(128)S(1)} %pad_add_fusion.refs_0_, s32[1]{0:T(128)} %bitcast.1.refs_0_.refs_1_, f32[3,8,16,256]{3,2,1,0:T(8,128)} %refs_2_.6, f32[3,8,16,256]{3,2,1,0:T(8,128)} %refs_3_.6, f32[8,16,256]{2,1,0:T(8,128)} %refs_4_.5, s32[8,16,256]{2,1,0:T(8,128)} %refs_5_.3, ...), custom_call_target="tpu_custom_call" | custom-call | tf_op jit(solution)/shard_map/pallas_call | solution.py:630
  19.3 0.1 collective-permute-start.2
  19.4 0.7 collective-permute-start.3
  20.1 0.0 copy-start
  20.1 0.1 collective-permute-start.4
  20.2 3.9 %collective-permute-done.4.refs_1_ = f32[8,1024]{1,0:T(8,128)S(1)} collective-permute-done((f32[8,1024]{1,0:T(8,128)S(1)}, f32[8,1024]{1,0:T(8,128)S(1)}, u32[]{:S(2)}, u32[]{:S(2)}) %collective-permute-start.4) | collective-permute-done | bytes 32800 | tf_op jit(solution)/shard_map/ppermute | solution.py:654
  24.1 1.7 %collective-permute-start.5 = (f32[8,2048]{1,0:T(8,128)S(1)}, f32[8,2048]{1,0:T(8,128)S(1)}, u32[]{:S(2)}, u32[]{:S(2)}) collective-permute-start(f32[8,2048]{1,0:T(8,128)S(1)} %pad_maximum_fusion), channel_id=1, source_target_pairs={{1,2},{2,1},{0,3},{3,0},{5,6},{6,5},{4,7},{7,4},{9,10},{10,9},{8,1... | collective-permute-start | bytes 196616 | tf_op jit(solution)/shard_map/ppermute | solution.py:657
  25.9 0.0 copy-done
  25.9 0.0 copy-start.6
  25.9 9.8 %shard_map.134 = (f32[32,1024]{1,0:T(8,128)S(1)}, f32[16,256]{1,0:T(8,128)S(1)}) custom-call(f32[8,1024]{1,0:T(8,128)S(1)} %get-tuple-element.27.refs_0_, f32[8,1024]{1,0:T(8,128)S(1)} %collective-permute-done.4.refs_1_, f32[3,1024]{1,0:T(4,128)S(1)} %copy-done), custom_call_target="tpu_custom_call" | custom-call | tf_op jit(solution)/shard_map/pallas_call | solution.py:630
  35.7 0.0 copy-start.5
  35.7 0.0 collective-permute-done.5.refs_0_
  35.7 0.0 copy-done.6
  35.7 0.7 copy-done.5
  36.4 11.5 %shard_map.135 = f32[32,1,1664]{2,1,0:T(1,128)} custom-call(f32[8,2048]{1,0:T(8,128)S(1)} %collective-permute-done.5.refs_0_, f32[32,1024]{1,0:T(8,128)S(1)} %get-tuple-element.28.refs_1_, f32[16,256]{1,0:T(8,128)S(1)} %get-tuple-element.29.refs_2_, f32[3,1024]{1,0:T(4,128)S(1)} %copy-done, s32[1,1024]{1,0:T(1,128)S(1)} %bitcast.9, s32[1,1024]{1,0:T(1,128)S(1)} %bitcast.10), custom_call_target="tpu_custom_call" | custom-call | tf_op jit(solution)/shard_map/pallas_call | solution.py:630
  47.9 6.0 %all-to-all-start = ((f32[32,1,1664]{2,1,0:T(1,128)}), f32[32,1,1664]{2,1,0:T(1,128)S(1)}, u32[]{:S(2)}, u32[]{:S(2)}) async-start(f32[32,1,1664]{2,1,0:T(1,128)} %shard_map.135), calls=%async_computation | async-start | bytes 425984 | tf_op jit(solution)/shard_map/all_to_all | solution.py:690
  53.9 0.0 collective-permute-done.2.refs_8_
  53.9 0.0 collective-permute-done.3.refs_9_
  53.9 6.6 %shard_map.133 = (f32[3,8,16,256]{3,2,1,0:T(8,128)}, f32[3,8,16,256]{3,2,1,0:T(8,128)}, f32[12,2,32,128]{3,2,1,0:T(8,128)}, f32[16,16,256]{2,1,0:T(8,128)}) custom-call(s32[2]{0:T(128)S(1)} %pad_add_fusion.refs_0_, s32[1]{0:T(128)} %bitcast.1.refs_0_.refs_1_, f32[3,8,16,256]{3,2,1,0:T(8,128)} %refs_2_.6, f32[3,8,16,256]{3,2,1,0:T(8,128)} %refs_3_.6, ...), custom_call_target="tpu_custom_call" | custom-call | tf_op jit(solution)/shard_map/pallas_call | solution.py:630
  60.5 1.0 %all-to-all-done.refs_1_.refs_0_ = f32[32,1,1664]{2,1,0:T(1,128)S(1)} async-done(((f32[32,1,1664]{2,1,0:T(1,128)}), f32[32,1,1664]{2,1,0:T(1,128)S(1)}, u32[]{:S(2)}, u32[]{:S(2)}) %all-to-all-start) | async-done | bytes 213024 | tf_op jit(solution)/shard_map/all_to_all | solution.py:690
  61.6 4.2 %shard_map.136 = (f32[3,12,16,256]{3,2,1,0:T(8,128)S(1)}, f32[3,8,16,256]{3,2,1,0:T(8,128)S(1)}, f32[3,8,8,256]{3,2,1,0:T(8,128)S(1)}, f32[3,8,8,256]{3,2,1,0:T(8,128)S(1)}) custom-call(s32[1]{0:T(128)} %bitcast.1.refs_0_.refs_1_, f32[32,1,1664]{2,1,0:T(1,128)S(1)} %all-to-all-done.refs_1_.refs_0_, f32[16,16,256]{2,1,0:T(8,128)} %get-tuple-element.30.refs_2_.refs_1_), custom_call_target="tpu_custom_call" | custom-call | tf_op jit(solution)/shard_map/pallas_call | solution.py:630
  65.8 2.2 %collective-permute-start.6 = (f32[3,8,8,256]{3,2,1,0:T(8,128)S(1)}, f32[3,8,8,256]{3,2,1,0:T(8,128)S(1)}, u32[]{:S(2)}, u32[]{:S(2)}) collective-permute-start(f32[3,8,8,256]{3,2,1,0:T(8,128)S(1)} %get-tuple-element.36), channel_id=1, source_target_pairs={{0,1},{2,3},{1,0},{3,2},{4,5},{6,7},{5,4},{7,6},{8,9},{10,11},{9,8... | collective-permute-start | bytes 589832 | tf_op jit(solution)/shard_map/ppermute | solution.py:300
  68.0 2.5 %collective-permute-start.7 = (f32[3,8,8,256]{3,2,1,0:T(8,128)S(1)}, f32[3,8,8,256]{3,2,1,0:T(8,128)S(1)}, u32[]{:S(2)}, u32[]{:S(2)}) collective-permute-start(f32[3,8,8,256]{3,2,1,0:T(8,128)S(1)} %get-tuple-element.37), channel_id=1, source_target_pairs={{1,2},{2,1},{5,6},{6,5},{9,10},{10,9},{13,14},{14,13},{17,18},{18,... | collective-permute-start | bytes 589832 | tf_op jit(solution)/shard_map/ppermute | solution.py:300
  70.5 3.8 %shard_map.137 = (f32[3,4,16,256]{3,2,1,0:T(8,128)S(1)}, f32[3,4,16,256]{3,2,1,0:T(8,128)S(1)}, f32[3,8,16,256]{3,2,1,0:T(8,128)S(1)}) custom-call(f32[32,1,1664]{2,1,0:T(1,128)S(1)} %all-to-all-done.refs_1_.refs_0_, f32[16,16,256]{2,1,0:T(8,128)} %get-tuple-element.30.refs_2_.refs_1_), custom_call_target="tpu_custom_call" | custom-call | tf_op jit(solution)/shard_map/pallas_call | solution.py:630
  74.3 0.0 collective-permute-done.6.refs_10_
  74.3 2.1 %collective-permute-done.7.refs_11_ = f32[3,8,8,256]{3,2,1,0:T(8,128)S(1)} collective-permute-done((f32[3,8,8,256]{3,2,1,0:T(8,128)S(1)}, f32[3,8,8,256]{3,2,1,0:T(8,128)S(1)}, u32[]{:S(2)}, u32[]{:S(2)}) %collective-permute-start.7) | collective-permute-done | bytes 196640 | tf_op jit(solution)/shard_map/ppermute | solution.py:300
  76.4 4.6 %shard_map.138 = (f32[3,8,16,256]{3,2,1,0:T(8,128)}, f32[3,8,16,256]{3,2,1,0:T(8,128)}) custom-call(s32[2]{0:T(128)S(1)} %pad_add_fusion.refs_0_, s32[1]{0:T(128)} %bitcast.1.refs_0_.refs_1_, f32[3,8,16,256]{3,2,1,0:T(8,128)} %get-tuple-element.24.refs_2_, f32[3,8,16,256]{3,2,1,0:T(8,128)} %get-tuple-element.25.refs_3_, ...), custom_call_target="tpu_custom_call" | custom-call | tf_op jit(solution)/shard_map/pallas_call | solution.py:630
  (1 shorter events, 0.0 us)
Async XLA Ops:
  0.6 0.7 copy-start.7
  0.6 0.7 copy-start.1
  0.7 0.7 copy-start.2
  1.4 0.7 copy-start.3
  2.1 0.7 copy-start.4
  4.0 9.5 %collective-permute-start = (f32[5,8,8,256]{3,2,1,0:T(8,128)S(1)}, f32[5,8,8,256]{3,2,1,0:T(8,128)S(1)}, u32[]{:S(2)}, u32[]{:S(2)}) collective-permute-start(f32[5,8,8,256]{3,2,1,0:T(8,128)S(1)} %get-tuple-element.20), channel_id=1, source_target_pairs={{0,1},{2,3},{1,0},{3,2},{4,5},{6,7},{5,4},{7,6},{8,9},{10,11},{9,8... | collective-permute-start | bytes 983048 | tf_op jit(solution)/shard_map/ppermute | solution.py:300
  4.1 12.5 %collective-permute-start.1 = (f32[5,8,8,256]{3,2,1,0:T(8,128)S(1)}, f32[5,8,8,256]{3,2,1,0:T(8,128)S(1)}, u32[]{:S(2)}, u32[]{:S(2)}) collective-permute-start(f32[5,8,8,256]{3,2,1,0:T(8,128)S(1)} %get-tuple-element.21), channel_id=1, source_target_pairs={{1,2},{2,1},{5,6},{6,5},{9,10},{10,9},{13,14},{14,13},{17,18},{18,... | collective-permute-start | bytes 983048 | tf_op jit(solution)/shard_map/ppermute | solution.py:300
  19.3 34.6 %collective-permute-start.2 = (f32[96,8,256]{2,1,0:T(8,128)}, f32[96,8,256]{2,1,0:T(8,128)S(1)}, u32[]{:S(2)}, u32[]{:S(2)}) collective-permute-start(f32[96,8,256]{2,1,0:T(8,128)} %get-tuple-element.22), channel_id=1, source_target_pairs={{0,4},{8,12},{16,20},{24,28},{4,0},{12,8},{20,16},{28,24},{1,5},{9... | collective-permute-start | bytes 2359304 | tf_op jit(solution)/shard_map/ppermute | solution.py:300
  19.4 34.5 %collective-permute-start.3 = (f32[96,8,256]{2,1,0:T(8,128)S(1)}, f32[96,8,256]{2,1,0:T(8,128)S(1)}, u32[]{:S(2)}, u32[]{:S(2)}) collective-permute-start(f32[96,8,256]{2,1,0:T(8,128)S(1)} %get-tuple-element.23), channel_id=1, source_target_pairs={{4,8},{12,16},{20,24},{8,4},{16,12},{24,20},{5,9},{13,17},{21,25},... | collective-permute-start | bytes 2359304 | tf_op jit(solution)/shard_map/ppermute | solution.py:300
  20.1 5.7 %copy-start = (f32[3,1024]{1,0:T(4,128)S(1)}, f32[3,1024]{1,0:T(4,128)}, u32[]{:S(2)}) copy-start(f32[3,1024]{1,0:T(4,128)} %refs_3_.7) | copy-start | bytes 36868
  20.1 4.0 %collective-permute-start.4 = (f32[8,1024]{1,0:T(8,128)S(1)}, f32[8,1024]{1,0:T(8,128)S(1)}, u32[]{:S(2)}, u32[]{:S(2)}) collective-permute-start(f32[8,1024]{1,0:T(8,128)S(1)} %get-tuple-element.27.refs_0_), channel_id=1, source_target_pairs={{0,1},{2,3},{1,0},{3,2},{4,5},{6,7},{5,4},{7,6},{8,9},{10,11},{9,8... | collective-permute-start | bytes 98312 | tf_op jit(solution)/shard_map/ppermute | solution.py:654
  24.1 11.6 %collective-permute-start.5 = (f32[8,2048]{1,0:T(8,128)S(1)}, f32[8,2048]{1,0:T(8,128)S(1)}, u32[]{:S(2)}, u32[]{:S(2)}) collective-permute-start(f32[8,2048]{1,0:T(8,128)S(1)} %pad_maximum_fusion), channel_id=1, source_target_pairs={{1,2},{2,1},{0,3},{3,0},{5,6},{6,5},{4,7},{7,4},{9,10},{10,9},{8,1... | collective-permute-start | bytes 196616 | tf_op jit(solution)/shard_map/ppermute | solution.py:657
  25.9 9.8 %copy-start.6 = (s32[1024]{0:T(1024)S(1)}, s32[1024]{0:T(1024)}, u32[]{:S(2)}) copy-start(s32[1024]{0:T(1024)} %param.18) | copy-start | bytes 12292
  35.7 0.7 copy-start.5
  47.9 13.7 %all-to-all-start = ((f32[32,1,1664]{2,1,0:T(1,128)}), f32[32,1,1664]{2,1,0:T(1,128)S(1)}, u32[]{:S(2)}, u32[]{:S(2)}) async-start(f32[32,1,1664]{2,1,0:T(1,128)} %shard_map.135), calls=%async_computation | async-start | bytes 425984 | tf_op jit(solution)/shard_map/all_to_all | solution.py:690
  65.8 8.5 %collective-permute-start.6 = (f32[3,8,8,256]{3,2,1,0:T(8,128)S(1)}, f32[3,8,8,256]{3,2,1,0:T(8,128)S(1)}, u32[]{:S(2)}, u32[]{:S(2)}) collective-permute-start(f32[3,8,8,256]{3,2,1,0:T(8,128)S(1)} %get-tuple-element.36), channel_id=1, source_target_pairs={{0,1},{2,3},{1,0},{3,2},{4,5},{6,7},{5,4},{7,6},{8,9},{10,11},{9,8... | collective-permute-start | bytes 589832 | tf_op jit(solution)/shard_map/ppermute | solution.py:300
  68.0 8.4 %collective-permute-start.7 = (f32[3,8,8,256]{3,2,1,0:T(8,128)S(1)}, f32[3,8,8,256]{3,2,1,0:T(8,128)S(1)}, u32[]{:S(2)}, u32[]{:S(2)}) collective-permute-start(f32[3,8,8,256]{3,2,1,0:T(8,128)S(1)} %get-tuple-element.37), channel_id=1, source_target_pairs={{1,2},{2,1},{5,6},{6,5},{9,10},{10,9},{13,14},{14,13},{17,18},{18,... | collective-permute-start | bytes 589832 | tf_op jit(solution)/shard_map/ppermute | solution.py:300

commit v8 on v7

--- a/solution.py
+++ b/solution.py
@@ -104,13 +104,15 @@
     return total
 
 
-def first_incident_kernel(count, *refs):
+def first_incident_kernel(count, ready, *refs):
+    ready()
     par_refs, (xyz_ref, acc_ref, total_ref, x8_ref) = refs[:count], refs[count:]
     acc_ref[...] = jnp.zeros(acc_ref.shape, F32)
     total_ref[...] = add_components(par_refs, xyz_ref, x8_ref, acc_ref)
 
 
-def last_incident_kernel(count, step, *refs):
+def last_incident_kernel(count, step, ready, *refs):
+    ready()
     par_refs, refs = refs[:count], refs[count:]
     first_ref, first_total_ref, xyz_ref, own_ref, off_ref, out_ref, x8_ref, acc_ref = refs
     points = xyz_ref.shape[1]
@@ -305,6 +307,7 @@
     ready, par_ref, cur_ref, ear_ref, coef_ref, wave_ref, freq_ref, amp_ref, index_ref, table_ref,
     block_out, even_out, odd_out,
 ):
+    ready()
     entries = table_ref.shape[1]
     comps = index_ref.shape[1]
     picked = (row_ids((entries, comps)) == index_ref[...]).astype(F32).astype(BF16)
@@ -314,7 +317,6 @@
     block_out[3:4, :] = freq_ref[...]
     block_out[4:7, :] = amp_ref[...]
     block_out[7:8, :] = phase[0:1] + phase[TILE : TILE + 1] + phase[2 * TILE : 2 * TILE + 1]
-    ready()
     _, cx, cy, nz = cur_ref.shape
     upper = row_ids((TILE, nz)) >= TILE // 2
 
@@ -347,54 +349,90 @@
 
 
 FIELD_PLAN = [(DEEP, MID)] * 3 + [(MID, NEAR)] * 4 + [(MID, 0)]
-
-
-def plan_tiles(plan, cy):
-    out = []
-    for name, (planes, corners) in enumerate(plan):
-        for dist in range(1, planes + 1):
-            for part in list(range(cy // TILE)) + ([-1] if dist <= corners else []):
-                out.append((name, dist, part, len(out)))
-    return out
-
-
-def side_kernel(plan, own_tile, halo_tile, cx, cy, nz, px_ref, py_ref, even_ref, odd_ref, even_out, odd_out):
+SIDE_PLANES = sum(planes for planes, _ in FIELD_PLAN)
+CORNERS = [(name, dist) for name, (_, corners) in enumerate(FIELD_PLAN) for dist in range(1, corners + 1)]
+
+
+def side_plane(name, dist, is_high):
+    planes = FIELD_PLAN[name][0]
+    first = sum(n for n, _ in FIELD_PLAN[:name])
+    return first + (dist - 1 if is_high else planes - dist)
+
+
+def corner_place(k, cy):
+    per_plane = cy // TILE
+    start = k % per_plane * TILE
+    return SIDE_PLANES + k // per_plane, slice(start, start + TILE)
+
+
+def side_planes_sent(cy):
+    return SIDE_PLANES + -(-len(CORNERS) // (cy // TILE))
+
+
+def sign_of(mask):
+    return (mask == 1).astype(F32) - (mask == 2).astype(F32)
+
+
+def field_side_kernel(
+    ready, px_ref, py_ref, cur_ref, ear_ref, coef_ref, mask_ref, even_ref, odd_ref, even_out, odd_out,
+    corner_ref, sign_ref, sems,
+):
+    _, cx, cy, nz = cur_ref.shape
     upper = row_ids((TILE, nz)) >= TILE // 2
     low = select_side(py_ref[0], even_ref, odd_ref, False)
     high = select_side(py_ref[0], even_ref, odd_ref, True)
-
-    def write(is_high, face_ref):
-        for name, dist, part, at in plan_tiles(plan, cy):
-            x = cx - dist if is_high else dist - 1
-            if part >= 0:
-                tile = own_tile(name, x, slice(part * TILE, (part + 1) * TILE))
-            else:
-                tile = jnp.where(
-                    upper,
-                    low(lambda ref: halo_tile(ref, name, x)),
-                    high(lambda ref: halo_tile(ref, name, x)),
+    sources = [cur_ref.at[i] for i in range(3)] + [ear_ref.at[i] for i in range(3)] + [coef_ref]
+
+    def copies_of(is_high, face, out):
+        out_copies = []
+        for name, source in enumerate(sources):
+            planes = FIELD_PLAN[name][0]
+            x = cx - planes if is_high else 0
+            first = sum(n for n, _ in FIELD_PLAN[:name])
+            out_copies.append(
+                pltpu.make_async_copy(
+                    source.at[pl.ds(x, planes)], out.at[pl.ds(first, planes)], sems.at[face, name]
                 )
-            face_ref[at] = tile
-
-    write_faces(px_ref[0], write, even_out, odd_out)
-
-
-def sign_of(mask):
-    return (mask == 1).astype(F32) - (mask == 2).astype(F32)
-
-
-def field_side_kernel(ready, px_ref, py_ref, cur_ref, ear_ref, coef_ref, mask_ref, *refs):
-    _, cx, cy, nz = cur_ref.shape
-    ready()
-
-    def own_tile(name, x, ys):
-        if name < 3:
-            return cur_ref[name, x, ys]
-        if name < 6:
-            return ear_ref[name - 3, x, ys]
-        return coef_ref[x, ys] if name == 6 else sign_of(mask_ref[x, ys])
-
-    side_kernel(FIELD_PLAN, own_tile, face_tile, cx, cy, nz, px_ref, py_ref, *refs)
+            )
+        return out_copies
+
+    def late_copies(face, out):
+        signs = pl.ds(SIDE_PLANES - MID, MID)
+        rest = pl.ds(SIDE_PLANES, corner_ref.shape[1])
+        return [
+            pltpu.make_async_copy(sign_ref.at[face], out.at[signs], sems.at[face, len(sources)]),
+            pltpu.make_async_copy(corner_ref.at[face], out.at[rest], sems.at[face, len(sources) + 1]),
+        ]
+
+    def run(high_out, low_out):
+        faces = ((True, 0, high_out), (False, 1, low_out))
+        early = [copy for is_high, face, out in faces for copy in copies_of(is_high, face, out)]
+        for copy in early:
+            copy.start()
+        for is_high, face, _ in faces:
+            for k, (name, dist) in enumerate(CORNERS):
+                x = cx - dist if is_high else dist - 1
+                below = low(lambda ref: face_tile(ref, name, x))
+                above = high(lambda ref: face_tile(ref, name, x))
+                plane, rows = corner_place(k, cy)
+                corner_ref[face, plane - SIDE_PLANES, rows] = jnp.where(upper, below, above)
+        ready()
+        for is_high, face, _ in faces:
+            for k in range(MID):
+                sign_ref[face, k] = sign_of(mask_ref[cx - MID + k if is_high else k])
+        late = [copy for _, face, out in faces for copy in late_copies(face, out)]
+        for copy in late:
+            copy.start()
+        for copy in early + late:
+            copy.wait()
+
+    @pl.when(px_ref[0] == 0)
+    def _():
+        run(even_out, odd_out)
+
+    @pl.when(px_ref[0] != 0)
+    def _():
+        run(odd_out, even_out)
 
 
 LANES = 128
@@ -461,14 +499,16 @@
         put(7, x, own, sign_of(mask_ref[x]))
     for is_high in (False, True):
         read = select_side(px_ref[0], xe_ref, xo_ref, is_high)
-        for name, dist, part, at in plan_tiles(FIELD_PLAN, cy):
+        for name, (planes, _) in enumerate(FIELD_PLAN):
+            for dist in range(1, planes + 1):
+                x = cx - 1 + dist if is_high else -dist
+                put(name, x, own, read(lambda ref: ref[side_plane(name, dist, is_high)]))
+        for k, (name, dist) in enumerate(CORNERS):
             x = cx - 1 + dist if is_high else -dist
-            tile = read(lambda ref: ref[at])
-            if part >= 0:
-                put(name, x, slice(TILE * (part + 1), TILE * (part + 2)), tile)
-            else:
-                put(name, x, lower, tile)
-                put(name, x, higher, tile)
+            plane, rows = corner_place(k, cy)
+            tile = read(lambda ref: ref[plane, rows])
+            put(name, x, lower, tile)
+            put(name, x, higher, tile)
 
     begin = px_ref[1]
     deep = cy + TILE
@@ -615,15 +655,19 @@
     smem = pl.BlockSpec(memory_space=pltpu.SMEM)
     vmem = pl.BlockSpec(memory_space=pltpu.VMEM)
 
-    def call(kernel, operands, shapes, scratch=(), scalars=0, from_hbm=(), to_hbm=False):
+    def call(kernel, operands, shapes, scratch=(), scalars=0, from_hbm=(), left_in_hbm=(), to_hbm=False, raw_outputs=False):
         shapes = [(pltpu.HBM if to_hbm else jax.ShapeDtypeStruct)(shape, F32) for shape in shapes]
         operands = list(operands)
         in_specs = [smem] * scalars + [vmem] * (len(operands) - scalars)
-        scratch_shapes = [pltpu.VMEM(shape, F32) for shape in scratch]
+        scratch_shapes = [pltpu.VMEM(shape, F32) if isinstance(shape, tuple) else shape for shape in scratch]
+        hbm = pl.BlockSpec(memory_space=pltpu.HBM)
+        for at in left_in_hbm:
+            operands[at] = pltpu.with_memory_space_constraint(operands[at], pltpu.HBM)
+            in_specs[at] = hbm
         if from_hbm:
             for at in from_hbm:
                 operands[at] = pltpu.with_memory_space_constraint(operands[at], pltpu.HBM)
-                in_specs[at] = pl.BlockSpec(memory_space=pltpu.HBM)
+                in_specs[at] = hbm
                 scratch_shapes.append(pltpu.VMEM(operands[at].shape, operands[at].dtype))
             scratch_shapes.append(pltpu.SemaphoreType.DMA((len(from_hbm),)))
             kernel = staged(kernel, from_hbm, len(operands))
@@ -631,7 +675,7 @@
             kernel,
             out_shape=shapes,
             in_specs=in_specs,
-            out_specs=[vmem] * len(shapes),
+            out_specs=[hbm if raw_outputs else vmem] * len(shapes),
             scratch_shapes=scratch_shapes,
             compiler_params=pltpu.CompilerParams(vmem_limit_bytes=VMEM_GRANT),
         )(*operands)
@@ -648,7 +692,7 @@
         ),
         [(8, local_comps)] + [(5, cx, TILE, nz)] * 2,
         scalars=1,
-        from_hbm=(1, 2, 3),
+        from_hbm=tuple(range(1, 9)),
     )
     if comp_count == 4:
         near_block = lax.ppermute(own_block, "comp", pair_list(4, 0))
@@ -668,14 +712,19 @@
         (*first_blocks, point_xyz),
         [(32, point_count), (16, 256)],
         [(8, point_count)],
-    )
-    field_tiles = len(plan_tiles(FIELD_PLAN, cy))
+        from_hbm=(len(first_blocks),),
+    )
+    sent = side_planes_sent(cy)
     sides = call(
         field_side_kernel,
         (px, py, *fields, layer_mask, ye, yo),
-        [(field_tiles, TILE, nz)] * 2,
+        [(sent, cy, nz)] * 2,
+        [(2, sent - SIDE_PLANES, cy, nz), (2, MID, cy, nz), pltpu.SemaphoreType.DMA((2, len(FIELD_PLAN) + 1))],
         scalars=2,
-        from_hbm=(2, 3, 4, 5),
+        from_hbm=(5,),
+        left_in_hbm=(2, 3, 4),
+        to_hbm=True,
+        raw_outputs=True,
     )
     xe, xo = swap_faces(sides, "slab")
     (packed,) = call(
@@ -686,6 +735,7 @@
         ),
         [(device_count, 1, LIST_ROWS * 2 * HALF)],
         [(8, point_count), (32, point_count)],
+        from_hbm=tuple(len(last_blocks) + k for k in (2, 3, 4)),
     )
     arrived = lax.all_to_all(packed, ("slab", "comp"), split_axis=0, concat_axis=0, tiled=True)
     free_final, free_prior, wide_coef, wide_sign = call(

time: 81.4 us -> 113 us (1.39)
  Pallas kernels: 44.5 us -> 79.1 us
  local copies, waits for them, and re-layouts: 2.77 us -> 0 us
    pallas_call x8, Pallas kernels: 44.5 us -> 79.1 us  [call(): pl.pallas_call(kernel, out_shape=shapes, in_specs=in_specs, out_specs=[hb...]
    unnamed x16 -> x0, local copies, waits for them, and re-layouts: 2.77 us -> none
  transfers between devices with their start and end apart: 9 -> 9, of which waited for: 5 -> 5; matrix products, arithmetic and copies ran while one was open for 0% -> 0% of each run, Pallas kernels for 39% -> 29%
where the time goes in v8:
time: 113 us
  Pallas kernels  79.1 us (70%)
  starting transfers between devices  18.4 us (16%)
  waiting for transfers between devices  14.3 us (13%)
    pallas_call x8, Pallas kernels, call(): pl.pallas_call(kernel, out_shape=shapes, in_specs=in_specs, out_specs=[hb...  79.1 us
    ppermute x6, starting transfers between devices, swap_faces(): out.append(lax.ppermute(faces[k], axis, pair_list(count, k)))  10.6 us
    ppermute x6, waiting for transfers between devices, swap_faces(): out.append(lax.ppermute(faces[k], axis, pair_list(count, k)))  9.43 us
    all_to_all x1, starting transfers between devices, local(): lax.all_to_all(packed, ('slab', 'comp'), split_axis=0, concat_axis=0, til...  5.98 us
    ppermute x1, waiting for transfers between devices, local(): near_block = lax.ppermute(own_block, 'comp', pair_list(4, 0))  3.9 us
  transfers between devices with their start and end apart: 9, of which 5 were waited for; matrix products, arithmetic and copies ran while one was open for 0% of the time, Pallas kernels for 29%

profile of v8, /device:TPU:8, one launch (start us, length us, event | category | flops | bytes accessed | tf_op | source)
XLA Modules:
  0.0 112.7 jit_solution(2437298671399814632)
XLA Ops:
  0.6 1.5 %shard_map.131 = (f32[8,1024]{1,0:T(8,128)S(1)}, f32[5,8,8,256]{3,2,1,0:T(8,128)S(1)}, f32[5,8,8,256]{3,2,1,0:T(8,128)S(1)}) custom-call(s32[1]{0:T(128)} %bitcast.1.refs_0_.refs_1_, f32[3,8,16,256]{3,2,1,0:T(8,128)} %refs_2_.6, f32[3,8,16,256]{3,2,1,0:T(8,128)} %refs_3_.6, f32[8,16,256]{2,1,0:T(8,128)} %refs_4_.5, f32[3,1024]{1,0:T(4,128)} %refs_4_.3, ...), custom_call_target="tpu_custom_call" | custom-call | tf_op jit(solution)/shard_map/pallas_call | solution.py:674
  2.1 0.1 collective-permute-start
  2.2 5.0 %collective-permute-start.1 = (f32[5,8,8,256]{3,2,1,0:T(8,128)S(1)}, f32[5,8,8,256]{3,2,1,0:T(8,128)S(1)}, u32[]{:S(2)}, u32[]{:S(2)}) collective-permute-start(f32[5,8,8,256]{3,2,1,0:T(8,128)S(1)} %get-tuple-element.21), channel_id=1, source_target_pairs={{1,2},{2,1},{5,6},{6,5},{9,10},{10,9},{13,14},{14,13},{17,18},{18,... | collective-permute-start | bytes 983048 | tf_op jit(solution)/shard_map/ppermute | solution.py:302
  7.3 0.1 pad_add_fusion.refs_0_
  7.4 4.3 %collective-permute-done.refs_6_ = f32[5,8,8,256]{3,2,1,0:T(8,128)S(1)} collective-permute-done((f32[5,8,8,256]{3,2,1,0:T(8,128)S(1)}, f32[5,8,8,256]{3,2,1,0:T(8,128)S(1)}, u32[]{:S(2)}, u32[]{:S(2)}) %collective-permute-start) | collective-permute-done | bytes 327712 | tf_op jit(solution)/shard_map/ppermute | solution.py:302
  11.7 3.0 %collective-permute-done.1.refs_7_ = f32[5,8,8,256]{3,2,1,0:T(8,128)S(1)} collective-permute-done((f32[5,8,8,256]{3,2,1,0:T(8,128)S(1)}, f32[5,8,8,256]{3,2,1,0:T(8,128)S(1)}, u32[]{:S(2)}, u32[]{:S(2)}) %collective-permute-start.1) | collective-permute-done | bytes 327712 | tf_op jit(solution)/shard_map/ppermute | solution.py:302
  14.7 35.6 %shard_map.132 = (f32[48,16,256]{2,1,0:T(8,128)}, f32[48,16,256]{2,1,0:T(8,128)}) custom-call(s32[2]{0:T(128)S(1)} %pad_add_fusion.refs_0_, s32[1]{0:T(128)} %bitcast.1.refs_0_.refs_1_, f32[3,8,16,256]{3,2,1,0:T(8,128)} %refs_2_.6, f32[3,8,16,256]{3,2,1,0:T(8,128)} %refs_3_.6, f32[8,16,256]{2,1,0:T(8,128)} %refs_4_.5, s32[8,16,256]{2,1,0:T(8,128)} %refs_5_.3, ...), custom_call_target="tpu_custom_call" | custom-call | tf_op jit(solution)/shard_map/pallas_call | solution.py:674
  50.3 0.1 collective-permute-start.2
  50.3 0.7 collective-permute-start.3
  51.1 0.1 collective-permute-start.4
  51.1 3.9 %collective-permute-done.4.refs_1_ = f32[8,1024]{1,0:T(8,128)S(1)} collective-permute-done((f32[8,1024]{1,0:T(8,128)S(1)}, f32[8,1024]{1,0:T(8,128)S(1)}, u32[]{:S(2)}, u32[]{:S(2)}) %collective-permute-start.4) | collective-permute-done | bytes 32800 | tf_op jit(solution)/shard_map/ppermute | solution.py:698
  55.0 1.7 %collective-permute-start.5 = (f32[8,2048]{1,0:T(8,128)S(1)}, f32[8,2048]{1,0:T(8,128)S(1)}, u32[]{:S(2)}, u32[]{:S(2)}) collective-permute-start(f32[8,2048]{1,0:T(8,128)S(1)} %pad_maximum_fusion), channel_id=1, source_target_pairs={{1,2},{2,1},{0,3},{3,0},{5,6},{6,5},{4,7},{7,4},{9,10},{10,9},{8,1... | collective-permute-start | bytes 196616 | tf_op jit(solution)/shard_map/ppermute | solution.py:701
  56.8 10.5 %shard_map.134 = (f32[32,1024]{1,0:T(8,128)S(1)}, f32[16,256]{1,0:T(8,128)S(1)}) custom-call(f32[8,1024]{1,0:T(8,128)S(1)} %get-tuple-element.27.refs_0_, f32[8,1024]{1,0:T(8,128)S(1)} %collective-permute-done.4.refs_1_, f32[3,1024]{1,0:T(4,128)} %refs_3_.7), custom_call_target="tpu_custom_call" | custom-call | tf_op jit(solution)/shard_map/pallas_call | solution.py:674
  67.3 0.0 collective-permute-done.5.refs_0_
  67.3 12.3 %shard_map.135 = f32[32,1,1664]{2,1,0:T(1,128)} custom-call(f32[8,2048]{1,0:T(8,128)S(1)} %collective-permute-done.5.refs_0_, f32[32,1024]{1,0:T(8,128)S(1)} %get-tuple-element.28.refs_1_, f32[16,256]{1,0:T(8,128)S(1)} %get-tuple-element.29.refs_2_, f32[3,1024]{1,0:T(4,128)} %refs_3_.7, s32[1,1024]{1,0:T(1,128)} %bitcast.9, s32[1,1024]{1,0:T(1,128)} %bitcast.10), custom_call_target="tpu_custom_call" | custom-call | tf_op jit(solution)/shard_map/pallas_call | solution.py:674
  79.6 6.0 %all-to-all-start = ((f32[32,1,1664]{2,1,0:T(1,128)}), f32[32,1,1664]{2,1,0:T(1,128)S(1)}, u32[]{:S(2)}, u32[]{:S(2)}) async-start(f32[32,1,1664]{2,1,0:T(1,128)} %shard_map.135), calls=%async_computation | async-start | bytes 425984 | tf_op jit(solution)/shard_map/all_to_all | solution.py:740
  85.6 0.0 collective-permute-done.2.refs_8_
  85.6 0.0 collective-permute-done.3.refs_9_
  85.6 6.6 %shard_map.133 = (f32[3,8,16,256]{3,2,1,0:T(8,128)}, f32[3,8,16,256]{3,2,1,0:T(8,128)}, f32[12,2,32,128]{3,2,1,0:T(8,128)}, f32[16,16,256]{2,1,0:T(8,128)}) custom-call(s32[2]{0:T(128)S(1)} %pad_add_fusion.refs_0_, s32[1]{0:T(128)} %bitcast.1.refs_0_.refs_1_, f32[3,8,16,256]{3,2,1,0:T(8,128)} %refs_2_.6, f32[3,8,16,256]{3,2,1,0:T(8,128)} %refs_3_.6, ...), custom_call_target="tpu_custom_call" | custom-call | tf_op jit(solution)/shard_map/pallas_call | solution.py:674
  92.3 1.0 all-to-all-done.refs_1_.refs_0_
  93.3 4.2 %shard_map.136 = (f32[3,12,16,256]{3,2,1,0:T(8,128)S(1)}, f32[3,8,16,256]{3,2,1,0:T(8,128)S(1)}, f32[3,8,8,256]{3,2,1,0:T(8,128)S(1)}, f32[3,8,8,256]{3,2,1,0:T(8,128)S(1)}) custom-call(s32[1]{0:T(128)} %bitcast.1.refs_0_.refs_1_, f32[32,1,1664]{2,1,0:T(1,128)S(1)} %all-to-all-done.refs_1_.refs_0_, f32[16,16,256]{2,1,0:T(8,128)} %get-tuple-element.30.refs_2_.refs_1_), custom_call_target="tpu_custom_call" | custom-call | tf_op jit(solution)/shard_map/pallas_call | solution.py:674
  97.5 2.2 %collective-permute-start.6 = (f32[3,8,8,256]{3,2,1,0:T(8,128)S(1)}, f32[3,8,8,256]{3,2,1,0:T(8,128)S(1)}, u32[]{:S(2)}, u32[]{:S(2)}) collective-permute-start(f32[3,8,8,256]{3,2,1,0:T(8,128)S(1)} %get-tuple-element.36), channel_id=1, source_target_pairs={{0,1},{2,3},{1,0},{3,2},{4,5},{6,7},{5,4},{7,6},{8,9},{10,11},{9,8... | collective-permute-start | bytes 589832 | tf_op jit(solution)/shard_map/ppermute | solution.py:302
  99.7 2.5 %collective-permute-start.7 = (f32[3,8,8,256]{3,2,1,0:T(8,128)S(1)}, f32[3,8,8,256]{3,2,1,0:T(8,128)S(1)}, u32[]{:S(2)}, u32[]{:S(2)}) collective-permute-start(f32[3,8,8,256]{3,2,1,0:T(8,128)S(1)} %get-tuple-element.37), channel_id=1, source_target_pairs={{1,2},{2,1},{5,6},{6,5},{9,10},{10,9},{13,14},{14,13},{17,18},{18,... | collective-permute-start | bytes 589832 | tf_op jit(solution)/shard_map/ppermute | solution.py:302
  102.2 3.8 %shard_map.137 = (f32[3,4,16,256]{3,2,1,0:T(8,128)S(1)}, f32[3,4,16,256]{3,2,1,0:T(8,128)S(1)}, f32[3,8,16,256]{3,2,1,0:T(8,128)S(1)}) custom-call(f32[32,1,1664]{2,1,0:T(1,128)S(1)} %all-to-all-done.refs_1_.refs_0_, f32[16,16,256]{2,1,0:T(8,128)} %get-tuple-element.30.refs_2_.refs_1_), custom_call_target="tpu_custom_call" | custom-call | tf_op jit(solution)/shard_map/pallas_call | solution.py:674
  106.0 0.0 collective-permute-done.6.refs_10_
  106.0 2.1 %collective-permute-done.7.refs_11_ = f32[3,8,8,256]{3,2,1,0:T(8,128)S(1)} collective-permute-done((f32[3,8,8,256]{3,2,1,0:T(8,128)S(1)}, f32[3,8,8,256]{3,2,1,0:T(8,128)S(1)}, u32[]{:S(2)}, u32[]{:S(2)}) %collective-permute-start.7) | collective-permute-done | bytes 196640 | tf_op jit(solution)/shard_map/ppermute | solution.py:302
  108.1 4.6 %shard_map.138 = (f32[3,8,16,256]{3,2,1,0:T(8,128)}, f32[3,8,16,256]{3,2,1,0:T(8,128)}) custom-call(s32[2]{0:T(128)S(1)} %pad_add_fusion.refs_0_, s32[1]{0:T(128)} %bitcast.1.refs_0_.refs_1_, f32[3,8,16,256]{3,2,1,0:T(8,128)} %get-tuple-element.24.refs_2_, f32[3,8,16,256]{3,2,1,0:T(8,128)} %get-tuple-element.25.refs_3_, ...), custom_call_target="tpu_custom_call" | custom-call | tf_op jit(solution)/shard_map/pallas_call | solution.py:674
  (1 shorter events, 0.0 us)
Async XLA Ops:
  2.1 9.5 %collective-permute-start = (f32[5,8,8,256]{3,2,1,0:T(8,128)S(1)}, f32[5,8,8,256]{3,2,1,0:T(8,128)S(1)}, u32[]{:S(2)}, u32[]{:S(2)}) collective-permute-start(f32[5,8,8,256]{3,2,1,0:T(8,128)S(1)} %get-tuple-element.20), channel_id=1, source_target_pairs={{0,1},{2,3},{1,0},{3,2},{4,5},{6,7},{5,4},{7,6},{8,9},{10,11},{9,8... | collective-permute-start | bytes 983048 | tf_op jit(solution)/shard_map/ppermute | solution.py:302
  2.2 12.5 %collective-permute-start.1 = (f32[5,8,8,256]{3,2,1,0:T(8,128)S(1)}, f32[5,8,8,256]{3,2,1,0:T(8,128)S(1)}, u32[]{:S(2)}, u32[]{:S(2)}) collective-permute-start(f32[5,8,8,256]{3,2,1,0:T(8,128)S(1)} %get-tuple-element.21), channel_id=1, source_target_pairs={{1,2},{2,1},{5,6},{6,5},{9,10},{10,9},{13,14},{14,13},{17,18},{18,... | collective-permute-start | bytes 983048 | tf_op jit(solution)/shard_map/ppermute | solution.py:302
  50.3 35.4 %collective-permute-start.2 = (f32[48,16,256]{2,1,0:T(8,128)}, f32[48,16,256]{2,1,0:T(8,128)S(1)}, u32[]{:S(2)}, u32[]{:S(2)}) collective-permute-start(f32[48,16,256]{2,1,0:T(8,128)} %get-tuple-element.22), channel_id=1, source_target_pairs={{0,4},{8,12},{16,20},{24,28},{4,0},{12,8},{20,16},{28,24},{1,5},{9... | collective-permute-start | bytes 2359304 | tf_op jit(solution)/shard_map/ppermute | solution.py:302
  50.3 35.3 %collective-permute-start.3 = (f32[48,16,256]{2,1,0:T(8,128)}, f32[48,16,256]{2,1,0:T(8,128)S(1)}, u32[]{:S(2)}, u32[]{:S(2)}) collective-permute-start(f32[48,16,256]{2,1,0:T(8,128)} %get-tuple-element.23), channel_id=1, source_target_pairs={{4,8},{12,16},{20,24},{8,4},{16,12},{24,20},{5,9},{13,17},{21,25},... | collective-permute-start | bytes 2359304 | tf_op jit(solution)/shard_map/ppermute | solution.py:302
  51.1 4.0 %collective-permute-start.4 = (f32[8,1024]{1,0:T(8,128)S(1)}, f32[8,1024]{1,0:T(8,128)S(1)}, u32[]{:S(2)}, u32[]{:S(2)}) collective-permute-start(f32[8,1024]{1,0:T(8,128)S(1)} %get-tuple-element.27.refs_0_), channel_id=1, source_target_pairs={{0,1},{2,3},{1,0},{3,2},{4,5},{6,7},{5,4},{7,6},{8,9},{10,11},{9,8... | collective-permute-start | bytes 98312 | tf_op jit(solution)/shard_map/ppermute | solution.py:698
  55.0 12.3 %collective-permute-start.5 = (f32[8,2048]{1,0:T(8,128)S(1)}, f32[8,2048]{1,0:T(8,128)S(1)}, u32[]{:S(2)}, u32[]{:S(2)}) collective-permute-start(f32[8,2048]{1,0:T(8,128)S(1)} %pad_maximum_fusion), channel_id=1, source_target_pairs={{1,2},{2,1},{0,3},{3,0},{5,6},{6,5},{4,7},{7,4},{9,10},{10,9},{8,1... | collective-permute-start | bytes 196616 | tf_op jit(solution)/shard_map/ppermute | solution.py:701
  79.6 13.7 %all-to-all-start = ((f32[32,1,1664]{2,1,0:T(1,128)}), f32[32,1,1664]{2,1,0:T(1,128)S(1)}, u32[]{:S(2)}, u32[]{:S(2)}) async-start(f32[32,1,1664]{2,1,0:T(1,128)} %shard_map.135), calls=%async_computation | async-start | bytes 425984 | tf_op jit(solution)/shard_map/all_to_all | solution.py:740
  97.5 8.5 %collective-permute-start.6 = (f32[3,8,8,256]{3,2,1,0:T(8,128)S(1)}, f32[3,8,8,256]{3,2,1,0:T(8,128)S(1)}, u32[]{:S(2)}, u32[]{:S(2)}) collective-permute-start(f32[3,8,8,256]{3,2,1,0:T(8,128)S(1)} %get-tuple-element.36), channel_id=1, source_target_pairs={{0,1},{2,3},{1,0},{3,2},{4,5},{6,7},{5,4},{7,6},{8,9},{10,11},{9,8... | collective-permute-start | bytes 589832 | tf_op jit(solution)/shard_map/ppermute | solution.py:302
  99.7 8.4 %collective-permute-start.7 = (f32[3,8,8,256]{3,2,1,0:T(8,128)S(1)}, f32[3,8,8,256]{3,2,1,0:T(8,128)S(1)}, u32[]{:S(2)}, u32[]{:S(2)}) collective-permute-start(f32[3,8,8,256]{3,2,1,0:T(8,128)S(1)} %get-tuple-element.37), channel_id=1, source_target_pairs={{1,2},{2,1},{5,6},{6,5},{9,10},{10,9},{13,14},{14,13},{17,18},{18,... | collective-permute-start | bytes 589832 | tf_op jit(solution)/shard_map/ppermute | solution.py:302

commit v9 on v8

--- a/solution.py
+++ b/solution.py
@@ -104,15 +104,13 @@
     return total
 
 
-def first_incident_kernel(count, ready, *refs):
-    ready()
+def first_incident_kernel(count, *refs):
     par_refs, (xyz_ref, acc_ref, total_ref, x8_ref) = refs[:count], refs[count:]
     acc_ref[...] = jnp.zeros(acc_ref.shape, F32)
     total_ref[...] = add_components(par_refs, xyz_ref, x8_ref, acc_ref)
 
 
-def last_incident_kernel(count, step, ready, *refs):
-    ready()
+def last_incident_kernel(count, step, *refs):
     par_refs, refs = refs[:count], refs[count:]
     first_ref, first_total_ref, xyz_ref, own_ref, off_ref, out_ref, x8_ref, acc_ref = refs
     points = xyz_ref.shape[1]
@@ -374,56 +372,41 @@
 
 
 def field_side_kernel(
-    ready, px_ref, py_ref, cur_ref, ear_ref, coef_ref, mask_ref, even_ref, odd_ref, even_out, odd_out,
-    corner_ref, sign_ref, sems,
+    ready, px_ref, py_ref, cur_ref, ear_ref, coef_ref, mask_ref, even_ref, odd_ref, even_out, odd_out, sems
 ):
-    _, cx, cy, nz = cur_ref.shape
+    cx, cy, nz = mask_ref.shape
     upper = row_ids((TILE, nz)) >= TILE // 2
     low = select_side(py_ref[0], even_ref, odd_ref, False)
     high = select_side(py_ref[0], even_ref, odd_ref, True)
     sources = [cur_ref.at[i] for i in range(3)] + [ear_ref.at[i] for i in range(3)] + [coef_ref]
 
-    def copies_of(is_high, face, out):
-        out_copies = []
-        for name, source in enumerate(sources):
-            planes = FIELD_PLAN[name][0]
-            x = cx - planes if is_high else 0
-            first = sum(n for n, _ in FIELD_PLAN[:name])
-            out_copies.append(
-                pltpu.make_async_copy(
-                    source.at[pl.ds(x, planes)], out.at[pl.ds(first, planes)], sems.at[face, name]
-                )
-            )
-        return out_copies
-
-    def late_copies(face, out):
-        signs = pl.ds(SIDE_PLANES - MID, MID)
-        rest = pl.ds(SIDE_PLANES, corner_ref.shape[1])
-        return [
-            pltpu.make_async_copy(sign_ref.at[face], out.at[signs], sems.at[face, len(sources)]),
-            pltpu.make_async_copy(corner_ref.at[face], out.at[rest], sems.at[face, len(sources) + 1]),
-        ]
-
     def run(high_out, low_out):
         faces = ((True, 0, high_out), (False, 1, low_out))
-        early = [copy for is_high, face, out in faces for copy in copies_of(is_high, face, out)]
-        for copy in early:
+        copies = []
+        for is_high, face, out in faces:
+            for name, source in enumerate(sources):
+                planes = FIELD_PLAN[name][0]
+                first = sum(n for n, _ in FIELD_PLAN[:name])
+                x = cx - planes if is_high else 0
+                copies.append(
+                    pltpu.make_async_copy(
+                        source.at[pl.ds(x, planes)], out.at[pl.ds(first, planes)], sems.at[face, name]
+                    )
+                )
+        for copy in copies:
             copy.start()
-        for is_high, face, _ in faces:
+        for is_high, face, out in faces:
             for k, (name, dist) in enumerate(CORNERS):
                 x = cx - dist if is_high else dist - 1
                 below = low(lambda ref: face_tile(ref, name, x))
                 above = high(lambda ref: face_tile(ref, name, x))
                 plane, rows = corner_place(k, cy)
-                corner_ref[face, plane - SIDE_PLANES, rows] = jnp.where(upper, below, above)
+                out[plane, rows] = jnp.where(upper, below, above)
         ready()
-        for is_high, face, _ in faces:
+        for is_high, face, out in faces:
             for k in range(MID):
-                sign_ref[face, k] = sign_of(mask_ref[cx - MID + k if is_high else k])
-        late = [copy for _, face, out in faces for copy in late_copies(face, out)]
-        for copy in late:
-            copy.start()
-        for copy in early + late:
+                out[SIDE_PLANES - MID + k] = sign_of(mask_ref[cx - MID + k if is_high else k])
+        for copy in copies:
             copy.wait()
 
     @pl.when(px_ref[0] == 0)
@@ -655,7 +638,7 @@
     smem = pl.BlockSpec(memory_space=pltpu.SMEM)
     vmem = pl.BlockSpec(memory_space=pltpu.VMEM)
 
-    def call(kernel, operands, shapes, scratch=(), scalars=0, from_hbm=(), left_in_hbm=(), to_hbm=False, raw_outputs=False):
+    def call(kernel, operands, shapes, scratch=(), scalars=0, from_hbm=(), left_in_hbm=(), to_hbm=False):
         shapes = [(pltpu.HBM if to_hbm else jax.ShapeDtypeStruct)(shape, F32) for shape in shapes]
         operands = list(operands)
         in_specs = [smem] * scalars + [vmem] * (len(operands) - scalars)
@@ -675,7 +658,7 @@
             kernel,
             out_shape=shapes,
             in_specs=in_specs,
-            out_specs=[hbm if raw_outputs else vmem] * len(shapes),
+            out_specs=[vmem] * len(shapes),
             scratch_shapes=scratch_shapes,
             compiler_params=pltpu.CompilerParams(vmem_limit_bytes=VMEM_GRANT),
         )(*operands)
@@ -712,19 +695,16 @@
         (*first_blocks, point_xyz),
         [(32, point_count), (16, 256)],
         [(8, point_count)],
-        from_hbm=(len(first_blocks),),
     )
     sent = side_planes_sent(cy)
     sides = call(
         field_side_kernel,
         (px, py, *fields, layer_mask, ye, yo),
         [(sent, cy, nz)] * 2,
-        [(2, sent - SIDE_PLANES, cy, nz), (2, MID, cy, nz), pltpu.SemaphoreType.DMA((2, len(FIELD_PLAN) + 1))],
+        [pltpu.SemaphoreType.DMA((2, len(FIELD_PLAN) - 1))],
         scalars=2,
         from_hbm=(5,),
         left_in_hbm=(2, 3, 4),
-        to_hbm=True,
-        raw_outputs=True,
     )
     xe, xo = swap_faces(sides, "slab")
     (packed,) = call(
@@ -735,7 +715,6 @@
         ),
         [(device_count, 1, LIST_ROWS * 2 * HALF)],
         [(8, point_count), (32, point_count)],
-        from_hbm=tuple(len(last_blocks) + k for k in (2, 3, 4)),
     )
     arrived = lax.all_to_all(packed, ("slab", "comp"), split_axis=0, concat_axis=0, tiled=True)
     free_final, free_prior, wide_coef, wide_sign = call(

time: 113 us -> 79.5 us (0.70)
  Pallas kernels: 79.1 us -> 44.9 us
    pallas_call x8, Pallas kernels: 79.1 us -> 44.9 us  [call(): pl.pallas_call(kernel, out_shape=shapes, in_specs=in_specs, out_specs=[vm...]
  transfers between devices with their start and end apart: 9 -> 9, of which waited for: 5 -> 5; matrix products, arithmetic and copies ran while one was open for 0% -> 0% of each run, Pallas kernels for 29% -> 40%
where the time goes in v9:
time: 79.5 us; the launch traced here: 79.2 us
  Pallas kernels  44.9 us (56%)
  starting transfers between devices  18.4 us (23%)
  waiting for transfers between devices  14.3 us (18%)
  between operations  0.81 us (1%)
    pallas_call x8, Pallas kernels, call(): pl.pallas_call(kernel, out_shape=shapes, in_specs=in_specs, out_specs=[vm...  44.9 us
    ppermute x6, starting transfers between devices, swap_faces(): out.append(lax.ppermute(faces[k], axis, pair_list(count, k)))  10.6 us
    ppermute x6, waiting for transfers between devices, swap_faces(): out.append(lax.ppermute(faces[k], axis, pair_list(count, k)))  9.42 us
    all_to_all x1, starting transfers between devices, local(): lax.all_to_all(packed, ('slab', 'comp'), split_axis=0, concat_axis=0, til...  5.98 us
    ppermute x1, waiting for transfers between devices, local(): near_block = lax.ppermute(own_block, 'comp', pair_list(4, 0))  3.9 us
    ppermute x1, starting transfers between devices, local(): lax.ppermute(jnp.concatenate(first_blocks, axis=1), 'comp', ring)  1.73 us
  transfers between devices with their start and end apart: 9, of which 5 were waited for; matrix products, arithmetic and copies ran while one was open for 0% of the time, Pallas kernels for 40%

profile of v9, /device:TPU:8, one launch (start us, length us, event | category | flops | bytes accessed | tf_op | source)
XLA Modules:
  0.0 79.2 jit_solution(14498452173817225672)
XLA Ops:
  0.6 1.5 %shard_map.131 = (f32[8,1024]{1,0:T(8,128)S(1)}, f32[5,8,8,256]{3,2,1,0:T(8,128)S(1)}, f32[5,8,8,256]{3,2,1,0:T(8,128)S(1)}) custom-call(s32[1]{0:T(128)} %bitcast.1.refs_0_.refs_1_, f32[3,8,16,256]{3,2,1,0:T(8,128)} %refs_2_.6, f32[3,8,16,256]{3,2,1,0:T(8,128)} %refs_3_.6, f32[8,16,256]{2,1,0:T(8,128)} %refs_4_.5, f32[3,1024]{1,0:T(4,128)} %refs_4_.3, ...), custom_call_target="tpu_custom_call" | custom-call | tf_op jit(solution)/shard_map/pallas_call | solution.py:657
  2.1 0.1 collective-permute-start
  2.2 5.0 %collective-permute-start.1 = (f32[5,8,8,256]{3,2,1,0:T(8,128)S(1)}, f32[5,8,8,256]{3,2,1,0:T(8,128)S(1)}, u32[]{:S(2)}, u32[]{:S(2)}) collective-permute-start(f32[5,8,8,256]{3,2,1,0:T(8,128)S(1)} %get-tuple-element.21), channel_id=1, source_target_pairs={{1,2},{2,1},{5,6},{6,5},{9,10},{10,9},{13,14},{14,13},{17,18},{18,... | collective-permute-start | bytes 983048 | tf_op jit(solution)/shard_map/ppermute | solution.py:300
  7.3 0.1 pad_add_fusion.refs_0_
  7.4 4.3 %collective-permute-done.refs_6_ = f32[5,8,8,256]{3,2,1,0:T(8,128)S(1)} collective-permute-done((f32[5,8,8,256]{3,2,1,0:T(8,128)S(1)}, f32[5,8,8,256]{3,2,1,0:T(8,128)S(1)}, u32[]{:S(2)}, u32[]{:S(2)}) %collective-permute-start) | collective-permute-done | bytes 327712 | tf_op jit(solution)/shard_map/ppermute | solution.py:300
  11.7 3.0 %collective-permute-done.1.refs_7_ = f32[5,8,8,256]{3,2,1,0:T(8,128)S(1)} collective-permute-done((f32[5,8,8,256]{3,2,1,0:T(8,128)S(1)}, f32[5,8,8,256]{3,2,1,0:T(8,128)S(1)}, u32[]{:S(2)}, u32[]{:S(2)}) %collective-permute-start.1) | collective-permute-done | bytes 327712 | tf_op jit(solution)/shard_map/ppermute | solution.py:300
  14.7 2.9 %shard_map.132 = (f32[48,16,256]{2,1,0:T(8,128)}, f32[48,16,256]{2,1,0:T(8,128)S(1)}) custom-call(s32[2]{0:T(128)S(1)} %pad_add_fusion.refs_0_, s32[1]{0:T(128)} %bitcast.1.refs_0_.refs_1_, f32[3,8,16,256]{3,2,1,0:T(8,128)} %refs_2_.6, f32[3,8,16,256]{3,2,1,0:T(8,128)} %refs_3_.6, f32[8,16,256]{2,1,0:T(8,128)} %refs_4_.5, s32[8,16,256]{2,1,0:T(8,128)} %refs_5_.3, ...), custom_call_target="tpu_custom_call" | custom-call | tf_op jit(solution)/shard_map/pallas_call | solution.py:657
  17.5 0.1 collective-permute-start.2
  17.6 0.7 collective-permute-start.3
  18.3 0.0 copy-start
  18.4 0.1 collective-permute-start.4
  18.4 3.9 %collective-permute-done.4.refs_1_ = f32[8,1024]{1,0:T(8,128)S(1)} collective-permute-done((f32[8,1024]{1,0:T(8,128)S(1)}, f32[8,1024]{1,0:T(8,128)S(1)}, u32[]{:S(2)}, u32[]{:S(2)}) %collective-permute-start.4) | collective-permute-done | bytes 32800 | tf_op jit(solution)/shard_map/ppermute | solution.py:681
  22.3 1.7 %collective-permute-start.5 = (f32[8,2048]{1,0:T(8,128)S(1)}, f32[8,2048]{1,0:T(8,128)S(1)}, u32[]{:S(2)}, u32[]{:S(2)}) collective-permute-start(f32[8,2048]{1,0:T(8,128)S(1)} %pad_maximum_fusion), channel_id=1, source_target_pairs={{1,2},{2,1},{0,3},{3,0},{5,6},{6,5},{4,7},{7,4},{9,10},{10,9},{8,1... | collective-permute-start | bytes 196616 | tf_op jit(solution)/shard_map/ppermute | solution.py:684
  24.1 0.0 copy-done
  24.1 0.0 copy-start.2
  24.1 9.8 %shard_map.134 = (f32[32,1024]{1,0:T(8,128)S(1)}, f32[16,256]{1,0:T(8,128)S(1)}) custom-call(f32[8,1024]{1,0:T(8,128)S(1)} %get-tuple-element.27.refs_0_, f32[8,1024]{1,0:T(8,128)S(1)} %collective-permute-done.4.refs_1_, f32[3,1024]{1,0:T(4,128)S(1)} %copy-done), custom_call_target="tpu_custom_call" | custom-call | tf_op jit(solution)/shard_map/pallas_call | solution.py:657
  33.9 0.0 copy-start.1
  33.9 0.0 collective-permute-done.5.refs_0_
  33.9 0.0 copy-done.2
  33.9 0.7 copy-done.1
  34.6 11.5 %shard_map.135 = f32[32,1,1664]{2,1,0:T(1,128)} custom-call(f32[8,2048]{1,0:T(8,128)S(1)} %collective-permute-done.5.refs_0_, f32[32,1024]{1,0:T(8,128)S(1)} %get-tuple-element.28.refs_1_, f32[16,256]{1,0:T(8,128)S(1)} %get-tuple-element.29.refs_2_, f32[3,1024]{1,0:T(4,128)S(1)} %copy-done, s32[1,1024]{1,0:T(1,128)S(1)} %bitcast.7, s32[1,1024]{1,0:T(1,128)S(1)} %bitcast.8), custom_call_target="tpu_custom_call" | custom-call | tf_op jit(solution)/shard_map/pallas_call | solution.py:657
  46.1 6.0 %all-to-all-start = ((f32[32,1,1664]{2,1,0:T(1,128)}), f32[32,1,1664]{2,1,0:T(1,128)S(1)}, u32[]{:S(2)}, u32[]{:S(2)}) async-start(f32[32,1,1664]{2,1,0:T(1,128)} %shard_map.135), calls=%async_computation | async-start | bytes 425984 | tf_op jit(solution)/shard_map/all_to_all | solution.py:719
  52.1 0.0 collective-permute-done.2.refs_8_
  52.1 0.0 collective-permute-done.3.refs_9_
  52.1 6.6 %shard_map.133 = (f32[3,8,16,256]{3,2,1,0:T(8,128)}, f32[3,8,16,256]{3,2,1,0:T(8,128)}, f32[12,2,32,128]{3,2,1,0:T(8,128)}, f32[16,16,256]{2,1,0:T(8,128)}) custom-call(s32[2]{0:T(128)S(1)} %pad_add_fusion.refs_0_, s32[1]{0:T(128)} %bitcast.1.refs_0_.refs_1_, f32[3,8,16,256]{3,2,1,0:T(8,128)} %refs_2_.6, f32[3,8,16,256]{3,2,1,0:T(8,128)} %refs_3_.6, ...), custom_call_target="tpu_custom_call" | custom-call | tf_op jit(solution)/shard_map/pallas_call | solution.py:657
  58.8 1.0 %all-to-all-done.refs_1_.refs_0_ = f32[32,1,1664]{2,1,0:T(1,128)S(1)} async-done(((f32[32,1,1664]{2,1,0:T(1,128)}), f32[32,1,1664]{2,1,0:T(1,128)S(1)}, u32[]{:S(2)}, u32[]{:S(2)}) %all-to-all-start) | async-done | bytes 213024 | tf_op jit(solution)/shard_map/all_to_all | solution.py:719
  59.8 4.2 %shard_map.136 = (f32[3,12,16,256]{3,2,1,0:T(8,128)S(1)}, f32[3,8,16,256]{3,2,1,0:T(8,128)S(1)}, f32[3,8,8,256]{3,2,1,0:T(8,128)S(1)}, f32[3,8,8,256]{3,2,1,0:T(8,128)S(1)}) custom-call(s32[1]{0:T(128)} %bitcast.1.refs_0_.refs_1_, f32[32,1,1664]{2,1,0:T(1,128)S(1)} %all-to-all-done.refs_1_.refs_0_, f32[16,16,256]{2,1,0:T(8,128)} %get-tuple-element.30.refs_2_.refs_1_), custom_call_target="tpu_custom_call" | custom-call | tf_op jit(solution)/shard_map/pallas_call | solution.py:657
  64.0 2.2 %collective-permute-start.6 = (f32[3,8,8,256]{3,2,1,0:T(8,128)S(1)}, f32[3,8,8,256]{3,2,1,0:T(8,128)S(1)}, u32[]{:S(2)}, u32[]{:S(2)}) collective-permute-start(f32[3,8,8,256]{3,2,1,0:T(8,128)S(1)} %get-tuple-element.36), channel_id=1, source_target_pairs={{0,1},{2,3},{1,0},{3,2},{4,5},{6,7},{5,4},{7,6},{8,9},{10,11},{9,8... | collective-permute-start | bytes 589832 | tf_op jit(solution)/shard_map/ppermute | solution.py:300
  66.2 2.5 %collective-permute-start.7 = (f32[3,8,8,256]{3,2,1,0:T(8,128)S(1)}, f32[3,8,8,256]{3,2,1,0:T(8,128)S(1)}, u32[]{:S(2)}, u32[]{:S(2)}) collective-permute-start(f32[3,8,8,256]{3,2,1,0:T(8,128)S(1)} %get-tuple-element.37), channel_id=1, source_target_pairs={{1,2},{2,1},{5,6},{6,5},{9,10},{10,9},{13,14},{14,13},{17,18},{18,... | collective-permute-start | bytes 589832 | tf_op jit(solution)/shard_map/ppermute | solution.py:300
  68.7 3.8 %shard_map.137 = (f32[3,4,16,256]{3,2,1,0:T(8,128)S(1)}, f32[3,4,16,256]{3,2,1,0:T(8,128)S(1)}, f32[3,8,16,256]{3,2,1,0:T(8,128)S(1)}) custom-call(f32[32,1,1664]{2,1,0:T(1,128)S(1)} %all-to-all-done.refs_1_.refs_0_, f32[16,16,256]{2,1,0:T(8,128)} %get-tuple-element.30.refs_2_.refs_1_), custom_call_target="tpu_custom_call" | custom-call | tf_op jit(solution)/shard_map/pallas_call | solution.py:657
  72.5 0.0 collective-permute-done.6.refs_10_
  72.5 2.1 %collective-permute-done.7.refs_11_ = f32[3,8,8,256]{3,2,1,0:T(8,128)S(1)} collective-permute-done((f32[3,8,8,256]{3,2,1,0:T(8,128)S(1)}, f32[3,8,8,256]{3,2,1,0:T(8,128)S(1)}, u32[]{:S(2)}, u32[]{:S(2)}) %collective-permute-start.7) | collective-permute-done | bytes 196640 | tf_op jit(solution)/shard_map/ppermute | solution.py:300
  74.6 4.6 %shard_map.138 = (f32[3,8,16,256]{3,2,1,0:T(8,128)}, f32[3,8,16,256]{3,2,1,0:T(8,128)}) custom-call(s32[2]{0:T(128)S(1)} %pad_add_fusion.refs_0_, s32[1]{0:T(128)} %bitcast.1.refs_0_.refs_1_, f32[3,8,16,256]{3,2,1,0:T(8,128)} %get-tuple-element.24.refs_2_, f32[3,8,16,256]{3,2,1,0:T(8,128)} %get-tuple-element.25.refs_3_, ...), custom_call_target="tpu_custom_call" | custom-call | tf_op jit(solution)/shard_map/pallas_call | solution.py:657
  (1 shorter events, 0.0 us)
Async XLA Ops:
  2.1 9.5 %collective-permute-start = (f32[5,8,8,256]{3,2,1,0:T(8,128)S(1)}, f32[5,8,8,256]{3,2,1,0:T(8,128)S(1)}, u32[]{:S(2)}, u32[]{:S(2)}) collective-permute-start(f32[5,8,8,256]{3,2,1,0:T(8,128)S(1)} %get-tuple-element.20), channel_id=1, source_target_pairs={{0,1},{2,3},{1,0},{3,2},{4,5},{6,7},{5,4},{7,6},{8,9},{10,11},{9,8... | collective-permute-start | bytes 983048 | tf_op jit(solution)/shard_map/ppermute | solution.py:300
  2.2 12.5 %collective-permute-start.1 = (f32[5,8,8,256]{3,2,1,0:T(8,128)S(1)}, f32[5,8,8,256]{3,2,1,0:T(8,128)S(1)}, u32[]{:S(2)}, u32[]{:S(2)}) collective-permute-start(f32[5,8,8,256]{3,2,1,0:T(8,128)S(1)} %get-tuple-element.21), channel_id=1, source_target_pairs={{1,2},{2,1},{5,6},{6,5},{9,10},{10,9},{13,14},{14,13},{17,18},{18,... | collective-permute-start | bytes 983048 | tf_op jit(solution)/shard_map/ppermute | solution.py:300
  17.5 34.6 %collective-permute-start.2 = (f32[48,16,256]{2,1,0:T(8,128)}, f32[48,16,256]{2,1,0:T(8,128)S(1)}, u32[]{:S(2)}, u32[]{:S(2)}) collective-permute-start(f32[48,16,256]{2,1,0:T(8,128)} %get-tuple-element.22), channel_id=1, source_target_pairs={{0,4},{8,12},{16,20},{24,28},{4,0},{12,8},{20,16},{28,24},{1,5},{9... | collective-permute-start | bytes 2359304 | tf_op jit(solution)/shard_map/ppermute | solution.py:300
  17.6 34.5 %collective-permute-start.3 = (f32[48,16,256]{2,1,0:T(8,128)S(1)}, f32[48,16,256]{2,1,0:T(8,128)S(1)}, u32[]{:S(2)}, u32[]{:S(2)}) collective-permute-start(f32[48,16,256]{2,1,0:T(8,128)S(1)} %get-tuple-element.23), channel_id=1, source_target_pairs={{4,8},{12,16},{20,24},{8,4},{16,12},{24,20},{5,9},{13,17},{21,25},... | collective-permute-start | bytes 2359304 | tf_op jit(solution)/shard_map/ppermute | solution.py:300
  18.3 5.7 %copy-start = (f32[3,1024]{1,0:T(4,128)S(1)}, f32[3,1024]{1,0:T(4,128)}, u32[]{:S(2)}) copy-start(f32[3,1024]{1,0:T(4,128)} %refs_3_.7) | copy-start | bytes 36868
  18.4 4.0 %collective-permute-start.4 = (f32[8,1024]{1,0:T(8,128)S(1)}, f32[8,1024]{1,0:T(8,128)S(1)}, u32[]{:S(2)}, u32[]{:S(2)}) collective-permute-start(f32[8,1024]{1,0:T(8,128)S(1)} %get-tuple-element.27.refs_0_), channel_id=1, source_target_pairs={{0,1},{2,3},{1,0},{3,2},{4,5},{6,7},{5,4},{7,6},{8,9},{10,11},{9,8... | collective-permute-start | bytes 98312 | tf_op jit(solution)/shard_map/ppermute | solution.py:681
  22.3 11.6 %collective-permute-start.5 = (f32[8,2048]{1,0:T(8,128)S(1)}, f32[8,2048]{1,0:T(8,128)S(1)}, u32[]{:S(2)}, u32[]{:S(2)}) collective-permute-start(f32[8,2048]{1,0:T(8,128)S(1)} %pad_maximum_fusion), channel_id=1, source_target_pairs={{1,2},{2,1},{0,3},{3,0},{5,6},{6,5},{4,7},{7,4},{9,10},{10,9},{8,1... | collective-permute-start | bytes 196616 | tf_op jit(solution)/shard_map/ppermute | solution.py:684
  24.1 9.8 %copy-start.2 = (s32[1024]{0:T(1024)S(1)}, s32[1024]{0:T(1024)}, u32[]{:S(2)}) copy-start(s32[1024]{0:T(1024)} %param.18) | copy-start | bytes 12292
  33.9 0.7 copy-start.1
  46.1 13.7 %all-to-all-start = ((f32[32,1,1664]{2,1,0:T(1,128)}), f32[32,1,1664]{2,1,0:T(1,128)S(1)}, u32[]{:S(2)}, u32[]{:S(2)}) async-start(f32[32,1,1664]{2,1,0:T(1,128)} %shard_map.135), calls=%async_computation | async-start | bytes 425984 | tf_op jit(solution)/shard_map/all_to_all | solution.py:719
  64.0 8.5 %collective-permute-start.6 = (f32[3,8,8,256]{3,2,1,0:T(8,128)S(1)}, f32[3,8,8,256]{3,2,1,0:T(8,128)S(1)}, u32[]{:S(2)}, u32[]{:S(2)}) collective-permute-start(f32[3,8,8,256]{3,2,1,0:T(8,128)S(1)} %get-tuple-element.36), channel_id=1, source_target_pairs={{0,1},{2,3},{1,0},{3,2},{4,5},{6,7},{5,4},{7,6},{8,9},{10,11},{9,8... | collective-permute-start | bytes 589832 | tf_op jit(solution)/shard_map/ppermute | solution.py:300
  66.2 8.4 %collective-permute-start.7 = (f32[3,8,8,256]{3,2,1,0:T(8,128)S(1)}, f32[3,8,8,256]{3,2,1,0:T(8,128)S(1)}, u32[]{:S(2)}, u32[]{:S(2)}) collective-permute-start(f32[3,8,8,256]{3,2,1,0:T(8,128)S(1)} %get-tuple-element.37), channel_id=1, source_target_pairs={{1,2},{2,1},{5,6},{6,5},{9,10},{10,9},{13,14},{14,13},{17,18},{18,... | collective-permute-start | bytes 589832 | tf_op jit(solution)/shard_map/ppermute | solution.py:300

commit v10 on v9

--- a/solution.py
+++ b/solution.py
@@ -15,6 +15,8 @@
 SIN_C = (4.442834854125977 / LEAD, -7.306587219238281 / LEAD, 3.588636875152588 / LEAD)
 SIN_SCALE = LEAD * abs(LEAD)
 VER_SCALE = LEAD * LEAD
+KC = 256
+AHEAD = 2
 HALF = 64
 OWN_TILES = 5
 SIDE_TILES = 4
@@ -47,25 +49,30 @@
     return lax.broadcasted_iota(jnp.int32, shape, 0)
 
 
-def add_components(par_refs, xyz_ref, x8_ref, acc_ref):
-    points = xyz_ref.shape[1]
-    kc = 256
-    tile = 256
-    x8_ref[...] = jnp.zeros(x8_ref.shape, F32)
-    x8_ref[0:3, :] = xyz_ref[...]
-    xhi, xmid, xlo = split_three(x8_ref[...])
-    right = jnp.concatenate([xhi, xmid, xlo, xhi, xmid, xhi], axis=0).astype(BF16)
+def add_components(par_refs, right_ref, acc_ref, u_ref):
+    points = right_ref.shape[1]
+    ahead, kc, tile = u_ref.shape
     rows8 = row_ids((8, kc))
     times = step_size * (rows8 + 1).astype(F32)
     rows16 = row_ids((16, kc))
     comp_row = jnp.where(rows16 < 6, rows16 % 3, (rows16 + 2) % 3)
     valued = (rows16 < 10) & (rows16 != 6)
 
-    def body(par_ref, step, total):
-        blk = par_ref[:, pl.ds(pl.multiple_of(step * kc, kc), kc)]
-        kv = jnp.where(rows8 < 3, blk * inv_two_pi, 0.0)
-        khi, kmid, klo = split_three(kv)
-        left = jnp.concatenate([khi, khi, khi, kmid, kmid, klo], axis=0).astype(BF16)
+    def block_of(par_ref, step):
+        return par_ref[:, pl.ds(pl.multiple_of(step * kc, kc), kc)]
+
+    def left_of(blk):
+        khi, kmid, klo = split_three(jnp.where(rows8 < 3, blk * inv_two_pi, 0.0))
+        return jnp.concatenate([khi, khi, khi, kmid, kmid, klo], axis=0).astype(BF16)
+
+    def angles(left, t):
+        cols = slice(t * tile, (t + 1) * tile)
+        return lax.dot_general(left, right_ref[:, cols], (((0,), (0,)), ((), ())), preferred_element_type=F32)
+
+    def body(par_ref, steps, step, total):
+        blk = block_of(par_ref, step)
+        left = left_of(blk)
+        later = left_of(block_of(par_ref, jnp.minimum(step + 1, steps - 1)))
         delays = times * blk[3:4, :] - blk[7:8, :]
         sd, qd = sin_versine(delays * inv_two_pi)
         sd, cd = SIN_SCALE * sd, 1.0 - VER_SCALE * qd
@@ -81,9 +88,8 @@
         wc = rows_of(cd)[0]
         lc = rows_of(-VER_SCALE * cd)[1]
         ls = rows_of(SIN_SCALE * sd)[1]
-        for t in range(points // tile):
-            cols = slice(t * tile, (t + 1) * tile)
-            u = lax.dot_general(left, right[:, cols], (((0,), (0,)), ((), ())), preferred_element_type=F32)
+
+        def add_tile(t, u):
             highs, lows = [], []
             for j in range(kc // 32):
                 for value in sin_versine(u[32 * j : 32 * j + 32]):
@@ -94,36 +100,57 @@
             part += jnp.dot(lc, jnp.concatenate(highs[1::2], axis=0), preferred_element_type=F32)
             part += jnp.dot(ls, jnp.concatenate(lows[0::2], axis=0), preferred_element_type=F32)
             part += jnp.dot(lc, jnp.concatenate(lows[1::2], axis=0), preferred_element_type=F32)
-            acc_ref[:, cols] += part
+            acc_ref[:, t * tile : (t + 1) * tile] += part
+
+        tiles = points // tile
+        rest = {t: angles(left, t) for t in range(ahead, tiles)}
+        for t in range(ahead):
+            add_tile(t, u_ref[t])
+        for t in range(ahead):
+            u_ref[t] = angles(later, t)
+        for t, u in rest.items():
+            add_tile(t, u)
         return total + wc
 
     total = jnp.zeros((16, kc), F32)
     for par_ref in par_refs:
         steps = par_ref.shape[1] // kc
-        total = lax.fori_loop(0, steps, lambda step, t, ref=par_ref: body(ref, step, t), total)
+        left = left_of(block_of(par_ref, 0))
+        for t in range(ahead):
+            u_ref[t] = angles(left, t)
+        total = lax.fori_loop(0, steps, lambda step, t, ref=par_ref, n=steps: body(ref, n, step, t), total)
     return total
 
 
 def first_incident_kernel(count, *refs):
-    par_refs, (xyz_ref, acc_ref, total_ref, x8_ref) = refs[:count], refs[count:]
+    par_refs, (right_ref, acc_ref, total_ref, u_ref) = refs[:count], refs[count:]
     acc_ref[...] = jnp.zeros(acc_ref.shape, F32)
-    total_ref[...] = add_components(par_refs, xyz_ref, x8_ref, acc_ref)
-
-
-def last_incident_kernel(count, step, *refs):
+    total_ref[...] = add_components(par_refs, right_ref, acc_ref, u_ref)
+
+
+def last_incident_kernel(count, step, ready, *refs):
     par_refs, refs = refs[:count], refs[count:]
-    first_ref, first_total_ref, xyz_ref, own_ref, off_ref, out_ref, x8_ref, acc_ref = refs
-    points = xyz_ref.shape[1]
+    first_ref, first_total_ref, right_ref, own_ref, off_ref, out_ref, acc_ref, u_ref = refs
+    points = right_ref.shape[1]
     owners = out_ref.shape[0]
     acc_ref[...] = first_ref[...]
-    total = add_components(par_refs, xyz_ref, x8_ref, acc_ref) + first_total_ref[...]
+    total = add_components(par_refs, right_ref, acc_ref, u_ref) + first_total_ref[...]
+    ready()
     vals = acc_ref[0:16, :] + acc_ref[16:32, :] + jnp.sum(total, axis=1, keepdims=True)
     vals = jnp.where(row_ids((16, points)) == 6, off_ref[...].astype(F32), vals)
     v1, v2, v3 = split_three(vals)
     named = own_ref[...] == row_ids((owners, points))
     named_one = named.astype(F32).astype(BF16)
-    earlier = row_ids((points, points)) < lax.broadcasted_iota(jnp.int32, (points, points), 1)
-    before = jnp.dot(named_one, earlier.astype(F32).astype(BF16), preferred_element_type=F32)
+    width = 128
+    square = (width, width)
+    earlier = (row_ids(square) < lax.broadcasted_iota(jnp.int32, square, 1)).astype(F32).astype(BF16)
+    sums = jnp.concatenate([earlier, jnp.ones(square, BF16)], axis=1)
+    before, past = [], jnp.zeros((owners, width), F32)
+    for k in range(0, points, width):
+        got = jnp.dot(named_one[:, k : k + width], sums, preferred_element_type=F32)
+        before.append(got[:, 0:width] + past)
+        past = past + got[:, width:]
+    before = jnp.concatenate(before, axis=1)
     rank = jnp.sum(jnp.where(named, before, 0.0), axis=0, keepdims=True).astype(jnp.int32)
     terms = [v.astype(BF16) for v in (v1, v2, v3)]
     tiles = 0.0
@@ -302,10 +329,14 @@
 
 
 def prepare_kernel(
-    ready, par_ref, cur_ref, ear_ref, coef_ref, wave_ref, freq_ref, amp_ref, index_ref, table_ref,
-    block_out, even_out, odd_out,
+    ready, par_ref, cur_ref, ear_ref, coef_ref, wave_ref, freq_ref, amp_ref, index_ref, table_ref, xyz_ref,
+    block_out, right_out, even_out, odd_out, x8_ref,
 ):
+    x8_ref[...] = jnp.zeros(x8_ref.shape, F32)
     ready()
+    x8_ref[0:3, :] = xyz_ref[...]
+    xhi, xmid, xlo = split_three(x8_ref[...])
+    right_out[...] = jnp.concatenate([xhi, xmid, xlo, xhi, xmid, xhi], axis=0).astype(BF16)
     entries = table_ref.shape[1]
     comps = index_ref.shape[1]
     picked = (row_ids((entries, comps)) == index_ref[...]).astype(F32).astype(BF16)
@@ -639,7 +670,8 @@
     vmem = pl.BlockSpec(memory_space=pltpu.VMEM)
 
     def call(kernel, operands, shapes, scratch=(), scalars=0, from_hbm=(), left_in_hbm=(), to_hbm=False):
-        shapes = [(pltpu.HBM if to_hbm else jax.ShapeDtypeStruct)(shape, F32) for shape in shapes]
+        kind = pltpu.HBM if to_hbm else jax.ShapeDtypeStruct
+        shapes = [kind(shape, F32) if isinstance(shape, tuple) else shape for shape in shapes]
         operands = list(operands)
         in_specs = [smem] * scalars + [vmem] * (len(operands) - scalars)
         scratch_shapes = [pltpu.VMEM(shape, F32) if isinstance(shape, tuple) else shape for shape in scratch]
@@ -667,15 +699,16 @@
     py = (lax.axis_index("comp") % 2).astype(jnp.int32).reshape(1)
     fields = (current_field, earlier_field, wave_coef)
     local_comps = frequency.shape[0]
-    own_block, *faces = call(
+    own_block, right, *faces = call(
         prepare_kernel,
         (
             py, *fields, wave_vector, frequency.reshape(1, local_comps), amplitude,
-            phase_index.reshape(1, local_comps), phase_table.reshape(1, -1),
+            phase_index.reshape(1, local_comps), phase_table.reshape(1, -1), point_xyz,
         ),
-        [(8, local_comps)] + [(5, cx, TILE, nz)] * 2,
+        [(8, local_comps), jax.ShapeDtypeStruct((48, point_count), BF16)] + [(5, cx, TILE, nz)] * 2,
+        [(8, point_count)],
         scalars=1,
-        from_hbm=tuple(range(1, 9)),
+        from_hbm=tuple(range(1, 10)),
     )
     if comp_count == 4:
         near_block = lax.ppermute(own_block, "comp", pair_list(4, 0))
@@ -692,9 +725,9 @@
     ye, yo = swap_faces(faces, "comp")
     (sum_one, total_one) = call(
         lambda *refs: first_incident_kernel(len(first_blocks), *refs),
-        (*first_blocks, point_xyz),
-        [(32, point_count), (16, 256)],
-        [(8, point_count)],
+        (*first_blocks, right),
+        [(32, point_count), (16, KC)],
+        [(AHEAD, KC, KC)],
     )
     sent = side_planes_sent(cy)
     sides = call(
@@ -710,11 +743,12 @@
     (packed,) = call(
         lambda *refs: last_incident_kernel(len(last_blocks), comp_count, *refs),
         (
-            *last_blocks, sum_one, total_one, point_xyz,
+            *last_blocks, sum_one, total_one, right,
             point_owner.reshape(1, point_count), cell_offset.reshape(1, point_count),
         ),
         [(device_count, 1, LIST_ROWS * 2 * HALF)],
-        [(8, point_count), (32, point_count)],
+        [(32, point_count), (AHEAD, KC, KC)],
+        from_hbm=tuple(len(last_blocks) + k for k in (3, 4)),
     )
     arrived = lax.all_to_all(packed, ("slab", "comp"), split_axis=0, concat_axis=0, tiled=True)
     free_final, free_prior, wide_coef, wide_sign = call(

time: 79.5 us -> 76.2 us (0.958)
  Pallas kernels: 44.9 us -> 42.3 us
    pallas_call x8, Pallas kernels: 44.9 us -> 42.3 us  [call(): pl.pallas_call(kernel, out_shape=shapes, in_specs=in_specs, out_specs=[vm...]
  transfers between devices with their start and end apart: 9 -> 9, of which waited for: 5 -> 5; matrix products, arithmetic and copies ran while one was open for 0% -> 0% of each run, Pallas kernels for 40% -> 38%
where the time goes in v10:
time: 76.2 us; the launch traced here: 75.9 us
  Pallas kernels  42.3 us (56%)
  starting transfers between devices  18.4 us (24%)
  waiting for transfers between devices  14.3 us (19%)
  between operations  0.79 us (1%)
    pallas_call x8, Pallas kernels, call(): pl.pallas_call(kernel, out_shape=shapes, in_specs=in_specs, out_specs=[vm...  42.3 us
    ppermute x6, starting transfers between devices, swap_faces(): out.append(lax.ppermute(faces[k], axis, pair_list(count, k)))  10.6 us
    ppermute x6, waiting for transfers between devices, swap_faces(): out.append(lax.ppermute(faces[k], axis, pair_list(count, k)))  9.42 us
    all_to_all x1, starting transfers between devices, local(): lax.all_to_all(packed, ('slab', 'comp'), split_axis=0, concat_axis=0, til...  5.98 us
    ppermute x1, waiting for transfers between devices, local(): near_block = lax.ppermute(own_block, 'comp', pair_list(4, 0))  3.9 us
    ppermute x1, starting transfers between devices, local(): lax.ppermute(jnp.concatenate(first_blocks, axis=1), 'comp', ring)  1.73 us
  transfers between devices with their start and end apart: 9, of which 5 were waited for; matrix products, arithmetic and copies ran while one was open for 0% of the time, Pallas kernels for 38%

profile of v10, /device:TPU:8, one launch (start us, length us, event | category | flops | bytes accessed | tf_op | source)
XLA Modules:
  0.0 75.9 jit_solution(16985568391413724257)
XLA Ops:
  0.6 1.5 %shard_map.131 = (f32[8,1024]{1,0:T(8,128)S(1)}, bf16[48,1024]{1,0:T(8,128)(2,1)S(1)}, f32[5,8,8,256]{3,2,1,0:T(8,128)S(1)}, f32[5,8,8,256]{3,2,1,0:T(8,128)S(1)}) custom-call(s32[1]{0:T(128)} %bitcast.1.refs_0_.refs_1_, f32[3,8,16,256]{3,2,1,0:T(8,128)} %refs_2_.5, f32[3,8,16,256]{3,2,1,0:T(8,128)} %refs_3_.5, f32[8,16,256]{2,1,0:T(8,128)} %refs_4_.5, ...), custom_call_target="tpu_custom_call" | custom-call | tf_op jit(solution)/shard_map/pallas_call | solution.py:689
  2.2 0.1 collective-permute-start
  2.2 5.0 %collective-permute-start.1 = (f32[5,8,8,256]{3,2,1,0:T(8,128)S(1)}, f32[5,8,8,256]{3,2,1,0:T(8,128)S(1)}, u32[]{:S(2)}, u32[]{:S(2)}) collective-permute-start(f32[5,8,8,256]{3,2,1,0:T(8,128)S(1)} %get-tuple-element.22), channel_id=1, source_target_pairs={{1,2},{2,1},{5,6},{6,5},{9,10},{10,9},{13,14},{14,13},{17,18},{18,... | collective-permute-start | bytes 983048 | tf_op jit(solution)/shard_map/ppermute | solution.py:327
  7.3 0.1 pad_add_fusion.refs_0_
  7.4 4.3 %collective-permute-done.refs_6_ = f32[5,8,8,256]{3,2,1,0:T(8,128)S(1)} collective-permute-done((f32[5,8,8,256]{3,2,1,0:T(8,128)S(1)}, f32[5,8,8,256]{3,2,1,0:T(8,128)S(1)}, u32[]{:S(2)}, u32[]{:S(2)}) %collective-permute-start) | collective-permute-done | bytes 327712 | tf_op jit(solution)/shard_map/ppermute | solution.py:327
  11.7 3.0 %collective-permute-done.1.refs_7_ = f32[5,8,8,256]{3,2,1,0:T(8,128)S(1)} collective-permute-done((f32[5,8,8,256]{3,2,1,0:T(8,128)S(1)}, f32[5,8,8,256]{3,2,1,0:T(8,128)S(1)}, u32[]{:S(2)}, u32[]{:S(2)}) %collective-permute-start.1) | collective-permute-done | bytes 327712 | tf_op jit(solution)/shard_map/ppermute | solution.py:327
  14.7 2.9 %shard_map.132 = (f32[48,16,256]{2,1,0:T(8,128)}, f32[48,16,256]{2,1,0:T(8,128)S(1)}) custom-call(s32[2]{0:T(128)S(1)} %pad_add_fusion.refs_0_, s32[1]{0:T(128)} %bitcast.1.refs_0_.refs_1_, f32[3,8,16,256]{3,2,1,0:T(8,128)} %refs_2_.5, f32[3,8,16,256]{3,2,1,0:T(8,128)} %refs_3_.5, f32[8,16,256]{2,1,0:T(8,128)} %refs_4_.5, s32[8,16,256]{2,1,0:T(8,128)} %refs_5_.3, ...), custom_call_target="tpu_custom_call" | custom-call | tf_op jit(solution)/shard_map/pallas_call | solution.py:689
  17.6 0.1 collective-permute-start.2
  17.7 0.7 collective-permute-start.3
  18.4 0.1 collective-permute-start.4
  18.5 3.9 %collective-permute-done.4.refs_1_ = f32[8,1024]{1,0:T(8,128)S(1)} collective-permute-done((f32[8,1024]{1,0:T(8,128)S(1)}, f32[8,1024]{1,0:T(8,128)S(1)}, u32[]{:S(2)}, u32[]{:S(2)}) %collective-permute-start.4) | collective-permute-done | bytes 32800 | tf_op jit(solution)/shard_map/ppermute | solution.py:714
  22.4 1.7 %collective-permute-start.5 = (f32[8,2048]{1,0:T(8,128)S(1)}, f32[8,2048]{1,0:T(8,128)S(1)}, u32[]{:S(2)}, u32[]{:S(2)}) collective-permute-start(f32[8,2048]{1,0:T(8,128)S(1)} %pad_maximum_fusion), channel_id=1, source_target_pairs={{1,2},{2,1},{0,3},{3,0},{5,6},{6,5},{4,7},{7,4},{9,10},{10,9},{8,1... | collective-permute-start | bytes 196616 | tf_op jit(solution)/shard_map/ppermute | solution.py:717
  24.1 8.7 %shard_map.134 = (f32[32,1024]{1,0:T(8,128)S(1)}, f32[16,256]{1,0:T(8,128)S(1)}) custom-call(f32[8,1024]{1,0:T(8,128)S(1)} %get-tuple-element.28.refs_0_, f32[8,1024]{1,0:T(8,128)S(1)} %collective-permute-done.4.refs_1_, bf16[48,1024]{1,0:T(8,128)(2,1)S(1)} %get-tuple-element.29.refs_2_.refs_3_), custom_call_target="tpu_custom_call" | custom-call | tf_op jit(solution)/shard_map/pallas_call | solution.py:689
  32.8 0.0 collective-permute-done.5.refs_0_
  32.8 10.0 %shard_map.135 = f32[32,1,1664]{2,1,0:T(1,128)} custom-call(f32[8,2048]{1,0:T(8,128)S(1)} %collective-permute-done.5.refs_0_, f32[32,1024]{1,0:T(8,128)S(1)} %get-tuple-element.30.refs_1_, f32[16,256]{1,0:T(8,128)S(1)} %get-tuple-element.31.refs_2_, bf16[48,1024]{1,0:T(8,128)(2,1)S(1)} %get-tuple-element.29.refs_2_.refs_3_, s32[1,1024]{1,0:T(1,128)} %bitcast.9, ...), custom_call_target="tpu_custom_call" | custom-call | tf_op jit(solution)/shard_map/pallas_call | solution.py:689
  42.8 6.0 %all-to-all-start = ((f32[32,1,1664]{2,1,0:T(1,128)}), f32[32,1,1664]{2,1,0:T(1,128)S(1)}, u32[]{:S(2)}, u32[]{:S(2)}) async-start(f32[32,1,1664]{2,1,0:T(1,128)} %shard_map.135), calls=%async_computation | async-start | bytes 425984 | tf_op jit(solution)/shard_map/all_to_all | solution.py:753
  48.8 0.0 collective-permute-done.2.refs_8_
  48.8 0.0 collective-permute-done.3.refs_9_
  48.8 6.6 %shard_map.133 = (f32[3,8,16,256]{3,2,1,0:T(8,128)}, f32[3,8,16,256]{3,2,1,0:T(8,128)}, f32[12,2,32,128]{3,2,1,0:T(8,128)}, f32[16,16,256]{2,1,0:T(8,128)}) custom-call(s32[2]{0:T(128)S(1)} %pad_add_fusion.refs_0_, s32[1]{0:T(128)} %bitcast.1.refs_0_.refs_1_, f32[3,8,16,256]{3,2,1,0:T(8,128)} %refs_2_.5, f32[3,8,16,256]{3,2,1,0:T(8,128)} %refs_3_.5, ...), custom_call_target="tpu_custom_call" | custom-call | tf_op jit(solution)/shard_map/pallas_call | solution.py:689
  55.4 1.0 %all-to-all-done.refs_1_.refs_0_ = f32[32,1,1664]{2,1,0:T(1,128)S(1)} async-done(((f32[32,1,1664]{2,1,0:T(1,128)}), f32[32,1,1664]{2,1,0:T(1,128)S(1)}, u32[]{:S(2)}, u32[]{:S(2)}) %all-to-all-start) | async-done | bytes 213024 | tf_op jit(solution)/shard_map/all_to_all | solution.py:753
  56.4 4.2 %shard_map.136 = (f32[3,12,16,256]{3,2,1,0:T(8,128)S(1)}, f32[3,8,16,256]{3,2,1,0:T(8,128)S(1)}, f32[3,8,8,256]{3,2,1,0:T(8,128)S(1)}, f32[3,8,8,256]{3,2,1,0:T(8,128)S(1)}) custom-call(s32[1]{0:T(128)} %bitcast.1.refs_0_.refs_1_, f32[32,1,1664]{2,1,0:T(1,128)S(1)} %all-to-all-done.refs_1_.refs_0_, f32[16,16,256]{2,1,0:T(8,128)} %get-tuple-element.32.refs_2_.refs_1_), custom_call_target="tpu_custom_call" | custom-call | tf_op jit(solution)/shard_map/pallas_call | solution.py:689
  60.7 2.2 %collective-permute-start.6 = (f32[3,8,8,256]{3,2,1,0:T(8,128)S(1)}, f32[3,8,8,256]{3,2,1,0:T(8,128)S(1)}, u32[]{:S(2)}, u32[]{:S(2)}) collective-permute-start(f32[3,8,8,256]{3,2,1,0:T(8,128)S(1)} %get-tuple-element.38), channel_id=1, source_target_pairs={{0,1},{2,3},{1,0},{3,2},{4,5},{6,7},{5,4},{7,6},{8,9},{10,11},{9,8... | collective-permute-start | bytes 589832 | tf_op jit(solution)/shard_map/ppermute | solution.py:327
  62.9 2.5 %collective-permute-start.7 = (f32[3,8,8,256]{3,2,1,0:T(8,128)S(1)}, f32[3,8,8,256]{3,2,1,0:T(8,128)S(1)}, u32[]{:S(2)}, u32[]{:S(2)}) collective-permute-start(f32[3,8,8,256]{3,2,1,0:T(8,128)S(1)} %get-tuple-element.39), channel_id=1, source_target_pairs={{1,2},{2,1},{5,6},{6,5},{9,10},{10,9},{13,14},{14,13},{17,18},{18,... | collective-permute-start | bytes 589832 | tf_op jit(solution)/shard_map/ppermute | solution.py:327
  65.4 3.8 %shard_map.137 = (f32[3,4,16,256]{3,2,1,0:T(8,128)S(1)}, f32[3,4,16,256]{3,2,1,0:T(8,128)S(1)}, f32[3,8,16,256]{3,2,1,0:T(8,128)S(1)}) custom-call(f32[32,1,1664]{2,1,0:T(1,128)S(1)} %all-to-all-done.refs_1_.refs_0_, f32[16,16,256]{2,1,0:T(8,128)} %get-tuple-element.32.refs_2_.refs_1_), custom_call_target="tpu_custom_call" | custom-call | tf_op jit(solution)/shard_map/pallas_call | solution.py:689
  69.2 0.0 collective-permute-done.6.refs_10_
  69.2 2.1 %collective-permute-done.7.refs_11_ = f32[3,8,8,256]{3,2,1,0:T(8,128)S(1)} collective-permute-done((f32[3,8,8,256]{3,2,1,0:T(8,128)S(1)}, f32[3,8,8,256]{3,2,1,0:T(8,128)S(1)}, u32[]{:S(2)}, u32[]{:S(2)}) %collective-permute-start.7) | collective-permute-done | bytes 196640 | tf_op jit(solution)/shard_map/ppermute | solution.py:327
  71.3 4.6 %shard_map.138 = (f32[3,8,16,256]{3,2,1,0:T(8,128)}, f32[3,8,16,256]{3,2,1,0:T(8,128)}) custom-call(s32[2]{0:T(128)S(1)} %pad_add_fusion.refs_0_, s32[1]{0:T(128)} %bitcast.1.refs_0_.refs_1_, f32[3,8,16,256]{3,2,1,0:T(8,128)} %get-tuple-element.25.refs_2_, f32[3,8,16,256]{3,2,1,0:T(8,128)} %get-tuple-element.26.refs_3_, ...), custom_call_target="tpu_custom_call" | custom-call | tf_op jit(solution)/shard_map/pallas_call | solution.py:689
  (1 shorter events, 0.0 us)
Async XLA Ops:
  2.2 9.5 %collective-permute-start = (f32[5,8,8,256]{3,2,1,0:T(8,128)S(1)}, f32[5,8,8,256]{3,2,1,0:T(8,128)S(1)}, u32[]{:S(2)}, u32[]{:S(2)}) collective-permute-start(f32[5,8,8,256]{3,2,1,0:T(8,128)S(1)} %get-tuple-element.21), channel_id=1, source_target_pairs={{0,1},{2,3},{1,0},{3,2},{4,5},{6,7},{5,4},{7,6},{8,9},{10,11},{9,8... | collective-permute-start | bytes 983048 | tf_op jit(solution)/shard_map/ppermute | solution.py:327
  2.2 12.5 %collective-permute-start.1 = (f32[5,8,8,256]{3,2,1,0:T(8,128)S(1)}, f32[5,8,8,256]{3,2,1,0:T(8,128)S(1)}, u32[]{:S(2)}, u32[]{:S(2)}) collective-permute-start(f32[5,8,8,256]{3,2,1,0:T(8,128)S(1)} %get-tuple-element.22), channel_id=1, source_target_pairs={{1,2},{2,1},{5,6},{6,5},{9,10},{10,9},{13,14},{14,13},{17,18},{18,... | collective-permute-start | bytes 983048 | tf_op jit(solution)/shard_map/ppermute | solution.py:327
  17.6 31.2 %collective-permute-start.2 = (f32[48,16,256]{2,1,0:T(8,128)}, f32[48,16,256]{2,1,0:T(8,128)S(1)}, u32[]{:S(2)}, u32[]{:S(2)}) collective-permute-start(f32[48,16,256]{2,1,0:T(8,128)} %get-tuple-element.23), channel_id=1, source_target_pairs={{0,4},{8,12},{16,20},{24,28},{4,0},{12,8},{20,16},{28,24},{1,5},{9... | collective-permute-start | bytes 2359304 | tf_op jit(solution)/shard_map/ppermute | solution.py:327
  17.7 31.1 %collective-permute-start.3 = (f32[48,16,256]{2,1,0:T(8,128)S(1)}, f32[48,16,256]{2,1,0:T(8,128)S(1)}, u32[]{:S(2)}, u32[]{:S(2)}) collective-permute-start(f32[48,16,256]{2,1,0:T(8,128)S(1)} %get-tuple-element.24), channel_id=1, source_target_pairs={{4,8},{12,16},{20,24},{8,4},{16,12},{24,20},{5,9},{13,17},{21,25},... | collective-permute-start | bytes 2359304 | tf_op jit(solution)/shard_map/ppermute | solution.py:327
  18.4 4.0 %collective-permute-start.4 = (f32[8,1024]{1,0:T(8,128)S(1)}, f32[8,1024]{1,0:T(8,128)S(1)}, u32[]{:S(2)}, u32[]{:S(2)}) collective-permute-start(f32[8,1024]{1,0:T(8,128)S(1)} %get-tuple-element.28.refs_0_), channel_id=1, source_target_pairs={{0,1},{2,3},{1,0},{3,2},{4,5},{6,7},{5,4},{7,6},{8,9},{10,11},{9,8... | collective-permute-start | bytes 98312 | tf_op jit(solution)/shard_map/ppermute | solution.py:714
  22.4 10.4 %collective-permute-start.5 = (f32[8,2048]{1,0:T(8,128)S(1)}, f32[8,2048]{1,0:T(8,128)S(1)}, u32[]{:S(2)}, u32[]{:S(2)}) collective-permute-start(f32[8,2048]{1,0:T(8,128)S(1)} %pad_maximum_fusion), channel_id=1, source_target_pairs={{1,2},{2,1},{0,3},{3,0},{5,6},{6,5},{4,7},{7,4},{9,10},{10,9},{8,1... | collective-permute-start | bytes 196616 | tf_op jit(solution)/shard_map/ppermute | solution.py:717
  42.8 13.7 %all-to-all-start = ((f32[32,1,1664]{2,1,0:T(1,128)}), f32[32,1,1664]{2,1,0:T(1,128)S(1)}, u32[]{:S(2)}, u32[]{:S(2)}) async-start(f32[32,1,1664]{2,1,0:T(1,128)} %shard_map.135), calls=%async_computation | async-start | bytes 425984 | tf_op jit(solution)/shard_map/all_to_all | solution.py:753
  60.7 8.5 %collective-permute-start.6 = (f32[3,8,8,256]{3,2,1,0:T(8,128)S(1)}, f32[3,8,8,256]{3,2,1,0:T(8,128)S(1)}, u32[]{:S(2)}, u32[]{:S(2)}) collective-permute-start(f32[3,8,8,256]{3,2,1,0:T(8,128)S(1)} %get-tuple-element.38), channel_id=1, source_target_pairs={{0,1},{2,3},{1,0},{3,2},{4,5},{6,7},{5,4},{7,6},{8,9},{10,11},{9,8... | collective-permute-start | bytes 589832 | tf_op jit(solution)/shard_map/ppermute | solution.py:327
  62.9 8.4 %collective-permute-start.7 = (f32[3,8,8,256]{3,2,1,0:T(8,128)S(1)}, f32[3,8,8,256]{3,2,1,0:T(8,128)S(1)}, u32[]{:S(2)}, u32[]{:S(2)}) collective-permute-start(f32[3,8,8,256]{3,2,1,0:T(8,128)S(1)} %get-tuple-element.39), channel_id=1, source_target_pairs={{1,2},{2,1},{5,6},{6,5},{9,10},{10,9},{13,14},{14,13},{17,18},{18,... | collective-permute-start | bytes 589832 | tf_op jit(solution)/shard_map/ppermute | solution.py:327

commit v11 on v10

--- a/solution.py
+++ b/solution.py
@@ -122,10 +122,49 @@
     return total
 
 
-def first_incident_kernel(count, *refs):
-    par_refs, (right_ref, acc_ref, total_ref, u_ref) = refs[:count], refs[count:]
+def first_incident_kernel(count, ready, px_ref, *refs):
+    par_refs, refs = refs[:count], refs[count:]
+    right_ref, cur_ref, ear_ref, coef_ref, mask_ref, acc_ref, total_ref, even_out, odd_out, u_ref, face_ref = refs[:11]
+    load_sems, store_sems = refs[11:]
+    cx = mask_ref.shape[0]
+    sources = [cur_ref.at[i] for i in range(3)] + [ear_ref.at[i] for i in range(3)] + [coef_ref]
+    loads = []
+    for face in (0, 1):
+        for name, source in enumerate(sources):
+            planes = FIELD_PLAN[name][0]
+            first = sum(n for n, _ in FIELD_PLAN[:name])
+            x = cx - planes if face == 0 else 0
+            held = face_ref.at[face, pl.ds(first, planes)]
+            loads.append(pltpu.make_async_copy(source.at[pl.ds(x, planes)], held, load_sems.at[face, name]))
+    for copy in loads:
+        copy.start()
+
+    def stores(high_out, low_out):
+        return [
+            pltpu.make_async_copy(face_ref.at[face], out.at[pl.ds(0, SIDE_PLANES)], store_sems.at[face])
+            for face, out in ((0, high_out), (1, low_out))
+        ]
+
+    def each_store(act):
+        for parity, outs in ((0, (even_out, odd_out)), (1, (odd_out, even_out))):
+
+            @pl.when(px_ref[0] == parity)
+            def _():
+                for copy in stores(*outs):
+                    act(copy)
+
     acc_ref[...] = jnp.zeros(acc_ref.shape, F32)
-    total_ref[...] = add_components(par_refs, right_ref, acc_ref, u_ref)
+    total = add_components(par_refs[:1], right_ref, acc_ref, u_ref)
+    for copy in loads:
+        copy.wait()
+    ready()
+    for face in (0, 1):
+        for k in range(MID):
+            x = cx - MID + k if face == 0 else k
+            face_ref[face, SIDE_PLANES - MID + k] = sign_of(mask_ref[x])
+    each_store(lambda copy: copy.start())
+    total_ref[...] = total + add_components(par_refs[1:], right_ref, acc_ref, u_ref)
+    each_store(lambda copy: copy.wait())
 
 
 def last_incident_kernel(count, step, ready, *refs):
@@ -236,7 +275,7 @@
                     at += 2 * size
         return carry
 
-    lax.fori_loop(0, groups // 2, body, 0)
+    lax.fori_loop(0, groups // 2, body, 0, unroll=4)
 
 
 STEP_ROWS = ((0, 1, 2), (3, 4, 5), (7, 8, 9))
@@ -402,41 +441,29 @@
     return (mask == 1).astype(F32) - (mask == 2).astype(F32)
 
 
-def field_side_kernel(
-    ready, px_ref, py_ref, cur_ref, ear_ref, coef_ref, mask_ref, even_ref, odd_ref, even_out, odd_out, sems
+def corner_kernel(
+    px_ref, py_ref, even_ref, odd_ref, even_in, odd_in, even_out, odd_out, corner_ref, sems
 ):
-    cx, cy, nz = mask_ref.shape
+    cx, nz = even_ref.shape[1], even_ref.shape[3]
+    cy = corner_ref.shape[2]
     upper = row_ids((TILE, nz)) >= TILE // 2
     low = select_side(py_ref[0], even_ref, odd_ref, False)
     high = select_side(py_ref[0], even_ref, odd_ref, True)
-    sources = [cur_ref.at[i] for i in range(3)] + [ear_ref.at[i] for i in range(3)] + [coef_ref]
-
-    def run(high_out, low_out):
-        faces = ((True, 0, high_out), (False, 1, low_out))
-        copies = []
-        for is_high, face, out in faces:
-            for name, source in enumerate(sources):
-                planes = FIELD_PLAN[name][0]
-                first = sum(n for n, _ in FIELD_PLAN[:name])
-                x = cx - planes if is_high else 0
-                copies.append(
-                    pltpu.make_async_copy(
-                        source.at[pl.ds(x, planes)], out.at[pl.ds(first, planes)], sems.at[face, name]
-                    )
-                )
+    for face in (0, 1):
+        for k, (name, dist) in enumerate(CORNERS):
+            x = cx - dist if face == 0 else dist - 1
+            below = low(lambda ref: face_tile(ref, name, x))
+            above = high(lambda ref: face_tile(ref, name, x))
+            plane, rows = corner_place(k, cy)
+            corner_ref[face, plane - SIDE_PLANES, rows] = jnp.where(upper, below, above)
+    rest = pl.ds(SIDE_PLANES, corner_ref.shape[1])
+
+    def run(*outs):
+        copies = [
+            pltpu.make_async_copy(corner_ref.at[face], out.at[rest], sems.at[face]) for face, out in enumerate(outs)
+        ]
         for copy in copies:
             copy.start()
-        for is_high, face, out in faces:
-            for k, (name, dist) in enumerate(CORNERS):
-                x = cx - dist if is_high else dist - 1
-                below = low(lambda ref: face_tile(ref, name, x))
-                above = high(lambda ref: face_tile(ref, name, x))
-                plane, rows = corner_place(k, cy)
-                out[plane, rows] = jnp.where(upper, below, above)
-        ready()
-        for is_high, face, out in faces:
-            for k in range(MID):
-                out[SIDE_PLANES - MID + k] = sign_of(mask_ref[cx - MID + k if is_high else k])
         for copy in copies:
             copy.wait()
 
@@ -669,9 +696,10 @@
     smem = pl.BlockSpec(memory_space=pltpu.SMEM)
     vmem = pl.BlockSpec(memory_space=pltpu.VMEM)
 
-    def call(kernel, operands, shapes, scratch=(), scalars=0, from_hbm=(), left_in_hbm=(), to_hbm=False):
+    def call(kernel, operands, shapes, scratch=(), scalars=0, from_hbm=(), left_in_hbm=(), to_hbm=False, raw=0, aliases=None):
         kind = pltpu.HBM if to_hbm else jax.ShapeDtypeStruct
         shapes = [kind(shape, F32) if isinstance(shape, tuple) else shape for shape in shapes]
+        out_specs = [vmem] * (len(shapes) - raw) + [pl.BlockSpec(memory_space=pltpu.HBM)] * raw
         operands = list(operands)
         in_specs = [smem] * scalars + [vmem] * (len(operands) - scalars)
         scratch_shapes = [pltpu.VMEM(shape, F32) if isinstance(shape, tuple) else shape for shape in scratch]
@@ -690,7 +718,8 @@
             kernel,
             out_shape=shapes,
             in_specs=in_specs,
-            out_specs=[vmem] * len(shapes),
+            out_specs=out_specs,
+            input_output_aliases=aliases or {},
             scratch_shapes=scratch_shapes,
             compiler_params=pltpu.CompilerParams(vmem_limit_bytes=VMEM_GRANT),
         )(*operands)
@@ -723,21 +752,31 @@
             for k in range(1, comp_count)
         ]
     ye, yo = swap_faces(faces, "comp")
-    (sum_one, total_one) = call(
-        lambda *refs: first_incident_kernel(len(first_blocks), *refs),
-        (*first_blocks, right),
-        [(32, point_count), (16, KC)],
-        [(AHEAD, KC, KC)],
-    )
     sent = side_planes_sent(cy)
+    side_kind = pltpu.HBM((sent, cy, nz), F32)
+    count = len(first_blocks)
+    sum_one, total_one, *sides = call(
+        lambda *refs: first_incident_kernel(count, *refs),
+        (px, *first_blocks, right, *fields, layer_mask),
+        [(32, point_count), (16, KC), side_kind, side_kind],
+        [
+            (AHEAD, KC, KC), (2, SIDE_PLANES, cy, nz),
+            pltpu.SemaphoreType.DMA((2, len(FIELD_PLAN) - 1)), pltpu.SemaphoreType.DMA((2,)),
+        ],
+        scalars=1,
+        left_in_hbm=tuple(range(count + 2, count + 5)),
+        from_hbm=(count + 5,),
+        raw=2,
+    )
     sides = call(
-        field_side_kernel,
-        (px, py, *fields, layer_mask, ye, yo),
-        [(sent, cy, nz)] * 2,
-        [pltpu.SemaphoreType.DMA((2, len(FIELD_PLAN) - 1))],
+        corner_kernel,
+        (px, py, ye, yo, *sides),
+        [side_kind, side_kind],
+        [(2, sent - SIDE_PLANES, cy, nz), pltpu.SemaphoreType.DMA((2,))],
         scalars=2,
-        from_hbm=(5,),
-        left_in_hbm=(2, 3, 4),
+        left_in_hbm=(4, 5),
+        raw=2,
+        aliases={4: 0, 5: 1},
     )
     xe, xo = swap_faces(sides, "slab")
     (packed,) = call(

time: 76.2 us -> 74.2 us (0.974)
  starting transfers between devices: 18.4 us -> 22 us
  Pallas kernels: 42.3 us -> 38.9 us
  waiting for transfers between devices: 14.3 us -> 12.1 us
    ppermute x6, waiting for transfers between devices: 9.42 us -> 3.49 us  [swap_faces(): out.append(lax.ppermute(faces[k], axis, pair_list(count, k)))]
    all_to_all x1, starting transfers between devices: 5.98 us -> 9.66 us  [local(): lax.all_to_all(packed, ('slab', 'comp'), split_axis=0, concat_axis=0, til...]
    pallas_call x8, Pallas kernels: 42.3 us -> 38.9 us  [call(): pl.pallas_call(kernel, out_shape=shapes, in_specs=in_specs, out_specs=out...]
    ppermute x1, waiting for transfers between devices: 0.01 us -> 2.72 us  [local(): lax.ppermute(jnp.concatenate(first_blocks, axis=1), 'comp', ring)]
    ppermute x1, waiting for transfers between devices: 3.9 us -> 4.93 us  [local(): near_block = lax.ppermute(own_block, 'comp', pair_list(4, 0))]
where the time goes in v11:
time: 74.2 us; the launch traced here: 73.9 us
  Pallas kernels  38.9 us (52%)
  starting transfers between devices  22 us (30%)
  waiting for transfers between devices  12.1 us (16%)
  between operations  0.81 us (1%)
    pallas_call x8, Pallas kernels, call(): pl.pallas_call(kernel, out_shape=shapes, in_specs=in_specs, out_specs=out...  38.9 us
    ppermute x6, starting transfers between devices, swap_faces(): out.append(lax.ppermute(faces[k], axis, pair_list(count, k)))  10.6 us
    all_to_all x1, starting transfers between devices, local(): lax.all_to_all(packed, ('slab', 'comp'), split_axis=0, concat_axis=0, til...  9.66 us
    ppermute x1, waiting for transfers between devices, local(): near_block = lax.ppermute(own_block, 'comp', pair_list(4, 0))  4.93 us
    ppermute x6, waiting for transfers between devices, swap_faces(): out.append(lax.ppermute(faces[k], axis, pair_list(count, k)))  3.49 us
    ppermute x1, waiting for transfers between devices, local(): lax.ppermute(jnp.concatenate(first_blocks, axis=1), 'comp', ring)  2.72 us
    ppermute x1, starting transfers between devices, local(): lax.ppermute(jnp.concatenate(first_blocks, axis=1), 'comp', ring)  1.63 us
  transfers between devices with their start and end apart: 9, of which 5 were waited for; matrix products, arithmetic and copies ran while one was open for 0% of the time, Pallas kernels for 38%

profile of v11, /device:TPU:8, one launch (start us, length us, event | category | flops | bytes accessed | tf_op | source)
XLA Modules:
  0.0 73.9 jit_solution(1822112664027446791)
XLA Ops:
  0.6 1.5 %shard_map.131 = (f32[8,1024]{1,0:T(8,128)S(1)}, bf16[48,1024]{1,0:T(8,128)(2,1)S(1)}, f32[5,8,8,256]{3,2,1,0:T(8,128)S(1)}, f32[5,8,8,256]{3,2,1,0:T(8,128)S(1)}) custom-call(s32[1]{0:T(128)} %bitcast.1.refs_0_.py_ref.refs_1_, f32[3,8,16,256]{3,2,1,0:T(8,128)} %refs_2_.3, f32[3,8,16,256]{3,2,1,0:T(8,128)} %refs_3_.3, f32[8,16,256]{2,1,0:T(8,128)} %refs_4_.5, ...), custom_call_target="tpu_custom_call" | custom-call | tf_op jit(solution)/shard_map/pallas_call | solution.py:717
  2.2 0.1 collective-permute-start
  2.2 5.0 %collective-permute-start.1 = (f32[5,8,8,256]{3,2,1,0:T(8,128)S(1)}, f32[5,8,8,256]{3,2,1,0:T(8,128)S(1)}, u32[]{:S(2)}, u32[]{:S(2)}) collective-permute-start(f32[5,8,8,256]{3,2,1,0:T(8,128)S(1)} %get-tuple-element.24), channel_id=1, source_target_pairs={{1,2},{2,1},{5,6},{6,5},{9,10},{10,9},{13,14},{14,13},{17,18},{18,... | collective-permute-start | bytes 983048 | tf_op jit(solution)/shard_map/ppermute | solution.py:366
  7.3 0.1 collective-permute-start.2
  7.4 0.1 pad_add_fusion.refs_0_.px_ref
  7.5 4.9 %collective-permute-done.2.refs_2_ = f32[8,1024]{1,0:T(8,128)S(1)} collective-permute-done((f32[8,1024]{1,0:T(8,128)S(1)}, f32[8,1024]{1,0:T(8,128)S(1)}, u32[]{:S(2)}, u32[]{:S(2)}) %collective-permute-start.2) | collective-permute-done | bytes 32800 | tf_op jit(solution)/shard_map/ppermute | solution.py:743
  12.4 9.5 %shard_map.132 = (f32[32,1024]{1,0:T(8,128)S(1)}, f32[16,256]{1,0:T(8,128)S(1)}, f32[48,16,256]{2,1,0:T(8,128)}, f32[48,16,256]{2,1,0:T(8,128)}) custom-call(s32[2]{0:T(128)S(1)} %pad_add_fusion.refs_0_.px_ref, f32[8,1024]{1,0:T(8,128)S(1)} %get-tuple-element.25.refs_1_, f32[8,1024]{1,0:T(8,128)S(1)} %collective-permute-done.2.refs_2_, ...), custom_call_target="tpu_custom_call" | custom-call | tf_op jit(solution)/shard_map/pallas_call | solution.py:717
  21.8 0.0 collective-permute-done.even_ref.refs_6_
  21.9 0.0 collective-permute-done.1.odd_ref.refs_7_
  21.9 1.3 %shard_map.133 = (f32[48,16,256]{2,1,0:T(8,128)}, f32[48,16,256]{2,1,0:T(8,128)}) custom-call(s32[2]{0:T(128)S(1)} %pad_add_fusion.refs_0_.px_ref, s32[1]{0:T(128)} %bitcast.1.refs_0_.py_ref.refs_1_, f32[5,8,8,256]{3,2,1,0:T(8,128)S(1)} %collective-permute-done.even_ref.refs_6_, ...), custom_call_target="tpu_custom_call", output_to_operand_aliasing={{0}: (4, {}), {1}: (5, {})} | custom-call | tf_op jit(solution)/shard_map/pallas_call | solution.py:717
  23.2 0.1 collective-permute-start.3
  23.3 0.7 collective-permute-start.4
  24.0 1.6 %collective-permute-start.5 = (f32[8,2048]{1,0:T(8,128)S(1)}, f32[8,2048]{1,0:T(8,128)S(1)}, u32[]{:S(2)}, u32[]{:S(2)}) collective-permute-start(f32[8,2048]{1,0:T(8,128)S(1)} %pad_maximum_fusion), channel_id=1, source_target_pairs={{1,2},{2,1},{0,3},{3,0},{5,6},{6,5},{4,7},{7,4},{9,10},{10,9},{8,1... | collective-permute-start | bytes 196616 | tf_op jit(solution)/shard_map/ppermute | solution.py:746
  25.7 2.7 %collective-permute-done.5.refs_0_ = f32[8,2048]{1,0:T(8,128)S(1)} collective-permute-done((f32[8,2048]{1,0:T(8,128)S(1)}, f32[8,2048]{1,0:T(8,128)S(1)}, u32[]{:S(2)}, u32[]{:S(2)}) %collective-permute-start.5) | collective-permute-done | bytes 65568 | tf_op jit(solution)/shard_map/ppermute | solution.py:746
  28.4 10.0 %shard_map.135 = f32[32,1,1664]{2,1,0:T(1,128)} custom-call(f32[8,2048]{1,0:T(8,128)S(1)} %collective-permute-done.5.refs_0_, f32[32,1024]{1,0:T(8,128)S(1)} %get-tuple-element.34.refs_1_, f32[16,256]{1,0:T(8,128)S(1)} %get-tuple-element.35.refs_2_, bf16[48,1024]{1,0:T(8,128)(2,1)S(1)} %get-tuple-element.26.refs_3_, s32[1,1024]{1,0:T(1,128)} %bitcast.9, ...), custom_call_target="tpu_custom_call" | custom-call | tf_op jit(solution)/shard_map/pallas_call | solution.py:717
  38.3 9.7 %all-to-all-start = ((f32[32,1,1664]{2,1,0:T(1,128)}), f32[32,1,1664]{2,1,0:T(1,128)S(1)}, u32[]{:S(2)}, u32[]{:S(2)}) async-start(f32[32,1,1664]{2,1,0:T(1,128)} %shard_map.135), calls=%async_computation | async-start | bytes 425984 | tf_op jit(solution)/shard_map/all_to_all | solution.py:792
  48.0 0.0 collective-permute-done.3.refs_8_
  48.0 0.0 collective-permute-done.4.refs_9_
  48.0 6.6 %shard_map.134 = (f32[3,8,16,256]{3,2,1,0:T(8,128)}, f32[3,8,16,256]{3,2,1,0:T(8,128)}, f32[12,2,32,128]{3,2,1,0:T(8,128)}, f32[16,16,256]{2,1,0:T(8,128)}) custom-call(s32[2]{0:T(128)S(1)} %pad_add_fusion.refs_0_.px_ref, s32[1]{0:T(128)} %bitcast.1.refs_0_.py_ref.refs_1_, f32[3,8,16,256]{3,2,1,0:T(8,128)} %refs_2_.3, f32[3,8,16,256]{3,2,1,0:T(8,128)} %refs_3_.3, ...), custom_call_target="tpu_custom_call" | custom-call | tf_op jit(solution)/shard_map/pallas_call | solution.py:717
  54.7 1.0 %all-to-all-done.refs_1_.refs_0_ = f32[32,1,1664]{2,1,0:T(1,128)S(1)} async-done(((f32[32,1,1664]{2,1,0:T(1,128)}), f32[32,1,1664]{2,1,0:T(1,128)S(1)}, u32[]{:S(2)}, u32[]{:S(2)}) %all-to-all-start) | async-done | bytes 213024 | tf_op jit(solution)/shard_map/all_to_all | solution.py:792
  55.7 3.0 %shard_map.136 = (f32[3,12,16,256]{3,2,1,0:T(8,128)S(1)}, f32[3,8,16,256]{3,2,1,0:T(8,128)S(1)}, f32[3,8,8,256]{3,2,1,0:T(8,128)S(1)}, f32[3,8,8,256]{3,2,1,0:T(8,128)S(1)}) custom-call(s32[1]{0:T(128)} %bitcast.1.refs_0_.py_ref.refs_1_, f32[32,1,1664]{2,1,0:T(1,128)S(1)} %all-to-all-done.refs_1_.refs_0_, f32[16,16,256]{2,1,0:T(8,128)} %get-tuple-element.36.refs_2_.refs_1_), custom_call_target="tpu_custom_call" | custom-call | tf_op jit(solution)/shard_map/pallas_call | solution.py:717
  58.7 2.2 %collective-permute-start.6 = (f32[3,8,8,256]{3,2,1,0:T(8,128)S(1)}, f32[3,8,8,256]{3,2,1,0:T(8,128)S(1)}, u32[]{:S(2)}, u32[]{:S(2)}) collective-permute-start(f32[3,8,8,256]{3,2,1,0:T(8,128)S(1)} %get-tuple-element.42), channel_id=1, source_target_pairs={{0,1},{2,3},{1,0},{3,2},{4,5},{6,7},{5,4},{7,6},{8,9},{10,11},{9,8... | collective-permute-start | bytes 589832 | tf_op jit(solution)/shard_map/ppermute | solution.py:366
  60.9 2.5 %collective-permute-start.7 = (f32[3,8,8,256]{3,2,1,0:T(8,128)S(1)}, f32[3,8,8,256]{3,2,1,0:T(8,128)S(1)}, u32[]{:S(2)}, u32[]{:S(2)}) collective-permute-start(f32[3,8,8,256]{3,2,1,0:T(8,128)S(1)} %get-tuple-element.43), channel_id=1, source_target_pairs={{1,2},{2,1},{5,6},{6,5},{9,10},{10,9},{13,14},{14,13},{17,18},{18,... | collective-permute-start | bytes 589832 | tf_op jit(solution)/shard_map/ppermute | solution.py:366
  63.4 2.4 %shard_map.137 = (f32[3,4,16,256]{3,2,1,0:T(8,128)S(1)}, f32[3,4,16,256]{3,2,1,0:T(8,128)S(1)}, f32[3,8,16,256]{3,2,1,0:T(8,128)S(1)}) custom-call(f32[32,1,1664]{2,1,0:T(1,128)S(1)} %all-to-all-done.refs_1_.refs_0_, f32[16,16,256]{2,1,0:T(8,128)} %get-tuple-element.36.refs_2_.refs_1_), custom_call_target="tpu_custom_call" | custom-call | tf_op jit(solution)/shard_map/pallas_call | solution.py:717
  65.9 0.1 collective-permute-done.6.refs_10_
  66.0 3.3 %collective-permute-done.7.refs_11_ = f32[3,8,8,256]{3,2,1,0:T(8,128)S(1)} collective-permute-done((f32[3,8,8,256]{3,2,1,0:T(8,128)S(1)}, f32[3,8,8,256]{3,2,1,0:T(8,128)S(1)}, u32[]{:S(2)}, u32[]{:S(2)}) %collective-permute-start.7) | collective-permute-done | bytes 196640 | tf_op jit(solution)/shard_map/ppermute | solution.py:366
  69.3 4.6 %shard_map.138 = (f32[3,8,16,256]{3,2,1,0:T(8,128)}, f32[3,8,16,256]{3,2,1,0:T(8,128)}) custom-call(s32[2]{0:T(128)S(1)} %pad_add_fusion.refs_0_.px_ref, s32[1]{0:T(128)} %bitcast.1.refs_0_.py_ref.refs_1_, f32[3,8,16,256]{3,2,1,0:T(8,128)} %get-tuple-element.31.refs_2_, f32[3,8,16,256]{3,2,1,0:T(8,128)} %get-tuple-element.32.refs_3_, ...), custom_call_target="tpu_custom_call" | custom-call | tf_op jit(solution)/shard_map/pallas_call | solution.py:717
  (1 shorter events, 0.0 us)
Async XLA Ops:
  2.2 19.7 %collective-permute-start = (f32[5,8,8,256]{3,2,1,0:T(8,128)S(1)}, f32[5,8,8,256]{3,2,1,0:T(8,128)S(1)}, u32[]{:S(2)}, u32[]{:S(2)}) collective-permute-start(f32[5,8,8,256]{3,2,1,0:T(8,128)S(1)} %get-tuple-element.23), channel_id=1, source_target_pairs={{0,1},{2,3},{1,0},{3,2},{4,5},{6,7},{5,4},{7,6},{8,9},{10,11},{9,8... | collective-permute-start | bytes 983048 | tf_op jit(solution)/shard_map/ppermute | solution.py:366
  2.2 19.6 %collective-permute-start.1 = (f32[5,8,8,256]{3,2,1,0:T(8,128)S(1)}, f32[5,8,8,256]{3,2,1,0:T(8,128)S(1)}, u32[]{:S(2)}, u32[]{:S(2)}) collective-permute-start(f32[5,8,8,256]{3,2,1,0:T(8,128)S(1)} %get-tuple-element.24), channel_id=1, source_target_pairs={{1,2},{2,1},{5,6},{6,5},{9,10},{10,9},{13,14},{14,13},{17,18},{18,... | collective-permute-start | bytes 983048 | tf_op jit(solution)/shard_map/ppermute | solution.py:366
  7.3 5.1 %collective-permute-start.2 = (f32[8,1024]{1,0:T(8,128)S(1)}, f32[8,1024]{1,0:T(8,128)S(1)}, u32[]{:S(2)}, u32[]{:S(2)}) collective-permute-start(f32[8,1024]{1,0:T(8,128)S(1)} %get-tuple-element.25.refs_1_), channel_id=1, source_target_pairs={{0,1},{2,3},{1,0},{3,2},{4,5},{6,7},{5,4},{7,6},{8,9},{10,11},{9,8... | collective-permute-start | bytes 98312 | tf_op jit(solution)/shard_map/ppermute | solution.py:743
  23.2 24.8 %collective-permute-start.3 = (f32[48,16,256]{2,1,0:T(8,128)}, f32[48,16,256]{2,1,0:T(8,128)S(1)}, u32[]{:S(2)}, u32[]{:S(2)}) collective-permute-start(f32[48,16,256]{2,1,0:T(8,128)} %get-tuple-element.29), channel_id=1, source_target_pairs={{0,4},{8,12},{16,20},{24,28},{4,0},{12,8},{20,16},{28,24},{1,5},{9... | collective-permute-start | bytes 2359304 | tf_op jit(solution)/shard_map/ppermute | solution.py:366
  23.3 24.7 %collective-permute-start.4 = (f32[48,16,256]{2,1,0:T(8,128)}, f32[48,16,256]{2,1,0:T(8,128)S(1)}, u32[]{:S(2)}, u32[]{:S(2)}) collective-permute-start(f32[48,16,256]{2,1,0:T(8,128)} %get-tuple-element.30), channel_id=1, source_target_pairs={{4,8},{12,16},{20,24},{8,4},{16,12},{24,20},{5,9},{13,17},{21,25},... | collective-permute-start | bytes 2359304 | tf_op jit(solution)/shard_map/ppermute | solution.py:366
  24.0 4.3 %collective-permute-start.5 = (f32[8,2048]{1,0:T(8,128)S(1)}, f32[8,2048]{1,0:T(8,128)S(1)}, u32[]{:S(2)}, u32[]{:S(2)}) collective-permute-start(f32[8,2048]{1,0:T(8,128)S(1)} %pad_maximum_fusion), channel_id=1, source_target_pairs={{1,2},{2,1},{0,3},{3,0},{5,6},{6,5},{4,7},{7,4},{9,10},{10,9},{8,1... | collective-permute-start | bytes 196616 | tf_op jit(solution)/shard_map/ppermute | solution.py:746
  38.3 17.3 %all-to-all-start = ((f32[32,1,1664]{2,1,0:T(1,128)}), f32[32,1,1664]{2,1,0:T(1,128)S(1)}, u32[]{:S(2)}, u32[]{:S(2)}) async-start(f32[32,1,1664]{2,1,0:T(1,128)} %shard_map.135), calls=%async_computation | async-start | bytes 425984 | tf_op jit(solution)/shard_map/all_to_all | solution.py:792
  58.7 7.3 %collective-permute-start.6 = (f32[3,8,8,256]{3,2,1,0:T(8,128)S(1)}, f32[3,8,8,256]{3,2,1,0:T(8,128)S(1)}, u32[]{:S(2)}, u32[]{:S(2)}) collective-permute-start(f32[3,8,8,256]{3,2,1,0:T(8,128)S(1)} %get-tuple-element.42), channel_id=1, source_target_pairs={{0,1},{2,3},{1,0},{3,2},{4,5},{6,7},{5,4},{7,6},{8,9},{10,11},{9,8... | collective-permute-start | bytes 589832 | tf_op jit(solution)/shard_map/ppermute | solution.py:366
  60.9 8.4 %collective-permute-start.7 = (f32[3,8,8,256]{3,2,1,0:T(8,128)S(1)}, f32[3,8,8,256]{3,2,1,0:T(8,128)S(1)}, u32[]{:S(2)}, u32[]{:S(2)}) collective-permute-start(f32[3,8,8,256]{3,2,1,0:T(8,128)S(1)} %get-tuple-element.43), channel_id=1, source_target_pairs={{1,2},{2,1},{5,6},{6,5},{9,10},{10,9},{13,14},{14,13},{17,18},{18,... | collective-permute-start | bytes 589832 | tf_op jit(solution)/shard_map/ppermute | solution.py:366

commit v12 on v11

--- a/solution.py
+++ b/solution.py
@@ -595,9 +595,9 @@
 
 def last_wave_kernel(
     ready, px_ref, py_ref, free_final_ref, free_prior_ref, coef_ref, zero_in, zero_far_in, one_in, one_side_in, two_in,
-    ye_ref, yo_ref, final_ref, prior_ref, one_ref, two_ref,
+    ye_ref, yo_ref, final_out, prior_out, one_ref, two_ref, final_ref, prior_ref, sems,
 ):
-    _, cx, cy, _ = two_in.shape
+    _, cx, cy, nz = two_in.shape
     own = slice(TILE, TILE + cy)
     lower, higher = slice(0, TILE), slice(TILE + cy, 2 * TILE + cy)
     low = select_side(py_ref[0], ye_ref, yo_ref, False)
@@ -636,13 +636,28 @@
                 lanes = slice(h * LANES, (h + 1) * LANES)
                 moved = 2.0 * c - one_ref[i, x + MID, h, own] + coef_ref[x + NEAR, h, own] * l
                 final_ref[i, x, :, lanes] = free_final_ref[i, x, :, lanes] + (moved + two_in[i, x, :, lanes])
-                prior_ref[i, x, :, lanes] = free_prior_ref[i, x, :, lanes] + c
+
+    def keep(x):
+        for i in range(3):
+            for h in range(nz // LANES):
+                lanes = slice(h * LANES, (h + 1) * LANES)
+                prior_ref[i, x, :, lanes] = free_prior_ref[i, x, :, lanes] + two_ref[i, x + NEAR, h, own]
 
     ready()
     run_planes(0, NEAR, second(TILE, cy))
     run_planes(NEAR, cx + NEAR, second(px_ref[1], cy + TILE))
     run_planes(cx + NEAR, cx + 2 * NEAR, second(TILE, cy))
-    run_planes(0, cx, third)
+    run_planes(0, cx, keep)
+    copies = [pltpu.make_async_copy(prior_ref, prior_out, sems.at[0])]
+    copies[0].start()
+    for part, (begin, end) in enumerate(((0, cx // 2), (cx // 2, cx))):
+        run_planes(begin, end, third)
+        planes = pl.ds(begin, end - begin)
+        copy = pltpu.make_async_copy(final_ref.at[:, planes], final_out.at[:, planes], sems.at[1 + part])
+        copy.start()
+        copies.append(copy)
+    for copy in copies:
+        copy.wait()
 
 
 def staged(kernel, positions, operand_count):
@@ -823,9 +838,14 @@
         last_wave_kernel,
         (px, py, free_final, free_prior, wide_coef, zero, zero_far, one, one_side, two, fye, fyo),
         [current_field.shape, current_field.shape],
-        [plane_stack(3, cx + 2 * MID), plane_stack(3, cx + 2 * NEAR)],
+        [
+            plane_stack(3, cx + 2 * MID), plane_stack(3, cx + 2 * NEAR),
+            current_field.shape, current_field.shape, pltpu.SemaphoreType.DMA((3,)),
+        ],
         scalars=2,
         from_hbm=(2, 3, 4),
+        to_hbm=True,
+        raw=2,
     )
     return (final, prior)
 

time: 74.2 us -> 74.2 us (level)
  no operation moved by 1% of the time
where the time goes in v12:
time: 74.2 us; the launch traced here: 73.9 us
  Pallas kernels  38.9 us (52%)
  starting transfers between devices  22 us (30%)
  waiting for transfers between devices  12.1 us (16%)
  between operations  0.81 us (1%)
    pallas_call x8, Pallas kernels, call(): pl.pallas_call(kernel, out_shape=shapes, in_specs=in_specs, out_specs=out...  38.9 us
    ppermute x6, starting transfers between devices, swap_faces(): out.append(lax.ppermute(faces[k], axis, pair_list(count, k)))  10.6 us
    all_to_all x1, starting transfers between devices, local(): lax.all_to_all(packed, ('slab', 'comp'), split_axis=0, concat_axis=0, til...  9.66 us
    ppermute x1, waiting for transfers between devices, local(): near_block = lax.ppermute(own_block, 'comp', pair_list(4, 0))  4.93 us
    ppermute x6, waiting for transfers between devices, swap_faces(): out.append(lax.ppermute(faces[k], axis, pair_list(count, k)))  3.49 us
    ppermute x1, waiting for transfers between devices, local(): lax.ppermute(jnp.concatenate(first_blocks, axis=1), 'comp', ring)  2.72 us
    ppermute x1, starting transfers between devices, local(): lax.ppermute(jnp.concatenate(first_blocks, axis=1), 'comp', ring)  1.63 us
  transfers between devices with their start and end apart: 9, of which 5 were waited for; matrix products, arithmetic and copies ran while one was open for 0% of the time, Pallas kernels for 38%

profile of v12, /device:TPU:8, one launch (start us, length us, event | category | flops | bytes accessed | tf_op | source)
XLA Modules:
  0.0 73.9 jit_solution(6086297805367714857)
XLA Ops:
  0.6 1.5 %shard_map.131 = (f32[8,1024]{1,0:T(8,128)S(1)}, bf16[48,1024]{1,0:T(8,128)(2,1)S(1)}, f32[5,8,8,256]{3,2,1,0:T(8,128)S(1)}, f32[5,8,8,256]{3,2,1,0:T(8,128)S(1)}) custom-call(s32[1]{0:T(128)} %bitcast.1.refs_0_.py_ref.refs_1_, f32[3,8,16,256]{3,2,1,0:T(8,128)} %refs_2_.3, f32[3,8,16,256]{3,2,1,0:T(8,128)} %refs_3_.3, f32[8,16,256]{2,1,0:T(8,128)} %refs_4_.5, ...), custom_call_target="tpu_custom_call" | custom-call | tf_op jit(solution)/shard_map/pallas_call | solution.py:732
  2.2 0.1 collective-permute-start
  2.2 5.0 %collective-permute-start.1 = (f32[5,8,8,256]{3,2,1,0:T(8,128)S(1)}, f32[5,8,8,256]{3,2,1,0:T(8,128)S(1)}, u32[]{:S(2)}, u32[]{:S(2)}) collective-permute-start(f32[5,8,8,256]{3,2,1,0:T(8,128)S(1)} %get-tuple-element.24), channel_id=1, source_target_pairs={{1,2},{2,1},{5,6},{6,5},{9,10},{10,9},{13,14},{14,13},{17,18},{18,... | collective-permute-start | bytes 983048 | tf_op jit(solution)/shard_map/ppermute | solution.py:366
  7.3 0.1 collective-permute-start.2
  7.4 0.1 pad_add_fusion.refs_0_.px_ref
  7.5 4.9 %collective-permute-done.2.refs_2_ = f32[8,1024]{1,0:T(8,128)S(1)} collective-permute-done((f32[8,1024]{1,0:T(8,128)S(1)}, f32[8,1024]{1,0:T(8,128)S(1)}, u32[]{:S(2)}, u32[]{:S(2)}) %collective-permute-start.2) | collective-permute-done | bytes 32800 | tf_op jit(solution)/shard_map/ppermute | solution.py:758
  12.4 9.5 %shard_map.132 = (f32[32,1024]{1,0:T(8,128)S(1)}, f32[16,256]{1,0:T(8,128)S(1)}, f32[48,16,256]{2,1,0:T(8,128)}, f32[48,16,256]{2,1,0:T(8,128)}) custom-call(s32[2]{0:T(128)S(1)} %pad_add_fusion.refs_0_.px_ref, f32[8,1024]{1,0:T(8,128)S(1)} %get-tuple-element.25.refs_1_, f32[8,1024]{1,0:T(8,128)S(1)} %collective-permute-done.2.refs_2_, ...), custom_call_target="tpu_custom_call" | custom-call | tf_op jit(solution)/shard_map/pallas_call | solution.py:732
  21.8 0.0 collective-permute-done.even_ref.refs_6_
  21.9 0.0 collective-permute-done.1.odd_ref.refs_7_
  21.9 1.3 %shard_map.133 = (f32[48,16,256]{2,1,0:T(8,128)}, f32[48,16,256]{2,1,0:T(8,128)}) custom-call(s32[2]{0:T(128)S(1)} %pad_add_fusion.refs_0_.px_ref, s32[1]{0:T(128)} %bitcast.1.refs_0_.py_ref.refs_1_, f32[5,8,8,256]{3,2,1,0:T(8,128)S(1)} %collective-permute-done.even_ref.refs_6_, ...), custom_call_target="tpu_custom_call", output_to_operand_aliasing={{0}: (4, {}), {1}: (5, {})} | custom-call | tf_op jit(solution)/shard_map/pallas_call | solution.py:732
  23.2 0.1 collective-permute-start.3
  23.3 0.7 collective-permute-start.4
  24.0 1.6 %collective-permute-start.5 = (f32[8,2048]{1,0:T(8,128)S(1)}, f32[8,2048]{1,0:T(8,128)S(1)}, u32[]{:S(2)}, u32[]{:S(2)}) collective-permute-start(f32[8,2048]{1,0:T(8,128)S(1)} %pad_maximum_fusion), channel_id=1, source_target_pairs={{1,2},{2,1},{0,3},{3,0},{5,6},{6,5},{4,7},{7,4},{9,10},{10,9},{8,1... | collective-permute-start | bytes 196616 | tf_op jit(solution)/shard_map/ppermute | solution.py:761
  25.7 2.7 %collective-permute-done.5.refs_0_ = f32[8,2048]{1,0:T(8,128)S(1)} collective-permute-done((f32[8,2048]{1,0:T(8,128)S(1)}, f32[8,2048]{1,0:T(8,128)S(1)}, u32[]{:S(2)}, u32[]{:S(2)}) %collective-permute-start.5) | collective-permute-done | bytes 65568 | tf_op jit(solution)/shard_map/ppermute | solution.py:761
  28.4 10.0 %shard_map.135 = f32[32,1,1664]{2,1,0:T(1,128)} custom-call(f32[8,2048]{1,0:T(8,128)S(1)} %collective-permute-done.5.refs_0_, f32[32,1024]{1,0:T(8,128)S(1)} %get-tuple-element.34.refs_1_, f32[16,256]{1,0:T(8,128)S(1)} %get-tuple-element.35.refs_2_, bf16[48,1024]{1,0:T(8,128)(2,1)S(1)} %get-tuple-element.26.refs_3_, s32[1,1024]{1,0:T(1,128)} %bitcast.9, ...), custom_call_target="tpu_custom_call" | custom-call | tf_op jit(solution)/shard_map/pallas_call | solution.py:732
  38.3 9.7 %all-to-all-start = ((f32[32,1,1664]{2,1,0:T(1,128)}), f32[32,1,1664]{2,1,0:T(1,128)S(1)}, u32[]{:S(2)}, u32[]{:S(2)}) async-start(f32[32,1,1664]{2,1,0:T(1,128)} %shard_map.135), calls=%async_computation | async-start | bytes 425984 | tf_op jit(solution)/shard_map/all_to_all | solution.py:807
  48.0 0.0 collective-permute-done.3.refs_8_
  48.0 0.0 collective-permute-done.4.refs_9_
  48.0 6.6 %shard_map.134 = (f32[3,8,16,256]{3,2,1,0:T(8,128)}, f32[3,8,16,256]{3,2,1,0:T(8,128)}, f32[12,2,32,128]{3,2,1,0:T(8,128)}, f32[16,16,256]{2,1,0:T(8,128)}) custom-call(s32[2]{0:T(128)S(1)} %pad_add_fusion.refs_0_.px_ref, s32[1]{0:T(128)} %bitcast.1.refs_0_.py_ref.refs_1_, f32[3,8,16,256]{3,2,1,0:T(8,128)} %refs_2_.3, f32[3,8,16,256]{3,2,1,0:T(8,128)} %refs_3_.3, ...), custom_call_target="tpu_custom_call" | custom-call | tf_op jit(solution)/shard_map/pallas_call | solution.py:732
  54.7 1.0 %all-to-all-done.refs_1_.refs_0_ = f32[32,1,1664]{2,1,0:T(1,128)S(1)} async-done(((f32[32,1,1664]{2,1,0:T(1,128)}), f32[32,1,1664]{2,1,0:T(1,128)S(1)}, u32[]{:S(2)}, u32[]{:S(2)}) %all-to-all-start) | async-done | bytes 213024 | tf_op jit(solution)/shard_map/all_to_all | solution.py:807
  55.7 3.0 %shard_map.136 = (f32[3,12,16,256]{3,2,1,0:T(8,128)S(1)}, f32[3,8,16,256]{3,2,1,0:T(8,128)S(1)}, f32[3,8,8,256]{3,2,1,0:T(8,128)S(1)}, f32[3,8,8,256]{3,2,1,0:T(8,128)S(1)}) custom-call(s32[1]{0:T(128)} %bitcast.1.refs_0_.py_ref.refs_1_, f32[32,1,1664]{2,1,0:T(1,128)S(1)} %all-to-all-done.refs_1_.refs_0_, f32[16,16,256]{2,1,0:T(8,128)} %get-tuple-element.36.refs_2_.refs_1_), custom_call_target="tpu_custom_call" | custom-call | tf_op jit(solution)/shard_map/pallas_call | solution.py:732
  58.7 2.2 %collective-permute-start.6 = (f32[3,8,8,256]{3,2,1,0:T(8,128)S(1)}, f32[3,8,8,256]{3,2,1,0:T(8,128)S(1)}, u32[]{:S(2)}, u32[]{:S(2)}) collective-permute-start(f32[3,8,8,256]{3,2,1,0:T(8,128)S(1)} %get-tuple-element.42), channel_id=1, source_target_pairs={{0,1},{2,3},{1,0},{3,2},{4,5},{6,7},{5,4},{7,6},{8,9},{10,11},{9,8... | collective-permute-start | bytes 589832 | tf_op jit(solution)/shard_map/ppermute | solution.py:366
  60.9 2.5 %collective-permute-start.7 = (f32[3,8,8,256]{3,2,1,0:T(8,128)S(1)}, f32[3,8,8,256]{3,2,1,0:T(8,128)S(1)}, u32[]{:S(2)}, u32[]{:S(2)}) collective-permute-start(f32[3,8,8,256]{3,2,1,0:T(8,128)S(1)} %get-tuple-element.43), channel_id=1, source_target_pairs={{1,2},{2,1},{5,6},{6,5},{9,10},{10,9},{13,14},{14,13},{17,18},{18,... | collective-permute-start | bytes 589832 | tf_op jit(solution)/shard_map/ppermute | solution.py:366
  63.4 2.4 %shard_map.137 = (f32[3,4,16,256]{3,2,1,0:T(8,128)S(1)}, f32[3,4,16,256]{3,2,1,0:T(8,128)S(1)}, f32[3,8,16,256]{3,2,1,0:T(8,128)S(1)}) custom-call(f32[32,1,1664]{2,1,0:T(1,128)S(1)} %all-to-all-done.refs_1_.refs_0_, f32[16,16,256]{2,1,0:T(8,128)} %get-tuple-element.36.refs_2_.refs_1_), custom_call_target="tpu_custom_call" | custom-call | tf_op jit(solution)/shard_map/pallas_call | solution.py:732
  65.9 0.1 collective-permute-done.6.refs_10_
  66.0 3.3 %collective-permute-done.7.refs_11_ = f32[3,8,8,256]{3,2,1,0:T(8,128)S(1)} collective-permute-done((f32[3,8,8,256]{3,2,1,0:T(8,128)S(1)}, f32[3,8,8,256]{3,2,1,0:T(8,128)S(1)}, u32[]{:S(2)}, u32[]{:S(2)}) %collective-permute-start.7) | collective-permute-done | bytes 196640 | tf_op jit(solution)/shard_map/ppermute | solution.py:366
  69.3 4.6 %shard_map.138 = (f32[3,8,16,256]{3,2,1,0:T(8,128)}, f32[3,8,16,256]{3,2,1,0:T(8,128)}) custom-call(s32[2]{0:T(128)S(1)} %pad_add_fusion.refs_0_.px_ref, s32[1]{0:T(128)} %bitcast.1.refs_0_.py_ref.refs_1_, f32[3,8,16,256]{3,2,1,0:T(8,128)} %get-tuple-element.31.refs_2_, f32[3,8,16,256]{3,2,1,0:T(8,128)} %get-tuple-element.32.refs_3_, ...), custom_call_target="tpu_custom_call" | custom-call | tf_op jit(solution)/shard_map/pallas_call | solution.py:732
  (1 shorter events, 0.0 us)
Async XLA Ops:
  2.2 19.7 %collective-permute-start = (f32[5,8,8,256]{3,2,1,0:T(8,128)S(1)}, f32[5,8,8,256]{3,2,1,0:T(8,128)S(1)}, u32[]{:S(2)}, u32[]{:S(2)}) collective-permute-start(f32[5,8,8,256]{3,2,1,0:T(8,128)S(1)} %get-tuple-element.23), channel_id=1, source_target_pairs={{0,1},{2,3},{1,0},{3,2},{4,5},{6,7},{5,4},{7,6},{8,9},{10,11},{9,8... | collective-permute-start | bytes 983048 | tf_op jit(solution)/shard_map/ppermute | solution.py:366
  2.2 19.6 %collective-permute-start.1 = (f32[5,8,8,256]{3,2,1,0:T(8,128)S(1)}, f32[5,8,8,256]{3,2,1,0:T(8,128)S(1)}, u32[]{:S(2)}, u32[]{:S(2)}) collective-permute-start(f32[5,8,8,256]{3,2,1,0:T(8,128)S(1)} %get-tuple-element.24), channel_id=1, source_target_pairs={{1,2},{2,1},{5,6},{6,5},{9,10},{10,9},{13,14},{14,13},{17,18},{18,... | collective-permute-start | bytes 983048 | tf_op jit(solution)/shard_map/ppermute | solution.py:366
  7.3 5.1 %collective-permute-start.2 = (f32[8,1024]{1,0:T(8,128)S(1)}, f32[8,1024]{1,0:T(8,128)S(1)}, u32[]{:S(2)}, u32[]{:S(2)}) collective-permute-start(f32[8,1024]{1,0:T(8,128)S(1)} %get-tuple-element.25.refs_1_), channel_id=1, source_target_pairs={{0,1},{2,3},{1,0},{3,2},{4,5},{6,7},{5,4},{7,6},{8,9},{10,11},{9,8... | collective-permute-start | bytes 98312 | tf_op jit(solution)/shard_map/ppermute | solution.py:758
  23.2 24.8 %collective-permute-start.3 = (f32[48,16,256]{2,1,0:T(8,128)}, f32[48,16,256]{2,1,0:T(8,128)S(1)}, u32[]{:S(2)}, u32[]{:S(2)}) collective-permute-start(f32[48,16,256]{2,1,0:T(8,128)} %get-tuple-element.29), channel_id=1, source_target_pairs={{0,4},{8,12},{16,20},{24,28},{4,0},{12,8},{20,16},{28,24},{1,5},{9... | collective-permute-start | bytes 2359304 | tf_op jit(solution)/shard_map/ppermute | solution.py:366
  23.3 24.7 %collective-permute-start.4 = (f32[48,16,256]{2,1,0:T(8,128)}, f32[48,16,256]{2,1,0:T(8,128)S(1)}, u32[]{:S(2)}, u32[]{:S(2)}) collective-permute-start(f32[48,16,256]{2,1,0:T(8,128)} %get-tuple-element.30), channel_id=1, source_target_pairs={{4,8},{12,16},{20,24},{8,4},{16,12},{24,20},{5,9},{13,17},{21,25},... | collective-permute-start | bytes 2359304 | tf_op jit(solution)/shard_map/ppermute | solution.py:366
  24.0 4.3 %collective-permute-start.5 = (f32[8,2048]{1,0:T(8,128)S(1)}, f32[8,2048]{1,0:T(8,128)S(1)}, u32[]{:S(2)}, u32[]{:S(2)}) collective-permute-start(f32[8,2048]{1,0:T(8,128)S(1)} %pad_maximum_fusion), channel_id=1, source_target_pairs={{1,2},{2,1},{0,3},{3,0},{5,6},{6,5},{4,7},{7,4},{9,10},{10,9},{8,1... | collective-permute-start | bytes 196616 | tf_op jit(solution)/shard_map/ppermute | solution.py:761
  38.3 17.3 %all-to-all-start = ((f32[32,1,1664]{2,1,0:T(1,128)}), f32[32,1,1664]{2,1,0:T(1,128)S(1)}, u32[]{:S(2)}, u32[]{:S(2)}) async-start(f32[32,1,1664]{2,1,0:T(1,128)} %shard_map.135), calls=%async_computation | async-start | bytes 425984 | tf_op jit(solution)/shard_map/all_to_all | solution.py:807
  58.7 7.3 %collective-permute-start.6 = (f32[3,8,8,256]{3,2,1,0:T(8,128)S(1)}, f32[3,8,8,256]{3,2,1,0:T(8,128)S(1)}, u32[]{:S(2)}, u32[]{:S(2)}) collective-permute-start(f32[3,8,8,256]{3,2,1,0:T(8,128)S(1)} %get-tuple-element.42), channel_id=1, source_target_pairs={{0,1},{2,3},{1,0},{3,2},{4,5},{6,7},{5,4},{7,6},{8,9},{10,11},{9,8... | collective-permute-start | bytes 589832 | tf_op jit(solution)/shard_map/ppermute | solution.py:366
  60.9 8.4 %collective-permute-start.7 = (f32[3,8,8,256]{3,2,1,0:T(8,128)S(1)}, f32[3,8,8,256]{3,2,1,0:T(8,128)S(1)}, u32[]{:S(2)}, u32[]{:S(2)}) collective-permute-start(f32[3,8,8,256]{3,2,1,0:T(8,128)S(1)} %get-tuple-element.43), channel_id=1, source_target_pairs={{1,2},{2,1},{5,6},{6,5},{9,10},{10,9},{13,14},{14,13},{17,18},{18,... | collective-permute-start | bytes 589832 | tf_op jit(solution)/shard_map/ppermute | solution.py:366

commit v13 on v11

--- a/solution.py
+++ b/solution.py
@@ -260,7 +260,10 @@
             masks, left = {}, []
             for _, ranks, plane, planes, ref, start in own_jobs:
                 if (plane, planes) not in masks:
-                    ids = row_ids((planes * cy, chunk)) + plane * cy
+                    if plane is None:
+                        ids = face_row_ids(planes, cy, chunk)
+                    else:
+                        ids = row_ids((planes * cy, chunk)) + plane * cy
                     masks[plane, planes] = (ids == row).astype(F32).astype(BF16)
                 for r in ranks:
                     at = base + r // 2
@@ -268,8 +271,8 @@
             left = jnp.concatenate(left, axis=0)
             got = lax.dot_general(left, zt, (((1,), (1,)), ((), ())), preferred_element_type=F32)
             at = 0
-            for _, ranks, _, planes, ref, start in own_jobs:
-                size = planes * cy
+            for _, ranks, plane, planes, ref, start in own_jobs:
+                size = planes * (TILE if plane is None else cy)
                 for i in range(len(ranks)):
                     ref[i, start : start + size] += got[at : at + size] + got[at + size : at + 2 * size]
                     at += 2 * size
@@ -281,13 +284,23 @@
 STEP_ROWS = ((0, 1, 2), (3, 4, 5), (7, 8, 9))
 
 
+def face_row_ids(planes, cy, width):
+    rid = row_ids((planes * TILE, width))
+    at = rid % TILE
+    middle = TILE // 2
+    y = jnp.where(at < middle, cy - middle + at, at - middle)
+    used = (at >= middle - NEAR) & (at < middle + NEAR)
+    return jnp.where(used, rid // TILE * cy + y, -1)
+
+
 def near_scatter_kernel(
-    ready, par_ref, val_ref, sign_ref, zero_out, one_out, even_out, odd_out, zero_ref, one_ref, even_ref, odd_ref
+    ready, par_ref, val_ref, sign_ref, zero_out, even_out, odd_out, zero_ref, one_ref, even_ref, odd_ref
 ):
-    _, cx, cy, nz = one_out.shape
+    _, planes, cy, nz = zero_out.shape
+    cx = planes - 2 * NEAR
     jobs = (
         (0, STEP_ROWS[0], 0, cx, zero_ref, NEAR * cy),
-        (0, STEP_ROWS[1], 0, cx, one_ref, 0),
+        (0, STEP_ROWS[1], None, cx, one_ref, 0),
         (HIGH_LIST, STEP_ROWS[0], 0, NEAR, zero_ref, (NEAR + cx) * cy),
         (LOW_LIST, STEP_ROWS[0], cx - NEAR, NEAR, zero_ref, 0),
     )
@@ -296,7 +309,6 @@
     sign = sign_ref[...]
     for i in range(3):
         zero_out[i] = zero_ref[i].reshape(zero_out.shape[1:]) * sign[MID - NEAR : MID + cx + NEAR]
-        one_out[i] = one_ref[i].reshape(one_out.shape[1:]) * sign[MID : MID + cx]
     at = row_ids((TILE, nz))
 
     def write(is_high, face_ref):
@@ -305,7 +317,8 @@
         corner = at < NEAR if is_high else at >= TILE - NEAR
         for i in range(3):
             for x in range(cx):
-                tile = jnp.where(half, zero_out[i, NEAR + x, ys], half_turn(one_out[i, x, ys]))
+                one = one_ref[i, x * TILE : (x + 1) * TILE] * half_turn(sign_ref[MID + x, ys])
+                tile = jnp.where(half, zero_out[i, NEAR + x, ys], one)
                 if x < 2 * NEAR:
                     moved = pltpu.roll(zero_out[i, NEAR + corner_plane(x, cx), ys], NEAR if is_high else TILE - NEAR, 0)
                     tile = jnp.where(corner, moved, tile)
@@ -315,15 +328,17 @@
 
 
 def rest_scatter_kernel(
-    ready, val_ref, sign_ref, zero_out, one_out, two_out, zero_ref, one_ref, two_ref, even_ref, odd_ref
+    ready, val_ref, sign_ref, zero_out, one_out, side_out, two_out,
+    zero_ref, one_ref, side_ref, two_ref, even_ref, odd_ref,
 ):
     _, cx, cy, nz = two_out.shape
     jobs = (
+        (0, STEP_ROWS[1], 0, cx, one_ref, 0),
         (0, STEP_ROWS[2], 0, cx, two_ref, 0),
         (HIGH_LIST, STEP_ROWS[0], NEAR, MID - NEAR, zero_ref, NEAR * cy),
         (LOW_LIST, STEP_ROWS[0], cx - MID, MID - NEAR, zero_ref, 0),
-        (HIGH_LIST, STEP_ROWS[1], 0, NEAR, one_ref, NEAR * cy),
-        (LOW_LIST, STEP_ROWS[1], cx - NEAR, NEAR, one_ref, 0),
+        (HIGH_LIST, STEP_ROWS[1], 0, NEAR, side_ref, NEAR * cy),
+        (LOW_LIST, STEP_ROWS[1], cx - NEAR, NEAR, side_ref, 0),
     )
     scatter_lists(val_ref, even_ref, odd_ref, jobs, cy, nz)
     ready()
@@ -333,7 +348,8 @@
     side = jnp.concatenate([sign[MID - NEAR : MID], sign[MID + cx : MID + cx + NEAR]], axis=0)
     for i in range(3):
         zero_out[i] = zero_ref[i].reshape(zero_out.shape[1:]) * far
-        one_out[i] = one_ref[i].reshape(one_out.shape[1:]) * side
+        one_out[i] = one_ref[i].reshape(one_out.shape[1:]) * sign[MID : MID + cx]
+        side_out[i] = side_ref[i].reshape(side_out.shape[1:]) * side
         two_out[i] = two_ref[i].reshape(two_out.shape[1:]) * sign[MID : MID + cx]
 
 
@@ -803,20 +819,23 @@
         to_hbm=True,
     )
     held = (device_count // 2 * ROWS_HELD, 2 * HALF)
-    zero, one, face_even, face_odd = call(
+    zero, face_even, face_odd = call(
         near_scatter_kernel,
         (py, arrived, wide_sign),
-        [(3, cx + 2 * NEAR, cy, nz), (3, cx, cy, nz)] + [(3, cx, TILE, nz)] * 2,
-        [(3, (cx + 2 * NEAR) * cy, nz), (3, cx * cy, nz), held, held],
+        [(3, cx + 2 * NEAR, cy, nz)] + [(3, cx, TILE, nz)] * 2,
+        [(3, (cx + 2 * NEAR) * cy, nz), (3, cx * TILE, nz), held, held],
         scalars=1,
         from_hbm=(2,),
     )
     fye, fyo = swap_faces((face_even, face_odd), "comp")
-    zero_far, one_side, two = call(
+    zero_far, one, one_side, two = call(
         rest_scatter_kernel,
         (arrived, wide_sign),
-        [(3, 2 * NEAR, cy, nz), (3, 2 * NEAR, cy, nz), (3, cx, cy, nz)],
-        [(3, 2 * NEAR * cy, nz), (3, 2 * NEAR * cy, nz), (3, cx * cy, nz), held, held],
+        [(3, 2 * NEAR, cy, nz), (3, cx, cy, nz), (3, 2 * NEAR, cy, nz), (3, cx, cy, nz)],
+        [
+            (3, 2 * NEAR * cy, nz), (3, cx * cy, nz), (3, 2 * NEAR * cy, nz), (3, cx * cy, nz),
+            held, held,
+        ],
         from_hbm=(1,),
     )
     final, prior = call(

time: 74.2 us -> 73.8 us (level)
  waiting for transfers between devices: 12.1 us -> 11.2 us
    ppermute x6, waiting for transfers between devices: 3.49 us -> 2.55 us  [swap_faces(): out.append(lax.ppermute(faces[k], axis, pair_list(count, k)))]
  transfers between devices with their start and end apart: 9 -> 9, of which waited for: 5 -> 4; matrix products, arithmetic and copies ran while one was open for 0% -> 0% of each run, Pallas kernels for 38% -> 40%
where the time goes in v13:
time: 73.8 us; the launch traced here: 73.6 us
  Pallas kernels  39.5 us (54%)
  starting transfers between devices  22 us (30%)
  waiting for transfers between devices  11.2 us (15%)
  between operations  0.82 us (1%)
    pallas_call x8, Pallas kernels, call(): pl.pallas_call(kernel, out_shape=shapes, in_specs=in_specs, out_specs=out...  39.5 us
    ppermute x6, starting transfers between devices, swap_faces(): out.append(lax.ppermute(faces[k], axis, pair_list(count, k)))  10.6 us
    all_to_all x1, starting transfers between devices, local(): lax.all_to_all(packed, ('slab', 'comp'), split_axis=0, concat_axis=0, til...  9.66 us
    ppermute x1, waiting for transfers between devices, local(): near_block = lax.ppermute(own_block, 'comp', pair_list(4, 0))  4.93 us
    ppermute x1, waiting for transfers between devices, local(): lax.ppermute(jnp.concatenate(first_blocks, axis=1), 'comp', ring)  2.72 us
    ppermute x6, waiting for transfers between devices, swap_faces(): out.append(lax.ppermute(faces[k], axis, pair_list(count, k)))  2.55 us
    ppermute x1, starting transfers between devices, local(): lax.ppermute(jnp.concatenate(first_blocks, axis=1), 'comp', ring)  1.63 us
  transfers between devices with their start and end apart: 9, of which 4 were waited for; matrix products, arithmetic and copies ran while one was open for 0% of the time, Pallas kernels for 40%

profile of v13, /device:TPU:8, one launch (start us, length us, event | category | flops | bytes accessed | tf_op | source)
XLA Modules:
  0.0 73.6 jit_solution(5939314689038470752)
XLA Ops:
  0.6 1.5 %shard_map.131 = (f32[8,1024]{1,0:T(8,128)S(1)}, bf16[48,1024]{1,0:T(8,128)(2,1)S(1)}, f32[5,8,8,256]{3,2,1,0:T(8,128)S(1)}, f32[5,8,8,256]{3,2,1,0:T(8,128)S(1)}) custom-call(s32[1]{0:T(128)} %bitcast.1.refs_0_.py_ref.refs_1_, f32[3,8,16,256]{3,2,1,0:T(8,128)} %refs_2_.3, f32[3,8,16,256]{3,2,1,0:T(8,128)} %refs_3_.3, f32[8,16,256]{2,1,0:T(8,128)} %refs_4_.5, ...), custom_call_target="tpu_custom_call" | custom-call | tf_op jit(solution)/shard_map/pallas_call | solution.py:733
  2.2 0.1 collective-permute-start
  2.2 5.0 %collective-permute-start.1 = (f32[5,8,8,256]{3,2,1,0:T(8,128)S(1)}, f32[5,8,8,256]{3,2,1,0:T(8,128)S(1)}, u32[]{:S(2)}, u32[]{:S(2)}) collective-permute-start(f32[5,8,8,256]{3,2,1,0:T(8,128)S(1)} %get-tuple-element.24), channel_id=1, source_target_pairs={{1,2},{2,1},{5,6},{6,5},{9,10},{10,9},{13,14},{14,13},{17,18},{18,... | collective-permute-start | bytes 983048 | tf_op jit(solution)/shard_map/ppermute | solution.py:382
  7.3 0.1 collective-permute-start.2
  7.4 0.1 pad_add_fusion.refs_0_.px_ref
  7.5 4.9 %collective-permute-done.2.refs_2_ = f32[8,1024]{1,0:T(8,128)S(1)} collective-permute-done((f32[8,1024]{1,0:T(8,128)S(1)}, f32[8,1024]{1,0:T(8,128)S(1)}, u32[]{:S(2)}, u32[]{:S(2)}) %collective-permute-start.2) | collective-permute-done | bytes 32800 | tf_op jit(solution)/shard_map/ppermute | solution.py:759
  12.4 9.5 %shard_map.132 = (f32[32,1024]{1,0:T(8,128)S(1)}, f32[16,256]{1,0:T(8,128)S(1)}, f32[48,16,256]{2,1,0:T(8,128)}, f32[48,16,256]{2,1,0:T(8,128)}) custom-call(s32[2]{0:T(128)S(1)} %pad_add_fusion.refs_0_.px_ref, f32[8,1024]{1,0:T(8,128)S(1)} %get-tuple-element.25.refs_1_, f32[8,1024]{1,0:T(8,128)S(1)} %collective-permute-done.2.refs_2_, ...), custom_call_target="tpu_custom_call" | custom-call | tf_op jit(solution)/shard_map/pallas_call | solution.py:733
  21.8 0.0 collective-permute-done.even_ref.refs_6_
  21.9 0.0 collective-permute-done.1.odd_ref.refs_7_
  21.9 1.3 %shard_map.133 = (f32[48,16,256]{2,1,0:T(8,128)}, f32[48,16,256]{2,1,0:T(8,128)}) custom-call(s32[2]{0:T(128)S(1)} %pad_add_fusion.refs_0_.px_ref, s32[1]{0:T(128)} %bitcast.1.refs_0_.py_ref.refs_1_, f32[5,8,8,256]{3,2,1,0:T(8,128)S(1)} %collective-permute-done.even_ref.refs_6_, ...), custom_call_target="tpu_custom_call", output_to_operand_aliasing={{0}: (4, {}), {1}: (5, {})} | custom-call | tf_op jit(solution)/shard_map/pallas_call | solution.py:733
  23.2 0.1 collective-permute-start.3
  23.3 0.7 collective-permute-start.4
  24.0 1.6 %collective-permute-start.5 = (f32[8,2048]{1,0:T(8,128)S(1)}, f32[8,2048]{1,0:T(8,128)S(1)}, u32[]{:S(2)}, u32[]{:S(2)}) collective-permute-start(f32[8,2048]{1,0:T(8,128)S(1)} %pad_maximum_fusion), channel_id=1, source_target_pairs={{1,2},{2,1},{0,3},{3,0},{5,6},{6,5},{4,7},{7,4},{9,10},{10,9},{8,1... | collective-permute-start | bytes 196616 | tf_op jit(solution)/shard_map/ppermute | solution.py:762
  25.7 2.7 %collective-permute-done.5.refs_0_ = f32[8,2048]{1,0:T(8,128)S(1)} collective-permute-done((f32[8,2048]{1,0:T(8,128)S(1)}, f32[8,2048]{1,0:T(8,128)S(1)}, u32[]{:S(2)}, u32[]{:S(2)}) %collective-permute-start.5) | collective-permute-done | bytes 65568 | tf_op jit(solution)/shard_map/ppermute | solution.py:762
  28.4 10.0 %shard_map.135 = f32[32,1,1664]{2,1,0:T(1,128)} custom-call(f32[8,2048]{1,0:T(8,128)S(1)} %collective-permute-done.5.refs_0_, f32[32,1024]{1,0:T(8,128)S(1)} %get-tuple-element.34.refs_1_, f32[16,256]{1,0:T(8,128)S(1)} %get-tuple-element.35.refs_2_, bf16[48,1024]{1,0:T(8,128)(2,1)S(1)} %get-tuple-element.26.refs_3_, s32[1,1024]{1,0:T(1,128)} %bitcast.9, ...), custom_call_target="tpu_custom_call" | custom-call | tf_op jit(solution)/shard_map/pallas_call | solution.py:733
  38.3 9.7 %all-to-all-start = ((f32[32,1,1664]{2,1,0:T(1,128)}), f32[32,1,1664]{2,1,0:T(1,128)S(1)}, u32[]{:S(2)}, u32[]{:S(2)}) async-start(f32[32,1,1664]{2,1,0:T(1,128)} %shard_map.135), calls=%async_computation | async-start | bytes 425984 | tf_op jit(solution)/shard_map/all_to_all | solution.py:808
  48.0 0.0 collective-permute-done.3.refs_8_
  48.0 0.0 collective-permute-done.4.refs_9_
  48.0 6.6 %shard_map.134 = (f32[3,8,16,256]{3,2,1,0:T(8,128)}, f32[3,8,16,256]{3,2,1,0:T(8,128)}, f32[12,2,32,128]{3,2,1,0:T(8,128)}, f32[16,16,256]{2,1,0:T(8,128)}) custom-call(s32[2]{0:T(128)S(1)} %pad_add_fusion.refs_0_.px_ref, s32[1]{0:T(128)} %bitcast.1.refs_0_.py_ref.refs_1_, f32[3,8,16,256]{3,2,1,0:T(8,128)} %refs_2_.3, f32[3,8,16,256]{3,2,1,0:T(8,128)} %refs_3_.3, ...), custom_call_target="tpu_custom_call" | custom-call | tf_op jit(solution)/shard_map/pallas_call | solution.py:733
  54.7 1.0 %all-to-all-done.refs_1_.refs_0_ = f32[32,1,1664]{2,1,0:T(1,128)S(1)} async-done(((f32[32,1,1664]{2,1,0:T(1,128)}), f32[32,1,1664]{2,1,0:T(1,128)S(1)}, u32[]{:S(2)}, u32[]{:S(2)}) %all-to-all-start) | async-done | bytes 213024 | tf_op jit(solution)/shard_map/all_to_all | solution.py:808
  55.7 2.7 %shard_map.136 = (f32[3,12,16,256]{3,2,1,0:T(8,128)S(1)}, f32[3,8,8,256]{3,2,1,0:T(8,128)S(1)}, f32[3,8,8,256]{3,2,1,0:T(8,128)S(1)}) custom-call(s32[1]{0:T(128)} %bitcast.1.refs_0_.py_ref.refs_1_, f32[32,1,1664]{2,1,0:T(1,128)S(1)} %all-to-all-done.refs_1_.refs_0_, f32[16,16,256]{2,1,0:T(8,128)} %get-tuple-element.36.refs_2_.refs_1_), custom_call_target="tpu_custom_call" | custom-call | tf_op jit(solution)/shard_map/pallas_call | solution.py:733
  58.4 2.2 %collective-permute-start.6 = (f32[3,8,8,256]{3,2,1,0:T(8,128)S(1)}, f32[3,8,8,256]{3,2,1,0:T(8,128)S(1)}, u32[]{:S(2)}, u32[]{:S(2)}) collective-permute-start(f32[3,8,8,256]{3,2,1,0:T(8,128)S(1)} %get-tuple-element.42), channel_id=1, source_target_pairs={{0,1},{2,3},{1,0},{3,2},{4,5},{6,7},{5,4},{7,6},{8,9},{10,11},{9,8... | collective-permute-start | bytes 589832 | tf_op jit(solution)/shard_map/ppermute | solution.py:382
  60.6 2.5 %collective-permute-start.7 = (f32[3,8,8,256]{3,2,1,0:T(8,128)S(1)}, f32[3,8,8,256]{3,2,1,0:T(8,128)S(1)}, u32[]{:S(2)}, u32[]{:S(2)}) collective-permute-start(f32[3,8,8,256]{3,2,1,0:T(8,128)S(1)} %get-tuple-element.43), channel_id=1, source_target_pairs={{1,2},{2,1},{5,6},{6,5},{9,10},{10,9},{13,14},{14,13},{17,18},{18,... | collective-permute-start | bytes 589832 | tf_op jit(solution)/shard_map/ppermute | solution.py:382
  63.1 3.3 %shard_map.137 = (f32[3,4,16,256]{3,2,1,0:T(8,128)S(1)}, f32[3,8,16,256]{3,2,1,0:T(8,128)S(1)}, f32[3,4,16,256]{3,2,1,0:T(8,128)S(1)}, f32[3,8,16,256]{3,2,1,0:T(8,128)S(1)}) custom-call(f32[32,1,1664]{2,1,0:T(1,128)S(1)} %all-to-all-done.refs_1_.refs_0_, f32[16,16,256]{2,1,0:T(8,128)} %get-tuple-element.36.refs_2_.refs_1_), custom_call_target="tpu_custom_call" | custom-call | tf_op jit(solution)/shard_map/pallas_call | solution.py:733
  66.5 0.0 collective-permute-done.6.refs_10_
  66.5 2.5 %collective-permute-done.7.refs_11_ = f32[3,8,8,256]{3,2,1,0:T(8,128)S(1)} collective-permute-done((f32[3,8,8,256]{3,2,1,0:T(8,128)S(1)}, f32[3,8,8,256]{3,2,1,0:T(8,128)S(1)}, u32[]{:S(2)}, u32[]{:S(2)}) %collective-permute-start.7) | collective-permute-done | bytes 196640 | tf_op jit(solution)/shard_map/ppermute | solution.py:382
  69.0 4.6 %shard_map.138 = (f32[3,8,16,256]{3,2,1,0:T(8,128)}, f32[3,8,16,256]{3,2,1,0:T(8,128)}) custom-call(s32[2]{0:T(128)S(1)} %pad_add_fusion.refs_0_.px_ref, s32[1]{0:T(128)} %bitcast.1.refs_0_.py_ref.refs_1_, f32[3,8,16,256]{3,2,1,0:T(8,128)} %get-tuple-element.31.refs_2_, f32[3,8,16,256]{3,2,1,0:T(8,128)} %get-tuple-element.32.refs_3_, ...), custom_call_target="tpu_custom_call" | custom-call | tf_op jit(solution)/shard_map/pallas_call | solution.py:733
  (1 shorter events, 0.0 us)
Async XLA Ops:
  2.2 19.7 %collective-permute-start = (f32[5,8,8,256]{3,2,1,0:T(8,128)S(1)}, f32[5,8,8,256]{3,2,1,0:T(8,128)S(1)}, u32[]{:S(2)}, u32[]{:S(2)}) collective-permute-start(f32[5,8,8,256]{3,2,1,0:T(8,128)S(1)} %get-tuple-element.23), channel_id=1, source_target_pairs={{0,1},{2,3},{1,0},{3,2},{4,5},{6,7},{5,4},{7,6},{8,9},{10,11},{9,8... | collective-permute-start | bytes 983048 | tf_op jit(solution)/shard_map/ppermute | solution.py:382
  2.2 19.6 %collective-permute-start.1 = (f32[5,8,8,256]{3,2,1,0:T(8,128)S(1)}, f32[5,8,8,256]{3,2,1,0:T(8,128)S(1)}, u32[]{:S(2)}, u32[]{:S(2)}) collective-permute-start(f32[5,8,8,256]{3,2,1,0:T(8,128)S(1)} %get-tuple-element.24), channel_id=1, source_target_pairs={{1,2},{2,1},{5,6},{6,5},{9,10},{10,9},{13,14},{14,13},{17,18},{18,... | collective-permute-start | bytes 983048 | tf_op jit(solution)/shard_map/ppermute | solution.py:382
  7.3 5.1 %collective-permute-start.2 = (f32[8,1024]{1,0:T(8,128)S(1)}, f32[8,1024]{1,0:T(8,128)S(1)}, u32[]{:S(2)}, u32[]{:S(2)}) collective-permute-start(f32[8,1024]{1,0:T(8,128)S(1)} %get-tuple-element.25.refs_1_), channel_id=1, source_target_pairs={{0,1},{2,3},{1,0},{3,2},{4,5},{6,7},{5,4},{7,6},{8,9},{10,11},{9,8... | collective-permute-start | bytes 98312 | tf_op jit(solution)/shard_map/ppermute | solution.py:759
  23.2 24.8 %collective-permute-start.3 = (f32[48,16,256]{2,1,0:T(8,128)}, f32[48,16,256]{2,1,0:T(8,128)S(1)}, u32[]{:S(2)}, u32[]{:S(2)}) collective-permute-start(f32[48,16,256]{2,1,0:T(8,128)} %get-tuple-element.29), channel_id=1, source_target_pairs={{0,4},{8,12},{16,20},{24,28},{4,0},{12,8},{20,16},{28,24},{1,5},{9... | collective-permute-start | bytes 2359304 | tf_op jit(solution)/shard_map/ppermute | solution.py:382
  23.3 24.7 %collective-permute-start.4 = (f32[48,16,256]{2,1,0:T(8,128)}, f32[48,16,256]{2,1,0:T(8,128)S(1)}, u32[]{:S(2)}, u32[]{:S(2)}) collective-permute-start(f32[48,16,256]{2,1,0:T(8,128)} %get-tuple-element.30), channel_id=1, source_target_pairs={{4,8},{12,16},{20,24},{8,4},{16,12},{24,20},{5,9},{13,17},{21,25},... | collective-permute-start | bytes 2359304 | tf_op jit(solution)/shard_map/ppermute | solution.py:382
  24.0 4.3 %collective-permute-start.5 = (f32[8,2048]{1,0:T(8,128)S(1)}, f32[8,2048]{1,0:T(8,128)S(1)}, u32[]{:S(2)}, u32[]{:S(2)}) collective-permute-start(f32[8,2048]{1,0:T(8,128)S(1)} %pad_maximum_fusion), channel_id=1, source_target_pairs={{1,2},{2,1},{0,3},{3,0},{5,6},{6,5},{4,7},{7,4},{9,10},{10,9},{8,1... | collective-permute-start | bytes 196616 | tf_op jit(solution)/shard_map/ppermute | solution.py:762
  38.3 17.3 %all-to-all-start = ((f32[32,1,1664]{2,1,0:T(1,128)}), f32[32,1,1664]{2,1,0:T(1,128)S(1)}, u32[]{:S(2)}, u32[]{:S(2)}) async-start(f32[32,1,1664]{2,1,0:T(1,128)} %shard_map.135), calls=%async_computation | async-start | bytes 425984 | tf_op jit(solution)/shard_map/all_to_all | solution.py:808
  58.4 8.1 %collective-permute-start.6 = (f32[3,8,8,256]{3,2,1,0:T(8,128)S(1)}, f32[3,8,8,256]{3,2,1,0:T(8,128)S(1)}, u32[]{:S(2)}, u32[]{:S(2)}) collective-permute-start(f32[3,8,8,256]{3,2,1,0:T(8,128)S(1)} %get-tuple-element.42), channel_id=1, source_target_pairs={{0,1},{2,3},{1,0},{3,2},{4,5},{6,7},{5,4},{7,6},{8,9},{10,11},{9,8... | collective-permute-start | bytes 589832 | tf_op jit(solution)/shard_map/ppermute | solution.py:382
  60.6 8.4 %collective-permute-start.7 = (f32[3,8,8,256]{3,2,1,0:T(8,128)S(1)}, f32[3,8,8,256]{3,2,1,0:T(8,128)S(1)}, u32[]{:S(2)}, u32[]{:S(2)}) collective-permute-start(f32[3,8,8,256]{3,2,1,0:T(8,128)S(1)} %get-tuple-element.43), channel_id=1, source_target_pairs={{1,2},{2,1},{5,6},{6,5},{9,10},{10,9},{13,14},{14,13},{17,18},{18,... | collective-permute-start | bytes 589832 | tf_op jit(solution)/shard_map/ppermute | solution.py:382

commit v14 on v13

--- a/solution.py
+++ b/solution.py
@@ -19,10 +19,12 @@
 AHEAD = 2
 HALF = 64
 OWN_TILES = 5
-SIDE_TILES = 4
+SIDE_TILES = 3
+OFFSET_TILE = 3
 HIGH_LIST = OWN_TILES
 LOW_LIST = OWN_TILES + SIDE_TILES
-LIST_ROWS = OWN_TILES + 2 * SIDE_TILES
+SIDE_OFFSETS = OWN_TILES + 2 * SIDE_TILES
+LIST_ROWS = SIDE_OFFSETS + 1
 VMEM_GRANT = 16 * 2**20
 
 F32 = jnp.float32
@@ -206,13 +208,20 @@
     def put(j, tile):
         out_ref[:, 0, 2 * HALF * j : 2 * HALF * (j + 1)] = tile
 
+    def shifted(tile):
+        above = jnp.where(owner_row < owners - step, pltpu.roll(tile, owners - step, 0), 0.0)
+        return above, jnp.where(owner_row >= step, pltpu.roll(tile, step, 0), 0.0)
+
     for j in range(OWN_TILES):
         tile = tiles[j * owners : (j + 1) * owners]
         put(j, tile)
+        above, below = shifted(tile)
         if j < SIDE_TILES:
-            above = pltpu.roll(tile, owners - step, 0)
-            put(HIGH_LIST + j, jnp.where(owner_row < owners - step, above, 0.0))
-            put(LOW_LIST + j, jnp.where(owner_row >= step, pltpu.roll(tile, step, 0), 0.0))
+            put(HIGH_LIST + j, above)
+            put(LOW_LIST + j, below)
+        if j == OFFSET_TILE:
+            first = lax.broadcasted_iota(jnp.int32, (owners, 2 * HALF), 1) < HALF
+            put(SIDE_OFFSETS, jnp.where(first, above, pltpu.roll(below, HALF, 1)))
 
 
 TILE = 8
@@ -254,7 +263,8 @@
         low = [(v - h.astype(F32)).astype(BF16) for v, h in zip(values, high)]
         for base in (0, HIGH_LIST, LOW_LIST):
             own_jobs = [job for job in jobs if job[0] == base]
-            off = values[0][base + 3 : base + 4, :].astype(jnp.int32)
+            at = OFFSET_TILE if base == 0 else SIDE_OFFSETS
+            off = values[1 if base == LOW_LIST else 0][at : at + 1, :].astype(jnp.int32)
             row = off // nz
             zt = (row_ids((nz, chunk)) == off - row * nz).astype(F32).astype(BF16)
             masks, left = {}, []

time: 73.8 us -> 73.5 us (level)
  no operation moved by 1% of the time
where the time goes in v14:
time: 73.5 us; the launch traced here: 73.2 us
  Pallas kernels  39.4 us (54%)
  starting transfers between devices  22 us (30%)
  waiting for transfers between devices  10.9 us (15%)
  between operations  0.82 us (1%)
    pallas_call x8, Pallas kernels, call(): pl.pallas_call(kernel, out_shape=shapes, in_specs=in_specs, out_specs=out...  39.4 us
    ppermute x6, starting transfers between devices, swap_faces(): out.append(lax.ppermute(faces[k], axis, pair_list(count, k)))  10.6 us
    all_to_all x1, starting transfers between devices, local(): lax.all_to_all(packed, ('slab', 'comp'), split_axis=0, concat_axis=0, til...  9.66 us
    ppermute x1, waiting for transfers between devices, local(): near_block = lax.ppermute(own_block, 'comp', pair_list(4, 0))  4.93 us
    ppermute x1, waiting for transfers between devices, local(): lax.ppermute(jnp.concatenate(first_blocks, axis=1), 'comp', ring)  2.72 us
    ppermute x6, waiting for transfers between devices, swap_faces(): out.append(lax.ppermute(faces[k], axis, pair_list(count, k)))  2.58 us
    ppermute x1, starting transfers between devices, local(): lax.ppermute(jnp.concatenate(first_blocks, axis=1), 'comp', ring)  1.63 us
  transfers between devices with their start and end apart: 9, of which 4 were waited for; matrix products, arithmetic and copies ran while one was open for 0% of the time, Pallas kernels for 40%

profile of v14, /device:TPU:8, one launch (start us, length us, event | category | flops | bytes accessed | tf_op | source)
XLA Modules:
  0.0 73.2 jit_solution(12060532290988287079)
XLA Ops:
  0.6 1.5 %shard_map.131 = (f32[8,1024]{1,0:T(8,128)S(1)}, bf16[48,1024]{1,0:T(8,128)(2,1)S(1)}, f32[5,8,8,256]{3,2,1,0:T(8,128)S(1)}, f32[5,8,8,256]{3,2,1,0:T(8,128)S(1)}) custom-call(s32[1]{0:T(128)} %bitcast.1.refs_0_.py_ref.refs_1_, f32[3,8,16,256]{3,2,1,0:T(8,128)} %refs_2_.3, f32[3,8,16,256]{3,2,1,0:T(8,128)} %refs_3_.3, f32[8,16,256]{2,1,0:T(8,128)} %refs_4_.5, ...), custom_call_target="tpu_custom_call" | custom-call | tf_op jit(solution)/shard_map/pallas_call | solution.py:743
  2.2 0.1 collective-permute-start
  2.2 5.0 %collective-permute-start.1 = (f32[5,8,8,256]{3,2,1,0:T(8,128)S(1)}, f32[5,8,8,256]{3,2,1,0:T(8,128)S(1)}, u32[]{:S(2)}, u32[]{:S(2)}) collective-permute-start(f32[5,8,8,256]{3,2,1,0:T(8,128)S(1)} %get-tuple-element.24), channel_id=1, source_target_pairs={{1,2},{2,1},{5,6},{6,5},{9,10},{10,9},{13,14},{14,13},{17,18},{18,... | collective-permute-start | bytes 983048 | tf_op jit(solution)/shard_map/ppermute | solution.py:392
  7.3 0.1 collective-permute-start.2
  7.4 0.1 pad_add_fusion.refs_0_.px_ref
  7.5 4.9 %collective-permute-done.2.refs_2_ = f32[8,1024]{1,0:T(8,128)S(1)} collective-permute-done((f32[8,1024]{1,0:T(8,128)S(1)}, f32[8,1024]{1,0:T(8,128)S(1)}, u32[]{:S(2)}, u32[]{:S(2)}) %collective-permute-start.2) | collective-permute-done | bytes 32800 | tf_op jit(solution)/shard_map/ppermute | solution.py:769
  12.4 9.5 %shard_map.132 = (f32[32,1024]{1,0:T(8,128)S(1)}, f32[16,256]{1,0:T(8,128)S(1)}, f32[48,16,256]{2,1,0:T(8,128)}, f32[48,16,256]{2,1,0:T(8,128)}) custom-call(s32[2]{0:T(128)S(1)} %pad_add_fusion.refs_0_.px_ref, f32[8,1024]{1,0:T(8,128)S(1)} %get-tuple-element.25.refs_1_, f32[8,1024]{1,0:T(8,128)S(1)} %collective-permute-done.2.refs_2_, ...), custom_call_target="tpu_custom_call" | custom-call | tf_op jit(solution)/shard_map/pallas_call | solution.py:743
  21.8 0.0 collective-permute-done.even_ref.refs_6_
  21.9 0.0 collective-permute-done.1.odd_ref.refs_7_
  21.9 1.3 %shard_map.133 = (f32[48,16,256]{2,1,0:T(8,128)}, f32[48,16,256]{2,1,0:T(8,128)}) custom-call(s32[2]{0:T(128)S(1)} %pad_add_fusion.refs_0_.px_ref, s32[1]{0:T(128)} %bitcast.1.refs_0_.py_ref.refs_1_, f32[5,8,8,256]{3,2,1,0:T(8,128)S(1)} %collective-permute-done.even_ref.refs_6_, ...), custom_call_target="tpu_custom_call", output_to_operand_aliasing={{0}: (4, {}), {1}: (5, {})} | custom-call | tf_op jit(solution)/shard_map/pallas_call | solution.py:743
  23.2 0.1 collective-permute-start.3
  23.3 0.7 collective-permute-start.4
  24.0 1.6 %collective-permute-start.5 = (f32[8,2048]{1,0:T(8,128)S(1)}, f32[8,2048]{1,0:T(8,128)S(1)}, u32[]{:S(2)}, u32[]{:S(2)}) collective-permute-start(f32[8,2048]{1,0:T(8,128)S(1)} %pad_maximum_fusion), channel_id=1, source_target_pairs={{1,2},{2,1},{0,3},{3,0},{5,6},{6,5},{4,7},{7,4},{9,10},{10,9},{8,1... | collective-permute-start | bytes 196616 | tf_op jit(solution)/shard_map/ppermute | solution.py:772
  25.7 2.7 %collective-permute-done.5.refs_0_ = f32[8,2048]{1,0:T(8,128)S(1)} collective-permute-done((f32[8,2048]{1,0:T(8,128)S(1)}, f32[8,2048]{1,0:T(8,128)S(1)}, u32[]{:S(2)}, u32[]{:S(2)}) %collective-permute-start.5) | collective-permute-done | bytes 65568 | tf_op jit(solution)/shard_map/ppermute | solution.py:772
  28.4 10.0 %shard_map.135 = f32[32,1,1536]{2,1,0:T(1,128)} custom-call(f32[8,2048]{1,0:T(8,128)S(1)} %collective-permute-done.5.refs_0_, f32[32,1024]{1,0:T(8,128)S(1)} %get-tuple-element.34.refs_1_, f32[16,256]{1,0:T(8,128)S(1)} %get-tuple-element.35.refs_2_, bf16[48,1024]{1,0:T(8,128)(2,1)S(1)} %get-tuple-element.26.refs_3_, s32[1,1024]{1,0:T(1,128)} %bitcast.9, ...), custom_call_target="tpu_custom_call" | custom-call | tf_op jit(solution)/shard_map/pallas_call | solution.py:743
  38.4 9.7 %all-to-all-start = ((f32[32,1,1536]{2,1,0:T(1,128)}), f32[32,1,1536]{2,1,0:T(1,128)S(1)}, u32[]{:S(2)}, u32[]{:S(2)}) async-start(f32[32,1,1536]{2,1,0:T(1,128)} %shard_map.135), calls=%async_computation | async-start | bytes 393216 | tf_op jit(solution)/shard_map/all_to_all | solution.py:818
  48.1 0.0 collective-permute-done.3.refs_8_
  48.1 0.0 collective-permute-done.4.refs_9_
  48.1 6.6 %shard_map.134 = (f32[3,8,16,256]{3,2,1,0:T(8,128)}, f32[3,8,16,256]{3,2,1,0:T(8,128)}, f32[12,2,32,128]{3,2,1,0:T(8,128)}, f32[16,16,256]{2,1,0:T(8,128)}) custom-call(s32[2]{0:T(128)S(1)} %pad_add_fusion.refs_0_.px_ref, s32[1]{0:T(128)} %bitcast.1.refs_0_.py_ref.refs_1_, f32[3,8,16,256]{3,2,1,0:T(8,128)} %refs_2_.3, f32[3,8,16,256]{3,2,1,0:T(8,128)} %refs_3_.3, ...), custom_call_target="tpu_custom_call" | custom-call | tf_op jit(solution)/shard_map/pallas_call | solution.py:743
  54.7 0.6 all-to-all-done.refs_1_.refs_0_
  55.4 2.7 %shard_map.136 = (f32[3,12,16,256]{3,2,1,0:T(8,128)S(1)}, f32[3,8,8,256]{3,2,1,0:T(8,128)S(1)}, f32[3,8,8,256]{3,2,1,0:T(8,128)S(1)}) custom-call(s32[1]{0:T(128)} %bitcast.1.refs_0_.py_ref.refs_1_, f32[32,1,1536]{2,1,0:T(1,128)S(1)} %all-to-all-done.refs_1_.refs_0_, f32[16,16,256]{2,1,0:T(8,128)} %get-tuple-element.36.refs_2_.refs_1_), custom_call_target="tpu_custom_call" | custom-call | tf_op jit(solution)/shard_map/pallas_call | solution.py:743
  58.0 2.3 %collective-permute-start.6 = (f32[3,8,8,256]{3,2,1,0:T(8,128)S(1)}, f32[3,8,8,256]{3,2,1,0:T(8,128)S(1)}, u32[]{:S(2)}, u32[]{:S(2)}) collective-permute-start(f32[3,8,8,256]{3,2,1,0:T(8,128)S(1)} %get-tuple-element.42), channel_id=1, source_target_pairs={{0,1},{2,3},{1,0},{3,2},{4,5},{6,7},{5,4},{7,6},{8,9},{10,11},{9,8... | collective-permute-start | bytes 589832 | tf_op jit(solution)/shard_map/ppermute | solution.py:392
  60.3 2.4 %collective-permute-start.7 = (f32[3,8,8,256]{3,2,1,0:T(8,128)S(1)}, f32[3,8,8,256]{3,2,1,0:T(8,128)S(1)}, u32[]{:S(2)}, u32[]{:S(2)}) collective-permute-start(f32[3,8,8,256]{3,2,1,0:T(8,128)S(1)} %get-tuple-element.43), channel_id=1, source_target_pairs={{1,2},{2,1},{5,6},{6,5},{9,10},{10,9},{13,14},{14,13},{17,18},{18,... | collective-permute-start | bytes 589832 | tf_op jit(solution)/shard_map/ppermute | solution.py:392
  62.8 3.3 %shard_map.137 = (f32[3,4,16,256]{3,2,1,0:T(8,128)S(1)}, f32[3,8,16,256]{3,2,1,0:T(8,128)S(1)}, f32[3,4,16,256]{3,2,1,0:T(8,128)S(1)}, f32[3,8,16,256]{3,2,1,0:T(8,128)S(1)}) custom-call(f32[32,1,1536]{2,1,0:T(1,128)S(1)} %all-to-all-done.refs_1_.refs_0_, f32[16,16,256]{2,1,0:T(8,128)} %get-tuple-element.36.refs_2_.refs_1_), custom_call_target="tpu_custom_call" | custom-call | tf_op jit(solution)/shard_map/pallas_call | solution.py:743
  66.1 0.0 collective-permute-done.6.refs_10_
  66.1 2.6 %collective-permute-done.7.refs_11_ = f32[3,8,8,256]{3,2,1,0:T(8,128)S(1)} collective-permute-done((f32[3,8,8,256]{3,2,1,0:T(8,128)S(1)}, f32[3,8,8,256]{3,2,1,0:T(8,128)S(1)}, u32[]{:S(2)}, u32[]{:S(2)}) %collective-permute-start.7) | collective-permute-done | bytes 196640 | tf_op jit(solution)/shard_map/ppermute | solution.py:392
  68.6 4.6 %shard_map.138 = (f32[3,8,16,256]{3,2,1,0:T(8,128)}, f32[3,8,16,256]{3,2,1,0:T(8,128)}) custom-call(s32[2]{0:T(128)S(1)} %pad_add_fusion.refs_0_.px_ref, s32[1]{0:T(128)} %bitcast.1.refs_0_.py_ref.refs_1_, f32[3,8,16,256]{3,2,1,0:T(8,128)} %get-tuple-element.31.refs_2_, f32[3,8,16,256]{3,2,1,0:T(8,128)} %get-tuple-element.32.refs_3_, ...), custom_call_target="tpu_custom_call" | custom-call | tf_op jit(solution)/shard_map/pallas_call | solution.py:743
  (1 shorter events, 0.0 us)
Async XLA Ops:
  2.2 19.7 %collective-permute-start = (f32[5,8,8,256]{3,2,1,0:T(8,128)S(1)}, f32[5,8,8,256]{3,2,1,0:T(8,128)S(1)}, u32[]{:S(2)}, u32[]{:S(2)}) collective-permute-start(f32[5,8,8,256]{3,2,1,0:T(8,128)S(1)} %get-tuple-element.23), channel_id=1, source_target_pairs={{0,1},{2,3},{1,0},{3,2},{4,5},{6,7},{5,4},{7,6},{8,9},{10,11},{9,8... | collective-permute-start | bytes 983048 | tf_op jit(solution)/shard_map/ppermute | solution.py:392
  2.2 19.6 %collective-permute-start.1 = (f32[5,8,8,256]{3,2,1,0:T(8,128)S(1)}, f32[5,8,8,256]{3,2,1,0:T(8,128)S(1)}, u32[]{:S(2)}, u32[]{:S(2)}) collective-permute-start(f32[5,8,8,256]{3,2,1,0:T(8,128)S(1)} %get-tuple-element.24), channel_id=1, source_target_pairs={{1,2},{2,1},{5,6},{6,5},{9,10},{10,9},{13,14},{14,13},{17,18},{18,... | collective-permute-start | bytes 983048 | tf_op jit(solution)/shard_map/ppermute | solution.py:392
  7.3 5.1 %collective-permute-start.2 = (f32[8,1024]{1,0:T(8,128)S(1)}, f32[8,1024]{1,0:T(8,128)S(1)}, u32[]{:S(2)}, u32[]{:S(2)}) collective-permute-start(f32[8,1024]{1,0:T(8,128)S(1)} %get-tuple-element.25.refs_1_), channel_id=1, source_target_pairs={{0,1},{2,3},{1,0},{3,2},{4,5},{6,7},{5,4},{7,6},{8,9},{10,11},{9,8... | collective-permute-start | bytes 98312 | tf_op jit(solution)/shard_map/ppermute | solution.py:769
  23.2 24.8 %collective-permute-start.3 = (f32[48,16,256]{2,1,0:T(8,128)}, f32[48,16,256]{2,1,0:T(8,128)S(1)}, u32[]{:S(2)}, u32[]{:S(2)}) collective-permute-start(f32[48,16,256]{2,1,0:T(8,128)} %get-tuple-element.29), channel_id=1, source_target_pairs={{0,4},{8,12},{16,20},{24,28},{4,0},{12,8},{20,16},{28,24},{1,5},{9... | collective-permute-start | bytes 2359304 | tf_op jit(solution)/shard_map/ppermute | solution.py:392
  23.3 24.8 %collective-permute-start.4 = (f32[48,16,256]{2,1,0:T(8,128)}, f32[48,16,256]{2,1,0:T(8,128)S(1)}, u32[]{:S(2)}, u32[]{:S(2)}) collective-permute-start(f32[48,16,256]{2,1,0:T(8,128)} %get-tuple-element.30), channel_id=1, source_target_pairs={{4,8},{12,16},{20,24},{8,4},{16,12},{24,20},{5,9},{13,17},{21,25},... | collective-permute-start | bytes 2359304 | tf_op jit(solution)/shard_map/ppermute | solution.py:392
  24.0 4.3 %collective-permute-start.5 = (f32[8,2048]{1,0:T(8,128)S(1)}, f32[8,2048]{1,0:T(8,128)S(1)}, u32[]{:S(2)}, u32[]{:S(2)}) collective-permute-start(f32[8,2048]{1,0:T(8,128)S(1)} %pad_maximum_fusion), channel_id=1, source_target_pairs={{1,2},{2,1},{0,3},{3,0},{5,6},{6,5},{4,7},{7,4},{9,10},{10,9},{8,1... | collective-permute-start | bytes 196616 | tf_op jit(solution)/shard_map/ppermute | solution.py:772
  38.4 17.0 %all-to-all-start = ((f32[32,1,1536]{2,1,0:T(1,128)}), f32[32,1,1536]{2,1,0:T(1,128)S(1)}, u32[]{:S(2)}, u32[]{:S(2)}) async-start(f32[32,1,1536]{2,1,0:T(1,128)} %shard_map.135), calls=%async_computation | async-start | bytes 393216 | tf_op jit(solution)/shard_map/all_to_all | solution.py:818
  58.0 8.0 %collective-permute-start.6 = (f32[3,8,8,256]{3,2,1,0:T(8,128)S(1)}, f32[3,8,8,256]{3,2,1,0:T(8,128)S(1)}, u32[]{:S(2)}, u32[]{:S(2)}) collective-permute-start(f32[3,8,8,256]{3,2,1,0:T(8,128)S(1)} %get-tuple-element.42), channel_id=1, source_target_pairs={{0,1},{2,3},{1,0},{3,2},{4,5},{6,7},{5,4},{7,6},{8,9},{10,11},{9,8... | collective-permute-start | bytes 589832 | tf_op jit(solution)/shard_map/ppermute | solution.py:392
  60.3 8.3 %collective-permute-start.7 = (f32[3,8,8,256]{3,2,1,0:T(8,128)S(1)}, f32[3,8,8,256]{3,2,1,0:T(8,128)S(1)}, u32[]{:S(2)}, u32[]{:S(2)}) collective-permute-start(f32[3,8,8,256]{3,2,1,0:T(8,128)S(1)} %get-tuple-element.43), channel_id=1, source_target_pairs={{1,2},{2,1},{5,6},{6,5},{9,10},{10,9},{13,14},{14,13},{17,18},{18,... | collective-permute-start | bytes 589832 | tf_op jit(solution)/shard_map/ppermute | solution.py:392
